TPU v7x, 32 devices: a whole 2x2x4 slice. The times are simulated.
32 devices in a mesh: rep: 4 (over x, core), seq: 8 (over z, y).
Axes of the slice: x: 2, y: 2, z: 4, core: 2. Of those that a mesh axis runs over, the one named last changes fastest.
Arguments:
- tokens: bfloat16 [4, 1536, 768], P('rep', 'seq'), may hold values from -6 to 6
- segment_ids: int32 [4, 1536], P('rep', 'seq'), may hold values from 0 to 3, never falling along the last dimension, each value on 1 to 768 neighbouring positions
- query_key_value_weight: bfloat16 [768, 2304], P('seq'), may hold values from -0.21875 to 0.21875
- output_weight: bfloat16 [768, 768], P('seq'), may hold values from -1.75 to 1.75
- up_weight: bfloat16 [768, 3072], P('seq'), may hold values from -0.21875 to 0.21875
- down_weight: bfloat16 [3072, 768], P('seq'), may hold values from -0.109375 to 0.109375
- ln_gains: bfloat16 [2, 768], P(None, 'seq'), may hold values from 0.5 to 1.5
- ln_biases: bfloat16 [2, 768], P(None, 'seq'), may hold values from -2 to 2
- biases: bfloat16 [4, 768], P(None, 'seq'), may hold values from -3 to 3
- up_projection_bias: bfloat16 [3072], P('seq'), may hold values from -3 to 3
- cotangent: bfloat16 [4, 1536, 768], P('rep', 'seq'), may hold values from -6 to 6
Outputs:
- output: bfloat16 [4, 1536, 768], P('rep', 'seq')
- grad_tokens: float32 [4, 1536, 768], P('rep', 'seq')
- grad_w_qkv: float32 [768, 2304], P('seq')
- grad_w_out: float32 [768, 768], P('seq')
- grad_w_up: float32 [768, 3072], P('seq')
- grad_w_down: float32 [3072, 768], P('seq')
- grad_ln_gains: float32 [2, 768], P(None, 'seq')
- grad_ln_biases: float32 [2, 768], P(None, 'seq')
- grad_biases: float32 [4, 768], P(None, 'seq')
- grad_up_bias: float32 [3072], P('seq')
Inputs may be any that keep to these rules, and one draw needn't show every extreme that they name: `segment_ids`: along each sequence the ids never fall; each of the 4 documents of a sequence holds 1 to 768 tokens, and one holds exactly 768.
All inputs are finite; a program needn't handle non-finite values.
Results may differ from a plain program's by a relative error of at most 0.015.
Values may be sent and summed in bfloat16 or wider, within the bound.
No kernel may reach another device: no remote copies, remote signals or barrier semaphores. Data moves between devices by JAX's collectives and lax.ppermute only.
A program may use at most 256 MiB of HBM per device.

v0:
```python
import math

import jax
import jax.numpy as jnp
from jax import lax
from jax.sharding import PartitionSpec as P

HEADS = 12
HD = 64


norm_eps = 1e-05
floor_score = -1e30


def layer_norm(values, gain, shift):
    center = values - jnp.mean(values, axis=-1, keepdims=True)
    spread = jnp.mean(center * center, axis=-1, keepdims=True)
    return center * lax.rsqrt(spread + norm_eps) * gain + shift


def head_split(matrix):
    return matrix.reshape(matrix.shape[0], HEADS, HD)


def masked_scores(queries, query_seg, query_pos, key_piece, seg_piece, offset):
    rows = key_piece.shape[0]
    scores = jnp.einsum(
        "qhd,khd->hqk", queries, head_split(key_piece), preferred_element_type=jnp.float32
    ) * HD ** (-0.5)
    key_pos = offset + jnp.arange(rows, dtype=jnp.int32)
    allowed = (query_seg[:, None] == seg_piece[None, :]) & (key_pos[None, :] <= query_pos[:, None])
    return (jnp.where(allowed[None], scores, floor_score), allowed)


def forward_block(running, pieces, offset, queries, query_seg, query_pos):
    top_run, total_run, accum = running
    key_piece, value_piece, seg_piece = pieces
    scores, allowed = masked_scores(queries, query_seg, query_pos, key_piece, seg_piece, offset)
    top_new = jnp.maximum(top_run, jnp.max(scores, axis=-1))
    probs = jnp.where(allowed[None], jnp.exp(scores - top_new[:, :, None]), 0.0)
    factor = jnp.exp(top_run - top_new)
    total_new = total_run * factor + jnp.sum(probs, axis=-1)
    update = jnp.einsum(
        "hqk,khd->qhd",
        probs.astype(jnp.bfloat16),
        head_split(value_piece),
        preferred_element_type=jnp.float32,
    )
    return (top_new, total_new, accum * factor.T[:, :, None] + update)


def in_blocks(block_fn, running, pieces):
    rows = pieces[0].shape[0]
    size = math.gcd(rows, 1024)
    stacked = tuple((member.reshape((rows // size, size) + member.shape[1:]) for member in pieces))
    offsets = jnp.arange(rows // size, dtype=jnp.int32) * size

    def scan_step(state_now, element):
        return (block_fn(state_now, element[0], element[1]), None)

    running, _unused = lax.scan(scan_step, running, (stacked, offsets))
    return running


def backward_block(
    number,
    state_now,
    whole,
    queries,
    query_seg,
    query_pos,
    grad_heads,
    log_total,
    delta,
    block_rows,
):
    grad_query, term = state_now
    offset = number * block_rows
    key_piece = lax.dynamic_slice_in_dim(whole[0], offset, block_rows, 0)
    value_piece = lax.dynamic_slice_in_dim(whole[1], offset, block_rows, 0)
    seg_piece = lax.dynamic_slice_in_dim(whole[2], offset, block_rows, 0)
    scores, allowed = masked_scores(queries, query_seg, query_pos, key_piece, seg_piece, offset)
    probs = jnp.where(allowed[None], jnp.exp(scores - log_total[:, :, None]), 0.0)
    grad_probs = jnp.einsum(
        "qhd,khd->hqk", grad_heads, head_split(value_piece), preferred_element_type=jnp.float32
    )
    grad_scores = (probs * (grad_probs - delta[:, :, None])).astype(jnp.bfloat16)
    grad_query = grad_query + jnp.einsum(
        "hqk,khd->qhd", grad_scores, head_split(key_piece), preferred_element_type=jnp.float32
    )
    grad_key = jnp.einsum(
        "hqk,qhd->khd", grad_scores, queries, preferred_element_type=jnp.float32
    ) * HD ** (-0.5)
    grad_value = jnp.einsum(
        "hqk,qhd->khd", probs.astype(jnp.bfloat16), grad_heads, preferred_element_type=jnp.float32
    )
    joined = jnp.concatenate(
        [grad_key.reshape(block_rows, -1), grad_value.reshape(block_rows, -1)], axis=1
    )
    term = lax.dynamic_update_slice_in_dim(term, joined, offset, 0)
    return (grad_query, term)


def on_device(
    tokens,
    segment_ids,
    query_key_value_weight,
    output_weight,
    up_weight,
    down_weight,
    ln_gains,
    ln_biases,
    biases,
    up_projection_bias,
    cotangent,
):
    gathered = (
        lax.all_gather(query_key_value_weight, "seq", axis=0, tiled=True),
        lax.all_gather(output_weight, "seq", axis=0, tiled=True),
        lax.all_gather(up_weight, "seq", axis=0, tiled=True),
        lax.all_gather(down_weight, "seq", axis=0, tiled=True),
        lax.all_gather(ln_gains, "seq", axis=1, tiled=True),
        lax.all_gather(ln_biases, "seq", axis=1, tiled=True),
        lax.all_gather(biases, "seq", axis=1, tiled=True),
        lax.all_gather(up_projection_bias, "seq", axis=0, tiled=True),
    )
    full_qkv, full_out, full_up, full_down, gains_all, shifts_all, biases_all, up_shift = gathered
    gains_f = gains_all.astype(jnp.float32)
    shifts_f = shifts_all.astype(jnp.float32)
    biases_f = biases_all.astype(jnp.float32)
    up_shift_f = up_shift.astype(jnp.float32)
    tokens_f = tokens[0].astype(jnp.float32)
    seg_local = segment_ids[0]
    tok_rows = tokens_f.shape[0]
    width = tokens_f.shape[1]
    seqlen = tok_rows * lax.axis_size("seq")
    query_pos = lax.axis_index("seq") * tok_rows + jnp.arange(tok_rows, dtype=jnp.int32)
    hidden_first = layer_norm(tokens_f, gains_f[0], shifts_f[0]).astype(jnp.bfloat16)
    query_key_value_bias = jnp.concatenate(
        [biases_f[0], jnp.zeros((width,), jnp.float32), biases_f[1]]
    )
    projected_rows = (
        jnp.dot(hidden_first, full_qkv, preferred_element_type=jnp.float32) + query_key_value_bias
    ).astype(jnp.bfloat16)
    queries = head_split(projected_rows[:, :width])
    key_rows = projected_rows[:, width : 2 * width]
    value_rows = projected_rows[:, 2 * width :]
    initial = (
        jnp.full((HEADS, tok_rows), floor_score, jnp.float32),
        jnp.zeros((HEADS, tok_rows), jnp.float32),
        jnp.zeros((tok_rows, HEADS, HD), jnp.float32),
    )

    def block_fn(running, pieces, offset):
        return forward_block(running, pieces, offset, queries, seg_local, query_pos)

    block_rows = math.gcd(seqlen, 1024)
    key_end = (lax.axis_index("seq") + 1) * tok_rows
    block_count = (key_end + block_rows - 1) // block_rows
    top_run, total_run, accum = in_blocks(
        block_fn,
        initial,
        (
            lax.all_gather(key_rows, "seq", axis=0, tiled=True),
            lax.all_gather(value_rows, "seq", axis=0, tiled=True),
            lax.all_gather(seg_local, "seq", axis=0, tiled=True),
        ),
    )
    log_total = top_run + jnp.log(total_run)
    attended_f = accum / total_run.T[:, :, None]
    attention_result = attended_f.reshape(tok_rows, width).astype(jnp.bfloat16)
    residual_first = (
        tokens_f
        + jnp.dot(attention_result, full_out, preferred_element_type=jnp.float32)
        + biases_f[2]
    )
    hidden_second = layer_norm(residual_first, gains_f[1], shifts_f[1]).astype(jnp.bfloat16)
    upward_rows = jnp.dot(hidden_second, full_up, preferred_element_type=jnp.float32) + up_shift_f
    activated_f, gelu_back = jax.vjp(jax.nn.gelu, upward_rows)
    activation_values = activated_f.astype(jnp.bfloat16)
    result = (
        residual_first
        + jnp.dot(activation_values, full_down, preferred_element_type=jnp.float32)
        + biases_f[3]
    )
    grad_y = cotangent[0]
    grad_y_f = grad_y.astype(jnp.float32)
    grad_down = jnp.einsum(
        "tf,td->fd", activation_values, grad_y, preferred_element_type=jnp.float32
    )
    grad_act = jnp.einsum("td,fd->tf", grad_y, full_down, preferred_element_type=jnp.float32)
    grad_up_pre = gelu_back(grad_act)[0].astype(jnp.bfloat16)
    grad_up = jnp.einsum(
        "td,tf->df", hidden_second, grad_up_pre, preferred_element_type=jnp.float32
    )
    grad_hidden_two = jnp.einsum(
        "tf,df->td", grad_up_pre, full_up, preferred_element_type=jnp.float32
    )
    _unused, norm_two_back = jax.vjp(layer_norm, residual_first, gains_f[1], shifts_f[1])
    grad_sum_part, grad_gain_two, grad_shift_two = norm_two_back(grad_hidden_two)
    grad_first = grad_y_f + grad_sum_part
    grad_first_bf = grad_first.astype(jnp.bfloat16)
    grad_out_w = jnp.einsum(
        "td,te->de", attention_result, grad_first_bf, preferred_element_type=jnp.float32
    )
    grad_attended = jnp.einsum(
        "te,de->td", grad_first_bf, full_out, preferred_element_type=jnp.float32
    ).astype(jnp.bfloat16)
    grad_heads = head_split(grad_attended)
    delta = jnp.einsum("qhd,qhd->hq", grad_heads.astype(jnp.float32), attended_f)
    whole = (
        lax.all_gather(key_rows, "seq", axis=0, tiled=True),
        lax.all_gather(value_rows, "seq", axis=0, tiled=True),
        lax.all_gather(seg_local, "seq", axis=0, tiled=True),
    )

    def backward_step(number, state_now):
        return backward_block(
            number,
            state_now,
            whole,
            queries,
            seg_local,
            query_pos,
            grad_heads,
            log_total,
            delta,
            block_rows,
        )

    start_state = (
        jnp.zeros((tok_rows, HEADS, HD), jnp.float32),
        jnp.zeros((seqlen, 2 * width), jnp.float32),
    )
    grad_query, term = lax.fori_loop(0, block_count, backward_step, start_state)
    grad_kv = lax.psum_scatter(term, "seq", scatter_dimension=0, tiled=True).astype(jnp.bfloat16)
    grad_q = (grad_query * HD ** (-0.5)).reshape(tok_rows, width).astype(jnp.bfloat16)
    grad_proj = jnp.concatenate([grad_q, grad_kv], axis=1)
    grad_qkv_w = jnp.einsum(
        "td,te->de", hidden_first, grad_proj, preferred_element_type=jnp.float32
    )
    grad_hidden_one = jnp.einsum(
        "te,de->td", grad_proj, full_qkv, preferred_element_type=jnp.float32
    )
    _unused_two, norm_one_back = jax.vjp(layer_norm, tokens_f, gains_f[0], shifts_f[0])
    grad_in_part, grad_gain_one, grad_shift_one = norm_one_back(grad_hidden_one)
    grad_tokens = grad_first + grad_in_part
    grad_proj_f = grad_proj.astype(jnp.float32)
    grad_bias_rows = jnp.stack(
        [
            jnp.sum(grad_proj_f[:, :width], axis=0),
            jnp.sum(grad_proj_f[:, 2 * width :], axis=0),
            jnp.sum(grad_first, axis=0),
            jnp.sum(grad_y_f, axis=0),
        ]
    )
    grad_up_shift = jnp.sum(grad_up_pre.astype(jnp.float32), axis=0)
    grad_gains = jnp.stack([grad_gain_one, grad_gain_two])
    grad_shifts = jnp.stack([grad_shift_one, grad_shift_two])
    shares = (
        lax.psum_scatter(grad_qkv_w, "seq", scatter_dimension=0, tiled=True),
        lax.psum_scatter(grad_out_w, "seq", scatter_dimension=0, tiled=True),
        lax.psum_scatter(grad_up, "seq", scatter_dimension=0, tiled=True),
        lax.psum_scatter(grad_down, "seq", scatter_dimension=0, tiled=True),
        lax.psum_scatter(grad_gains, "seq", scatter_dimension=1, tiled=True),
        lax.psum_scatter(grad_shifts, "seq", scatter_dimension=1, tiled=True),
        lax.psum_scatter(grad_bias_rows, "seq", scatter_dimension=1, tiled=True),
        lax.psum_scatter(grad_up_shift, "seq", scatter_dimension=0, tiled=True),
    )
    totals = (
        lax.psum(shares[0].astype(jnp.bfloat16), "rep").astype(jnp.float32),
        lax.psum(shares[1].astype(jnp.bfloat16), "rep").astype(jnp.float32),
        lax.psum(shares[2].astype(jnp.bfloat16), "rep").astype(jnp.float32),
        lax.psum(shares[3].astype(jnp.bfloat16), "rep").astype(jnp.float32),
        lax.psum(shares[4].astype(jnp.bfloat16), "rep").astype(jnp.float32),
        lax.psum(shares[5].astype(jnp.bfloat16), "rep").astype(jnp.float32),
        lax.psum(shares[6].astype(jnp.bfloat16), "rep").astype(jnp.float32),
        lax.psum(shares[7].astype(jnp.bfloat16), "rep").astype(jnp.float32),
    )
    return (
        result.astype(jnp.bfloat16)[None],
        grad_tokens[None],
        totals[0],
        totals[1],
        totals[2],
        totals[3],
        totals[4],
        totals[5],
        totals[6],
        totals[7],
    )


def solution(mesh):
    placed = (
        P("rep", "seq", None),
        P("rep", "seq"),
        P("seq", None),
        P("seq", None),
        P("seq", None),
        P("seq", None),
        P(None, "seq"),
        P(None, "seq"),
        P(None, "seq"),
        P("seq"),
        P("rep", "seq", None),
    )
    return jax.shard_map(
        on_device,
        mesh=mesh,
        in_specs=placed,
        out_specs=(
            P("rep", "seq", None),
            P("rep", "seq", None),
            P("seq", None),
            P("seq", None),
            P("seq", None),
            P("seq", None),
            P(None, "seq"),
            P(None, "seq"),
            P(None, "seq"),
            P("seq"),
        ),
        check_vma=False,
    )
```

profile of v0, /device:TPU:0, one launch (start us, length us, event | category | flops | bytes accessed | tf_op | source)
XLA Modules:
  0.0 1416.0 jit_solution(10778686054061372195)
XLA Ops:
  8.0 22.3 %all-gather.1 = bf16[8,96,2]{1,2,0:T(2,128)(2,1)S(1)} all-gather(bf16[1,96,2]{1,2,0:T(2,128)(2,1)} %bitcast.279), channel_id=1, replica_groups=mesh['rep'=4,'seq'=8] {'seq'}, dimensions={0}, use_global_device_ids=true | all-gather | bytes 3456 | tf_op jit(solution)/shard_map/all_gather | solution.py:123
  30.4 16.4 %all-gather.2 = bf16[8,96,2]{1,2,0:T(2,128)(2,1)S(1)} all-gather(bf16[1,96,2]{1,2,0:T(2,128)(2,1)} %bitcast.280), channel_id=1, replica_groups=mesh['rep'=4,'seq'=8] {'seq'}, dimensions={0}, use_global_device_ids=true | all-gather | bytes 3456 | tf_op jit(solution)/shard_map/all_gather | solution.py:124
  46.9 18.7 %all-gather.3 = bf16[8,96,4]{1,2,0:T(4,128)(2,1)S(1)} all-gather(bf16[1,96,4]{1,2,0:T(4,128)(2,1)} %bitcast.278), channel_id=1, replica_groups=mesh['rep'=4,'seq'=8] {'seq'}, dimensions={0}, use_global_device_ids=true | all-gather | bytes 6912 | tf_op jit(solution)/shard_map/all_gather | solution.py:125
  68.7 9.6 all-gather.12.cloned.1.call-done
  86.5 10.8 all-reduce
  98.0 26.3 %all-gather.4 = bf16[8,1,384]{2,1,0:T(2,128)(2,1)S(1)} all-gather(bf16[1,1,384]{2,1,0:T(2,128)(2,1)S(1)} %reshape.277), channel_id=1, replica_groups=mesh['rep'=4,'seq'=8] {'seq'}, dimensions={0}, use_global_device_ids=true | all-gather | bytes 6912 | tf_op jit(solution)/shard_map/all_gather | solution.py:126
  124.5 8.6 all-gather.16.cloned.1.call-done
  133.1 53.4 %all-gather.14.cloned.1.call-done = bf16[1536,768]{1,0:T(8,128)(2,1)} async-done(((bf16[192,768]{1,0:T(8,128)(2,1)}), bf16[1536,768]{1,0:T(8,128)(2,1)}) %all-gather.14.cloned.1.call-update) | async-done | bytes 2359312 | tf_op jit(solution)/shard_map/all_gather | solution.py:165
  186.5 23.5 %while.29 = (s32[]{:T(128)}, f32[12,192]{1,0:T(8,128)S(1)}, f32[12,192]{1,0:T(8,128)S(1)}, f32[192,12,64]{0,2,1:T(8,128)}, s32[1,192]{1,0:T(1,128)S(1)}, /*index...) while((s32[]{:T(128)}, f32[12,192]{1,0:T(8,128)S(1)}, ...), condition=%wide.region_5.6_spmd.clone, body=%wide.region_2.5_spmd.clone.sunk | while | flops 318077120 | bytes 28766692 | solution.py:62
  211.2 17.0 %all-gather.18.cloned.1.call-done = bf16[768,768]{1,0:T(8,128)(2,1)} async-done(((bf16[96,768]{1,0:T(8,128)(2,1)}), bf16[768,768]{1,0:T(8,128)(2,1)}) %all-gather.18.cloned.1.call-update) | async-done | bytes 1179664 | tf_op jit(solution)/shard_map/all_gather | solution.py:120
  230.9 78.0 %all-gather.20.cloned.1.call-done = bf16[768,3072]{1,0:T(8,128)(2,1)} async-done(((bf16[96,3072]{1,0:T(8,128)(2,1)}), bf16[768,3072]{1,0:T(8,128)(2,1)}) %all-gather.20.cloned.1.call-update) | async-done | bytes 4718608 | tf_op jit(solution)/shard_map/all_gather | solution.py:121
  308.9 3.5 convolution_add_fusion.1
  312.5 76.6 %all-gather.22.cloned.1.call-done = bf16[3072,768]{1,0:T(8,128)(2,1)} async-done(((bf16[384,768]{1,0:T(8,128)(2,1)}), bf16[3072,768]{1,0:T(8,128)(2,1)}) %all-gather.22.cloned.1.call-update) | async-done | bytes 4718608 | tf_op jit(solution)/shard_map/all_gather | solution.py:122
  389.0 5.6 convert_reduce_fusion
  402.4 4.9 broadcast_in_dim.97.clone
  407.3 19.0 %while.28 = (s32[]{:T(128)}, f32[192,12,64]{0,2,1:T(8,128)}, f32[1536,1536]{1,0:T(8,128)}, s32[]{:T(128)}, bf16[1536,768]{1,0:T(8,128)(2,1)}, /*index=5*/s32[1,1...) while((s32[]{:T(128)}, f32[192,12,64]{0,2,1:T(8,128)}, ...), condition=%wide.region_11.12_spmd.clone, body=%wide.region_10.11_spmd.clone.sunk | while | flops 770753216 | bytes 54599132 | solution.py:236
  430.5 5.6 fusion.62
  437.2 6.5 fusion.78
  445.8 180.4 %reduce-scatter.25.cloned.1.call-done = f32[192,1536]{1,0:T(8,128)} async-done(((f32[1536,1536]{1,0:T(8,128)}), f32[192,1536]{1,0:T(8,128)}) %reduce-scatter.25.cloned.1.call-update) | async-done | bytes 1179664
  628.6 5.4 fusion.59
  635.7 3.8 fusion.80
  652.6 45.2 %reduce-scatter.19.cloned.1.call-done = f32[96,768]{1,0:T(8,128)} async-done(((f32[768,768]{1,0:T(8,128)}), f32[96,768]{1,0:T(8,128)}) %reduce-scatter.19.cloned.1.call-update) | async-done | bytes 294928 | tf_op jit(solution)/shard_map/reduce_scatter | solution.py:263
  699.4 164.5 %reduce-scatter.23.cloned.1.call-done = f32[384,768]{1,0:T(8,128)} async-done(((f32[3072,768]{1,0:T(8,128)}), f32[384,768]{1,0:T(8,128)}) %reduce-scatter.23.cloned.1.call-update) | async-done | bytes 1179664 | tf_op jit(solution)/shard_map/reduce_scatter | solution.py:265
  866.0 163.9 %reduce-scatter.21.cloned.1.call-done = f32[96,3072]{1,0:T(8,128)} async-done(((f32[768,3072]{1,0:T(8,128)}), f32[96,3072]{1,0:T(8,128)}) %reduce-scatter.21.cloned.1.call-update) | async-done | bytes 1179664 | tf_op jit(solution)/shard_map/reduce_scatter | solution.py:264
  1032.1 129.7 %reduce-scatter.17.cloned.1.call-done = f32[96,2304]{1,0:T(8,128)} async-done(((f32[768,2304]{1,0:T(8,128)}), f32[96,2304]{1,0:T(8,128)}) %reduce-scatter.17.cloned.1.call-update) | async-done | bytes 884752 | tf_op jit(solution)/shard_map/reduce_scatter | solution.py:262
  1164.4 35.2 %all-reduce.1 = bf16[3072]{0:T(1024)(128)(2,1)S(1)} all-reduce(f32[3072]{0:T(1024)S(1)} %copy-done.35), channel_id=11, replica_groups=mesh['rep'=4,'seq'=8] {'seq'}, use_global_device_ids=true, to_apply=%region_38.39.clone | all-reduce | flops 3072 | bytes 18432
  1199.7 4.6 fusion.44
  1204.3 21.4 %reduce-scatter.27.cloned.1.call-done = f32[96,2]{1,0:T(8,128)} async-done(((f32[768,2]{1,0:T(8,128)}), f32[96,2]{1,0:T(8,128)}) %reduce-scatter.27.cloned.1.call-update) | async-done | bytes 784
  1226.6 63.2 %reduce-scatter.29.cloned.1.call-done = f32[96,2]{1,0:T(8,128)} async-done(((f32[768,2]{1,0:T(8,128)}), f32[96,2]{1,0:T(8,128)}) %reduce-scatter.29.cloned.1.call-update) | async-done | bytes 784
  1290.7 63.0 %reduce-scatter.31.cloned.1.call-done = f32[96,4]{1,0:T(8,128)} async-done(((f32[768,4]{1,0:T(8,128)}), f32[96,4]{1,0:T(8,128)}) %reduce-scatter.31.cloned.1.call-update) | async-done | bytes 1552
  1354.5 5.7 all-reduce.2
  1362.5 40.0 %all-reduce.6.cloned.1.call-done = (bf16[96,2304]{1,0:T(8,128)(2,1)}, bf16[96,768]{1,0:T(8,128)(2,1)}, bf16[96,3072]{1,0:T(8,128)(2,1)}, bf16[384,768]{1,0:T(8,128)(2,1)}) async-done(((bf16[96,2304]{1,0:T(8,128)(2,1)}, bf16[96,768]{1,0:T(8,128)(2,1)}, bf16[96,3072]{1,0:T(8,128)(2,1)}, bf16[384,768]{1,0:T(8,128)(2,1)}), (bf16[96,2304]{1,0:T(8,128)(2,1)}, bf16[96,768]{1,0:T(8,128)(2,1)}, ...) | async-done | bytes 1769488 | tf_op jit(solution)/shard_map/psum | solution.py:272
  (265 shorter events, 109.9 us)
Async XLA Ops:
  7.2 71.1 %all-gather.12.cloned.1.call-start = ((), (), s32[]{:S(2)}) async-start(), calls=%async_computation.8 | async-start | bytes 3981312 | tf_op jit(solution)/shard_map/all_gather | solution.py:119
  7.9 125.2 %all-gather.16.cloned.1.call-start = ((), (), s32[]{:S(2)}) async-start(), calls=%async_computation.10 | async-start | bytes 2654208 | tf_op jit(solution)/shard_map/all_gather | solution.py:166
  66.3 15.0 %copy-start.21 = (f32[768]{0:T(1024)}, f32[768]{0:T(1024)S(1)}, u32[]{:S(2)}) copy-start(f32[768]{0:T(1024)S(1)} %get-tuple-element.405) | copy-start | bytes 9220
  66.3 15.0 %copy-start.24 = (f32[768]{0:T(1024)}, f32[768]{0:T(1024)S(1)}, u32[]{:S(2)}) copy-start(f32[768]{0:T(1024)S(1)} %get-tuple-element.326) | copy-start | bytes 9220
  67.4 13.9 copy-start.28
  68.6 12.7 copy-start.38
  68.7 12.7 copy-start.30
  82.3 104.2 %all-gather.14.cloned.1.call-start = ((), (), s32[]{:S(2)}) async-start(), calls=%async_computation.9 | async-start | bytes 2654208 | tf_op jit(solution)/shard_map/all_gather | solution.py:165
  83.0 145.2 %all-gather.18.cloned.1.call-start = ((), (), s32[]{:S(2)}) async-start(), calls=%async_computation.11 | async-start | bytes 1327104 | tf_op jit(solution)/shard_map/all_gather | solution.py:120
  83.6 225.3 %all-gather.20.cloned.1.call-start = ((), (), s32[]{:S(2)}) async-start(), calls=%async_computation.12 | async-start | bytes 5308416 | tf_op jit(solution)/shard_map/all_gather | solution.py:121
  84.2 304.8 %all-gather.22.cloned.1.call-start = ((), (), s32[]{:S(2)}) async-start(), calls=%async_computation.13 | async-start | bytes 5308416 | tf_op jit(solution)/shard_map/all_gather | solution.py:122
  84.8 541.4 %reduce-scatter.25.cloned.1.call-start = ((), (), s32[]{:S(2)}) async-start(), calls=%async_computation.18 | async-start | bytes 10616832
  186.5 41.7 %copy-start.5 = (bf16[1,192,768]{2,1,0:T(8,128)(2,1)S(1)}, bf16[1,192,768]{2,1,0:T(8,128)(2,1)}, u32[]{:S(2)}) copy-start(bf16[1,192,768]{2,1,0:T(8,128)(2,1)} %param.15) | copy-start | bytes 884740
  211.2 97.7 %copy-start.13 = (bf16[192,12,64]{0,2,1:T(8,128)(2,1)}, bf16[192,12,64]{0,2,1:T(8,128)(2,1)S(1)}, u32[]{:S(2)}) copy-start(bf16[192,12,64]{0,2,1:T(8,128)(2,1)S(1)} %fusion.61) | copy-start | bytes 884740
  230.0 167.0 %copy-start = (f32[192,768]{1,0:T(8,128)}, f32[192,768]{1,0:T(8,128)S(1)}, u32[]{:S(2)}) copy-start(f32[192,768]{1,0:T(8,128)S(1)} %get-tuple-element.400) | copy-start | bytes 1769476
  230.3 166.8 %copy-start.26 = (f32[192]{0:T(256)}, f32[192]{0:T(256)S(1)}, u32[]{:S(2)}) copy-start(f32[192]{0:T(256)S(1)} %fusion.72) | copy-start | bytes 2308
  312.4 82.2 %copy-start.2 = (f32[192,3072]{1,0:T(8,128)}, f32[192,3072]{1,0:T(8,128)S(1)}, u32[]{:S(2)}) copy-start(f32[192,3072]{1,0:T(8,128)S(1)} %convolution_add_fusion.1) | copy-start | bytes 7077892
  426.4 271.3 %reduce-scatter.19.cloned.1.call-start = ((), (), s32[]{:S(2)}) async-start(), calls=%async_computation.15 | async-start | bytes 2654208 | tf_op jit(solution)/shard_map/reduce_scatter | solution.py:263
  430.5 433.4 %reduce-scatter.23.cloned.1.call-start = ((), (), s32[]{:S(2)}) async-start(), calls=%async_computation.17 | async-start | bytes 10616832 | tf_op jit(solution)/shard_map/reduce_scatter | solution.py:265
  436.2 593.8 %reduce-scatter.21.cloned.1.call-start = ((), (), s32[]{:S(2)}) async-start(), calls=%async_computation.16 | async-start | bytes 10616832 | tf_op jit(solution)/shard_map/reduce_scatter | solution.py:264
  443.7 184.9 %copy-start.6 = (bf16[1,192,768]{2,1,0:T(8,128)(2,1)S(1)}, bf16[1,192,768]{2,1,0:T(8,128)(2,1)}, u32[]{:S(2)}) copy-start(bf16[1,192,768]{2,1,0:T(8,128)(2,1)} %param.15) | copy-start | bytes 884740
  443.7 184.9 %copy-start.22 = (f32[768]{0:T(1024)S(1)}, f32[768]{0:T(1024)}, u32[]{:S(2)}) copy-start(f32[768]{0:T(1024)} %copy-done.21) | copy-start | bytes 9220
  443.7 184.9 %copy-start.25 = (f32[768]{0:T(1024)S(1)}, f32[768]{0:T(1024)}, u32[]{:S(2)}) copy-start(f32[768]{0:T(1024)} %copy-done.24) | copy-start | bytes 9220
  443.7 184.9 %copy-start.29 = (f32[192]{0:T(256)S(1)}, f32[192]{0:T(256)}, u32[]{:S(2)}) copy-start(f32[192]{0:T(256)} %copy-done.28) | copy-start | bytes 2308
  443.7 184.9 %copy-start.31 = (f32[192]{0:T(256)S(1)}, f32[192]{0:T(256)}, u32[]{:S(2)}) copy-start(f32[192]{0:T(256)} %copy-done.30) | copy-start | bytes 2308
  443.8 718.0 %reduce-scatter.17.cloned.1.call-start = ((), (), s32[]{:S(2)}) async-start(), calls=%async_computation.14 | async-start | bytes 7962624 | tf_op jit(solution)/shard_map/reduce_scatter | solution.py:262
  634.1 591.6 %reduce-scatter.27.cloned.1.call-start = ((), (), s32[]{:S(2)}) async-start(), calls=%async_computation.19 | async-start | bytes 442368
  647.6 642.1 %reduce-scatter.29.cloned.1.call-start = ((), (), s32[]{:S(2)}) async-start(), calls=%async_computation.20 | async-start | bytes 442368
  651.5 702.2 %reduce-scatter.31.cloned.1.call-start = ((), (), s32[]{:S(2)}) async-start(), calls=%async_computation.21 | async-start | bytes 442368
  652.5 750.0 %all-reduce.6.cloned.1.call-start = ((), (), s32[]{:S(2)}) async-start(), calls=%async_computation.22 | async-start | bytes 3538944 | tf_op jit(solution)/shard_map/psum | solution.py:272
  866.0 298.4 %copy-start.35 = (f32[3072]{0:T(1024)S(1)}, f32[3072]{0:T(1024)}, u32[]{:S(2)}) copy-start(f32[3072]{0:T(1024)} %get-tuple-element.403) | copy-start | bytes 36868
  866.0 333.7 %copy-start.41 = (f32[768]{0:T(1024)S(1)}, f32[768]{0:T(1024)}, u32[]{:S(2)}) copy-start(f32[768]{0:T(1024)} %get-tuple-element.319) | copy-start | bytes 9220
  (32 other events, 78.2 us)
Sparse Core Ops, SparseCore 0:
  10.2 68.0 all-gather.11
  82.4 50.6 all-gather.15
  135.9 50.6 all-gather.13
  188.6 39.6 all-gather.17
  230.2 78.6 all-gather.19
  311.0 78.0 all-gather.21
  426.5 199.6 reduce-scatter.24
  629.7 68.0 reduce-scatter.18
  701.3 162.5 reduce-scatter.22
  867.3 162.5 reduce-scatter.20
  1033.6 128.0 reduce-scatter.16
  1165.2 60.4 reduce-scatter.26
  1229.3 60.4 reduce-scatter.28
  1293.2 60.3 reduce-scatter.30
  1356.9 45.5 all-reduce.5
where the time goes:
time: 1420 us
  waiting for transfers between devices  1120 us (79%)
  blocking collectives  136 us (10%)
  matrix products  63.2 us (4%)
  local copies, waits for them, and re-layouts  41.4 us (3%)
  other arithmetic  41.3 us (3%)
  between operations  15.8 us (1%)
    unnamed x19, waiting for transfers between devices  331 us
    reduce_scatter x1, waiting for transfers between devices, on_device(): lax.psum_scatter(grad_down, 'seq', scatter_dimension=0, tiled=True)  165 us
    reduce_scatter x1, waiting for transfers between devices, on_device(): lax.psum_scatter(grad_up, 'seq', scatter_dimension=0, tiled=True)  164 us
    reduce_scatter x1, waiting for transfers between devices, on_device(): lax.psum_scatter(grad_qkv_w, 'seq', scatter_dimension=0, tiled=True)  130 us
    all_gather x1, waiting for transfers between devices, on_device(): lax.all_gather(up_weight, 'seq', axis=0, tiled=True)  78 us
    all_gather x1, waiting for transfers between devices, on_device(): lax.all_gather(down_weight, 'seq', axis=0, tiled=True)  76.6 us
    all_gather x1, waiting for transfers between devices, on_device(): lax.all_gather(key_rows, 'seq', axis=0, tiled=True)  53.4 us
    reduce_scatter x1, waiting for transfers between devices, on_device(): lax.psum_scatter(grad_out_w, 'seq', scatter_dimension=0, tiled=True)  45.2 us
  transfers between devices with their start and end apart: 15, of which 15 were waited for; matrix products, arithmetic and copies ran while one was open for 7% of the time, Pallas kernels for 0%

commit v1 on v0

--- a/solution.py
+++ b/solution.py
@@ -3,6 +3,8 @@
 import jax
 import jax.numpy as jnp
 from jax import lax
+from jax.experimental import pallas as pl
+from jax.experimental.pallas import tpu as pltpu
 from jax.sharding import PartitionSpec as P
 
 HEADS = 12
@@ -292,6 +294,695 @@
     )
 
 
+def f32(value):
+    return value.astype(jnp.float32)
+
+
+def b16(value):
+    return value.astype(jnp.bfloat16)
+
+
+def dot_nn(left, right):
+    return jnp.dot(left, right, preferred_element_type=jnp.float32)
+
+
+def dot_nt(left, right):
+    return lax.dot_general(
+        left, right, (((1,), (1,)), ((), ())), preferred_element_type=jnp.float32
+    )
+
+
+def dot_tn(left, right):
+    return lax.dot_general(
+        left, right, (((0,), (0,)), ((), ())), preferred_element_type=jnp.float32
+    )
+
+
+def norm_parts(values):
+    center = values - jnp.mean(values, axis=-1, keepdims=True)
+    rate = lax.rsqrt(jnp.mean(center * center, axis=-1, keepdims=True) + norm_eps)
+    return center * rate, rate
+
+
+def norm_back(grad, hat, rate, gain):
+    scaled = grad * gain
+    return rate * (
+        scaled
+        - jnp.mean(scaled, axis=-1, keepdims=True)
+        - hat * jnp.mean(scaled * hat, axis=-1, keepdims=True)
+    )
+
+
+def place(coords):
+    return coords[0], coords[1], coords[2], coords[3]
+
+
+def piece_shard(number, y, z):
+    if number < 3:
+        return 2 * lax.rem(z + 3 - number, 4) + y
+    return 2 * lax.rem(z + 7 - number, 4) + 1 - y
+
+
+class Copies:
+    def __init__(self, sems):
+        self.sems = sems
+        self.held = []
+
+    def add(self, source, target):
+        copy = pltpu.make_async_copy(source, target, self.sems.at[len(self.held)])
+        copy.start()
+        self.held.append(copy)
+
+    def wait(self):
+        for copy in self.held:
+            copy.wait()
+        self.held = []
+
+
+def fetch_qkv(copies, coords, own, pieces, full):
+    x, c, y, z = place(coords)
+    rows, cols = own.shape[0], own.shape[1] // 2
+    half = rows // 2
+    copies.add(own, full.at[pl.ds(pl.multiple_of((2 * z + y) * rows, 16), rows), :])
+    for piece, xx, cc in zip(pieces, (x, 1 - x, x, 1 - x), (c, c, 1 - c, 1 - c), strict=True):
+        for number in range(7):
+            row = piece_shard(number, y, z) * rows + half * cc
+            copies.add(
+                piece.at[number, pl.ds(0, half), :],
+                full.at[
+                    pl.ds(pl.multiple_of(row, 16), half),
+                    pl.ds(pl.multiple_of(cols * xx, 128), cols),
+                ],
+            )
+
+
+def mask_bias(start, me, tok, target):
+    keys, lanes = target.shape
+    key_pos = (me - 4) * tok + lax.broadcasted_iota(jnp.int32, (keys, lanes), 0)
+    lane = lax.broadcasted_iota(jnp.int32, (keys, lanes), 1)
+    query_pos = me * tok + jnp.where(lane >= tok, lane - tok, lane)
+    target[...] = jnp.where((key_pos >= start) & (key_pos <= query_pos), 0.0, floor_score)
+
+
+def pair_stack(rows):
+    lane = lax.broadcasted_iota(jnp.int32, rows.shape, 1)
+    zero = jnp.zeros_like(rows)
+    return jnp.concatenate([jnp.where(lane < HD, rows, zero), jnp.where(lane < HD, zero, rows)], axis=0)
+
+
+def pair_join(transposed):
+    both = transposed.T
+    tok = both.shape[0] // 2
+    lane = lax.broadcasted_iota(jnp.int32, (tok, 2 * HD), 1)
+    return jnp.where(lane < HD, both[:tok], both[tok:])
+
+
+def front_kernel(
+    coords, seg, xo, x1, x2, x3, x4, first, own, m7, x7, c7, cx7,
+    q_out, kv_out, h_out, a_out, lse_out, start_out, vec_out, upb_out,
+    full, small, bias, sems, vsems,
+):
+    x, c, y, z = place(coords)
+    me = 2 * z + y
+    tok, width = q_out.shape
+    copies, vcopies = Copies(sems), Copies(vsems)
+    vcopies.add(first.at[pl.ds(48, 16), pl.ds(0, 512)], small.at[me])
+    for number in range(7):
+        vcopies.add(m7.at[number, pl.ds(48, 16), pl.ds(0, 512)], small.at[piece_shard(number, y, z)])
+    fetch_qkv(copies, coords, own, (m7, x7, c7, cx7), full)
+    blocks = (xo, x1, x2, x3, x4)
+    lane1 = lax.broadcasted_iota(jnp.int32, (1, tok), 1)
+    start = jnp.full(seg.shape, 1 << 30, jnp.int32)
+    for number in range(4):
+        first_pos = jnp.full((1, 1), 1 << 30, jnp.int32)
+        for back in range(5):
+            ids = f32(blocks[back][pl.ds(tok, 16), pl.ds(0, tok)])[:1]
+            pos = (me - back) * tok + lane1
+            hit = (ids == float(number)) & (pos >= 0)
+            first_pos = jnp.minimum(
+                first_pos, jnp.min(jnp.where(hit, pos, 1 << 30), axis=1, keepdims=True)
+            )
+        start = jnp.where(seg[...] == number, first_pos, start)
+    start_out[...] = start
+    mask_bias(start, me, tok, bias)
+    vcopies.wait()
+    lane = lax.broadcasted_iota(jnp.int32, (8, width), 1)
+    part = width // 8
+    vec = jnp.zeros((8, width), jnp.float32)
+    for shard in range(8):
+        block = f32(small[shard])
+        spread = jnp.concatenate([block[:8, :128], jnp.zeros((8, width - 128), jnp.float32)], axis=1)
+        spread = pltpu.roll(spread, shard * part, 1) if shard else spread
+        vec = jnp.where((lane >= shard * part) & (lane < shard * part + part), spread, vec)
+        upb_out[:, pl.ds(shard * 384, 384)] = block[:1, 128:512]
+    vec_out[...] = vec
+    for back in range(5):
+        hat, _rate = norm_parts(f32(blocks[back][pl.ds(0, tok), :]))
+        h_out[pl.ds((4 - back) * tok, tok), :] = b16(hat * vec[0:1] + vec[2:3])
+    copies.wait()
+    q_out[...] = b16(dot_nn(h_out[pl.ds(4 * tok, tok), :], full[:, pl.ds(0, width)]) + vec[4:5])
+
+    def project(number, carry):
+        col = pl.multiple_of(number * 256, 256)
+        shift = jnp.where(number >= width // 256, 1.0, 0.0)
+        bias_at = lax.rem(number, width // 256)
+        piece = vec_out[pl.ds(5, 1), pl.ds(pl.multiple_of(bias_at * 256, 256), 256)]
+        kv_out[:, pl.ds(col, 256)] = b16(
+            dot_nn(h_out[...], full[:, pl.ds(pl.multiple_of(width + col, 256), 256)]) + piece * shift
+        )
+        return carry
+
+    lax.fori_loop(0, 2 * width // 256, project, 0)
+
+    def pair(number, carry):
+        col = pl.multiple_of(number * 128, 128)
+        queries = pair_stack(q_out[:, pl.ds(col, 128)] * jnp.bfloat16(0.125))
+        scores = dot_nt(kv_out[:, pl.ds(col, 128)], queries) + bias[...]
+        top = jnp.max(scores, axis=0, keepdims=True)
+        probs = jnp.exp(scores - top)
+        total = jnp.sum(probs, axis=0, keepdims=True)
+        mixed = dot_tn(kv_out[:, pl.ds(pl.multiple_of(width + col, 128), 128)], b16(probs))
+        a_out[:, pl.ds(col, 128)] = b16(pair_join(mixed / total))
+        lse_out[number] = top + jnp.log(total)
+        return carry
+
+    lax.fori_loop(0, width // 128, pair, 0)
+
+
+def mid_kernel(
+    coords, a_in, xo, dy_in, vec_in, upb_in,
+    up_own, out_own, um7, ux7, uc7, ucx7, down_own, dm7, dx7, dc7, dcx7,
+    y_out, dr_out, da_out, d_other, d_mine, u_other, u_mine, vec_out, upb_out,
+    w_up, w_out, w_down, stage_d, stage_u, stage_o, h2_s, dh_s, acc_s, sems, osems,
+):
+    x, c, y, z = place(coords)
+    me = 2 * z + y
+    tok, width = a_in.shape
+    hidden = w_up.shape[1]
+    copies = Copies(sems)
+    copies.add(out_own, w_out.at[pl.ds(pl.multiple_of(me * 96, 16), 96), :])
+    copies.add(up_own, w_up.at[pl.ds(pl.multiple_of(me * 96, 16), 96), :])
+    copies.add(down_own, w_down.at[pl.ds(pl.multiple_of(me * 384, 16), 384), :])
+    half_h, half_w = hidden // 2, width // 2
+    for piece, xx, cc in zip(
+        (um7, ux7, uc7, ucx7), (x, 1 - x, x, 1 - x), (c, c, 1 - c, 1 - c), strict=True
+    ):
+        for number in range(7):
+            row = pl.multiple_of(piece_shard(number, y, z) * 96 + 48 * cc, 16)
+            copies.add(
+                piece.at[number, :, pl.ds(0, half_h)],
+                w_up.at[pl.ds(row, 48), pl.ds(pl.multiple_of(half_h * xx, 128), half_h)],
+            )
+            copies.add(
+                piece.at[number, :, pl.ds(half_h, half_w)],
+                w_out.at[pl.ds(row, 48), pl.ds(pl.multiple_of(half_w * xx, 128), half_w)],
+            )
+    for piece, xx, cc in zip(
+        (dm7, dx7, dc7, dcx7), (x, 1 - x, x, 1 - x), (c, c, 1 - c, 1 - c), strict=True
+    ):
+        for number in range(7):
+            row = pl.multiple_of(piece_shard(number, y, z) * 384 + 192 * cc + 96 * xx, 16)
+            copies.add(piece.at[number], w_down.at[pl.ds(row, 96), :])
+    copies.wait()
+    vec = vec_in[...]
+    dy = dy_in[...]
+    residual = f32(xo[pl.ds(0, tok), :]) + dot_nn(a_in[...], w_out[...]) + vec[6:7]
+    hat, _rate = norm_parts(residual)
+    acc_s[...] = residual + vec[7:8]
+    h2_s[...] = b16(hat * vec[1:2] + vec[3:4])
+    dh_s[...] = jnp.zeros_like(dh_s)
+    chunk = 512
+    root = math.sqrt(2.0 / math.pi)
+
+    def feed(number, carry):
+        col = pl.multiple_of(number * chunk, chunk)
+        h2 = h2_s[...]
+        pre = dot_nn(h2, w_up[:, pl.ds(col, chunk)]) + upb_in[:, pl.ds(col, chunk)]
+        square = pre * pre
+        bend = jnp.tanh(root * pre * (1.0 + 0.044715 * square))
+        act = b16(0.5 * pre * (1.0 + bend))
+        acc_s[...] += dot_nn(act, w_down[pl.ds(col, chunk), :])
+        slope = 0.5 * (1.0 + bend) + 0.5 * pre * (1.0 - bend * bend) * (
+            root * (1.0 + 3.0 * 0.044715 * square)
+        )
+        grad = dot_nt(dy, w_down[pl.ds(col, chunk), :]) * slope
+        low = b16(grad)
+        upb_out[:, pl.ds(col, chunk)] = jnp.sum(f32(low), axis=0, keepdims=True)
+        dh_s[...] += dot_nt(low, w_up[:, pl.ds(col, chunk)])
+        stage_d[pl.ds(col, chunk), :] = b16(dot_tn(act, dy))
+        stage_u[:, pl.ds(col, chunk)] = b16(dot_tn(h2, low))
+        return carry
+
+    lax.fori_loop(0, hidden // chunk, feed, 0)
+    outs = Copies(osems)
+
+    def spread(target_other, target_mine, source_of, where_of):
+        for shard in range(8):
+            zz = lax.rem(shard // 2 + 4 - z, 4)
+            yy = jnp.where(y == shard % 2, 0, 1)
+            for xx in range(2):
+                far = jnp.where(x == xx, 0, 1)
+                outs.add(source_of(shard, 1 - c, xx), where_of(target_other, far, yy, zz))
+                outs.add(source_of(shard, c, xx), where_of(target_mine, far, yy, zz))
+
+    spread(
+        d_other,
+        d_mine,
+        lambda s, cc, xx: stage_d.at[pl.ds(pl.multiple_of(s * 384 + 192 * cc + 96 * xx, 16), 96), :],
+        lambda ref, far, yy, zz: ref.at[far, yy, zz],
+    )
+    spread(
+        u_other,
+        u_mine,
+        lambda s, cc, xx: stage_u.at[pl.ds(pl.multiple_of(s * 96 + 48 * cc, 16), 48), pl.ds(half_h * xx, half_h)],
+        lambda ref, far, yy, zz: ref.at[yy, far, zz, :, pl.ds(0, half_h)],
+    )
+    y_out[...] = b16(acc_s[...])
+    grad_hidden = dh_s[...]
+    residual = f32(xo[pl.ds(0, tok), :]) + dot_nn(a_in[...], w_out[...]) + vec[6:7]
+    hat, rate = norm_parts(residual)
+    dyf = f32(dy)
+    grad_first = dyf + norm_back(grad_hidden, hat, rate, vec[1:2])
+    dr_out[...] = grad_first
+    low_first = b16(grad_first)
+    da_out[...] = b16(dot_nt(low_first, w_out[...]))
+    stage_o[...] = b16(dot_tn(a_in[...], low_first))
+    zero = jnp.zeros((1, width), jnp.float32)
+    vec_out[...] = jnp.concatenate(
+        [
+            zero,
+            jnp.sum(grad_hidden * hat, axis=0, keepdims=True),
+            zero,
+            jnp.sum(grad_hidden, axis=0, keepdims=True),
+            zero,
+            zero,
+            jnp.sum(grad_first, axis=0, keepdims=True),
+            jnp.sum(dyf, axis=0, keepdims=True),
+        ],
+        axis=0,
+    )
+    spread(
+        u_other,
+        u_mine,
+        lambda s, cc, xx: stage_o.at[pl.ds(pl.multiple_of(s * 96 + 48 * cc, 16), 48), pl.ds(half_w * xx, half_w)],
+        lambda ref, far, yy, zz: ref.at[yy, far, zz, :, pl.ds(half_h, half_w)],
+    )
+    outs.wait()
+
+
+def back_kernel(
+    coords, start_in, q_in, kv_in, h_in, lse_in, da_in, vec_in, upb_in, xo, x1, x2, x3, x4,
+    own, m7, x7, c7, cx7,
+    q_other, q_mine, p_own, p_y, p_z,
+    full, bias, dq_s, dkv_s, stage, sems, osems,
+):
+    x, c, y, z = place(coords)
+    me = 2 * z + y
+    tok, width = q_in.shape
+    copies = Copies(sems)
+    fetch_qkv(copies, coords, own, (m7, x7, c7, cx7), full)
+    mask_bias(start_in[...], me, tok, bias)
+
+    def pair(number, carry):
+        col = pl.multiple_of(number * 128, 128)
+        vcol = pl.multiple_of(width + col, 128)
+        queries = pair_stack(q_in[:, pl.ds(col, 128)] * jnp.bfloat16(0.125))
+        grads = pair_stack(da_in[:, pl.ds(col, 128)])
+        keys = kv_in[:, pl.ds(col, 128)]
+        probs = jnp.exp(dot_nt(keys, queries) + bias[...] - lse_in[number])
+        dkv_s[:, pl.ds(vcol, 128)] = b16(dot_nn(b16(probs), grads))
+        term = probs * dot_nt(kv_in[:, pl.ds(vcol, 128)], grads)
+        low = b16(term - probs * jnp.sum(term, axis=0, keepdims=True))
+        dkv_s[:, pl.ds(col, 128)] = b16(dot_nn(low, queries))
+        dq_s[:, pl.ds(col, 128)] = b16(pair_join(dot_tn(keys, low)) * 0.125)
+        return carry
+
+    lax.fori_loop(0, width // 128, pair, 0)
+    copies.wait()
+    gain_sum = jnp.zeros((1, width), jnp.float32)
+    shift_sum = jnp.zeros((1, width), jnp.float32)
+    for back, block in enumerate((xo, x1, x2, x3, x4)):
+        rows = pl.ds((4 - back) * tok, tok)
+        grad = dot_nt(dkv_s[rows, :], full[:, pl.ds(width, 2 * width)])
+        if back == 0:
+            grad = grad + dot_nt(dq_s[...], full[:, pl.ds(0, width)])
+            p_own[...] = grad
+        elif back in (1, 3):
+            p_y[back // 2] = b16(grad)
+        else:
+            p_z[back // 2 - 1] = b16(grad)
+        hat, _rate = norm_parts(f32(block[pl.ds(0, tok), :]))
+        gain_sum = gain_sum + jnp.sum(grad * hat, axis=0, keepdims=True)
+        shift_sum = shift_sum + jnp.sum(grad, axis=0, keepdims=True)
+    part = 384
+
+    def weight(number, carry):
+        col = pl.multiple_of(number * part, 128)
+        half = number // 3
+        at = pl.multiple_of((number - 3 * half) * part, 128)
+
+        def put(value):
+            value = b16(value)
+            for shard in range(8):
+                for cc in range(2):
+                    row = shard * 96 + cc * 48
+                    stage[cc, half, shard, pl.ds(0, 48), pl.ds(at, part)] = value[row : row + 48]
+
+        @pl.when(number < 2)
+        def _():
+            put(dot_tn(h_in[pl.ds(4 * tok, tok), :], dq_s[:, pl.ds(col, part)]))
+
+        @pl.when(number >= 2)
+        def _():
+            put(dot_tn(h_in[...], dkv_s[:, pl.ds(pl.multiple_of(col - width, 128), part)]))
+
+        return carry
+
+    lax.fori_loop(0, 3 * width // part, weight, 0)
+    vec = vec_in[...]
+    bias_q = jnp.sum(f32(dq_s[...]), axis=0, keepdims=True)
+    bias_v = jnp.sum(f32(dkv_s[:, pl.ds(width, width)]), axis=0, keepdims=True)
+    zero = jnp.zeros((1, width), jnp.float32)
+    vec = vec + jnp.concatenate([gain_sum, zero, shift_sum, zero, bias_q, bias_v, zero, zero], axis=0)
+    lane = lax.broadcasted_iota(jnp.int32, (8, 128), 1)
+    zrow = jnp.zeros((8, 128), jnp.float32)
+    for shard in range(8):
+        rolled = pltpu.roll(vec, width - shard * 96, 1) if shard else vec
+        top = jnp.concatenate([jnp.where(lane < 96, rolled[:, :128], 0.0), zrow], axis=0)
+        tail = jnp.broadcast_to(upb_in[:, pl.ds(shard * 384, 384)], (16, 384))
+        both = b16(jnp.concatenate([top, tail], axis=1))
+        for cc in range(2):
+            for xx in range(2):
+                stage[cc, xx, shard, pl.ds(48, 16), pl.ds(0, 512)] = both
+                stage[cc, xx, shard, pl.ds(48, 16), pl.ds(512, 640)] = jnp.zeros((16, 640), jnp.bfloat16)
+    outs = Copies(osems)
+    for shard in range(8):
+        zz = lax.rem(shard // 2 + 4 - z, 4)
+        yy = jnp.where(y == shard % 2, 0, 1)
+        for xx in range(2):
+            far = jnp.where(x == xx, 0, 1)
+            outs.add(stage.at[1 - c, xx, shard], q_other.at[far, yy, zz])
+            outs.add(stage.at[c, xx, shard], q_mine.at[far, yy, zz])
+    outs.wait()
+
+
+def finish_d_kernel(coords, f, fx, cf, cfx, out):
+    x, c, _y, _z = place(coords)
+    for piece, xx, cc in zip((f, fx, cf, cfx), (x, 1 - x, x, 1 - x), (c, c, 1 - c, 1 - c), strict=True):
+        out[pl.ds(pl.multiple_of(192 * cc + 96 * xx, 16), 96), :] = f32(piece[...])
+
+
+def finish_u_kernel(coords, f, fx, cf, cfx, up, out):
+    x, c, _y, _z = place(coords)
+    half_h, half_w = up.shape[1] // 2, out.shape[1] // 2
+    for piece, xx, cc in zip((f, fx, cf, cfx), (x, 1 - x, x, 1 - x), (c, c, 1 - c, 1 - c), strict=True):
+        rows = pl.ds(pl.multiple_of(48 * cc, 16), 48)
+        up[rows, pl.ds(pl.multiple_of(half_h * xx, 128), half_h)] = f32(piece[:, pl.ds(0, half_h)])
+        out[rows, pl.ds(pl.multiple_of(half_w * xx, 128), half_w)] = f32(piece[:, pl.ds(half_h, half_w)])
+
+
+def finish_q_kernel(coords, f, fx, cf, cfx, qkv):
+    x, c, _y, _z = place(coords)
+    cols = qkv.shape[1] // 2
+    for piece, xx, cc in zip((f, fx, cf, cfx), (x, 1 - x, x, 1 - x), (c, c, 1 - c, 1 - c), strict=True):
+        qkv[pl.ds(pl.multiple_of(48 * cc, 16), 48), pl.ds(pl.multiple_of(cols * xx, 128), cols)] = f32(
+            piece[pl.ds(0, 48), :]
+        )
+
+
+VM = pl.BlockSpec(memory_space=pltpu.VMEM)
+SM = pl.BlockSpec(memory_space=pltpu.SMEM)
+AN = pl.BlockSpec(memory_space=pl.ANY)
+
+
+def shape_of(shape, dtype):
+    return jax.ShapeDtypeStruct(shape, dtype)
+
+
+def call(kernel, ins, outs, out_shape, scratch=(), vmem=40, flops=0, moved=0):
+    return pl.pallas_call(
+        kernel,
+        in_specs=ins,
+        out_specs=outs,
+        out_shape=out_shape,
+        scratch_shapes=list(scratch),
+        compiler_params=pltpu.CompilerParams(vmem_limit_bytes=vmem << 20),
+        cost_estimate=pl.CostEstimate(flops=flops, bytes_accessed=moved, transcendentals=0),
+    )
+
+
+def swap_rep(value, bit):
+    return lax.ppermute(value, "rep", [(k, k ^ bit) for k in range(4)])
+
+
+def to_core(value):
+    return swap_rep(value, 1)
+
+
+def to_x(value):
+    return swap_rep(value, 2)
+
+
+def to_y(value):
+    return lax.ppermute(value, "seq", [(k, k ^ 1) for k in range(8)])
+
+
+def to_z(value, steps):
+    return lax.ppermute(value, "seq", [(k, (k + 2 * steps) % 8) for k in range(8)])
+
+
+def gather(piece):
+    rows, cols = piece.shape
+    along = [to_z(piece, k) for k in (1, 2, 3)]
+    across = to_y(jnp.concatenate([piece] + along, axis=0))
+    seven = jnp.concatenate(along + [across], axis=0)
+    other = to_x(seven)
+    return [v.reshape(7, rows, cols) for v in (seven, other, to_core(seven), to_core(other))]
+
+
+def reduce_pieces(other, mine, first, second):
+    came = to_core(other)
+
+    def part(index):
+        return f32(mine[index]) + f32(came[index])
+
+    came_1 = first(b16(part(1)))
+
+    def part_1(index):
+        return part((0,) + index) + f32(came_1[index])
+
+    came_2 = second(b16(part_1((1,))))
+
+    def part_2(index):
+        return part_1((0, index)) + f32(came_2[index])
+
+    total = part_2(0)
+    for step in (1, 2, 3):
+        total = total + f32(to_z(b16(part_2(step)), step))
+    total = b16(total)
+    over = to_x(total)
+    return total, over, to_core(total), to_core(over)
+
+
+def on_device_fast(
+    tokens,
+    segment_ids,
+    query_key_value_weight,
+    output_weight,
+    up_weight,
+    down_weight,
+    ln_gains,
+    ln_biases,
+    biases,
+    up_projection_bias,
+    cotangent,
+):
+    rep, seq = lax.axis_index("rep"), lax.axis_index("seq")
+    x, c, z, y = rep // 2, rep % 2, seq // 2, seq % 2
+    coords = jnp.stack([x, c, y, z]).astype(jnp.int32)
+    tok, width = tokens.shape[1:]
+    hidden = up_weight.shape[1]
+    keys = 5 * tok
+    bf, fl = jnp.bfloat16, jnp.float32
+    ids = jnp.pad(segment_ids.astype(bf), ((0, 15), (0, width - tok)))
+    own_tokens = jnp.concatenate([tokens[0], ids], axis=0)
+    small = jnp.concatenate([ln_gains, ln_biases, biases], axis=0)
+    small = jnp.concatenate(
+        [
+            jnp.pad(small, ((0, 0), (0, 128 - small.shape[1]))),
+            jnp.pad(up_projection_bias[None], ((0, 7), (0, 0))),
+        ],
+        axis=1,
+    )
+    small = jnp.pad(small, ((0, 8), (0, 3 * width // 2 - small.shape[1])))
+    piece_q = jnp.concatenate(
+        [
+            lax.dynamic_slice(
+                query_key_value_weight, (48 * c, 3 * width // 2 * x), (48, 3 * width // 2)
+            ),
+            small,
+        ],
+        axis=0,
+    )
+    piece_u = jnp.concatenate(
+        [
+            lax.dynamic_slice(up_weight, (48 * c, hidden // 2 * x), (48, hidden // 2)),
+            lax.dynamic_slice(output_weight, (48 * c, width // 2 * x), (48, width // 2)),
+        ],
+        axis=1,
+    )
+    piece_d = lax.dynamic_slice(down_weight, (192 * c + 96 * x, 0), (96, width))
+    x2 = to_z(own_tokens, 1)
+    x4 = to_z(own_tokens, 2)
+    near = jnp.where(y == 0, own_tokens, x2)
+    far = jnp.where(y == 0, x2, x4)
+    crossed = to_y(jnp.stack([near, far]))
+    x1, x3 = crossed[0], crossed[1]
+    got_q = gather(piece_q)
+    got_u = gather(piece_u)
+    got_d = gather(piece_d)
+    seg = jnp.concatenate([segment_ids, segment_ids], axis=1)
+    queries, kv, normed, attended, lse, start, vec, upb = call(
+        front_kernel,
+        [SM] + [VM] * 6 + [AN] * 6,
+        [VM] * 8,
+        [
+            shape_of((tok, width), bf),
+            shape_of((keys, 2 * width), bf),
+            shape_of((keys, width), bf),
+            shape_of((tok, width), bf),
+            shape_of((width // 128, 1, 2 * tok), fl),
+            shape_of((1, 2 * tok), jnp.int32),
+            shape_of((8, width), fl),
+            shape_of((1, hidden), fl),
+        ],
+        [
+            pltpu.VMEM((width, 3 * width), bf),
+            pltpu.VMEM((8, 16, 512), bf),
+            pltpu.VMEM((keys, 2 * tok), fl),
+            pltpu.SemaphoreType.DMA((29,)),
+            pltpu.SemaphoreType.DMA((8,)),
+        ],
+        flops=7 * 10**9,
+        moved=12 * 10**6,
+    )(coords, seg, own_tokens, x1, x2, x3, x4, piece_q, query_key_value_weight, *got_q)
+    grad_y = cotangent[0]
+    result, grad_first, grad_attended, d_other, d_mine, u_other, u_mine, vec_g, upb_g = call(
+        mid_kernel,
+        [SM] + [VM] * 5 + [AN] * 11,
+        [VM] * 3 + [AN] * 4 + [VM] * 2,
+        [
+            shape_of((tok, width), bf),
+            shape_of((tok, width), fl),
+            shape_of((tok, width), bf),
+            shape_of((2, 2, 4, 96, width), bf),
+            shape_of((2, 2, 4, 96, width), bf),
+            shape_of((2, 2, 4, 48, hidden // 2 + width // 2), bf),
+            shape_of((2, 2, 4, 48, hidden // 2 + width // 2), bf),
+            shape_of((8, width), fl),
+            shape_of((1, hidden), fl),
+        ],
+        [
+            pltpu.VMEM((width, hidden), bf),
+            pltpu.VMEM((width, width), bf),
+            pltpu.VMEM((hidden, width), bf),
+            pltpu.VMEM((hidden, width), bf),
+            pltpu.VMEM((width, hidden), bf),
+            pltpu.VMEM((width, width), bf),
+            pltpu.VMEM((tok, width), bf),
+            pltpu.VMEM((tok, width), fl),
+            pltpu.VMEM((tok, width), fl),
+            pltpu.SemaphoreType.DMA((3 + 84,)),
+            pltpu.SemaphoreType.DMA((96,)),
+        ],
+        vmem=48,
+        flops=12 * 10**9,
+        moved=24 * 10**6,
+    )(
+        coords, attended, own_tokens, grad_y, vec, upb,
+        up_weight, output_weight, *got_u, down_weight, *got_d,
+    )
+    done_d = reduce_pieces(d_other, d_mine, to_x, to_y)
+    done_u = reduce_pieces(u_other, u_mine, to_y, to_x)
+    q_other, q_mine, p_own, p_y, p_z = call(
+        back_kernel,
+        [SM] + [VM] * 13 + [AN] * 5,
+        [AN] * 2 + [VM] * 3,
+        [
+            shape_of((2, 2, 4, 64, 3 * width // 2), bf),
+            shape_of((2, 2, 4, 64, 3 * width // 2), bf),
+            shape_of((tok, width), fl),
+            shape_of((2, tok, width), bf),
+            shape_of((2, tok, width), bf),
+        ],
+        [
+            pltpu.VMEM((width, 3 * width), bf),
+            pltpu.VMEM((keys, 2 * tok), fl),
+            pltpu.VMEM((tok, width), bf),
+            pltpu.VMEM((keys, 2 * width), bf),
+            pltpu.VMEM((2, 2, 8, 64, 3 * width // 2), bf),
+            pltpu.SemaphoreType.DMA((29,)),
+            pltpu.SemaphoreType.DMA((32,)),
+        ],
+        flops=14 * 10**9,
+        moved=20 * 10**6,
+    )(
+        coords, start, queries, kv, normed, lse, grad_attended, vec_g, upb_g,
+        own_tokens, x1, x2, x3, x4, query_key_value_weight, *got_q,
+    )
+    done_q = reduce_pieces(q_other, q_mine, to_x, to_y)
+    came = to_y(p_y)
+    even = y == 0
+    sum_own = p_own + jnp.where(even, f32(came[0]), 0.0)
+    sum_2 = b16(f32(p_z[0]) + jnp.where(even, f32(came[1]), f32(came[0])))
+    sum_4 = b16(f32(p_z[1]) + jnp.where(even, 0.0, f32(came[1])))
+    back_2, back_4 = to_z(sum_2, 3), to_z(sum_4, 2)
+    grad_tokens = call(
+        tokens_kernel,
+        [VM] * 6,
+        VM,
+        shape_of((tok, width), fl),
+        vmem=16,
+        flops=10**6,
+        moved=3 * 10**6,
+    )(sum_own, back_2, back_4, grad_first, own_tokens, vec)
+    grad_down = call(
+        finish_d_kernel, [SM] + [VM] * 4, VM, shape_of(down_weight.shape, fl), vmem=16, moved=2 * 10**6
+    )(coords, *done_d)
+    grad_up, grad_out = call(
+        finish_u_kernel,
+        [SM] + [VM] * 4,
+        [VM] * 2,
+        [shape_of(up_weight.shape, fl), shape_of(output_weight.shape, fl)],
+        vmem=16,
+        moved=2 * 10**6,
+    )(coords, *done_u)
+    grad_qkv = call(
+        finish_q_kernel, [SM] + [VM] * 4, VM, shape_of(query_key_value_weight.shape, fl), vmem=16, moved=2 * 10**6
+    )(coords, *done_q)
+    sums = f32(done_q[0][48:56, :512])
+    part = ln_gains.shape[1]
+    return (
+        result[None],
+        grad_tokens[None],
+        grad_qkv,
+        grad_out,
+        grad_up,
+        grad_down,
+        sums[0:2, :part],
+        sums[2:4, :part],
+        sums[4:8, :part],
+        sums[0, 128:512],
+    )
+
+
+def tokens_kernel(own, near, far, dr, xo, vec_in, grad_out):
+    tok = own.shape[0]
+    hat, rate = norm_parts(f32(xo[pl.ds(0, tok), :]))
+    grad = own[...] + f32(near[...]) + f32(far[...])
+    grad_out[...] = dr[...] + norm_back(grad, hat, rate, vec_in[0:1, :])
+
+
 def solution(mesh):
     placed = (
         P("rep", "seq", None),
@@ -306,8 +997,10 @@
         P("seq"),
         P("rep", "seq", None),
     )
+    shape = dict(mesh.shape)
+    small_slice = shape["rep"] == 4 and shape["seq"] == 8
     return jax.shard_map(
-        on_device,
+        on_device_fast if small_slice else on_device,
         mesh=mesh,
         in_specs=placed,
         out_specs=(

time: 1420 us -> 357 us (0.25)
  waiting for transfers between devices: 1120 us -> 180 us
  blocking collectives: 136 us -> 0 us
  starting transfers between devices: 0.86 us -> 84.9 us
  Pallas kernels: 0 us -> 67.4 us
  matrix products: 63.2 us -> 0 us
  other arithmetic: 41.3 us -> 5.79 us
  local copies, waits for them, and re-layouts: 41.4 us -> 17.6 us
  between operations: 15.8 us -> 1.1 us
    reduce_scatter x4 -> x0, waiting for transfers between devices: 503 us -> none  [the longest x1 165 us: on_device(): lax.psum_scatter(grad_down, 'seq', scatter_dimension=0, tiled=True)]
    unnamed x19 -> x0, waiting for transfers between devices: 331 us -> none
    all_gather x6 -> x0, waiting for transfers between devices: 243 us -> none  [the longest x1 78 us: on_device(): lax.all_gather(up_weight, 'seq', axis=0, tiled=True)]
    ppermute x0 -> x54, waiting for transfers between devices: none -> 180 us  [the longest x24 79.5 us: swap_rep(): return lax.ppermute(value, 'rep', [(k, k ^ bit) for k in range(4)])]
    all_gather x5 -> x0, blocking collectives: 94.6 us -> none  [the longest x1 26.3 us: on_device(): lax.all_gather(up_projection_bias, 'seq', axis=0, tiled=True)]
    ppermute x0 -> x54, starting transfers between devices: none -> 84.9 us  [the longest x22 61 us: to_z(): lax.ppermute(value, 'seq', [(k, (k + 2 * steps) % 8) for k in range(8)])]
    pallas_call x0 -> x7, Pallas kernels: none -> 67.4 us  [the longest x1 25.9 us: on_device_fast(): call(back_kernel, [SM] + [VM] * 13 + [AN] * 5, [AN] * 2 + [VM] * 3, [shap...]
    dot_general x23 -> x0, matrix products: 63.2 us -> none  [the longest x1 6.47 us: on_device(): jnp.einsum('td,tf->df', hidden_second, grad_up_pre, preferred_element_typ...]
  transfers between devices with their start and end apart: 15 -> 54, of which waited for: 15 -> 20; matrix products, arithmetic and copies ran while one was open for 7% -> 5% of each run, Pallas kernels for 0% -> 5%
where the time goes in v1:
time: 357 us; the launch traced here: 356 us
  waiting for transfers between devices  180 us (50%)
  starting transfers between devices  84.9 us (24%)
  Pallas kernels  67.4 us (19%)
  local copies, waits for them, and re-layouts  17.6 us (5%)
  other arithmetic  5.79 us (2%)
    ppermute x24, waiting for transfers between devices, swap_rep(): return lax.ppermute(value, 'rep', [(k, k ^ bit) for k in range(4)])  79.5 us
    ppermute x22, starting transfers between devices, to_z(): lax.ppermute(value, 'seq', [(k, (k + 2 * steps) % 8) for k in range(8)])  61 us
    ppermute x8, waiting for transfers between devices, to_y(): return lax.ppermute(value, 'seq', [(k, k ^ 1) for k in range(8)])  58.3 us
    ppermute x22, waiting for transfers between devices, to_z(): lax.ppermute(value, 'seq', [(k, (k + 2 * steps) % 8) for k in range(8)])  41.7 us
    pallas_call x1, Pallas kernels, on_device_fast(): call(back_kernel, [SM] + [VM] * 13 + [AN] * 5, [AN] * 2 + [VM] * 3, [shap...  25.9 us
    pallas_call x1, Pallas kernels, on_device_fast(): call(mid_kernel, [SM] + [VM] * 5 + [AN] * 11, [VM] * 3 + [AN] * 4 + [VM]...  22.6 us
    pallas_call x1, Pallas kernels, on_device_fast(): call(front_kernel, [SM] + [VM] * 6 + [AN] * 6, [VM] * 8, [shape_of((tok,...  12.7 us
    ppermute x24, starting transfers between devices, swap_rep(): return lax.ppermute(value, 'rep', [(k, k ^ bit) for k in range(4)])  12.3 us
  transfers between devices with their start and end apart: 54, of which 20 were waited for; matrix products, arithmetic and copies ran while one was open for 5% of the time, Pallas kernels for 5%

profile of v1, /device:TPU:0, one launch (start us, length us, event | category | flops | bytes accessed | tf_op | source)
XLA Modules:
  0.0 356.2 jit_solution(4519167240748650767)
XLA Ops:
  1.7 5.1 %collective-permute-start.19 = (bf16[96,768]{1,0:T(8,128)(2,1)S(1)}, bf16[96,768]{1,0:T(8,128)(2,1)S(1)}, u32[]{:S(2)}, u32[]{:S(2)}) collective-permute-start(bf16[96,768]{1,0:T(8,128)(2,1)S(1)} %constant_dynamic-slice_fusion), channel_id=1, source_target_pairs={{0,6},{1,7},{2,0},{3,1},{4,2},{5,3},{6,4},{7,5},{8,14},{9,15},{10,... | collective-permute-start | bytes 442376 | tf_op jit(solution)/shard_map/ppermute | solution.py:751
  11.4 2.0 collective-permute-start.4
  16.6 6.9 %collective-permute-done.3 = bf16[64,1152]{1,0:T(8,128)(2,1)S(1)} collective-permute-done((bf16[64,1152]{1,0:T(8,128)(2,1)S(1)}, bf16[64,1152]{1,0:T(8,128)(2,1)S(1)}, u32[]{:S(2)}, u32[]{:S(2)}) %collective-permute-start.3) | collective-permute-done | bytes 147488 | tf_op jit(solution)/shard_map/ppermute | solution.py:751
  24.2 4.5 %collective-permute-done.4 = bf16[64,1152]{1,0:T(8,128)(2,1)S(1)} collective-permute-done((bf16[64,1152]{1,0:T(8,128)(2,1)S(1)}, bf16[64,1152]{1,0:T(8,128)(2,1)S(1)}, u32[]{:S(2)}, u32[]{:S(2)}) %collective-permute-start.4) | collective-permute-done | bytes 147488 | tf_op jit(solution)/shard_map/ppermute | solution.py:751
  28.7 7.4 %collective-permute-start.11 = (bf16[48,1920]{1,0:T(8,128)(2,1)S(1)}, bf16[48,1920]{1,0:T(8,128)(2,1)S(1)}, u32[]{:S(2)}, u32[]{:S(2)}) collective-permute-start(bf16[48,1920]{1,0:T(8,128)(2,1)S(1)} %pad_maximum_fusion.3), channel_id=1, source_target_pairs={{0,4},{1,5},{2,6},{3,7},{4,0},{5,1},{6,2},{7,3},{8,12},{9,13},{10,... | collective-permute-start | bytes 552968 | tf_op jit(solution)/shard_map/ppermute | solution.py:751
  41.1 3.3 collective-permute-done.5
  44.5 25.8 %collective-permute-start = (bf16[208,768]{1,0:T(8,128)(2,1)S(1)}, bf16[208,768]{1,0:T(8,128)(2,1)S(1)}, u32[]{:S(2)}, u32[]{:S(2)}) collective-permute-start(bf16[208,768]{1,0:T(8,128)(2,1)S(1)} %fusion.20.xo), channel_id=1, source_target_pairs={{0,2},{1,3},{2,4},{3,5},{4,6},{5,7},{6,0},{7,1},{8,10},{9,11},{10,... | collective-permute-start | bytes 958472 | tf_op jit(solution)/shard_map/ppermute | solution.py:751
  76.1 23.2 %collective-permute-done.6 = bf16[256,1152]{1,0:T(8,128)(2,1)S(1)} collective-permute-done((bf16[256,1152]{1,0:T(8,128)(2,1)S(1)}, bf16[256,1152]{1,0:T(8,128)(2,1)S(1)}, u32[]{:S(2)}, u32[]{:S(2)}) %collective-permute-start.6) | collective-permute-done | bytes 589856 | tf_op jit(solution)/shard_map/ppermute | solution.py:747
  100.9 9.9 %collective-permute-done.13 = bf16[192,1920]{1,0:T(8,128)(2,1)S(1)} collective-permute-done((bf16[192,1920]{1,0:T(8,128)(2,1)S(1)}, bf16[192,1920]{1,0:T(8,128)(2,1)S(1)}, u32[]{:S(2)}, u32[]{:S(2)}) %collective-permute-start.13) | collective-permute-done | bytes 737312 | tf_op jit(solution)/shard_map/ppermute | solution.py:747
  117.9 3.2 collective-permute-done.7
  121.0 11.8 %collective-permute-done.2 = bf16[2,208,768]{2,1,0:T(8,128)(2,1)S(1)} collective-permute-done((bf16[2,208,768]{2,1,0:T(8,128)(2,1)S(1)}, bf16[2,208,768]{2,1,0:T(8,128)(2,1)S(1)}, u32[]{:S(2)}, u32[]{:S(2)}) %collective-permute-start.2) | collective-permute-done | bytes 639008 | tf_op jit(solution)/shard_map/ppermute | solution.py:747
  132.9 15.8 %collective-permute-done.14 = bf16[336,1920]{1,0:T(8,128)(2,1)} collective-permute-done((bf16[336,1920]{1,0:T(8,128)(2,1)}, bf16[336,1920]{1,0:T(8,128)(2,1)}, u32[]{:S(2)}, u32[]{:S(2)}) %collective-permute-start.14) | collective-permute-done | bytes 1290272 | tf_op jit(solution)/shard_map/ppermute | solution.py:735
  149.2 16.5 %collective-permute-done.21 = bf16[672,768]{1,0:T(8,128)(2,1)} collective-permute-done((bf16[672,768]{1,0:T(8,128)(2,1)}, bf16[672,768]{1,0:T(8,128)(2,1)}, u32[]{:S(2)}, u32[]{:S(2)}) %collective-permute-start.21) | collective-permute-done | bytes 1032224 | tf_op jit(solution)/shard_map/ppermute | solution.py:735
  165.9 12.7 %shard_map.186 = (bf16[192,768]{1,0:T(8,128)(2,1)S(1)}, bf16[960,1536]{1,0:T(8,128)(2,1)S(1)}, bf16[960,768]{1,0:T(8,128)(2,1)S(1)}, bf16[192,768]{1,0:T(8,128)(...) custom-call(s32[4]{0:T(128)S(1)} %pad_add_fusion.1.coords, ...), custom_call_target="tpu_custom_call" | custom-call | flops 7000000000 | bytes 12000000 | tf_op jit(solution)/shard_map/pallas_call | solution.py:845
  181.6 22.6 %shard_map.187 = (bf16[192,768]{1,0:T(8,128)(2,1)}, f32[192,768]{1,0:T(8,128)S(1)}, bf16[192,768]{1,0:T(8,128)(2,1)S(1)}, bf16[2,2,4,96,768]{4,3,2,1,0:T(8,128)(...) custom-call(s32[4]{0:T(128)S(1)} %pad_add_fusion.1.coords, ...), custom_call_target="tpu_custom_call" | custom-call | flops 12000000000 | bytes 24000000 | tf_op jit(solution)/shard_map/pallas_call | solution.py:870
  204.2 25.9 %shard_map.188 = (bf16[2,2,4,64,1152]{4,3,2,1,0:T(8,128)(2,1)S(1)}, bf16[2,2,4,64,1152]{4,3,2,1,0:T(8,128)(2,1)}, f32[192,768]{1,0:T(8,128)S(1)}, bf16[2,192,768...) custom-call(s32[4]{0:T(128)S(1)} %pad_add_fusion.1.coords, s32[1,384]{1,0:T(1,128)S(1)} %get-tuple-element.38.start_in, ...), custom_call_target="tpu_custom_call" | custom-call | flops 14000000000 | bytes 20000000 | tf_op jit(solution)/shard_map/pallas_call | solution.py:907
  231.2 6.2 %collective-permute-done.27 = bf16[2,2,4,64,1152]{4,3,2,1,0:T(8,128)(2,1)S(1)} collective-permute-done((bf16[2,2,4,64,1152]{4,3,2,1,0:T(8,128)(2,1)S(1)}, bf16[2,2,4,64,1152]{4,3,2,1,0:T(8,128)(2,1)S(1)}, u32[]{:S(2)}, u32[]{:S(2)}) %collective-permute-start.27) | collective-permute-done | bytes 2359328 | tf_op jit(solution)/shard_map/ppermute | solution.py:735
  237.4 1.7 fusion.2
  246.3 21.8 %collective-permute-done.28 = bf16[2,4,64,1152]{3,2,1,0:T(8,128)(2,1)S(1)} collective-permute-done((bf16[2,4,64,1152]{3,2,1,0:T(8,128)(2,1)S(1)}, bf16[2,4,64,1152]{3,2,1,0:T(8,128)(2,1)S(1)}, u32[]{:S(2)}, u32[]{:S(2)}) %collective-permute-start.28) | collective-permute-done | bytes 1179680 | tf_op jit(solution)/shard_map/ppermute | solution.py:735
  270.1 2.9 collective-permute-start.25
  273.1 12.0 %collective-permute-done.26.far = bf16[192,768]{1,0:T(8,128)(2,1)S(1)} collective-permute-done((bf16[192,768]{1,0:T(8,128)(2,1)S(1)}, bf16[192,768]{1,0:T(8,128)(2,1)S(1)}, u32[]{:S(2)}, u32[]{:S(2)}) %collective-permute-start.26) | collective-permute-done | bytes 294944 | tf_op jit(solution)/shard_map/ppermute | solution.py:751
  286.4 6.4 %collective-permute-done.46 = bf16[2,4,96,768]{3,2,1,0:T(8,128)(2,1)S(1)} collective-permute-done((bf16[2,4,96,768]{3,2,1,0:T(8,128)(2,1)S(1)}, bf16[2,4,96,768]{3,2,1,0:T(8,128)(2,1)S(1)}, u32[]{:S(2)}, u32[]{:S(2)}) %collective-permute-start.46) | collective-permute-done | bytes 1179680 | tf_op jit(solution)/shard_map/ppermute | solution.py:735
  294.5 6.6 %collective-permute-done.29 = bf16[4,64,1152]{2,1,0:T(8,128)(2,1)S(1)} collective-permute-done((bf16[4,64,1152]{2,1,0:T(8,128)(2,1)S(1)}, bf16[4,64,1152]{2,1,0:T(8,128)(2,1)S(1)}, u32[]{:S(2)}, u32[]{:S(2)}) %collective-permute-start.29) | collective-permute-done | bytes 589856 | tf_op jit(solution)/shard_map/ppermute | solution.py:747
  302.0 3.2 collective-permute-start.32
  306.1 6.8 %collective-permute-done.47 = bf16[4,96,768]{2,1,0:T(8,128)(2,1)S(1)} collective-permute-done((bf16[4,96,768]{2,1,0:T(8,128)(2,1)S(1)}, bf16[4,96,768]{2,1,0:T(8,128)(2,1)S(1)}, u32[]{:S(2)}, u32[]{:S(2)}) %collective-permute-start.47) | collective-permute-done | bytes 589856 | tf_op jit(solution)/shard_map/ppermute | solution.py:747
  313.8 3.2 collective-permute-start.50
  317.3 5.0 %collective-permute-done.38 = bf16[4,48,1920]{2,1,0:T(8,128)(2,1)S(1)} collective-permute-done((bf16[4,48,1920]{2,1,0:T(8,128)(2,1)S(1)}, bf16[4,48,1920]{2,1,0:T(8,128)(2,1)S(1)}, u32[]{:S(2)}, u32[]{:S(2)}) %collective-permute-start.38) | collective-permute-done | bytes 737312 | tf_op jit(solution)/shard_map/ppermute | solution.py:735
  323.7 3.3 collective-permute-start.41
  327.0 6.8 %collective-permute-done.49 = bf16[96,768]{1,0:T(8,128)(2,1)S(1)} collective-permute-done((bf16[96,768]{1,0:T(8,128)(2,1)S(1)}, bf16[96,768]{1,0:T(8,128)(2,1)S(1)}, u32[]{:S(2)}, u32[]{:S(2)}) %collective-permute-start.49) | collective-permute-done | bytes 147488 | tf_op jit(solution)/shard_map/ppermute | solution.py:751
  335.5 8.2 %collective-permute-done.40 = bf16[48,1920]{1,0:T(8,128)(2,1)S(1)} collective-permute-done((bf16[48,1920]{1,0:T(8,128)(2,1)S(1)}, bf16[48,1920]{1,0:T(8,128)(2,1)S(1)}, u32[]{:S(2)}, u32[]{:S(2)}) %collective-permute-start.40) | collective-permute-done | bytes 184352 | tf_op jit(solution)/shard_map/ppermute | solution.py:751
  345.1 4.5 %collective-permute-done.42.fx = bf16[48,1920]{1,0:T(8,128)(2,1)S(1)} collective-permute-done((bf16[48,1920]{1,0:T(8,128)(2,1)S(1)}, bf16[48,1920]{1,0:T(8,128)(2,1)S(1)}, u32[]{:S(2)}, u32[]{:S(2)}) %collective-permute-start.42) | collective-permute-done | bytes 184352 | tf_op jit(solution)/shard_map/ppermute | solution.py:735
  354.5 1.7 shard_map.191
  (162 shorter events, 58.3 us)
Async XLA Ops:
  1.7 37.3 %collective-permute-start.19 = (bf16[96,768]{1,0:T(8,128)(2,1)S(1)}, bf16[96,768]{1,0:T(8,128)(2,1)S(1)}, u32[]{:S(2)}, u32[]{:S(2)}) collective-permute-start(bf16[96,768]{1,0:T(8,128)(2,1)S(1)} %constant_dynamic-slice_fusion), channel_id=1, source_target_pairs={{0,6},{1,7},{2,0},{3,1},{4,2},{5,3},{6,4},{7,5},{8,14},{9,15},{10,... | collective-permute-start | bytes 442376 | tf_op jit(solution)/shard_map/ppermute | solution.py:751
  6.8 32.8 %collective-permute-start.18 = (bf16[96,768]{1,0:T(8,128)(2,1)S(1)}, bf16[96,768]{1,0:T(8,128)(2,1)S(1)}, u32[]{:S(2)}, u32[]{:S(2)}) collective-permute-start(bf16[96,768]{1,0:T(8,128)(2,1)S(1)} %constant_dynamic-slice_fusion), channel_id=1, source_target_pairs={{0,4},{1,5},{2,6},{3,7},{4,0},{5,1},{6,2},{7,3},{8,12},{9,13},{10,... | collective-permute-start | bytes 442376 | tf_op jit(solution)/shard_map/ppermute | solution.py:751
  6.8 30.1 %collective-permute-start.17 = (bf16[96,768]{1,0:T(8,128)(2,1)S(1)}, bf16[96,768]{1,0:T(8,128)(2,1)S(1)}, u32[]{:S(2)}, u32[]{:S(2)}) collective-permute-start(bf16[96,768]{1,0:T(8,128)(2,1)S(1)} %constant_dynamic-slice_fusion), channel_id=1, source_target_pairs={{0,2},{1,3},{2,4},{3,5},{4,6},{5,7},{6,0},{7,1},{8,10},{9,11},{10,... | collective-permute-start | bytes 442376 | tf_op jit(solution)/shard_map/ppermute | solution.py:751
  11.4 17.3 %collective-permute-start.4 = (bf16[64,1152]{1,0:T(8,128)(2,1)S(1)}, bf16[64,1152]{1,0:T(8,128)(2,1)S(1)}, u32[]{:S(2)}, u32[]{:S(2)}) collective-permute-start(bf16[64,1152]{1,0:T(8,128)(2,1)S(1)} %pad_maximum_fusion.4.first), channel_id=1, source_target_pairs={{0,4},{1,5},{2,6},{3,7},{4,0},{5,1},{6,2},{7,3},{8,12},{9,13},{10,... | collective-permute-start | bytes 442376 | tf_op jit(solution)/shard_map/ppermute | solution.py:751
  23.5 46.8 %collective-permute-start.12 = (bf16[48,1920]{1,0:T(8,128)(2,1)S(1)}, bf16[48,1920]{1,0:T(8,128)(2,1)S(1)}, u32[]{:S(2)}, u32[]{:S(2)}) collective-permute-start(bf16[48,1920]{1,0:T(8,128)(2,1)S(1)} %pad_maximum_fusion.3), channel_id=1, source_target_pairs={{0,6},{1,7},{2,0},{3,1},{4,2},{5,3},{6,4},{7,5},{8,14},{9,15},{10,... | collective-permute-start | bytes 552968 | tf_op jit(solution)/shard_map/ppermute | solution.py:751
  28.7 43.2 %collective-permute-start.11 = (bf16[48,1920]{1,0:T(8,128)(2,1)S(1)}, bf16[48,1920]{1,0:T(8,128)(2,1)S(1)}, u32[]{:S(2)}, u32[]{:S(2)}) collective-permute-start(bf16[48,1920]{1,0:T(8,128)(2,1)S(1)} %pad_maximum_fusion.3), channel_id=1, source_target_pairs={{0,4},{1,5},{2,6},{3,7},{4,0},{5,1},{6,2},{7,3},{8,12},{9,13},{10,... | collective-permute-start | bytes 552968 | tf_op jit(solution)/shard_map/ppermute | solution.py:751
  39.0 33.4 %collective-permute-start.10 = (bf16[48,1920]{1,0:T(8,128)(2,1)S(1)}, bf16[48,1920]{1,0:T(8,128)(2,1)S(1)}, u32[]{:S(2)}, u32[]{:S(2)}) collective-permute-start(bf16[48,1920]{1,0:T(8,128)(2,1)S(1)} %pad_maximum_fusion.3), channel_id=1, source_target_pairs={{0,2},{1,3},{2,4},{3,5},{4,6},{5,7},{6,0},{7,1},{8,10},{9,11},{10,... | collective-permute-start | bytes 552968 | tf_op jit(solution)/shard_map/ppermute | solution.py:751
  39.6 76.0 %collective-permute-start.1 = (bf16[208,768]{1,0:T(8,128)(2,1)S(1)}, bf16[208,768]{1,0:T(8,128)(2,1)S(1)}, u32[]{:S(2)}, u32[]{:S(2)}) collective-permute-start(bf16[208,768]{1,0:T(8,128)(2,1)S(1)} %fusion.20.xo), channel_id=1, source_target_pairs={{0,4},{1,5},{2,6},{3,7},{4,0},{5,1},{6,2},{7,3},{8,12},{9,13},{10,... | collective-permute-start | bytes 958472 | tf_op jit(solution)/shard_map/ppermute | solution.py:751
  44.5 71.6 %collective-permute-start = (bf16[208,768]{1,0:T(8,128)(2,1)S(1)}, bf16[208,768]{1,0:T(8,128)(2,1)S(1)}, u32[]{:S(2)}, u32[]{:S(2)}) collective-permute-start(bf16[208,768]{1,0:T(8,128)(2,1)S(1)} %fusion.20.xo), channel_id=1, source_target_pairs={{0,2},{1,3},{2,4},{3,5},{4,6},{5,7},{6,0},{7,1},{8,10},{9,11},{10,... | collective-permute-start | bytes 958472 | tf_op jit(solution)/shard_map/ppermute | solution.py:751
  70.3 44.3 %collective-permute-start.20 = (bf16[384,768]{1,0:T(8,128)(2,1)S(1)}, bf16[384,768]{1,0:T(8,128)(2,1)S(1)}, u32[]{:S(2)}, u32[]{:S(2)}) collective-permute-start(bf16[384,768]{1,0:T(8,128)(2,1)S(1)} %pad_maximum_fusion.2), channel_id=1, source_target_pairs={{0,1},{1,0},{2,3},{3,2},{4,5},{5,4},{6,7},{7,6},{8,9},{9,8},{10,11... | collective-permute-start | bytes 1769480 | tf_op jit(solution)/shard_map/ppermute | solution.py:747
  71.9 27.4 %collective-permute-start.6 = (bf16[256,1152]{1,0:T(8,128)(2,1)S(1)}, bf16[256,1152]{1,0:T(8,128)(2,1)S(1)}, u32[]{:S(2)}, u32[]{:S(2)}) collective-permute-start(bf16[256,1152]{1,0:T(8,128)(2,1)S(1)} %get-tuple-element.75), channel_id=1, source_target_pairs={{0,1},{1,0},{2,3},{3,2},{4,5},{5,4},{6,7},{7,6},{8,9},{9,8},{10,11... | collective-permute-start | bytes 1769480 | tf_op jit(solution)/shard_map/ppermute | solution.py:747
  72.5 38.4 %collective-permute-start.13 = (bf16[192,1920]{1,0:T(8,128)(2,1)S(1)}, bf16[192,1920]{1,0:T(8,128)(2,1)S(1)}, u32[]{:S(2)}, u32[]{:S(2)}) collective-permute-start(bf16[192,1920]{1,0:T(8,128)(2,1)S(1)} %pad_maximum_fusion), channel_id=1, source_target_pairs={{0,1},{1,0},{2,3},{3,2},{4,5},{5,4},{6,7},{7,6},{8,9},{9,8},{10,11... | collective-permute-start | bytes 2211848 | tf_op jit(solution)/shard_map/ppermute | solution.py:747
  99.4 21.7 %collective-permute-start.7 = (bf16[448,1152]{1,0:T(8,128)(2,1)S(1)}, bf16[448,1152]{1,0:T(8,128)(2,1)}, u32[]{:S(2)}, u32[]{:S(2)}) collective-permute-start(bf16[448,1152]{1,0:T(8,128)(2,1)S(1)} %constant_dynamic-update-slice_fusion.5), channel_id=1, source_target_pairs={{0,16},{8,24},{16,0},{24,8},{1,17},{9,25},{17,1},{25,9},{2,18},{10... | collective-permute-start | bytes 3096584 | tf_op jit(solution)/shard_map/ppermute | solution.py:735
  111.8 36.9 %collective-permute-start.14 = (bf16[336,1920]{1,0:T(8,128)(2,1)}, bf16[336,1920]{1,0:T(8,128)(2,1)}, u32[]{:S(2)}, u32[]{:S(2)}) collective-permute-start(bf16[336,1920]{1,0:T(8,128)(2,1)} %constant_dynamic-update-slice_fusion.9), channel_id=1, source_target_pairs={{0,16},{8,24},{16,0},{24,8},{1,17},{9,25},{17,1},{25,9},{2,18},{10... | collective-permute-start | bytes 3870728 | tf_op jit(solution)/shard_map/ppermute | solution.py:735
  114.6 34.0 %collective-permute-start.8 = (bf16[448,1152]{1,0:T(8,128)(2,1)S(1)}, bf16[448,1152]{1,0:T(8,128)(2,1)}, u32[]{:S(2)}, u32[]{:S(2)}) collective-permute-start(bf16[448,1152]{1,0:T(8,128)(2,1)S(1)} %constant_dynamic-update-slice_fusion.5), channel_id=1, source_target_pairs={{0,8},{8,0},{16,24},{24,16},{1,9},{9,1},{17,25},{25,17},{2,10},{10... | collective-permute-start | bytes 3096584 | tf_op jit(solution)/shard_map/ppermute | solution.py:735
  115.5 50.2 %collective-permute-start.21 = (bf16[672,768]{1,0:T(8,128)(2,1)}, bf16[672,768]{1,0:T(8,128)(2,1)}, u32[]{:S(2)}, u32[]{:S(2)}) collective-permute-start(bf16[672,768]{1,0:T(8,128)(2,1)} %constant_dynamic-update-slice_fusion.13), channel_id=1, source_target_pairs={{0,16},{8,24},{16,0},{24,8},{1,17},{9,25},{17,1},{25,9},{2,18},{10... | collective-permute-start | bytes 3096584 | tf_op jit(solution)/shard_map/ppermute | solution.py:735
  116.3 16.6 %collective-permute-start.2 = (bf16[2,208,768]{2,1,0:T(8,128)(2,1)S(1)}, bf16[2,208,768]{2,1,0:T(8,128)(2,1)S(1)}, u32[]{:S(2)}, u32[]{:S(2)}) collective-permute-start(bf16[2,208,768]{2,1,0:T(8,128)(2,1)S(1)} %pad_maximum_fusion.1), channel_id=1, source_target_pairs={{0,1},{1,0},{2,3},{3,2},{4,5},{5,4},{6,7},{7,6},{8,9},{9,8},{10,11... | collective-permute-start | bytes 1916936 | tf_op jit(solution)/shard_map/ppermute | solution.py:747
  121.0 44.8 %collective-permute-start.9 = (bf16[448,1152]{1,0:T(8,128)(2,1)}, bf16[448,1152]{1,0:T(8,128)(2,1)}, u32[]{:S(2)}, u32[]{:S(2)}) collective-permute-start(bf16[448,1152]{1,0:T(8,128)(2,1)} %collective-permute-done.7), channel_id=1, source_target_pairs={{0,8},{8,0},{16,24},{24,16},{1,9},{9,1},{17,25},{25,17},{2,10},{10... | collective-permute-start | bytes 3096584 | tf_op jit(solution)/shard_map/ppermute | solution.py:735
  132.9 47.3 %collective-permute-start.15 = (bf16[336,1920]{1,0:T(8,128)(2,1)}, bf16[336,1920]{1,0:T(8,128)(2,1)}, u32[]{:S(2)}, u32[]{:S(2)}) collective-permute-start(bf16[336,1920]{1,0:T(8,128)(2,1)} %constant_dynamic-update-slice_fusion.9), channel_id=1, source_target_pairs={{0,8},{8,0},{16,24},{24,16},{1,9},{9,1},{17,25},{25,17},{2,10},{10... | collective-permute-start | bytes 3870728 | tf_op jit(solution)/shard_map/ppermute | solution.py:735
  148.7 31.5 %collective-permute-start.16 = (bf16[336,1920]{1,0:T(8,128)(2,1)}, bf16[336,1920]{1,0:T(8,128)(2,1)}, u32[]{:S(2)}, u32[]{:S(2)}) collective-permute-start(bf16[336,1920]{1,0:T(8,128)(2,1)} %collective-permute-done.14), channel_id=1, source_target_pairs={{0,8},{8,0},{16,24},{24,16},{1,9},{9,1},{17,25},{25,17},{2,10},{10... | collective-permute-start | bytes 3870728 | tf_op jit(solution)/shard_map/ppermute | solution.py:735
  148.7 31.5 %collective-permute-start.22 = (bf16[672,768]{1,0:T(8,128)(2,1)}, bf16[672,768]{1,0:T(8,128)(2,1)S(1)}, u32[]{:S(2)}, u32[]{:S(2)}) collective-permute-start(bf16[672,768]{1,0:T(8,128)(2,1)} %constant_dynamic-update-slice_fusion.13), channel_id=1, source_target_pairs={{0,8},{8,0},{16,24},{24,16},{1,9},{9,1},{17,25},{25,17},{2,10},{10... | collective-permute-start | bytes 3096584 | tf_op jit(solution)/shard_map/ppermute | solution.py:735
  239.1 28.9 %collective-permute-start.28 = (bf16[2,4,64,1152]{3,2,1,0:T(8,128)(2,1)S(1)}, bf16[2,4,64,1152]{3,2,1,0:T(8,128)(2,1)S(1)}, u32[]{:S(2)}, u32[]{:S(2)}) collective-permute-start(bf16[2,4,64,1152]{3,2,1,0:T(8,128)(2,1)S(1)} %fusion.2), channel_id=1, source_target_pairs={{0,16},{8,24},{16,0},{24,8},{1,17},{9,25},{17,1},{25,9},{2,18},{10... | collective-permute-start | bytes 3538952 | tf_op jit(solution)/shard_map/ppermute | solution.py:735
  240.7 29.1 %collective-permute-start.24 = (bf16[2,192,768]{2,1,0:T(8,128)(2,1)S(1)}, bf16[2,192,768]{2,1,0:T(8,128)(2,1)S(1)}, u32[]{:S(2)}, u32[]{:S(2)}) collective-permute-start(bf16[2,192,768]{2,1,0:T(8,128)(2,1)S(1)} %get-tuple-element.47), channel_id=1, source_target_pairs={{0,1},{1,0},{2,3},{3,2},{4,5},{5,4},{6,7},{7,6},{8,9},{9,8},{10,11... | collective-permute-start | bytes 1769480 | tf_op jit(solution)/shard_map/ppermute | solution.py:747
  242.7 50.0 %collective-permute-start.46 = (bf16[2,4,96,768]{3,2,1,0:T(8,128)(2,1)S(1)}, bf16[2,4,96,768]{3,2,1,0:T(8,128)(2,1)S(1)}, u32[]{:S(2)}, u32[]{:S(2)}) collective-permute-start(bf16[2,4,96,768]{3,2,1,0:T(8,128)(2,1)S(1)} %fusion.3), channel_id=1, source_target_pairs={{0,16},{8,24},{16,0},{24,8},{1,17},{9,25},{17,1},{25,9},{2,18},{10... | collective-permute-start | bytes 3538952 | tf_op jit(solution)/shard_map/ppermute | solution.py:735
  244.7 60.6 %collective-permute-start.37 = (bf16[2,4,48,1920]{3,2,1,0:T(8,128)(2,1)S(1)}, bf16[2,4,48,1920]{3,2,1,0:T(8,128)(2,1)S(1)}, u32[]{:S(2)}, u32[]{:S(2)}) collective-permute-start(bf16[2,4,48,1920]{3,2,1,0:T(8,128)(2,1)S(1)} %fusion), channel_id=1, source_target_pairs={{0,1},{1,0},{2,3},{3,2},{4,5},{5,4},{6,7},{7,6},{8,9},{9,8},{10,11... | collective-permute-start | bytes 4423688 | tf_op jit(solution)/shard_map/ppermute | solution.py:747
  268.2 32.9 %collective-permute-start.29 = (bf16[4,64,1152]{2,1,0:T(8,128)(2,1)S(1)}, bf16[4,64,1152]{2,1,0:T(8,128)(2,1)S(1)}, u32[]{:S(2)}, u32[]{:S(2)}) collective-permute-start(bf16[4,64,1152]{2,1,0:T(8,128)(2,1)S(1)} %fusion.5), channel_id=1, source_target_pairs={{0,1},{1,0},{2,3},{3,2},{4,5},{5,4},{6,7},{7,6},{8,9},{9,8},{10,11... | collective-permute-start | bytes 1769480 | tf_op jit(solution)/shard_map/ppermute | solution.py:747
  293.0 19.9 %collective-permute-start.47 = (bf16[4,96,768]{2,1,0:T(8,128)(2,1)S(1)}, bf16[4,96,768]{2,1,0:T(8,128)(2,1)S(1)}, u32[]{:S(2)}, u32[]{:S(2)}) collective-permute-start(bf16[4,96,768]{2,1,0:T(8,128)(2,1)S(1)} %fusion.4), channel_id=1, source_target_pairs={{0,1},{1,0},{2,3},{3,2},{4,5},{5,4},{6,7},{7,6},{8,9},{9,8},{10,11... | collective-permute-start | bytes 1769480 | tf_op jit(solution)/shard_map/ppermute | solution.py:747
  305.5 16.7 %collective-permute-start.38 = (bf16[4,48,1920]{2,1,0:T(8,128)(2,1)S(1)}, bf16[4,48,1920]{2,1,0:T(8,128)(2,1)S(1)}, u32[]{:S(2)}, u32[]{:S(2)}) collective-permute-start(bf16[4,48,1920]{2,1,0:T(8,128)(2,1)S(1)} %fusion.1), channel_id=1, source_target_pairs={{0,16},{8,24},{16,0},{24,8},{1,17},{9,25},{17,1},{25,9},{2,18},{10... | collective-permute-start | bytes 2211848 | tf_op jit(solution)/shard_map/ppermute | solution.py:735
  317.0 16.7 %collective-permute-start.49 = (bf16[96,768]{1,0:T(8,128)(2,1)S(1)}, bf16[96,768]{1,0:T(8,128)(2,1)S(1)}, u32[]{:S(2)}, u32[]{:S(2)}) collective-permute-start(bf16[96,768]{1,0:T(8,128)(2,1)S(1)} %get-tuple-element.65), channel_id=1, source_target_pairs={{0,4},{1,5},{2,6},{3,7},{4,0},{5,1},{6,2},{7,3},{8,12},{9,13},{10,... | collective-permute-start | bytes 442376 | tf_op jit(solution)/shard_map/ppermute | solution.py:751
  317.2 27.8 %collective-permute-start.34 = (bf16[64,1152]{1,0:T(8,128)(2,1)S(1)}, bf16[64,1152]{1,0:T(8,128)(2,1)S(1)}, u32[]{:S(2)}, u32[]{:S(2)}) collective-permute-start(bf16[64,1152]{1,0:T(8,128)(2,1)S(1)} %fusion.36.f), channel_id=1, source_target_pairs={{0,8},{8,0},{16,24},{24,16},{1,9},{9,1},{17,25},{25,17},{2,10},{10... | collective-permute-start | bytes 442376 | tf_op jit(solution)/shard_map/ppermute | solution.py:735
  322.2 22.2 %collective-permute-start.33 = (bf16[64,1152]{1,0:T(8,128)(2,1)S(1)}, bf16[64,1152]{1,0:T(8,128)(2,1)S(1)}, u32[]{:S(2)}, u32[]{:S(2)}) collective-permute-start(bf16[64,1152]{1,0:T(8,128)(2,1)S(1)} %fusion.36.f), channel_id=1, source_target_pairs={{0,16},{8,24},{16,0},{24,8},{1,17},{9,25},{17,1},{25,9},{2,18},{10... | collective-permute-start | bytes 442376 | tf_op jit(solution)/shard_map/ppermute | solution.py:735
  333.9 18.9 %collective-permute-start.52 = (bf16[96,768]{1,0:T(8,128)(2,1)S(1)}, bf16[96,768]{1,0:T(8,128)(2,1)S(1)}, u32[]{:S(2)}, u32[]{:S(2)}) collective-permute-start(bf16[96,768]{1,0:T(8,128)(2,1)S(1)} %fusion.29.f), channel_id=1, source_target_pairs={{0,8},{8,0},{16,24},{24,16},{1,9},{9,1},{17,25},{25,17},{2,10},{10... | collective-permute-start | bytes 442376 | tf_op jit(solution)/shard_map/ppermute | solution.py:735
  (37 other events, 469.4 us)

commit v2 on v0

--- a/solution.py
+++ b/solution.py
@@ -3,6 +3,8 @@
 import jax
 import jax.numpy as jnp
 from jax import lax
+from jax.experimental import pallas as pl
+from jax.experimental.pallas import tpu as pltpu
 from jax.sharding import PartitionSpec as P
 
 HEADS = 12
@@ -292,6 +294,910 @@
     )
 
 
+def f32(value):
+    return value.astype(jnp.float32)
+
+
+def b16(value):
+    return value.astype(jnp.bfloat16)
+
+
+def dot_nn(left, right):
+    return jnp.dot(left, right, preferred_element_type=jnp.float32)
+
+
+def dot_nt(left, right):
+    return lax.dot_general(
+        left, right, (((1,), (1,)), ((), ())), preferred_element_type=jnp.float32
+    )
+
+
+def dot_tn(left, right):
+    return lax.dot_general(
+        left, right, (((0,), (0,)), ((), ())), preferred_element_type=jnp.float32
+    )
+
+
+def norm_parts(values):
+    center = values - jnp.mean(values, axis=-1, keepdims=True)
+    rate = lax.rsqrt(jnp.mean(center * center, axis=-1, keepdims=True) + norm_eps)
+    return center * rate, rate
+
+
+def norm_back(grad, hat, rate, gain):
+    scaled = grad * gain
+    return rate * (
+        scaled
+        - jnp.mean(scaled, axis=-1, keepdims=True)
+        - hat * jnp.mean(scaled * hat, axis=-1, keepdims=True)
+    )
+
+
+def place(coords):
+    return coords[0], coords[1], coords[2], coords[3]
+
+
+def piece_shard(number, y, z):
+    if number < 3:
+        return 2 * lax.rem(z + 3 - number, 4) + y
+    return 2 * lax.rem(z + 7 - number, 4) + 1 - y
+
+
+def pack96(parts):
+    lane = lax.broadcasted_iota(jnp.int32, parts[0].shape, 1)
+    one, two, three = (pltpu.roll(parts[k], 128 - 32 * k, 1) for k in (1, 2, 3))
+    return jnp.concatenate(
+        [
+            jnp.where(lane < 96, parts[0], one),
+            jnp.where(lane < 64, one, two),
+            jnp.where(lane < 32, two, three),
+        ],
+        axis=1,
+    )
+
+
+def unpack96(block):
+    tiles = [block[:, 128 * k : 128 * k + 128] for k in range(3)]
+    lane = lax.broadcasted_iota(jnp.int32, tiles[0].shape, 1)
+    return [
+        tiles[0],
+        jnp.where(lane < 32, pltpu.roll(tiles[0], 32, 1), pltpu.roll(tiles[1], 32, 1)),
+        jnp.where(lane < 64, pltpu.roll(tiles[1], 64, 1), pltpu.roll(tiles[2], 64, 1)),
+        pltpu.roll(tiles[2], 96, 1),
+    ]
+
+
+def choose(parts, index):
+    out = parts[0]
+    for number in range(1, len(parts)):
+        out = jnp.where(index == number, parts[number], out)
+    return out
+
+
+class Copies:
+    def __init__(self, sems):
+        self.sems = sems
+        self.held = []
+
+    def add(self, source, target):
+        copy = pltpu.make_async_copy(source, target, self.sems.at[len(self.held)])
+        copy.start()
+        self.held.append(copy)
+
+    def wait(self):
+        for copy in self.held:
+            copy.wait()
+        self.held = []
+
+
+def corners(x, c):
+    return ((x, c), (1 - x, c), (x, 1 - c), (1 - x, 1 - c))
+
+
+def fetch_qkv(copies, coords, own, pieces_a, pieces_b, full, full_out=None, own_out=None):
+    x, c, y, z = place(coords)
+    rows = own.shape[0]
+    half, width = rows // 2, own.shape[1] // 3
+    row = pl.multiple_of((2 * z + y) * rows, 16)
+    copies.add(own, full.at[pl.ds(row, rows), :])
+    if full_out is not None:
+        copies.add(own_out, full_out.at[pl.ds(row, rows), :])
+    for (xx, cc), first, second in zip(corners(x, c), pieces_a, pieces_b, strict=True):
+        for number in range(7):
+            at = pl.ds(pl.multiple_of(piece_shard(number, y, z) * rows + half * cc, 16), half)
+            copies.add(
+                first.at[number, pl.ds(0, half), :],
+                full.at[at, pl.ds(pl.multiple_of(width * xx, 128), width)],
+            )
+            side = width // 2
+            copies.add(
+                second.at[number, :, pl.ds(0, side)],
+                full.at[at, pl.ds(pl.multiple_of(2 * width + side * xx, 128), side)],
+            )
+            if full_out is not None:
+                copies.add(
+                    second.at[number, :, pl.ds(side, side)],
+                    full_out.at[at, pl.ds(pl.multiple_of(side * xx, 128), side)],
+                )
+
+
+def mask_bias(start, me, tok, target):
+    keys, lanes = target.shape
+    key_pos = (me - 4) * tok + lax.broadcasted_iota(jnp.int32, (keys, lanes), 0)
+    lane = lax.broadcasted_iota(jnp.int32, (keys, lanes), 1)
+    query_pos = me * tok + jnp.where(lane >= tok, lane - tok, lane)
+    target[...] = jnp.where((key_pos >= start) & (key_pos <= query_pos), 0.0, floor_score)
+
+
+def pair_stack(rows):
+    lane = lax.broadcasted_iota(jnp.int32, rows.shape, 1)
+    zero = jnp.zeros_like(rows)
+    return jnp.concatenate([jnp.where(lane < HD, rows, zero), jnp.where(lane < HD, zero, rows)], axis=0)
+
+
+def pair_join(transposed):
+    both = transposed.T
+    tok = both.shape[0] // 2
+    lane = lax.broadcasted_iota(jnp.int32, (tok, 2 * HD), 1)
+    return jnp.where(lane < HD, both[:tok], both[tok:])
+
+
+def prep_kernel(
+    coords, tokens, segs, qkv, out, up, down, gains, shifts, biases, up_bias,
+    t_out, qa_out, qb_out, fu_out, fd_out, scratch,
+):
+    x, c, _y, _z = place(coords)
+    tok, width = tokens.shape
+    rows = qkv.shape[0]
+    half, side = rows // 2, width // 2
+    p = 2 * x + c
+    at = pl.ds(pl.multiple_of(half * c, 16), half)
+    qa_out[pl.ds(0, half), :] = qkv[at, pl.ds(pl.multiple_of(width * x, 128), width)]
+    scratch[...] = jnp.zeros_like(scratch)
+    scratch[pl.ds(0, 2), pl.ds(0, rows)] = f32(gains[...])
+    scratch[pl.ds(2, 2), pl.ds(0, rows)] = f32(shifts[...])
+    scratch[pl.ds(4, 4), pl.ds(0, rows)] = f32(biases[...])
+    scratch[pl.ds(0, 1), pl.ds(128, 384)] = f32(up_bias[...])
+    qa_out[pl.ds(half, 8), :] = b16(scratch[...])
+    qb_out[:, pl.ds(0, side)] = qkv[at, pl.ds(pl.multiple_of(2 * width + side * x, 128), side)]
+    qb_out[:, pl.ds(side, side)] = out[at, pl.ds(pl.multiple_of(side * x, 128), side)]
+    t_out[pl.ds(0, tok), :] = tokens[...]
+    scratch[...] = jnp.zeros_like(scratch)
+    scratch[pl.ds(0, 1), pl.ds(0, tok)] = f32(segs[...])
+    t_out[pl.ds(tok, 8), :] = b16(scratch[...])
+    for group in range(2):
+        parts = []
+        for shard in range(4 * group, 4 * group + 4):
+            parts.append(choose(unpack96(f32(up[:, pl.ds(384 * shard, 384)])), p))
+        fu_out[:, pl.ds(384 * group, 384)] = b16(pack96(parts))
+    fd_out[...] = down[pl.ds(pl.multiple_of(rows * p, 16), rows), :]
+
+
+def front_kernel(
+    coords, seg, xo, x1, x2, x3, x4, first, own, own_o,
+    a7, ax7, ac7, acx7, b7, bx7, bc7, bcx7,
+    q_out, kv_out, h_out, a_out, lse_out, start_out, vec_out, upb_out, wo_out, r_out, h2_out,
+    full, small, bias, sems, vsems,
+):
+    x, c, y, z = place(coords)
+    me = 2 * z + y
+    p = 2 * x + c
+    tok, width = q_out.shape
+    copies, vcopies = Copies(sems), Copies(vsems)
+    vcopies.add(first.at[pl.ds(48, 8), pl.ds(0, 512)], small.at[me])
+    for number in range(7):
+        vcopies.add(a7.at[number, pl.ds(48, 8), pl.ds(0, 512)], small.at[piece_shard(number, y, z)])
+    fetch_qkv(
+        copies, coords, own, (a7, ax7, ac7, acx7), (b7, bx7, bc7, bcx7), full, wo_out, own_o
+    )
+    blocks = (xo, x1, x2, x3, x4)
+    lane1 = lax.broadcasted_iota(jnp.int32, (1, tok), 1)
+    start = jnp.full(seg.shape, 1 << 30, jnp.int32)
+    for number in range(4):
+        first_pos = jnp.full((1, 1), 1 << 30, jnp.int32)
+        for back in range(5):
+            ids = f32(blocks[back][pl.ds(tok, 8), pl.ds(0, tok)])[:1]
+            pos = (me - back) * tok + lane1
+            hit = (ids == float(number)) & (pos >= 0)
+            first_pos = jnp.minimum(
+                first_pos, jnp.min(jnp.where(hit, pos, 1 << 30), axis=1, keepdims=True)
+            )
+        start = jnp.where(seg[...] == number, first_pos, start)
+    start_out[...] = start
+    mask_bias(start, me, tok, bias)
+    vcopies.wait()
+    for group in range(2):
+        held = [f32(small[4 * group + k]) for k in range(4)]
+        vec_out[:, pl.ds(384 * group, 384)] = pack96([block[:, :128] for block in held])
+        upb_out[:, pl.ds(384 * group, 384)] = pack96(
+            [choose(unpack96(block[:, 128:512]), p) for block in held]
+        )
+    vec = vec_out[...]
+    for back in range(5):
+        hat, _rate = norm_parts(f32(blocks[back][pl.ds(0, tok), :]))
+        h_out[pl.ds((4 - back) * tok, tok), :] = b16(hat * vec[0:1] + vec[2:3])
+    copies.wait()
+    q_out[...] = b16(dot_nn(h_out[pl.ds(4 * tok, tok), :], full[:, pl.ds(0, width)]) + vec[4:5])
+
+    def project(number, carry):
+        col = pl.multiple_of(number * 256, 256)
+        shift = jnp.where(number >= width // 256, 1.0, 0.0)
+        bias_at = lax.rem(number, width // 256)
+        piece = vec_out[pl.ds(5, 1), pl.ds(pl.multiple_of(bias_at * 256, 256), 256)]
+        kv_out[:, pl.ds(col, 256)] = b16(
+            dot_nn(h_out[...], full[:, pl.ds(pl.multiple_of(width + col, 256), 256)]) + piece * shift
+        )
+        return carry
+
+    lax.fori_loop(0, 2 * width // 256, project, 0)
+
+    def pair(number, carry):
+        col = pl.multiple_of(number * 128, 128)
+        queries = pair_stack(q_out[:, pl.ds(col, 128)] * jnp.bfloat16(0.125))
+        scores = dot_nt(kv_out[:, pl.ds(col, 128)], queries) + bias[...]
+        top = jnp.max(scores, axis=0, keepdims=True)
+        probs = jnp.exp(scores - top)
+        total = jnp.sum(probs, axis=0, keepdims=True)
+        mixed = dot_tn(kv_out[:, pl.ds(pl.multiple_of(width + col, 128), 128)], b16(probs))
+        a_out[:, pl.ds(col, 128)] = b16(pair_join(mixed / total))
+        lse_out[number] = top + jnp.log(total)
+        return carry
+
+    lax.fori_loop(0, width // 128, pair, 0)
+    residual = f32(xo[pl.ds(0, tok), :]) + dot_nn(a_out[...], wo_out[...]) + vec[6:7]
+    r_out[...] = residual
+    hat, _rate = norm_parts(residual)
+    h2_out[...] = b16(hat * vec[1:2] + vec[3:4])
+
+
+def feed_tokens(h2, dy, w_up, w_down, upb, act_out, du_out, y_acc, dh_acc):
+    root = math.sqrt(2.0 / math.pi)
+    chunk = 256
+
+    def feed(number, carry):
+        col = pl.multiple_of(number * chunk, chunk)
+        pre = dot_nn(h2[...], w_up[:, pl.ds(col, chunk)]) + upb[pl.ds(0, 1), pl.ds(col, chunk)]
+        square = pre * pre
+        bend = jnp.tanh(root * pre * (1.0 + 0.044715 * square))
+        act = b16(0.5 * pre * (1.0 + bend))
+        slope = 0.5 * (1.0 + bend) + 0.5 * pre * (1.0 - bend * bend) * (
+            root * (1.0 + 3.0 * 0.044715 * square)
+        )
+        low = b16(dot_nt(dy[...], w_down[pl.ds(col, chunk), :]) * slope)
+        act_out[:, pl.ds(col, chunk)] = act
+        du_out[:, pl.ds(col, chunk)] = low
+        return carry
+
+    lax.fori_loop(0, w_up.shape[1] // chunk, feed, 0)
+    dh_acc[...] = dot_nt(du_out[...], w_up[...])
+    y_acc[...] = dot_nn(act_out[...], w_down[...])
+
+
+def near_kernel(
+    coords, h_own, h_c, dy_own, dy_c, upb, u_own, uz1, uz2, uz3, uy, d_own, dz1, dz2, dz3, dy4,
+    act_out, du_out, keep_out, send_out, wu_out, wd_out,
+    h2, dy, y_acc, dh_acc, sems,
+):
+    _x, _c, y, z = place(coords)
+    tok = h_own.shape[0]
+    copies = Copies(sems)
+    for own, ones, four, full in (
+        (u_own, (uz1, uz2, uz3), uy, wu_out),
+        (d_own, (dz1, dz2, dz3), dy4, wd_out),
+    ):
+        rows = own.shape[0]
+        copies.add(own, full.at[pl.ds(pl.multiple_of((2 * z + y) * rows, 16), rows), :])
+        for number in range(7):
+            at = pl.ds(pl.multiple_of(piece_shard(number, y, z) * rows, 16), rows)
+            copies.add(ones[number] if number < 3 else four.at[pl.ds((number - 3) * rows, rows), :], full.at[at, :])
+    h2[pl.ds(0, tok), :] = h_own[...]
+    h2[pl.ds(tok, tok), :] = h_c[...]
+    dy[pl.ds(0, tok), :] = dy_own[...]
+    dy[pl.ds(tok, tok), :] = dy_c[...]
+    copies.wait()
+    feed_tokens(h2, dy, wu_out, wd_out, upb, act_out, du_out, y_acc, dh_acc)
+    keep_out[0] = dh_acc[pl.ds(0, tok), :]
+    keep_out[1] = y_acc[pl.ds(0, tok), :]
+    send_out[0] = b16(dh_acc[pl.ds(tok, tok), :])
+    send_out[1] = b16(y_acc[pl.ds(tok, tok), :])
+
+
+def far_kernel(
+    h_x, h_xc, dy_x, dy_xc, upb, w_up, w_down,
+    act_out, du_out, keep_out, send_out,
+    h2, dy, y_acc, dh_acc,
+):
+    tok = h_x.shape[0]
+    h2[pl.ds(0, tok), :] = h_x[...]
+    h2[pl.ds(tok, tok), :] = h_xc[...]
+    dy[pl.ds(0, tok), :] = dy_x[...]
+    dy[pl.ds(tok, tok), :] = dy_xc[...]
+    feed_tokens(h2, dy, w_up, w_down, upb, act_out, du_out, y_acc, dh_acc)
+    keep_out[0] = dh_acc[pl.ds(0, tok), :]
+    keep_out[1] = y_acc[pl.ds(0, tok), :]
+    send_out[0] = b16(dh_acc[pl.ds(tok, tok), :])
+    send_out[1] = b16(y_acc[pl.ds(tok, tok), :])
+
+
+def weights_kernel(
+    coords, h0, h1, h2, h3, d0, d1, d2, d3, act_a, act_b, du_a, du_b,
+    u_out, d_out, upb_out,
+    hs, dys, acts, dus, stage, sems,
+):
+    _x, _c, y, z = place(coords)
+    tok, width = h0.shape
+    for number, (h, d) in enumerate(((h0, d0), (h1, d1), (h2, d2), (h3, d3))):
+        hs[pl.ds(number * tok, tok), :] = h[...]
+        dys[pl.ds(number * tok, tok), :] = d[...]
+    for number, (act, du) in enumerate(((act_a, du_a), (act_b, du_b))):
+        acts[pl.ds(2 * number * tok, 2 * tok), :] = act[...]
+        dus[pl.ds(2 * number * tok, 2 * tok), :] = du[...]
+    upb_out[...] = jnp.sum(f32(dus[...]), axis=0, keepdims=True)
+
+    def weight(number, carry):
+        col = pl.multiple_of(number * 256, 256)
+        stage[0, pl.ds(col, 256), :] = b16(dot_tn(hs[:, pl.ds(col, 256)], dus[...]))
+        stage[1, pl.ds(col, 256), :] = b16(dot_tn(acts[:, pl.ds(col, 256)], dys[...]))
+        return carry
+
+    lax.fori_loop(0, width // 256, weight, 0)
+    outs = Copies(sems)
+    for shard in range(8):
+        zz = lax.rem(shard // 2 + 4 - z, 4)
+        yy = jnp.where(y == shard % 2, 0, 1)
+        rows = pl.ds(shard * (width // 8), width // 8)
+        outs.add(stage.at[0, rows, :], u_out.at[yy, zz])
+        outs.add(stage.at[1, rows, :], d_out.at[yy, zz])
+    outs.wait()
+
+
+def post_kernel(residual, own, near, across, dy_in, vec_in, w_out, a_in, dr_out, da_out, dw_out, vec_out):
+    vec = vec_in[...]
+    grad_hidden = own[0] + f32(near[0]) + f32(across[...])
+    hat, rate = norm_parts(residual[...])
+    dy = f32(dy_in[...])
+    grad_first = dy + norm_back(grad_hidden, hat, rate, vec[1:2])
+    dr_out[...] = grad_first
+    low = b16(grad_first)
+    da_out[...] = b16(dot_nt(low, w_out[...]))
+    dw_out[...] = b16(dot_tn(a_in[...], low))
+    zero = jnp.zeros((1, dy.shape[1]), jnp.float32)
+    vec_out[...] = jnp.concatenate(
+        [
+            zero,
+            jnp.sum(grad_hidden * hat, axis=0, keepdims=True),
+            zero,
+            jnp.sum(grad_hidden, axis=0, keepdims=True),
+            zero,
+            zero,
+            jnp.sum(grad_first, axis=0, keepdims=True),
+            jnp.sum(dy, axis=0, keepdims=True),
+        ],
+        axis=0,
+    )
+
+
+def back_pairs(first, q_in, kv_in, lse_in, da_in, bias, dq, dkv):
+    width = q_in.shape[1]
+
+    def pair(number, carry):
+        col = pl.multiple_of((first + number) * 128, 128)
+        vcol = pl.multiple_of(width + col, 128)
+        to = pl.multiple_of(number * 128, 128)
+        queries = pair_stack(q_in[:, pl.ds(col, 128)] * jnp.bfloat16(0.125))
+        grads = pair_stack(da_in[:, pl.ds(col, 128)])
+        keys = kv_in[:, pl.ds(col, 128)]
+        probs = jnp.exp(dot_nt(keys, queries) + bias[...] - lse_in[first + number])
+        dkv[:, pl.ds(pl.multiple_of(width // 2 + to, 128), 128)] = b16(dot_nn(b16(probs), grads))
+        term = probs * dot_nt(kv_in[:, pl.ds(vcol, 128)], grads)
+        low = b16(term - probs * jnp.sum(term, axis=0, keepdims=True))
+        dkv[:, pl.ds(to, 128)] = b16(dot_nn(low, queries))
+        dq[:, pl.ds(to, 128)] = b16(pair_join(dot_tn(keys, low)) * 0.125)
+        return carry
+
+    lax.fori_loop(0, 3, pair, 0)
+
+
+def qkv_weight(h_in, dq, dkv, stage):
+    tok, part = dq.shape
+    keys = h_in.shape[0]
+
+    def weight(number, carry):
+        col = pl.multiple_of(number * 384, 384)
+        key = dot_tn(h_in[:, pl.ds(col, 384)], dkv[...])
+        query = dot_tn(h_in[pl.ds(keys - tok, tok), pl.ds(col, 384)], dq[...])
+        for shard in range(4):
+            for cc in range(2):
+                for xx in range(2):
+                    row = 96 * shard + 48 * cc + 24 * xx
+                    stage[cc, xx, 4 * number + shard, pl.ds(0, 24), pl.ds(0, part)] = b16(query[row : row + 24])
+                    stage[cc, xx, 4 * number + shard, pl.ds(0, 24), pl.ds(part, 2 * part)] = b16(key[row : row + 24])
+        return carry
+
+    lax.fori_loop(0, 2, weight, 0)
+
+
+def back_a_kernel(
+    coords, start_in, q_in, kv_in, h_in, lse_in, da_in, dw_in,
+    other, mine, dq_out, dkv_out,
+    bias, stage, sems,
+):
+    x, c, y, z = place(coords)
+    tok, width = q_in.shape
+    mask_bias(start_in[...], 2 * z + y, tok, bias)
+    for shard in range(8):
+        for cc in range(2):
+            block = f32(dw_in[pl.ds(96 * shard + 48 * cc, 48), :])
+            for xx in range(2):
+                stage[cc, xx, shard, :, pl.ds(3 * width // 2, width)] = b16(block[24 * xx : 24 * xx + 24])
+    back_pairs(0, q_in, kv_in, lse_in, da_in, bias, dq_out, dkv_out)
+    qkv_weight(h_in, dq_out, dkv_out, stage)
+    outs = Copies(sems)
+    for shard in range(8):
+        zz = lax.rem(shard // 2 + 4 - z, 4)
+        yy = jnp.where(y == shard % 2, 0, 1)
+        for xx in range(2):
+            far = jnp.where(x == xx, 0, 1)
+            outs.add(stage.at[1 - c, xx, shard], other.at[far, yy, zz])
+            outs.add(stage.at[c, xx, shard], mine.at[far, yy, zz])
+    outs.wait()
+
+
+def back_b_kernel(
+    coords, start_in, q_in, kv_in, h_in, lse_in, da_in, vec_in, upb_in, dq_a, dkv_a, xo, x1, x2, x3, x4,
+    own, a7, ax7, ac7, acx7, b7, bx7, bc7, bcx7,
+    other, mine, p_own, p_y, p_z,
+    full, bias, dq_s, dkv_s, stage, sems, osems,
+):
+    x, c, y, z = place(coords)
+    p = 2 * x + c
+    tok, width = q_in.shape
+    side = width // 2
+    copies = Copies(sems)
+    fetch_qkv(copies, coords, own, (a7, ax7, ac7, acx7), (b7, bx7, bc7, bcx7), full)
+    mask_bias(start_in[...], 2 * z + y, tok, bias)
+    back_pairs(3, q_in, kv_in, lse_in, da_in, bias, dq_s, dkv_s)
+    copies.wait()
+    gain_sum = jnp.zeros((1, width), jnp.float32)
+    shift_sum = jnp.zeros((1, width), jnp.float32)
+    for back, block in enumerate((xo, x1, x2, x3, x4)):
+        rows = pl.ds((4 - back) * tok, tok)
+        grad = jnp.zeros((tok, width), jnp.float32)
+        for number, (dq, dkv) in enumerate(((dq_a, dkv_a), (dq_s, dkv_s))):
+            at = number * side
+            grad = grad + dot_nt(dkv[rows, pl.ds(0, side)], full[:, pl.ds(width + at, side)])
+            grad = grad + dot_nt(dkv[rows, pl.ds(side, side)], full[:, pl.ds(2 * width + at, side)])
+            if back == 0:
+                grad = grad + dot_nt(dq[...], full[:, pl.ds(at, side)])
+        if back == 0:
+            p_own[...] = grad
+        elif back in (1, 3):
+            p_y[back // 2] = b16(grad)
+        else:
+            p_z[back // 2 - 1] = b16(grad)
+        hat, _rate = norm_parts(f32(block[pl.ds(0, tok), :]))
+        gain_sum = gain_sum + jnp.sum(grad * hat, axis=0, keepdims=True)
+        shift_sum = shift_sum + jnp.sum(grad, axis=0, keepdims=True)
+    qkv_weight(h_in, dq_s, dkv_s, stage)
+    zero = jnp.zeros((1, width), jnp.float32)
+    bias_q = jnp.concatenate([jnp.sum(f32(d[...]), axis=0, keepdims=True) for d in (dq_a, dq_s)], axis=1)
+    bias_v = jnp.concatenate(
+        [jnp.sum(f32(d[:, pl.ds(side, side)]), axis=0, keepdims=True) for d in (dkv_a, dkv_s)], axis=1
+    )
+    vec = vec_in[...] + jnp.concatenate(
+        [gain_sum, zero, shift_sum, zero, bias_q, bias_v, zero, zero], axis=0
+    )
+    lane = lax.broadcasted_iota(jnp.int32, (8, 128), 1)
+    line = lax.broadcasted_iota(jnp.int32, (8, 128), 0)
+    for group in range(2):
+        cols = pl.ds(384 * group, 384)
+        vec_parts = unpack96(vec[:, 384 * group : 384 * group + 384])
+        upb_parts = unpack96(jnp.broadcast_to(upb_in[:, cols], (8, 384)))
+        for k in range(4):
+            both = jnp.concatenate(
+                [
+                    jnp.where(lane < 96, vec_parts[k], 0.0),
+                    jnp.where((lane < 96) & (line == p), upb_parts[k], 0.0),
+                    jnp.zeros((8, 3 * side - 256), jnp.float32),
+                ],
+                axis=1,
+            )
+            for cc in range(2):
+                for xx in range(2):
+                    stage[cc, xx, 4 * group + k, pl.ds(24, 8), :] = b16(both)
+    outs = Copies(osems)
+    for shard in range(8):
+        zz = lax.rem(shard // 2 + 4 - z, 4)
+        yy = jnp.where(y == shard % 2, 0, 1)
+        for xx in range(2):
+            far = jnp.where(x == xx, 0, 1)
+            outs.add(stage.at[1 - c, xx, shard], other.at[far, yy, zz])
+            outs.add(stage.at[c, xx, shard], mine.at[far, yy, zz])
+    outs.wait()
+
+
+def tokens_kernel(own, near, far, dr, xo, vec_in, grad_out):
+    tok = own.shape[0]
+    hat, rate = norm_parts(f32(xo[pl.ds(0, tok), :]))
+    grad = own[...] + f32(near[...]) + f32(far[...])
+    grad_out[...] = dr[...] + norm_back(grad, hat, rate, vec_in[0:1, :])
+
+
+def finish_f_kernel(coords, u0, ux, uc, ucx, d0, dx, dc, dcx, up, down, held):
+    x, c, _y, _z = place(coords)
+    rows = u0.shape[0]
+    for (xx, cc), u, d in zip(corners(x, c), (u0, ux, uc, ucx), (d0, dx, dc, dcx), strict=True):
+        p = 2 * xx + cc
+        held[p] = u[...]
+        down[pl.ds(pl.multiple_of(rows * p, 16), rows), :] = f32(d[...])
+    for group in range(2):
+        parts = [unpack96(f32(held[k, :, pl.ds(384 * group, 384)])) for k in range(4)]
+        for shard in range(4):
+            up[:, pl.ds(384 * (4 * group + shard), 384)] = pack96([part[shard] for part in parts])
+
+
+def finish_q_kernel(coords, a0, ax, ac, acx, b0, bx, bc, bcx, qkv, out):
+    x, c, _y, _z = place(coords)
+    side = out.shape[1] // 2
+    for (xx, cc), a, b in zip(corners(x, c), (a0, ax, ac, acx), (b0, bx, bc, bcx), strict=True):
+        rows = pl.ds(pl.multiple_of(48 * cc + 24 * xx, 8), 24)
+        first, second = f32(a[...]), f32(b[...])[:24]
+        for number in range(3):
+            qkv[rows, pl.ds(2 * side * number, side)] = first[:, side * number : side * (number + 1)]
+            qkv[rows, pl.ds(2 * side * number + side, side)] = second[:, side * number : side * (number + 1)]
+        out[rows, :] = first[:, 3 * side :]
+
+
+VM = pl.BlockSpec(memory_space=pltpu.VMEM)
+SM = pl.BlockSpec(memory_space=pltpu.SMEM)
+AN = pl.BlockSpec(memory_space=pl.ANY)
+
+
+def shape_of(shape, dtype):
+    return jax.ShapeDtypeStruct(shape, dtype)
+
+
+def call(kernel, ins, outs, out_shape, scratch=(), vmem=40, flops=0, moved=0):
+    return pl.pallas_call(
+        kernel,
+        in_specs=ins,
+        out_specs=outs,
+        out_shape=out_shape,
+        scratch_shapes=list(scratch),
+        compiler_params=pltpu.CompilerParams(vmem_limit_bytes=vmem << 20),
+        cost_estimate=pl.CostEstimate(flops=flops, bytes_accessed=moved, transcendentals=0),
+    )
+
+
+def after(value, *done):
+    return lax.optimization_barrier((value,) + done)[0]
+
+
+def swap_rep(value, bit):
+    return lax.ppermute(value, "rep", [(k, k ^ bit) for k in range(4)])
+
+
+def to_core(value):
+    return swap_rep(value, 1)
+
+
+def to_x(value):
+    return swap_rep(value, 2)
+
+
+def to_y(value):
+    return lax.ppermute(value, "seq", [(k, k ^ 1) for k in range(8)])
+
+
+def to_z(value, steps):
+    return lax.ppermute(value, "seq", [(k, (k + 2 * steps) % 8) for k in range(8)])
+
+
+def join(*parts):
+    return jnp.concatenate(parts, axis=0)
+
+
+def on_device_fast(
+    tokens,
+    segment_ids,
+    query_key_value_weight,
+    output_weight,
+    up_weight,
+    down_weight,
+    ln_gains,
+    ln_biases,
+    biases,
+    up_projection_bias,
+    cotangent,
+):
+    rep, seq = lax.axis_index("rep"), lax.axis_index("seq")
+    x, c, z, y = rep // 2, rep % 2, seq // 2, seq % 2
+    coords = jnp.stack([x, c, y, z]).astype(jnp.int32)
+    tok, width = tokens.shape[1:]
+    hidden = up_weight.shape[1]
+    keys = 5 * tok
+    bf, fl = jnp.bfloat16, jnp.float32
+    dma = pltpu.SemaphoreType.DMA
+    grad_y = cotangent[0]
+    dy_x = to_x(grad_y)
+    own_tokens, piece_a, piece_b, piece_u, piece_d = call(
+        prep_kernel,
+        [SM] + [VM] * 10,
+        [VM] * 5,
+        [
+            shape_of((tok + 8, width), bf),
+            shape_of((56, width), bf),
+            shape_of((48, width), bf),
+            shape_of((96, width), bf),
+            shape_of((96, width), bf),
+        ],
+        [pltpu.VMEM((8, width), fl)],
+        vmem=16,
+        moved=4 * 10**6,
+    )(
+        coords, tokens[0], segment_ids, query_key_value_weight, output_weight, up_weight, down_weight,
+        ln_gains, ln_biases, biases, up_projection_bias[None],
+    )
+
+    az = [to_z(piece_a, k) for k in (1, 2, 3)]
+    bz = [to_z(after(piece_b, az[k - 1]), k) for k in (1, 2, 3)]
+    ay = to_y(join(piece_a, *az))
+    x2 = to_z(after(own_tokens, az[2]), 1)
+    by = to_y(after(join(piece_b, *bz), ay))
+    a7 = join(*az, ay)
+    ax7 = to_x(after(a7, dy_x))
+    x4 = to_z(x2, 1)
+    near = jnp.where(y == 0, own_tokens, x2)
+    far = jnp.where(y == 0, x2, x4)
+    crossed = to_y(after(jnp.stack([near, far]), by))
+    x1, x3 = crossed[0], crossed[1]
+    b7 = join(*bz, by)
+    bx7 = to_x(after(b7, ax7))
+    ac7, bc7 = to_core(a7), to_core(b7)
+    acx7, bcx7 = to_core(ax7), to_core(bx7)
+    uz = [to_z(after(piece_u, x4), k) for k in (1, 2, 3)]
+    dz = [to_z(after(piece_d, uz[k - 1]), k) for k in (1, 2, 3)]
+    uy = to_y(after(join(piece_u, *uz), crossed))
+    down_y = to_y(after(join(piece_d, *dz), uy))
+    dy_c, dy_xc = to_core(grad_y), to_core(dy_x)
+
+    def seven(value):
+        return value.reshape(7, value.shape[0] // 7, value.shape[1])
+
+    got_a = [seven(v) for v in (a7, ax7, ac7, acx7)]
+    got_b = [seven(v) for v in (b7, bx7, bc7, bcx7)]
+    seg = jnp.concatenate([segment_ids, segment_ids], axis=1)
+    queries, kv, normed, attended, lse, start, vec, upb, w_out, residual, hidden_2 = call(
+        front_kernel,
+        [SM] + [VM] * 6 + [AN] * 11,
+        [VM] * 11,
+        [
+            shape_of((tok, width), bf),
+            shape_of((keys, 2 * width), bf),
+            shape_of((keys, width), bf),
+            shape_of((tok, width), bf),
+            shape_of((width // 128, 1, 2 * tok), fl),
+            shape_of((1, 2 * tok), jnp.int32),
+            shape_of((8, width), fl),
+            shape_of((8, width), fl),
+            shape_of((width, width), bf),
+            shape_of((tok, width), fl),
+            shape_of((tok, width), bf),
+        ],
+        [
+            pltpu.VMEM((width, 3 * width), bf),
+            pltpu.VMEM((8, 8, 512), bf),
+            pltpu.VMEM((keys, 2 * tok), fl),
+            dma((2 + 84,)),
+            dma((8,)),
+        ],
+        flops=7 * 10**9,
+        moved=12 * 10**6,
+    )(
+        coords, seg, own_tokens, x1, x2, x3, x4, piece_a, query_key_value_weight, output_weight,
+        *got_a, *got_b,
+    )
+    h_x = to_x(hidden_2)
+    h_c = to_core(hidden_2)
+    feed_shapes = [
+        shape_of((2 * tok, width), bf),
+        shape_of((2 * tok, width), bf),
+        shape_of((2, tok, width), fl),
+        shape_of((2, tok, width), bf),
+    ]
+    feed_scratch = [
+        pltpu.VMEM((2 * tok, width), bf),
+        pltpu.VMEM((2 * tok, width), bf),
+        pltpu.VMEM((2 * tok, width), fl),
+        pltpu.VMEM((2 * tok, width), fl),
+    ]
+    act_a, du_a, keep_a, send_a, w_up, w_down = call(
+        near_kernel,
+        [SM] + [VM] * 5 + [AN] * 10,
+        [VM] * 6,
+        feed_shapes + [shape_of((width, width), bf)] * 2,
+        feed_scratch + [dma((16,))],
+        flops=3 * 10**9,
+        moved=6 * 10**6,
+    )(coords, hidden_2, h_c, grad_y, dy_c, upb, piece_u, *uz, uy, piece_d, *dz, down_y)
+    came_a = to_core(send_a)
+    h_xc = to_core(h_x)
+    act_b, du_b, keep_b, send_b = call(
+        far_kernel,
+        [VM] * 7,
+        [VM] * 4,
+        feed_shapes,
+        feed_scratch,
+        flops=3 * 10**9,
+        moved=6 * 10**6,
+    )(h_x, h_xc, dy_x, dy_xc, upb, w_up, w_down)
+    came_b = to_core(send_b)
+    back_x = to_x(b16(keep_b[0] + f32(came_b[0])))
+    u_terms, d_terms, upb_g = call(
+        weights_kernel,
+        [SM] + [VM] * 12,
+        [AN] * 2 + [VM],
+        [shape_of((2, 4, 96, width), bf), shape_of((2, 4, 96, width), bf), shape_of((1, width), fl)],
+        [pltpu.VMEM((4 * tok, width), bf)] * 4 + [pltpu.VMEM((2, width, width), bf), dma((16,))],
+        flops=3 * 10**9,
+        moved=6 * 10**6,
+    )(coords, hidden_2, h_c, h_x, h_xc, grad_y, dy_c, dy_x, dy_xc, act_a, act_b, du_a, du_b)
+    u_came = to_y(u_terms[1])
+    d_came = to_y(after(d_terms[1], u_came))
+    back_y = to_x(after(b16(keep_b[1] + f32(came_b[1])), back_x))
+    grad_first, grad_attended, dw_out, vec_g = call(
+        post_kernel,
+        [VM] * 8,
+        [VM] * 4,
+        [
+            shape_of((tok, width), fl),
+            shape_of((tok, width), bf),
+            shape_of((width, width), bf),
+            shape_of((8, width), fl),
+        ],
+        vmem=24,
+        flops=10**9,
+        moved=4 * 10**6,
+    )(residual, keep_a, came_a, back_x, grad_y, vec, w_out, attended)
+    back_scratch = [
+        pltpu.VMEM((keys, 2 * tok), fl),
+    ]
+    qa_other, qa_mine, dq_a, dkv_a = call(
+        back_a_kernel,
+        [SM] + [VM] * 7,
+        [AN] * 2 + [VM] * 2,
+        [
+            shape_of((2, 2, 4, 24, 5 * width // 2), bf),
+            shape_of((2, 2, 4, 24, 5 * width // 2), bf),
+            shape_of((tok, width // 2), bf),
+            shape_of((keys, width), bf),
+        ],
+        back_scratch + [pltpu.VMEM((2, 2, 8, 24, 5 * width // 2), bf), dma((32,))],
+        flops=5 * 10**9,
+        moved=10 * 10**6,
+    )(coords, start, queries, kv, normed, lse, grad_attended, dw_out)
+    qb_other, qb_mine, p_own, p_y, p_z = call(
+        back_b_kernel,
+        [SM] + [VM] * 15 + [AN] * 9,
+        [AN] * 2 + [VM] * 3,
+        [
+            shape_of((2, 2, 4, 32, 3 * width // 2), bf),
+            shape_of((2, 2, 4, 32, 3 * width // 2), bf),
+            shape_of((tok, width), fl),
+            shape_of((2, tok, width), bf),
+            shape_of((2, tok, width), bf),
+        ],
+        [pltpu.VMEM((width, 3 * width), bf)]
+        + back_scratch
+        + [
+            pltpu.VMEM((tok, width // 2), bf),
+            pltpu.VMEM((keys, width), bf),
+            pltpu.VMEM((2, 2, 8, 32, 3 * width // 2), bf),
+            dma((1 + 56,)),
+            dma((32,)),
+        ],
+        flops=9 * 10**9,
+        moved=14 * 10**6,
+    )(
+        coords, start, queries, kv, normed, lse, grad_attended, vec_g, upb_g, dq_a, dkv_a,
+        own_tokens, x1, x2, x3, x4, query_key_value_weight, *got_a, *got_b,
+    )
+    result = b16(
+        residual + vec[7:8] + keep_a[1] + f32(came_a[1]) + f32(back_y)
+    )
+
+    def across_core(other, mine):
+        came = to_core(other)
+        return lambda *index: f32(mine[index]) + f32(came[index])
+
+    def along_z(part, *done):
+        total = part(0)
+        for step in (1, 2, 3):
+            total = total + f32(to_z(after(b16(part(step)), *done), step))
+        return b16(total)
+
+    def u_part(*index):
+        return f32(u_terms[(0,) + index]) + f32(u_came[index])
+
+    def d_part(*index):
+        return f32(d_terms[(0,) + index]) + f32(d_came[index])
+
+    u_sum = along_z(u_part)
+    d_sum = along_z(d_part, u_sum)
+    qa_1 = across_core(qa_other, qa_mine)
+    qa_x = to_x(b16(qa_1(1)))
+    p_came = to_y(after(p_y, d_came))
+    qb_1 = across_core(qb_other, qb_mine)
+    qb_x = to_x(after(b16(qb_1(1)), qa_x))
+    even = y == 0
+    sum_own = p_own + jnp.where(even, f32(p_came[0]), 0.0)
+    sum_4 = b16(f32(p_z[1]) + jnp.where(even, 0.0, f32(p_came[1])))
+    hop = to_z(after(sum_4, d_sum), 3)
+    sum_2 = b16(f32(p_z[0]) + jnp.where(even, f32(p_came[1]), f32(p_came[0])) + f32(hop))
+    back_2 = to_z(sum_2, 3)
+
+    def qa_2(*index):
+        return qa_1(0, *index) + f32(qa_x[index])
+
+    def qb_2(*index):
+        return qb_1(0, *index) + f32(qb_x[index])
+
+    qa_y = to_y(after(b16(qa_2(1)), p_came))
+    qb_y = to_y(after(b16(qb_2(1)), qa_y))
+
+    def qa_3(*index):
+        return qa_2(0, *index) + f32(qa_y[index])
+
+    def qb_3(*index):
+        return qb_2(0, *index) + f32(qb_y[index])
+
+    qa_sum = along_z(qa_3, back_2)
+    qb_sum = along_z(qb_3, qa_sum)
+
+    def spread(total, *done):
+        over = to_x(after(total, *done))
+        return total, over, to_core(total), to_core(over)
+
+    done_u = spread(u_sum)
+    done_d = spread(d_sum)
+    done_a = spread(qa_sum)
+    done_b = spread(qb_sum)
+    grad_tokens = call(
+        tokens_kernel, [VM] * 6, VM, shape_of((tok, width), fl), vmem=16, moved=3 * 10**6
+    )(sum_own, back_2, jnp.zeros_like(back_2), grad_first, own_tokens, vec)
+    grad_up, grad_down = call(
+        finish_f_kernel,
+        [SM] + [VM] * 8,
+        [VM] * 2,
+        [shape_of(up_weight.shape, fl), shape_of(down_weight.shape, fl)],
+        [pltpu.VMEM((4, 96, width), bf)],
+        vmem=16,
+        moved=4 * 10**6,
+    )(coords, *done_u, *done_d)
+    grad_qkv, grad_out = call(
+        finish_q_kernel,
+        [SM] + [VM] * 8,
+        [VM] * 2,
+        [shape_of(query_key_value_weight.shape, fl), shape_of(output_weight.shape, fl)],
+        vmem=16,
+        moved=3 * 10**6,
+    )(coords, *done_a, *done_b)
+    sums = f32(qb_sum[24:32, :256])
+    part = ln_gains.shape[1]
+    return (
+        result[None],
+        grad_tokens[None],
+        grad_qkv,
+        grad_out,
+        grad_up,
+        grad_down,
+        sums[0:2, :part],
+        sums[2:4, :part],
+        sums[4:8, :part],
+        sums[0:4, 128 : 128 + part].reshape(4 * part),
+    )
+
+
 def solution(mesh):
     placed = (
         P("rep", "seq", None),
@@ -306,8 +1212,10 @@
         P("seq"),
         P("rep", "seq", None),
     )
+    shape = dict(mesh.shape)
+    small_slice = shape["rep"] == 4 and shape["seq"] == 8
     return jax.shard_map(
-        on_device,
+        on_device_fast if small_slice else on_device,
         mesh=mesh,
         in_specs=placed,
         out_specs=(

time: 1420 us -> 279 us (0.20)
  waiting for transfers between devices: 1120 us -> 118 us
  blocking collectives: 136 us -> 0 us
  Pallas kernels: 0 us -> 69.5 us
  starting transfers between devices: 0.86 us -> 70.2 us
  matrix products: 63.2 us -> 0 us
  other arithmetic: 41.3 us -> 5.17 us
  local copies, waits for them, and re-layouts: 41.4 us -> 13.8 us
  between operations: 15.8 us -> 1.27 us
    reduce_scatter x4 -> x0, waiting for transfers between devices: 503 us -> none  [the longest x1 165 us: on_device(): lax.psum_scatter(grad_down, 'seq', scatter_dimension=0, tiled=True)]
    unnamed x19 -> x0, waiting for transfers between devices: 331 us -> none
    all_gather x6 -> x0, waiting for transfers between devices: 243 us -> none  [the longest x1 78 us: on_device(): lax.all_gather(up_weight, 'seq', axis=0, tiled=True)]
    ppermute x0 -> x70, waiting for transfers between devices: none -> 118 us  [the longest x28 67.2 us: to_z(): lax.ppermute(value, 'seq', [(k, (k + 2 * steps) % 8) for k in range(8)])]
    all_gather x5 -> x0, blocking collectives: 94.6 us -> none  [the longest x1 26.3 us: on_device(): lax.all_gather(up_projection_bias, 'seq', axis=0, tiled=True)]
    ppermute x0 -> x70, starting transfers between devices: none -> 70.2 us  [the longest x28 40 us: to_z(): lax.ppermute(value, 'seq', [(k, (k + 2 * steps) % 8) for k in range(8)])]
    pallas_call x0 -> x11, Pallas kernels: none -> 69.5 us  [the longest x1 18.3 us: on_device_fast(): call(back_b_kernel, [SM] + [VM] * 15 + [AN] * 9, [AN] * 2 + [VM] * 3, [sh...]
    dot_general x23 -> x0, matrix products: 63.2 us -> none  [the longest x1 6.47 us: on_device(): jnp.einsum('td,tf->df', hidden_second, grad_up_pre, preferred_element_typ...]
  transfers between devices with their start and end apart: 15 -> 70, of which waited for: 15 -> 24; matrix products, arithmetic and copies ran while one was open for 7% -> 3% of each run, Pallas kernels for 0% -> 23%
where the time goes in v2:
time: 279 us; the launch traced here: 278 us
  waiting for transfers between devices  118 us (42%)
  starting transfers between devices  70.2 us (25%)
  Pallas kernels  69.5 us (25%)
  local copies, waits for them, and re-layouts  13.8 us (5%)
  other arithmetic  5.17 us (2%)
    ppermute x28, waiting for transfers between devices, to_z(): lax.ppermute(value, 'seq', [(k, (k + 2 * steps) % 8) for k in range(8)])  67.2 us
    ppermute x28, starting transfers between devices, to_z(): lax.ppermute(value, 'seq', [(k, (k + 2 * steps) % 8) for k in range(8)])  40 us
    ppermute x10, waiting for transfers between devices, to_y(): return lax.ppermute(value, 'seq', [(k, k ^ 1) for k in range(8)])  32.5 us
    ppermute x32, waiting for transfers between devices, swap_rep(): return lax.ppermute(value, 'rep', [(k, k ^ bit) for k in range(4)])  18.5 us
    pallas_call x1, Pallas kernels, on_device_fast(): call(back_b_kernel, [SM] + [VM] * 15 + [AN] * 9, [AN] * 2 + [VM] * 3, [sh...  18.3 us
    ppermute x32, starting transfers between devices, swap_rep(): return lax.ppermute(value, 'rep', [(k, k ^ bit) for k in range(4)])  16.3 us
    pallas_call x1, Pallas kernels, on_device_fast(): call(front_kernel, [SM] + [VM] * 6 + [AN] * 11, [VM] * 11, [shape_of((tok...  15.2 us
    ppermute x10, starting transfers between devices, to_y(): return lax.ppermute(value, 'seq', [(k, k ^ 1) for k in range(8)])  13.8 us
  transfers between devices with their start and end apart: 70, of which 24 were waited for; matrix products, arithmetic and copies ran while one was open for 3% of the time, Pallas kernels for 23%

profile of v2, /device:TPU:0, one launch (start us, length us, event | category | flops | bytes accessed | tf_op | source)
XLA Modules:
  0.0 278.2 jit_solution(4028663485489489456)
XLA Ops:
  10.1 5.1 %collective-permute-start = (bf16[56,768]{1,0:T(8,128)(2,1)S(1)}, bf16[56,768]{1,0:T(8,128)(2,1)S(1)}, u32[]{:S(2)}, u32[]{:S(2)}) collective-permute-start(bf16[56,768]{1,0:T(8,128)(2,1)S(1)} %get-tuple-element.87.first), channel_id=1, source_target_pairs={{0,6},{1,7},{2,0},{3,1},{4,2},{5,3},{6,4},{7,5},{8,14},{9,15},{10,... | collective-permute-start | bytes 258056 | tf_op jit(solution)/shard_map/ppermute | solution.py:893
  20.2 2.3 collective-permute-start.7
  22.5 7.6 %collective-permute-done.5 = bf16[56,768]{1,0:T(8,128)(2,1)S(1)} collective-permute-done((bf16[56,768]{1,0:T(8,128)(2,1)S(1)}, bf16[56,768]{1,0:T(8,128)(2,1)S(1)}, u32[]{:S(2)}, u32[]{:S(2)}) %collective-permute-start.5) | collective-permute-done | bytes 86048 | tf_op jit(solution)/shard_map/ppermute | solution.py:893
  31.8 5.0 %collective-permute-done.4 = bf16[48,768]{1,0:T(8,128)(2,1)S(1)} collective-permute-done((bf16[48,768]{1,0:T(8,128)(2,1)S(1)}, bf16[48,768]{1,0:T(8,128)(2,1)S(1)}, u32[]{:S(2)}, u32[]{:S(2)}) %collective-permute-start.4) | collective-permute-done | bytes 73760 | tf_op jit(solution)/shard_map/ppermute | solution.py:893
  36.9 9.9 %collective-permute-done.6 = bf16[48,768]{1,0:T(8,128)(2,1)S(1)} collective-permute-done((bf16[48,768]{1,0:T(8,128)(2,1)S(1)}, bf16[48,768]{1,0:T(8,128)(2,1)S(1)}, u32[]{:S(2)}, u32[]{:S(2)}) %collective-permute-start.6) | collective-permute-done | bytes 73760 | tf_op jit(solution)/shard_map/ppermute | solution.py:893
  50.2 5.0 %collective-permute-done.9 = bf16[192,768]{1,0:T(8,128)(2,1)S(1)} collective-permute-done((bf16[192,768]{1,0:T(8,128)(2,1)S(1)}, bf16[192,768]{1,0:T(8,128)(2,1)S(1)}, u32[]{:S(2)}, u32[]{:S(2)}) %collective-permute-start.9) | collective-permute-done | bytes 294944 | tf_op jit(solution)/shard_map/ppermute | solution.py:889
  56.8 6.4 %collective-permute-done.12 = bf16[392,768]{1,0:T(8,128)(2,1)S(1)} collective-permute-done((bf16[392,768]{1,0:T(8,128)(2,1)S(1)}, bf16[392,768]{1,0:T(8,128)(2,1)S(1)}, u32[]{:S(2)}, u32[]{:S(2)}) %collective-permute-start.12) | collective-permute-done | bytes 602144 | tf_op jit(solution)/shard_map/ppermute | solution.py:877
  65.1 3.3 %collective-permute-start.22 = (bf16[96,768]{1,0:T(8,128)(2,1)S(1)}, bf16[96,768]{1,0:T(8,128)(2,1)S(1)}, u32[]{:S(2)}, u32[]{:S(2)}) collective-permute-start(bf16[96,768]{1,0:T(8,128)(2,1)S(1)} %get-tuple-element.102.u_own), channel_id=1, source_target_pairs={{0,6},{1,7},{2,0},{3,1},{4,2},{5,3},{6,4},{7,5},{8,14},{9,15},{10,... | collective-permute-start | bytes 442376 | tf_op jit(solution)/shard_map/ppermute | solution.py:893
  68.5 4.8 %collective-permute-done.20.uz1 = bf16[96,768]{1,0:T(8,128)(2,1)S(1)} collective-permute-done((bf16[96,768]{1,0:T(8,128)(2,1)S(1)}, bf16[96,768]{1,0:T(8,128)(2,1)S(1)}, u32[]{:S(2)}, u32[]{:S(2)}) %collective-permute-start.20) | collective-permute-done | bytes 147488 | tf_op jit(solution)/shard_map/ppermute | solution.py:893
  73.7 7.7 %collective-permute-done.21.uz2 = bf16[96,768]{1,0:T(8,128)(2,1)S(1)} collective-permute-done((bf16[96,768]{1,0:T(8,128)(2,1)S(1)}, bf16[96,768]{1,0:T(8,128)(2,1)S(1)}, u32[]{:S(2)}, u32[]{:S(2)}) %collective-permute-start.21) | collective-permute-done | bytes 147488 | tf_op jit(solution)/shard_map/ppermute | solution.py:893
  83.3 5.4 %collective-permute-done.25.dz2 = bf16[96,768]{1,0:T(8,128)(2,1)S(1)} collective-permute-done((bf16[96,768]{1,0:T(8,128)(2,1)S(1)}, bf16[96,768]{1,0:T(8,128)(2,1)S(1)}, u32[]{:S(2)}, u32[]{:S(2)}) %collective-permute-start.25) | collective-permute-done | bytes 147488 | tf_op jit(solution)/shard_map/ppermute | solution.py:893
  92.1 10.2 %collective-permute-done.23.uy = bf16[384,768]{1,0:T(8,128)(2,1)S(1)} collective-permute-done((bf16[384,768]{1,0:T(8,128)(2,1)S(1)}, bf16[384,768]{1,0:T(8,128)(2,1)S(1)}, u32[]{:S(2)}, u32[]{:S(2)}) %collective-permute-start.23) | collective-permute-done | bytes 589856 | tf_op jit(solution)/shard_map/ppermute | solution.py:889
  102.9 15.2 %shard_map.187 = (bf16[192,768]{1,0:T(8,128)(2,1)S(1)}, bf16[960,1536]{1,0:T(8,128)(2,1)S(1)}, bf16[960,768]{1,0:T(8,128)(2,1)S(1)}, bf16[192,768]{1,0:T(8,128)(...) custom-call(s32[4]{0:T(128)S(1)} %pad_add_fusion.1.coords, ...), custom_call_target="tpu_custom_call" | custom-call | flops 7000000000 | bytes 12000000 | tf_op jit(solution)/shard_map/pallas_call | solution.py:970
  119.3 5.7 %collective-permute-done.29.h_x.h2 = bf16[192,768]{1,0:T(8,128)(2,1)S(1)} collective-permute-done((bf16[192,768]{1,0:T(8,128)(2,1)S(1)}, bf16[192,768]{1,0:T(8,128)(2,1)S(1)}, u32[]{:S(2)}, u32[]{:S(2)}) %collective-permute-start.29) | collective-permute-done | bytes 294944 | tf_op jit(solution)/shard_map/ppermute | solution.py:877
  125.0 7.2 %shard_map.188 = (bf16[384,768]{1,0:T(8,128)(2,1)S(1)}, bf16[384,768]{1,0:T(8,128)(2,1)S(1)}, f32[2,192,768]{2,1,0:T(8,128)S(1)}, bf16[2,192,768]{2,1,0:T(8,128)...) custom-call(s32[4]{0:T(128)S(1)} %pad_add_fusion.1.coords, ...), custom_call_target="tpu_custom_call" | custom-call | flops 3000000000 | bytes 6000000 | tf_op jit(solution)/shard_map/pallas_call | solution.py:1014
  132.2 4.1 %shard_map.189 = (bf16[384,768]{1,0:T(8,128)(2,1)S(1)}, bf16[384,768]{1,0:T(8,128)(2,1)S(1)}, f32[2,192,768]{2,1,0:T(8,128)S(1)}, bf16[2,192,768]{2,1,0:T(8,128)(2,1)S(1)}) custom-call(bf16[192,768]{1,0:T(8,128)(2,1)S(1)} %collective-permute-done.29.h_x.h2, bf16[192,768]{1,0:T(8,128)(2,1)S(1)} %collective-permute-done.30.h_xc.h3, ...), custom_call_target="tpu_custom_call" | custom-call | flops 3000000000 | bytes 6000000 | tf_op jit(solution)/shard_map/pallas_call | solution.py:1025
  136.9 7.1 %shard_map.191 = (bf16[2,4,96,768]{3,2,1,0:T(8,128)(2,1)S(1)}, bf16[2,4,96,768]{3,2,1,0:T(8,128)(2,1)S(1)}, f32[1,768]{1,0:T(1,128)S(1)}) custom-call(s32[4]{0:T(128)S(1)} %pad_add_fusion.1.coords, bf16[192,768]{1,0:T(8,128)(2,1)S(1)} %get-tuple-element.99.h_own.h0, bf16[192,768]{1,0:T(8,128)(2,1)S(1)} %collective-permute-done.18.h_c.h1, ...), custom_call_target="tpu_custom_call" | custom-call | flops 3000000000 | bytes 6000000 | tf_op jit(solution)/shard_map/pallas_call | solution.py:1036
  146.4 13.0 %collective-permute-done.35 = bf16[4,96,768]{2,1,0:T(8,128)(2,1)S(1)} collective-permute-done((bf16[4,96,768]{2,1,0:T(8,128)(2,1)S(1)}, bf16[4,96,768]{2,1,0:T(8,128)(2,1)S(1)}, u32[]{:S(2)}, u32[]{:S(2)}) %collective-permute-start.35) | collective-permute-done | bytes 589856 | tf_op jit(solution)/shard_map/ppermute | solution.py:889
  159.5 4.8 %collective-permute-start.40 = (bf16[96,768]{1,0:T(8,128)(2,1)S(1)}, bf16[96,768]{1,0:T(8,128)(2,1)S(1)}, u32[]{:S(2)}, u32[]{:S(2)}) collective-permute-start(bf16[96,768]{1,0:T(8,128)(2,1)S(1)} %get-tuple-element.172), channel_id=1, source_target_pairs={{0,6},{1,7},{2,0},{3,1},{4,2},{5,3},{6,4},{7,5},{8,14},{9,15},{10,... | collective-permute-start | bytes 442376 | tf_op jit(solution)/shard_map/ppermute | solution.py:893
  167.3 9.8 %shard_map.192 = (bf16[2,2,4,24,1920]{4,3,2,1,0:T(8,128)(2,1)}, bf16[2,2,4,24,1920]{4,3,2,1,0:T(8,128)(2,1)S(1)}, bf16[192,384]{1,0:T(8,128)(2,1)S(1)}, bf16[960,768]{1,0:T(8,128)(2,1)S(1)}) custom-call(s32[4]{0:T(128)S(1)} %pad_add_fusion.1.coords, s32[1,384]{1,0:T(1,128)S(1)} %get-tuple-element.116.start_in, bf16[192,768]{1,0:T(8,128)(2,1)S(1)} %copy-done.28, ...), custom_call_target="tpu_custom_call" | custom-call | flops 5000000000 | bytes 10000000 | tf_op jit(solution)/shard_map/pallas_call | solution.py:1065
  182.0 18.3 %shard_map.193 = (bf16[2,2,4,32,1152]{4,3,2,1,0:T(8,128)(2,1)S(1)}, bf16[2,2,4,32,1152]{4,3,2,1,0:T(8,128)(2,1)S(1)}, f32[192,768]{1,0:T(8,128)S(1)}, bf16[2,192...) custom-call(s32[4]{0:T(128)S(1)} %pad_add_fusion.1.coords, s32[1,384]{1,0:T(1,128)S(1)} %get-tuple-element.116.start_in, ...), custom_call_target="tpu_custom_call" | custom-call | flops 8999999488 | bytes 14000000 | tf_op jit(solution)/shard_map/pallas_call | solution.py:1079
  202.5 3.5 %collective-permute-start.43 = (bf16[96,768]{1,0:T(8,128)(2,1)S(1)}, bf16[96,768]{1,0:T(8,128)(2,1)S(1)}, u32[]{:S(2)}, u32[]{:S(2)}) collective-permute-start(bf16[96,768]{1,0:T(8,128)(2,1)S(1)} %get-tuple-element.142), channel_id=1, source_target_pairs={{0,6},{1,7},{2,0},{3,1},{4,2},{5,3},{6,4},{7,5},{8,14},{9,15},{10,... | collective-permute-start | bytes 442376 | tf_op jit(solution)/shard_map/ppermute | solution.py:893
  210.9 9.1 %collective-permute-done.42 = bf16[96,768]{1,0:T(8,128)(2,1)S(1)} collective-permute-done((bf16[96,768]{1,0:T(8,128)(2,1)S(1)}, bf16[96,768]{1,0:T(8,128)(2,1)S(1)}, u32[]{:S(2)}, u32[]{:S(2)}) %collective-permute-start.42) | collective-permute-done | bytes 147488 | tf_op jit(solution)/shard_map/ppermute | solution.py:893
  227.0 3.5 %collective-permute-done.44 = bf16[192,768]{1,0:T(8,128)(2,1)S(1)} collective-permute-done((bf16[192,768]{1,0:T(8,128)(2,1)S(1)}, bf16[192,768]{1,0:T(8,128)(2,1)S(1)}, u32[]{:S(2)}, u32[]{:S(2)}) %collective-permute-start.44) | collective-permute-done | bytes 294944 | tf_op jit(solution)/shard_map/ppermute | solution.py:893
  230.8 2.6 collective-permute-start.45
  233.6 6.0 %collective-permute-done.45.near = bf16[192,768]{1,0:T(8,128)(2,1)S(1)} collective-permute-done((bf16[192,768]{1,0:T(8,128)(2,1)S(1)}, bf16[192,768]{1,0:T(8,128)(2,1)S(1)}, u32[]{:S(2)}, u32[]{:S(2)}) %collective-permute-start.45) | collective-permute-done | bytes 294944 | tf_op jit(solution)/shard_map/ppermute | solution.py:893
  239.6 4.3 %collective-permute-start.51 = (bf16[24,1920]{1,0:T(8,128)(2,1)S(1)}, bf16[24,1920]{1,0:T(8,128)(2,1)S(1)}, u32[]{:S(2)}, u32[]{:S(2)}) collective-permute-start(bf16[24,1920]{1,0:T(8,128)(2,1)S(1)} %get-tuple-element.150), channel_id=1, source_target_pairs={{0,6},{1,7},{2,0},{3,1},{4,2},{5,3},{6,4},{7,5},{8,14},{9,15},{10,... | collective-permute-start | bytes 276488 | tf_op jit(solution)/shard_map/ppermute | solution.py:893
  248.2 2.6 collective-permute-done.50
  252.2 2.3 collective-permute-start.57
  256.7 4.3 %collective-permute-done.57 = bf16[4,32,1152]{2,1,0:T(8,128)(2,1)S(1)} collective-permute-done((bf16[4,32,1152]{2,1,0:T(8,128)(2,1)S(1)}, bf16[4,32,1152]{2,1,0:T(8,128)(2,1)S(1)}, u32[]{:S(2)}, u32[]{:S(2)}) %collective-permute-start.57) | collective-permute-done | bytes 294944 | tf_op jit(solution)/shard_map/ppermute | solution.py:889
  265.7 2.5 shard_map.196
  272.7 2.6 collective-permute-done.61.bx
  (219 shorter events, 75.7 us)
Async XLA Ops:
  15.2 14.9 %collective-permute-start.5 = (bf16[56,768]{1,0:T(8,128)(2,1)S(1)}, bf16[56,768]{1,0:T(8,128)(2,1)S(1)}, u32[]{:S(2)}, u32[]{:S(2)}) collective-permute-start(bf16[56,768]{1,0:T(8,128)(2,1)S(1)} %get-tuple-element.87.first), channel_id=1, source_target_pairs={{0,4},{1,5},{2,6},{3,7},{4,0},{5,1},{6,2},{7,3},{8,12},{9,13},{10,... | collective-permute-start | bytes 258056 | tf_op jit(solution)/shard_map/ppermute | solution.py:893
  15.2 14.9 %collective-permute-start.3 = (bf16[56,768]{1,0:T(8,128)(2,1)S(1)}, bf16[56,768]{1,0:T(8,128)(2,1)S(1)}, u32[]{:S(2)}, u32[]{:S(2)}) collective-permute-start(bf16[56,768]{1,0:T(8,128)(2,1)S(1)} %get-tuple-element.87.first), channel_id=1, source_target_pairs={{0,2},{1,3},{2,4},{3,5},{4,6},{5,7},{6,0},{7,1},{8,10},{9,11},{10,... | collective-permute-start | bytes 258056 | tf_op jit(solution)/shard_map/ppermute | solution.py:893
  16.3 32.2 %collective-permute-start.11 = (bf16[192,768]{1,0:T(8,128)(2,1)S(1)}, bf16[192,768]{1,0:T(8,128)(2,1)}, u32[]{:S(2)}, u32[]{:S(2)}) collective-permute-start(bf16[192,768]{1,0:T(8,128)(2,1)S(1)} %bitcast.235), channel_id=1, source_target_pairs={{0,16},{8,24},{16,0},{24,8},{1,17},{9,25},{17,1},{25,9},{2,18},{10... | collective-permute-start | bytes 884744 | tf_op jit(solution)/shard_map/ppermute | solution.py:877
  18.2 18.6 %collective-permute-start.1 = (bf16[200,768]{1,0:T(8,128)(2,1)S(1)}, bf16[200,768]{1,0:T(8,128)(2,1)S(1)}, u32[]{:S(2)}, u32[]{:S(2)}) collective-permute-start(bf16[200,768]{1,0:T(8,128)(2,1)S(1)} %get-tuple-element.88.xo), channel_id=1, source_target_pairs={{0,2},{1,3},{2,4},{3,5},{4,6},{5,7},{6,0},{7,1},{8,10},{9,11},{10,... | collective-permute-start | bytes 921608 | tf_op jit(solution)/shard_map/ppermute | solution.py:893
  20.2 16.7 %collective-permute-start.7 = (bf16[48,768]{1,0:T(8,128)(2,1)S(1)}, bf16[48,768]{1,0:T(8,128)(2,1)S(1)}, u32[]{:S(2)}, u32[]{:S(2)}) collective-permute-start(bf16[48,768]{1,0:T(8,128)(2,1)S(1)} %get-tuple-element.90), channel_id=1, source_target_pairs={{0,6},{1,7},{2,0},{3,1},{4,2},{5,3},{6,4},{7,5},{8,14},{9,15},{10,... | collective-permute-start | bytes 221192 | tf_op jit(solution)/shard_map/ppermute | solution.py:893
  30.2 16.7 %collective-permute-start.8 = (bf16[224,768]{1,0:T(8,128)(2,1)S(1)}, bf16[224,768]{1,0:T(8,128)(2,1)S(1)}, u32[]{:S(2)}, u32[]{:S(2)}) collective-permute-start(bf16[224,768]{1,0:T(8,128)(2,1)S(1)} %pad_maximum_fusion.3), channel_id=1, source_target_pairs={{0,1},{1,0},{2,3},{3,2},{4,5},{5,4},{6,7},{7,6},{8,9},{9,8},{10,11... | collective-permute-start | bytes 1032200 | tf_op jit(solution)/shard_map/ppermute | solution.py:889
  36.8 13.2 %collective-permute-start.2 = (bf16[200,768]{1,0:T(8,128)(2,1)S(1)}, bf16[200,768]{1,0:T(8,128)(2,1)S(1)}, u32[]{:S(2)}, u32[]{:S(2)}) collective-permute-start(bf16[200,768]{1,0:T(8,128)(2,1)S(1)} %collective-permute-done.1.x2), channel_id=1, source_target_pairs={{0,2},{1,3},{2,4},{3,5},{4,6},{5,7},{6,0},{7,1},{8,10},{9,11},{10,... | collective-permute-start | bytes 921608 | tf_op jit(solution)/shard_map/ppermute | solution.py:893
  48.5 14.7 %collective-permute-start.12 = (bf16[392,768]{1,0:T(8,128)(2,1)S(1)}, bf16[392,768]{1,0:T(8,128)(2,1)S(1)}, u32[]{:S(2)}, u32[]{:S(2)}) collective-permute-start(bf16[392,768]{1,0:T(8,128)(2,1)S(1)} %constant_dynamic-update-slice_fusion), channel_id=1, source_target_pairs={{0,16},{8,24},{16,0},{24,8},{1,17},{9,25},{17,1},{25,9},{2,18},{10... | collective-permute-start | bytes 1806344 | tf_op jit(solution)/shard_map/ppermute | solution.py:877
  55.2 28.1 %collective-permute-start.10 = (bf16[2,200,768]{2,1,0:T(8,128)(2,1)S(1)}, bf16[2,200,768]{2,1,0:T(8,128)(2,1)S(1)}, u32[]{:S(2)}, u32[]{:S(2)}) collective-permute-start(bf16[2,200,768]{2,1,0:T(8,128)(2,1)S(1)} %pad_maximum_fusion), channel_id=1, source_target_pairs={{0,1},{1,0},{2,3},{3,2},{4,5},{5,4},{6,7},{7,6},{8,9},{9,8},{10,11... | collective-permute-start | bytes 1843208 | tf_op jit(solution)/shard_map/ppermute | solution.py:889
  63.1 28.3 %collective-permute-start.15 = (bf16[336,768]{1,0:T(8,128)(2,1)S(1)}, bf16[336,768]{1,0:T(8,128)(2,1)S(1)}, u32[]{:S(2)}, u32[]{:S(2)}) collective-permute-start(bf16[336,768]{1,0:T(8,128)(2,1)S(1)} %constant_dynamic-update-slice_fusion.4), channel_id=1, source_target_pairs={{0,16},{8,24},{16,0},{24,8},{1,17},{9,25},{17,1},{25,9},{2,18},{10... | collective-permute-start | bytes 1548296 | tf_op jit(solution)/shard_map/ppermute | solution.py:877
  64.6 16.7 %collective-permute-start.21 = (bf16[96,768]{1,0:T(8,128)(2,1)S(1)}, bf16[96,768]{1,0:T(8,128)(2,1)S(1)}, u32[]{:S(2)}, u32[]{:S(2)}) collective-permute-start(bf16[96,768]{1,0:T(8,128)(2,1)S(1)} %get-tuple-element.102.u_own), channel_id=1, source_target_pairs={{0,4},{1,5},{2,6},{3,7},{4,0},{5,1},{6,2},{7,3},{8,12},{9,13},{10,... | collective-permute-start | bytes 442376 | tf_op jit(solution)/shard_map/ppermute | solution.py:893
  65.1 16.3 %collective-permute-start.22 = (bf16[96,768]{1,0:T(8,128)(2,1)S(1)}, bf16[96,768]{1,0:T(8,128)(2,1)S(1)}, u32[]{:S(2)}, u32[]{:S(2)}) collective-permute-start(bf16[96,768]{1,0:T(8,128)(2,1)S(1)} %get-tuple-element.102.u_own), channel_id=1, source_target_pairs={{0,6},{1,7},{2,0},{3,1},{4,2},{5,3},{6,4},{7,5},{8,14},{9,15},{10,... | collective-permute-start | bytes 442376 | tf_op jit(solution)/shard_map/ppermute | solution.py:893
  81.4 21.4 %collective-permute-start.13 = (bf16[392,768]{1,0:T(8,128)(2,1)S(1)}, bf16[392,768]{1,0:T(8,128)(2,1)S(1)}, u32[]{:S(2)}, u32[]{:S(2)}) collective-permute-start(bf16[392,768]{1,0:T(8,128)(2,1)S(1)} %constant_dynamic-update-slice_fusion), channel_id=1, source_target_pairs={{0,8},{8,0},{16,24},{24,16},{1,9},{9,1},{17,25},{25,17},{2,10},{10... | collective-permute-start | bytes 1806344 | tf_op jit(solution)/shard_map/ppermute | solution.py:877
  83.3 19.6 %collective-permute-start.14 = (bf16[392,768]{1,0:T(8,128)(2,1)S(1)}, bf16[392,768]{1,0:T(8,128)(2,1)S(1)}, u32[]{:S(2)}, u32[]{:S(2)}) collective-permute-start(bf16[392,768]{1,0:T(8,128)(2,1)S(1)} %collective-permute-done.12), channel_id=1, source_target_pairs={{0,8},{8,0},{16,24},{24,16},{1,9},{9,1},{17,25},{25,17},{2,10},{10... | collective-permute-start | bytes 1806344 | tf_op jit(solution)/shard_map/ppermute | solution.py:877
  88.7 13.6 %collective-permute-start.23 = (bf16[384,768]{1,0:T(8,128)(2,1)S(1)}, bf16[384,768]{1,0:T(8,128)(2,1)S(1)}, u32[]{:S(2)}, u32[]{:S(2)}) collective-permute-start(bf16[384,768]{1,0:T(8,128)(2,1)S(1)} %pad_maximum_fusion.1), channel_id=1, source_target_pairs={{0,1},{1,0},{2,3},{3,2},{4,5},{5,4},{6,7},{7,6},{8,9},{9,8},{10,11... | collective-permute-start | bytes 1769480 | tf_op jit(solution)/shard_map/ppermute | solution.py:889
  102.3 22.7 %collective-permute-start.27 = (bf16[384,768]{1,0:T(8,128)(2,1)S(1)}, bf16[384,768]{1,0:T(8,128)(2,1)S(1)}, u32[]{:S(2)}, u32[]{:S(2)}) collective-permute-start(bf16[384,768]{1,0:T(8,128)(2,1)S(1)} %pad_maximum_fusion.2), channel_id=1, source_target_pairs={{0,1},{1,0},{2,3},{3,2},{4,5},{5,4},{6,7},{7,6},{8,9},{9,8},{10,11... | collective-permute-start | bytes 1769480 | tf_op jit(solution)/shard_map/ppermute | solution.py:889
  144.1 15.3 %collective-permute-start.35 = (bf16[4,96,768]{2,1,0:T(8,128)(2,1)S(1)}, bf16[4,96,768]{2,1,0:T(8,128)(2,1)S(1)}, u32[]{:S(2)}, u32[]{:S(2)}) collective-permute-start(bf16[4,96,768]{2,1,0:T(8,128)(2,1)S(1)} %slice_bitcast_fusion), channel_id=1, source_target_pairs={{0,1},{1,0},{2,3},{3,2},{4,5},{5,4},{6,7},{7,6},{8,9},{9,8},{10,11... | collective-permute-start | bytes 1769480 | tf_op jit(solution)/shard_map/ppermute | solution.py:889
  145.7 19.3 %collective-permute-start.28 = (bf16[2,192,768]{2,1,0:T(8,128)(2,1)S(1)}, bf16[2,192,768]{2,1,0:T(8,128)(2,1)S(1)}, u32[]{:S(2)}, u32[]{:S(2)}) collective-permute-start(bf16[2,192,768]{2,1,0:T(8,128)(2,1)S(1)} %get-tuple-element.110), channel_id=1, source_target_pairs={{0,8},{8,0},{16,24},{24,16},{1,9},{9,1},{17,25},{25,17},{2,10},{10... | collective-permute-start | bytes 1769480 | tf_op jit(solution)/shard_map/ppermute | solution.py:877
  145.8 19.2 %collective-permute-start.33 = (bf16[192,768]{1,0:T(8,128)(2,1)S(1)}, bf16[192,768]{1,0:T(8,128)(2,1)S(1)}, u32[]{:S(2)}, u32[]{:S(2)}) collective-permute-start(bf16[192,768]{1,0:T(8,128)(2,1)S(1)} %get-tuple-element.174), channel_id=1, source_target_pairs={{0,16},{8,24},{16,0},{24,8},{1,17},{9,25},{17,1},{25,9},{2,18},{10... | collective-permute-start | bytes 884744 | tf_op jit(solution)/shard_map/ppermute | solution.py:877
  159.5 19.3 %collective-permute-start.40 = (bf16[96,768]{1,0:T(8,128)(2,1)S(1)}, bf16[96,768]{1,0:T(8,128)(2,1)S(1)}, u32[]{:S(2)}, u32[]{:S(2)}) collective-permute-start(bf16[96,768]{1,0:T(8,128)(2,1)S(1)} %get-tuple-element.172), channel_id=1, source_target_pairs={{0,6},{1,7},{2,0},{3,1},{4,2},{5,3},{6,4},{7,5},{8,14},{9,15},{10,... | collective-permute-start | bytes 442376 | tf_op jit(solution)/shard_map/ppermute | solution.py:893
  164.4 14.5 %collective-permute-start.39 = (bf16[96,768]{1,0:T(8,128)(2,1)S(1)}, bf16[96,768]{1,0:T(8,128)(2,1)S(1)}, u32[]{:S(2)}, u32[]{:S(2)}) collective-permute-start(bf16[96,768]{1,0:T(8,128)(2,1)S(1)} %get-tuple-element.173), channel_id=1, source_target_pairs={{0,4},{1,5},{2,6},{3,7},{4,0},{5,1},{6,2},{7,3},{8,12},{9,13},{10,... | collective-permute-start | bytes 442376 | tf_op jit(solution)/shard_map/ppermute | solution.py:893
  164.4 14.5 %collective-permute-start.38 = (bf16[96,768]{1,0:T(8,128)(2,1)S(1)}, bf16[96,768]{1,0:T(8,128)(2,1)S(1)}, u32[]{:S(2)}, u32[]{:S(2)}) collective-permute-start(bf16[96,768]{1,0:T(8,128)(2,1)S(1)} %get-tuple-element.171), channel_id=1, source_target_pairs={{0,2},{1,3},{2,4},{3,5},{4,6},{5,7},{6,0},{7,1},{8,10},{9,11},{10,... | collective-permute-start | bytes 442376 | tf_op jit(solution)/shard_map/ppermute | solution.py:893
  177.1 28.9 %collective-permute-start.46 = (bf16[2,2,4,24,1920]{4,3,2,1,0:T(8,128)(2,1)}, bf16[2,2,4,24,1920]{4,3,2,1,0:T(8,128)(2,1)S(1)}, u32[]{:S(2)}, u32[]{:S(2)}) collective-permute-start(bf16[2,2,4,24,1920]{4,3,2,1,0:T(8,128)(2,1)} %get-tuple-element.146), channel_id=1, source_target_pairs={{0,8},{8,0},{16,24},{24,16},{1,9},{9,1},{17,25},{25,17},{2,10},{10... | collective-permute-start | bytes 4423688 | tf_op jit(solution)/shard_map/ppermute | solution.py:877
  177.3 23.0 %collective-permute-start.36 = (bf16[4,96,768]{2,1,0:T(8,128)(2,1)S(1)}, bf16[4,96,768]{2,1,0:T(8,128)(2,1)}, u32[]{:S(2)}, u32[]{:S(2)}) collective-permute-start(bf16[4,96,768]{2,1,0:T(8,128)(2,1)S(1)} %slice_bitcast_fusion.1), channel_id=1, source_target_pairs={{0,1},{1,0},{2,3},{3,2},{4,5},{5,4},{6,7},{7,6},{8,9},{9,8},{10,11... | collective-permute-start | bytes 1769480 | tf_op jit(solution)/shard_map/ppermute | solution.py:889
  179.0 28.3 %collective-permute-start.64 = (bf16[96,768]{1,0:T(8,128)(2,1)S(1)}, bf16[96,768]{1,0:T(8,128)(2,1)S(1)}, u32[]{:S(2)}, u32[]{:S(2)}) collective-permute-start(bf16[96,768]{1,0:T(8,128)(2,1)S(1)} %fusion.26.u0), channel_id=1, source_target_pairs={{0,16},{8,24},{16,0},{24,8},{1,17},{9,25},{17,1},{25,9},{2,18},{10... | collective-permute-start | bytes 442376 | tf_op jit(solution)/shard_map/ppermute | solution.py:877
  200.3 21.1 %collective-permute-start.37 = (bf16[2,192,768]{2,1,0:T(8,128)(2,1)S(1)}, bf16[2,192,768]{2,1,0:T(8,128)(2,1)S(1)}, u32[]{:S(2)}, u32[]{:S(2)}) collective-permute-start(bf16[2,192,768]{2,1,0:T(8,128)(2,1)S(1)} %get-tuple-element.138), channel_id=1, source_target_pairs={{0,1},{1,0},{2,3},{3,2},{4,5},{5,4},{6,7},{7,6},{8,9},{9,8},{10,11... | collective-permute-start | bytes 1769480 | tf_op jit(solution)/shard_map/ppermute | solution.py:889
  206.2 17.4 %collective-permute-start.47 = (bf16[2,4,24,1920]{3,2,1,0:T(8,128)(2,1)S(1)}, bf16[2,4,24,1920]{3,2,1,0:T(8,128)(2,1)S(1)}, u32[]{:S(2)}, u32[]{:S(2)}) collective-permute-start(bf16[2,4,24,1920]{3,2,1,0:T(8,128)(2,1)S(1)} %fusion), channel_id=1, source_target_pairs={{0,16},{8,24},{16,0},{24,8},{1,17},{9,25},{17,1},{25,9},{2,18},{10... | collective-permute-start | bytes 2211848 | tf_op jit(solution)/shard_map/ppermute | solution.py:877
  207.3 18.0 %collective-permute-start.55 = (bf16[2,2,4,32,1152]{4,3,2,1,0:T(8,128)(2,1)S(1)}, bf16[2,2,4,32,1152]{4,3,2,1,0:T(8,128)(2,1)S(1)}, u32[]{:S(2)}, u32[]{:S(2)}) collective-permute-start(bf16[2,2,4,32,1152]{4,3,2,1,0:T(8,128)(2,1)S(1)} %get-tuple-element.152), channel_id=1, source_target_pairs={{0,8},{8,0},{16,24},{24,16},{1,9},{9,1},{17,25},{25,17},{2,10},{10... | collective-permute-start | bytes 3538952 | tf_op jit(solution)/shard_map/ppermute | solution.py:877
  219.9 41.1 %collective-permute-start.65 = (bf16[96,768]{1,0:T(8,128)(2,1)S(1)}, bf16[96,768]{1,0:T(8,128)(2,1)S(1)}, u32[]{:S(2)}, u32[]{:S(2)}) collective-permute-start(bf16[96,768]{1,0:T(8,128)(2,1)S(1)} %fusion.26.u0), channel_id=1, source_target_pairs={{0,8},{8,0},{16,24},{24,16},{1,9},{9,1},{17,25},{25,17},{2,10},{10... | collective-permute-start | bytes 442376 | tf_op jit(solution)/shard_map/ppermute | solution.py:877
  220.0 41.4 %collective-permute-start.66 = (bf16[96,768]{1,0:T(8,128)(2,1)S(1)}, bf16[96,768]{1,0:T(8,128)(2,1)S(1)}, u32[]{:S(2)}, u32[]{:S(2)}) collective-permute-start(bf16[96,768]{1,0:T(8,128)(2,1)S(1)} %collective-permute-done.64.ux), channel_id=1, source_target_pairs={{0,8},{8,0},{16,24},{24,16},{1,9},{9,1},{17,25},{25,17},{2,10},{10... | collective-permute-start | bytes 442376 | tf_op jit(solution)/shard_map/ppermute | solution.py:877
  225.5 18.4 %collective-permute-start.56 = (bf16[2,4,32,1152]{3,2,1,0:T(8,128)(2,1)S(1)}, bf16[2,4,32,1152]{3,2,1,0:T(8,128)(2,1)S(1)}, u32[]{:S(2)}, u32[]{:S(2)}) collective-permute-start(bf16[2,4,32,1152]{3,2,1,0:T(8,128)(2,1)S(1)} %fusion.10), channel_id=1, source_target_pairs={{0,16},{8,24},{16,0},{24,8},{1,17},{9,25},{17,1},{25,9},{2,18},{10... | collective-permute-start | bytes 1769480 | tf_op jit(solution)/shard_map/ppermute | solution.py:877
  246.8 15.5 %collective-permute-start.34 = (bf16[192,768]{1,0:T(8,128)(2,1)S(1)}, bf16[192,768]{1,0:T(8,128)(2,1)S(1)}, u32[]{:S(2)}, u32[]{:S(2)}) collective-permute-start(bf16[192,768]{1,0:T(8,128)(2,1)S(1)} %get-tuple-element.115), channel_id=1, source_target_pairs={{0,16},{8,24},{16,0},{24,8},{1,17},{9,25},{17,1},{25,9},{2,18},{10... | collective-permute-start | bytes 884744 | tf_op jit(solution)/shard_map/ppermute | solution.py:877
  (67 other events, 507.9 us)

commit v3 on v2

--- a/solution.py
+++ b/solution.py
@@ -375,12 +375,13 @@
 
 
 class Copies:
-    def __init__(self, sems):
+    def __init__(self, sems, first=0):
         self.sems = sems
+        self.first = first
         self.held = []
 
     def add(self, source, target):
-        copy = pltpu.make_async_copy(source, target, self.sems.at[len(self.held)])
+        copy = pltpu.make_async_copy(source, target, self.sems.at[self.first + len(self.held)])
         copy.start()
         self.held.append(copy)
 
@@ -394,7 +395,7 @@
     return ((x, c), (1 - x, c), (x, 1 - c), (1 - x, 1 - c))
 
 
-def fetch_qkv(copies, coords, own, pieces_a, pieces_b, full, full_out=None, own_out=None):
+def fetch_qkv(copies, coords, own, groups, full, full_out=None, own_out=None):
     x, c, y, z = place(coords)
     rows = own.shape[0]
     half, width = rows // 2, own.shape[1] // 3
@@ -402,23 +403,27 @@
     copies.add(own, full.at[pl.ds(row, rows), :])
     if full_out is not None:
         copies.add(own_out, full_out.at[pl.ds(row, rows), :])
-    for (xx, cc), first, second in zip(corners(x, c), pieces_a, pieces_b, strict=True):
-        for number in range(7):
+    wide, side = 3 * width // 2, width // 2
+    for number in range(7):
+        for (xx, cc), group in zip(corners(x, c), groups, strict=True):
+            piece = piece_of(group, number)
             at = pl.ds(pl.multiple_of(piece_shard(number, y, z) * rows + half * cc, 16), half)
             copies.add(
-                first.at[number, pl.ds(0, half), :],
-                full.at[at, pl.ds(pl.multiple_of(width * xx, 128), width)],
-            )
-            side = width // 2
-            copies.add(
-                second.at[number, :, pl.ds(0, side)],
-                full.at[at, pl.ds(pl.multiple_of(2 * width + side * xx, 128), side)],
+                piece.at[pl.ds(0, half), pl.ds(0, wide)],
+                full.at[at, pl.ds(pl.multiple_of(wide * xx, 128), wide)],
             )
             if full_out is not None:
                 copies.add(
-                    second.at[number, :, pl.ds(side, side)],
+                    piece.at[pl.ds(0, half), pl.ds(wide, side)],
                     full_out.at[at, pl.ds(pl.multiple_of(side * xx, 128), side)],
                 )
+
+
+def piece_of(group, number):
+    behind, across, behind_across = group
+    if number < 3:
+        return behind.at[number]
+    return across.at[0] if number == 3 else behind_across.at[number - 4]
 
 
 def mask_bias(start, me, tok, target):
@@ -444,38 +449,53 @@
 
 def prep_kernel(
     coords, tokens, segs, qkv, out, up, down, gains, shifts, biases, up_bias,
-    t_out, qa_out, qb_out, fu_out, fd_out, scratch,
+    t_out, q_out, f_out,
+    scratch, wide, held_g, held_s, held_b, ids, line, sems,
 ):
     x, c, _y, _z = place(coords)
-    tok, width = tokens.shape
+    tok, width = tokens.shape[1:]
     rows = qkv.shape[0]
     half, side = rows // 2, width // 2
     p = 2 * x + c
     at = pl.ds(pl.multiple_of(half * c, 16), half)
-    qa_out[pl.ds(0, half), :] = qkv[at, pl.ds(pl.multiple_of(width * x, 128), width)]
+    copies, others = Copies(sems), Copies(sems, 5)
+    for source, target in ((gains, held_g), (shifts, held_s), (biases, held_b)):
+        copies.add(source, target)
+    copies.add(segs, ids)
+    copies.add(up_bias, line)
+    others.add(up, wide)
+    wide_cols = 3 * side
+    others.add(
+        qkv.at[at, pl.ds(pl.multiple_of(wide_cols * x, 128), wide_cols)],
+        q_out.at[pl.ds(0, half), pl.ds(0, wide_cols)],
+    )
+    others.add(
+        out.at[at, pl.ds(pl.multiple_of(side * x, 128), side)],
+        q_out.at[pl.ds(0, half), pl.ds(wide_cols, side)],
+    )
+    others.add(tokens.at[0], t_out.at[pl.ds(0, tok), :])
+    others.add(down.at[pl.ds(pl.multiple_of(rows * p, 16), rows), :], f_out.at[pl.ds(rows, rows), :])
+    copies.wait()
     scratch[...] = jnp.zeros_like(scratch)
-    scratch[pl.ds(0, 2), pl.ds(0, rows)] = f32(gains[...])
-    scratch[pl.ds(2, 2), pl.ds(0, rows)] = f32(shifts[...])
-    scratch[pl.ds(4, 4), pl.ds(0, rows)] = f32(biases[...])
-    scratch[pl.ds(0, 1), pl.ds(128, 384)] = f32(up_bias[...])
-    qa_out[pl.ds(half, 8), :] = b16(scratch[...])
-    qb_out[:, pl.ds(0, side)] = qkv[at, pl.ds(pl.multiple_of(2 * width + side * x, 128), side)]
-    qb_out[:, pl.ds(side, side)] = out[at, pl.ds(pl.multiple_of(side * x, 128), side)]
-    t_out[pl.ds(0, tok), :] = tokens[...]
+    for first, held in ((0, held_g), (2, held_s), (4, held_b)):
+        scratch[pl.ds(first, held.shape[0]), pl.ds(0, rows)] = f32(held[...])
+    scratch[pl.ds(0, 1), pl.ds(128, 384)] = f32(line[...])
+    q_out[pl.ds(half, 8), pl.ds(0, width)] = b16(scratch[...])
+    q_out[pl.ds(half, 8), pl.ds(width, width)] = jnp.zeros((8, width), jnp.bfloat16)
     scratch[...] = jnp.zeros_like(scratch)
-    scratch[pl.ds(0, 1), pl.ds(0, tok)] = f32(segs[...])
+    scratch[pl.ds(0, 1), pl.ds(0, tok)] = f32(ids[...])
     t_out[pl.ds(tok, 8), :] = b16(scratch[...])
+    others.wait()
     for group in range(2):
         parts = []
         for shard in range(4 * group, 4 * group + 4):
-            parts.append(choose(unpack96(f32(up[:, pl.ds(384 * shard, 384)])), p))
-        fu_out[:, pl.ds(384 * group, 384)] = b16(pack96(parts))
-    fd_out[...] = down[pl.ds(pl.multiple_of(rows * p, 16), rows), :]
+            parts.append(choose(unpack96(f32(wide[:, pl.ds(384 * shard, 384)])), p))
+        f_out[pl.ds(0, rows), pl.ds(384 * group, 384)] = b16(pack96(parts))
 
 
 def front_kernel(
     coords, seg, xo, x1, x2, x3, x4, first, own, own_o,
-    a7, ax7, ac7, acx7, b7, bx7, bc7, bcx7,
+    g0, g1, g2, g3, g4, g5, g6, g7, g8, g9, g10, g11,
     q_out, kv_out, h_out, a_out, lse_out, start_out, vec_out, upb_out, wo_out, r_out, h2_out,
     full, small, bias, sems, vsems,
 ):
@@ -486,10 +506,10 @@
     copies, vcopies = Copies(sems), Copies(vsems)
     vcopies.add(first.at[pl.ds(48, 8), pl.ds(0, 512)], small.at[me])
     for number in range(7):
-        vcopies.add(a7.at[number, pl.ds(48, 8), pl.ds(0, 512)], small.at[piece_shard(number, y, z)])
-    fetch_qkv(
-        copies, coords, own, (a7, ax7, ac7, acx7), (b7, bx7, bc7, bcx7), full, wo_out, own_o
-    )
+        source = piece_of((g0, g1, g2), number)
+        vcopies.add(source.at[pl.ds(48, 8), pl.ds(0, 512)], small.at[piece_shard(number, y, z)])
+    groups = ((g0, g1, g2), (g3, g4, g5), (g6, g7, g8), (g9, g10, g11))
+    fetch_qkv(copies, coords, own, groups, full, wo_out, own_o)
     blocks = (xo, x1, x2, x3, x4)
     lane1 = lax.broadcasted_iota(jnp.int32, (1, tok), 1)
     start = jnp.full(seg.shape, 1 << 30, jnp.int32)
@@ -574,22 +594,22 @@
 
 
 def near_kernel(
-    coords, h_own, h_c, dy_own, dy_c, upb, u_own, uz1, uz2, uz3, uy, d_own, dz1, dz2, dz3, dy4,
-    act_out, du_out, keep_out, send_out, wu_out, wd_out,
-    h2, dy, y_acc, dh_acc, sems,
+    coords, h_own, h_c, dy_own, dy_c, upb, own, z1, z2, z3, y0, y13, y2,
+    h2, dy, act_out, du_out, keep_out, send_out, wu_out, wd_out,
+    y_acc, dh_acc, sems,
 ):
     _x, _c, y, z = place(coords)
-    tok = h_own.shape[0]
+    tok, width = h_own.shape
+    rows = width // 8
     copies = Copies(sems)
-    for own, ones, four, full in (
-        (u_own, (uz1, uz2, uz3), uy, wu_out),
-        (d_own, (dz1, dz2, dz3), dy4, wd_out),
-    ):
-        rows = own.shape[0]
-        copies.add(own, full.at[pl.ds(pl.multiple_of((2 * z + y) * rows, 16), rows), :])
-        for number in range(7):
-            at = pl.ds(pl.multiple_of(piece_shard(number, y, z) * rows, 16), rows)
-            copies.add(ones[number] if number < 3 else four.at[pl.ds((number - 3) * rows, rows), :], full.at[at, :])
+    across = (y0, y13.at[pl.ds(0, 2 * rows), :], y2, y13.at[pl.ds(2 * rows, 2 * rows), :])
+    shards = [(own, 2 * z + y)] + [
+        (ref, piece_shard(number, y, z)) for number, ref in enumerate((z1, z2, z3) + across)
+    ]
+    for ref, shard in shards:
+        at = pl.ds(pl.multiple_of(shard * rows, 16), rows)
+        copies.add(ref.at[pl.ds(0, rows), :], wu_out.at[at, :])
+        copies.add(ref.at[pl.ds(rows, rows), :], wd_out.at[at, :])
     h2[pl.ds(0, tok), :] = h_own[...]
     h2[pl.ds(tok, tok), :] = h_c[...]
     dy[pl.ds(0, tok), :] = dy_own[...]
@@ -603,35 +623,33 @@
 
 
 def far_kernel(
-    h_x, h_xc, dy_x, dy_xc, upb, w_up, w_down,
-    act_out, du_out, keep_out, send_out,
-    h2, dy, y_acc, dh_acc,
+    h_x, h_xc, dy_x, dy_xc, upb, w_up, w_down, h_near, dy_near, act_near, du_near,
+    hs, dys, acts, dus, keep_out, send_out,
+    y_acc, dh_acc, sems,
 ):
     tok = h_x.shape[0]
-    h2[pl.ds(0, tok), :] = h_x[...]
-    h2[pl.ds(tok, tok), :] = h_xc[...]
-    dy[pl.ds(0, tok), :] = dy_x[...]
-    dy[pl.ds(tok, tok), :] = dy_xc[...]
-    feed_tokens(h2, dy, w_up, w_down, upb, act_out, du_out, y_acc, dh_acc)
+    copies = Copies(sems)
+    for source, target in ((h_near, hs), (dy_near, dys), (act_near, acts), (du_near, dus)):
+        copies.add(source, target.at[pl.ds(0, 2 * tok), :])
+    later = pl.ds(2 * tok, 2 * tok)
+    hs[pl.ds(2 * tok, tok), :] = h_x[...]
+    hs[pl.ds(3 * tok, tok), :] = h_xc[...]
+    dys[pl.ds(2 * tok, tok), :] = dy_x[...]
+    dys[pl.ds(3 * tok, tok), :] = dy_xc[...]
+    feed_tokens(
+        hs.at[later, :], dys.at[later, :], w_up, w_down, upb, acts.at[later, :], dus.at[later, :], y_acc, dh_acc
+    )
     keep_out[0] = dh_acc[pl.ds(0, tok), :]
     keep_out[1] = y_acc[pl.ds(0, tok), :]
     send_out[0] = b16(dh_acc[pl.ds(tok, tok), :])
     send_out[1] = b16(y_acc[pl.ds(tok, tok), :])
-
-
-def weights_kernel(
-    coords, h0, h1, h2, h3, d0, d1, d2, d3, act_a, act_b, du_a, du_b,
-    u_out, d_out, upb_out,
-    hs, dys, acts, dus, stage, sems,
-):
+    copies.wait()
+
+
+def weights_kernel(coords, hs, dys, acts, dus, u_out, d_out, upb_out, stage, sems):
     _x, _c, y, z = place(coords)
-    tok, width = h0.shape
-    for number, (h, d) in enumerate(((h0, d0), (h1, d1), (h2, d2), (h3, d3))):
-        hs[pl.ds(number * tok, tok), :] = h[...]
-        dys[pl.ds(number * tok, tok), :] = d[...]
-    for number, (act, du) in enumerate(((act_a, du_a), (act_b, du_b))):
-        acts[pl.ds(2 * number * tok, 2 * tok), :] = act[...]
-        dus[pl.ds(2 * number * tok, 2 * tok), :] = du[...]
+    width = hs.shape[1]
+    rows = width // 8
     upb_out[...] = jnp.sum(f32(dus[...]), axis=0, keepdims=True)
 
     def weight(number, carry):
@@ -645,9 +663,8 @@
     for shard in range(8):
         zz = lax.rem(shard // 2 + 4 - z, 4)
         yy = jnp.where(y == shard % 2, 0, 1)
-        rows = pl.ds(shard * (width // 8), width // 8)
-        outs.add(stage.at[0, rows, :], u_out.at[yy, zz])
-        outs.add(stage.at[1, rows, :], d_out.at[yy, zz])
+        outs.add(stage.at[0, pl.ds(shard * rows, rows), :], u_out.at[yy, zz])
+        outs.add(stage.at[1, pl.ds(shard * rows, rows), :], d_out.at[yy, zz])
     outs.wait()
 
 
@@ -744,26 +761,27 @@
 
 
 def back_b_kernel(
-    coords, start_in, q_in, kv_in, h_in, lse_in, da_in, vec_in, upb_in, dq_a, dkv_a, xo, x1, x2, x3, x4,
-    own, a7, ax7, ac7, acx7, b7, bx7, bc7, bcx7,
-    other, mine, p_own, p_y, p_z,
-    full, bias, dq_s, dkv_s, stage, sems, osems,
+    coords, start_in, q_in, kv_in, lse_in, da_in, vec_in, upb_in, dq_a, dkv_a, xo, x1, x2, x3, x4,
+    own, g0, g1, g2, g3, g4, g5, g6, g7, g8, g9, g10, g11,
+    dq_out, dkv_out, p_own, p_y, p_z, sums_out,
+    full, bias, sems,
 ):
     x, c, y, z = place(coords)
     p = 2 * x + c
     tok, width = q_in.shape
     side = width // 2
     copies = Copies(sems)
-    fetch_qkv(copies, coords, own, (a7, ax7, ac7, acx7), (b7, bx7, bc7, bcx7), full)
+    groups = ((g0, g1, g2), (g3, g4, g5), (g6, g7, g8), (g9, g10, g11))
+    fetch_qkv(copies, coords, own, groups, full)
     mask_bias(start_in[...], 2 * z + y, tok, bias)
-    back_pairs(3, q_in, kv_in, lse_in, da_in, bias, dq_s, dkv_s)
+    back_pairs(3, q_in, kv_in, lse_in, da_in, bias, dq_out, dkv_out)
     copies.wait()
     gain_sum = jnp.zeros((1, width), jnp.float32)
     shift_sum = jnp.zeros((1, width), jnp.float32)
     for back, block in enumerate((xo, x1, x2, x3, x4)):
         rows = pl.ds((4 - back) * tok, tok)
         grad = jnp.zeros((tok, width), jnp.float32)
-        for number, (dq, dkv) in enumerate(((dq_a, dkv_a), (dq_s, dkv_s))):
+        for number, (dq, dkv) in enumerate(((dq_a, dkv_a), (dq_out, dkv_out))):
             at = number * side
             grad = grad + dot_nt(dkv[rows, pl.ds(0, side)], full[:, pl.ds(width + at, side)])
             grad = grad + dot_nt(dkv[rows, pl.ds(side, side)], full[:, pl.ds(2 * width + at, side)])
@@ -778,11 +796,10 @@
         hat, _rate = norm_parts(f32(block[pl.ds(0, tok), :]))
         gain_sum = gain_sum + jnp.sum(grad * hat, axis=0, keepdims=True)
         shift_sum = shift_sum + jnp.sum(grad, axis=0, keepdims=True)
-    qkv_weight(h_in, dq_s, dkv_s, stage)
     zero = jnp.zeros((1, width), jnp.float32)
-    bias_q = jnp.concatenate([jnp.sum(f32(d[...]), axis=0, keepdims=True) for d in (dq_a, dq_s)], axis=1)
+    bias_q = jnp.concatenate([jnp.sum(f32(d[...]), axis=0, keepdims=True) for d in (dq_a, dq_out)], axis=1)
     bias_v = jnp.concatenate(
-        [jnp.sum(f32(d[:, pl.ds(side, side)]), axis=0, keepdims=True) for d in (dkv_a, dkv_s)], axis=1
+        [jnp.sum(f32(d[:, pl.ds(side, side)]), axis=0, keepdims=True) for d in (dkv_a, dkv_out)], axis=1
     )
     vec = vec_in[...] + jnp.concatenate(
         [gain_sum, zero, shift_sum, zero, bias_q, bias_v, zero, zero], axis=0
@@ -794,18 +811,26 @@
         vec_parts = unpack96(vec[:, 384 * group : 384 * group + 384])
         upb_parts = unpack96(jnp.broadcast_to(upb_in[:, cols], (8, 384)))
         for k in range(4):
-            both = jnp.concatenate(
+            sums_out[4 * group + k] = jnp.concatenate(
                 [
                     jnp.where(lane < 96, vec_parts[k], 0.0),
                     jnp.where((lane < 96) & (line == p), upb_parts[k], 0.0),
-                    jnp.zeros((8, 3 * side - 256), jnp.float32),
                 ],
                 axis=1,
             )
-            for cc in range(2):
-                for xx in range(2):
-                    stage[cc, xx, 4 * group + k, pl.ds(24, 8), :] = b16(both)
-    outs = Copies(osems)
+
+
+def back_c_kernel(coords, h_in, dq, dkv, sums_in, other, mine, stage, sems):
+    x, c, y, z = place(coords)
+    qkv_weight(h_in, dq, dkv, stage)
+    for shard in range(8):
+        row = b16(
+            jnp.concatenate([sums_in[shard], jnp.zeros((8, stage.shape[4] - 256), jnp.float32)], axis=1)
+        )
+        for cc in range(2):
+            for xx in range(2):
+                stage[cc, xx, shard, pl.ds(24, 8), :] = row
+    outs = Copies(sems)
     for shard in range(8):
         zz = lax.rem(shard // 2 + 4 - z, 4)
         yy = jnp.where(y == shard % 2, 0, 1)
@@ -816,10 +841,10 @@
     outs.wait()
 
 
-def tokens_kernel(own, near, far, dr, xo, vec_in, grad_out):
+def tokens_kernel(own, near, dr, xo, vec_in, grad_out):
     tok = own.shape[0]
     hat, rate = norm_parts(f32(xo[pl.ds(0, tok), :]))
-    grad = own[...] + f32(near[...]) + f32(far[...])
+    grad = own[...] + f32(near[...])
     grad_out[...] = dr[...] + norm_back(grad, hat, rate, vec_in[0:1, :])
 
 
@@ -848,6 +873,7 @@
         out[rows, :] = first[:, 3 * side :]
 
 
+HB = pl.BlockSpec(memory_space=pltpu.HBM)
 VM = pl.BlockSpec(memory_space=pltpu.VMEM)
 SM = pl.BlockSpec(memory_space=pltpu.SMEM)
 AN = pl.BlockSpec(memory_space=pl.ANY)
@@ -865,7 +891,7 @@
         out_shape=out_shape,
         scratch_shapes=list(scratch),
         compiler_params=pltpu.CompilerParams(vmem_limit_bytes=vmem << 20),
-        cost_estimate=pl.CostEstimate(flops=flops, bytes_accessed=moved, transcendentals=0),
+        cost_estimate=pl.CostEstimate(flops=flops // 20, bytes_accessed=moved // 20, transcendentals=0),
     )
 
 
@@ -919,57 +945,69 @@
     bf, fl = jnp.bfloat16, jnp.float32
     dma = pltpu.SemaphoreType.DMA
     grad_y = cotangent[0]
-    dy_x = to_x(grad_y)
-    own_tokens, piece_a, piece_b, piece_u, piece_d = call(
+    own_tokens, piece_q, piece_f = call(
         prep_kernel,
-        [SM] + [VM] * 10,
-        [VM] * 5,
+        [SM] + [HB] * 10,
+        [VM] * 3,
         [
             shape_of((tok + 8, width), bf),
-            shape_of((56, width), bf),
-            shape_of((48, width), bf),
-            shape_of((96, width), bf),
-            shape_of((96, width), bf),
+            shape_of((56, 2 * width), bf),
+            shape_of((192, width), bf),
         ],
-        [pltpu.VMEM((8, width), fl)],
-        vmem=16,
-        moved=4 * 10**6,
+        [
+            pltpu.VMEM((8, width), fl),
+            pltpu.VMEM((96, hidden), bf),
+            pltpu.VMEM((2, 96), bf),
+            pltpu.VMEM((2, 96), bf),
+            pltpu.VMEM((4, 96), bf),
+            pltpu.VMEM((1, tok), jnp.int32),
+            pltpu.VMEM((1, 384), bf),
+            dma((10,)),
+        ],
+        vmem=60, moved=4 * 10**6,
     )(
-        coords, tokens[0], segment_ids, query_key_value_weight, output_weight, up_weight, down_weight,
+        coords, tokens, segment_ids, query_key_value_weight, output_weight, up_weight, down_weight,
         ln_gains, ln_biases, biases, up_projection_bias[None],
     )
 
-    az = [to_z(piece_a, k) for k in (1, 2, 3)]
-    bz = [to_z(after(piece_b, az[k - 1]), k) for k in (1, 2, 3)]
-    ay = to_y(join(piece_a, *az))
-    x2 = to_z(after(own_tokens, az[2]), 1)
-    by = to_y(after(join(piece_b, *bz), ay))
-    a7 = join(*az, ay)
-    ax7 = to_x(after(a7, dy_x))
-    x4 = to_z(x2, 1)
+    q1, q3 = to_z(piece_q, 1), to_z(piece_q, 3)
+    q_y0 = to_y(piece_q)
+    dy_x = to_x(grad_y)
+    f_y0 = to_y(after(piece_f, q_y0))
+    q2 = to_z(after(q1, q3), 1)
+    q_xy0 = to_x(after(q_y0, dy_x))
+    x2 = to_z(after(own_tokens, q2), 1)
+    q_z = join(q1, q2, q3)
+    q_y = to_y(after(q_z, f_y0))
+    q_xz = to_x(after(q_z, q_xy0))
+    f1 = to_z(after(piece_f, q2), 1)
+    x4 = to_z(after(x2, f1), 1)
     near = jnp.where(y == 0, own_tokens, x2)
     far = jnp.where(y == 0, x2, x4)
-    crossed = to_y(after(jnp.stack([near, far]), by))
+    crossed = to_y(after(jnp.stack([near, far]), q_y))
     x1, x3 = crossed[0], crossed[1]
-    b7 = join(*bz, by)
-    bx7 = to_x(after(b7, ax7))
-    ac7, bc7 = to_core(a7), to_core(b7)
-    acx7, bcx7 = to_core(ax7), to_core(bx7)
-    uz = [to_z(after(piece_u, x4), k) for k in (1, 2, 3)]
-    dz = [to_z(after(piece_d, uz[k - 1]), k) for k in (1, 2, 3)]
-    uy = to_y(after(join(piece_u, *uz), crossed))
-    down_y = to_y(after(join(piece_d, *dz), uy))
+    q_xy = to_x(after(q_y, q_xz))
+    f3 = to_z(after(piece_f, x4), 3)
+    f2 = to_z(after(f1, f3), 1)
+    q_cy0, q_cxy0 = to_core(after(q_y0, q_xz)), to_core(after(q_xy0, q_xz))
+    q_cz, q_cxz = to_core(after(q_z, q_cy0)), to_core(after(q_xz, q_cxy0))
+    q_cy = to_core(after(q_y, q_cz))
+    f_y13 = to_y(after(join(f1, f3), crossed))
+    q_cxy = to_core(after(q_xy, q_cy, q_cxz))
+    f_y2 = to_y(after(f2, f_y13))
     dy_c, dy_xc = to_core(grad_y), to_core(dy_x)
 
-    def seven(value):
-        return value.reshape(7, value.shape[0] // 7, value.shape[1])
-
-    got_a = [seven(v) for v in (a7, ax7, ac7, acx7)]
-    got_b = [seven(v) for v in (b7, bx7, bc7, bcx7)]
+    def pieces(value):
+        return value.reshape(value.shape[0] // 56, 56, value.shape[1])
+
+    got_q = [
+        pieces(v)
+        for v in (q_z, q_y0, q_y, q_xz, q_xy0, q_xy, q_cz, q_cy0, q_cy, q_cxz, q_cxy0, q_cxy)
+    ]
     seg = jnp.concatenate([segment_ids, segment_ids], axis=1)
     queries, kv, normed, attended, lse, start, vec, upb, w_out, residual, hidden_2 = call(
         front_kernel,
-        [SM] + [VM] * 6 + [AN] * 11,
+        [SM] + [VM] * 6 + [AN] * 15,
         [VM] * 11,
         [
             shape_of((tok, width), bf),
@@ -988,60 +1026,51 @@
             pltpu.VMEM((width, 3 * width), bf),
             pltpu.VMEM((8, 8, 512), bf),
             pltpu.VMEM((keys, 2 * tok), fl),
-            dma((2 + 84,)),
+            dma((2 + 56,)),
             dma((8,)),
         ],
         flops=7 * 10**9,
-        moved=12 * 10**6,
+        vmem=16, moved=12 * 10**6,
     )(
-        coords, seg, own_tokens, x1, x2, x3, x4, piece_a, query_key_value_weight, output_weight,
-        *got_a, *got_b,
+        coords, seg, own_tokens, x1, x2, x3, x4, piece_q, query_key_value_weight, output_weight, *got_q,
     )
     h_x = to_x(hidden_2)
     h_c = to_core(hidden_2)
-    feed_shapes = [
-        shape_of((2 * tok, width), bf),
-        shape_of((2 * tok, width), bf),
-        shape_of((2, tok, width), fl),
-        shape_of((2, tok, width), bf),
-    ]
-    feed_scratch = [
-        pltpu.VMEM((2 * tok, width), bf),
-        pltpu.VMEM((2 * tok, width), bf),
-        pltpu.VMEM((2 * tok, width), fl),
-        pltpu.VMEM((2 * tok, width), fl),
-    ]
-    act_a, du_a, keep_a, send_a, w_up, w_down = call(
+    act = shape_of((2 * tok, width), bf)
+    acts = shape_of((4 * tok, width), bf)
+    feed_shapes = [shape_of((2, tok, width), fl), shape_of((2, tok, width), bf)]
+    feed_scratch = [pltpu.VMEM((2 * tok, width), fl), pltpu.VMEM((2 * tok, width), fl)]
+    *near_acts, keep_a, send_a, w_up, w_down = call(
         near_kernel,
-        [SM] + [VM] * 5 + [AN] * 10,
-        [VM] * 6,
-        feed_shapes + [shape_of((width, width), bf)] * 2,
+        [SM] + [VM] * 5 + [AN] * 7,
+        [VM] * 8,
+        [act] * 4 + feed_shapes + [shape_of((width, width), bf)] * 2,
         feed_scratch + [dma((16,))],
         flops=3 * 10**9,
-        moved=6 * 10**6,
-    )(coords, hidden_2, h_c, grad_y, dy_c, upb, piece_u, *uz, uy, piece_d, *dz, down_y)
+        vmem=8, moved=6 * 10**6,
+    )(coords, hidden_2, h_c, grad_y, dy_c, upb, piece_f, f1, f2, f3, f_y0, f_y13, f_y2)
     came_a = to_core(send_a)
     h_xc = to_core(h_x)
-    act_b, du_b, keep_b, send_b = call(
+    *all_acts, keep_b, send_b = call(
         far_kernel,
-        [VM] * 7,
-        [VM] * 4,
-        feed_shapes,
-        feed_scratch,
+        [VM] * 7 + [AN] * 4,
+        [VM] * 6,
+        [acts] * 4 + feed_shapes,
+        feed_scratch + [dma((4,))],
         flops=3 * 10**9,
-        moved=6 * 10**6,
-    )(h_x, h_xc, dy_x, dy_xc, upb, w_up, w_down)
+        vmem=8, moved=6 * 10**6,
+    )(h_x, h_xc, dy_x, dy_xc, upb, w_up, w_down, *near_acts)
     came_b = to_core(send_b)
     back_x = to_x(b16(keep_b[0] + f32(came_b[0])))
     u_terms, d_terms, upb_g = call(
         weights_kernel,
-        [SM] + [VM] * 12,
-        [AN] * 2 + [VM],
+        [SM] + [VM] * 4,
+        [AN, AN, VM],
         [shape_of((2, 4, 96, width), bf), shape_of((2, 4, 96, width), bf), shape_of((1, width), fl)],
-        [pltpu.VMEM((4 * tok, width), bf)] * 4 + [pltpu.VMEM((2, width, width), bf), dma((16,))],
+        [pltpu.VMEM((2, width, width), bf), dma((16,))],
         flops=3 * 10**9,
-        moved=6 * 10**6,
-    )(coords, hidden_2, h_c, h_x, h_xc, grad_y, dy_c, dy_x, dy_xc, act_a, act_b, du_a, du_b)
+        vmem=12, moved=6 * 10**6,
+    )(coords, *all_acts)
     u_came = to_y(u_terms[1])
     d_came = to_y(after(d_terms[1], u_came))
     back_y = to_x(after(b16(keep_b[1] + f32(came_b[1])), back_x))
@@ -1055,9 +1084,8 @@
             shape_of((width, width), bf),
             shape_of((8, width), fl),
         ],
-        vmem=24,
         flops=10**9,
-        moved=4 * 10**6,
+        vmem=10, moved=4 * 10**6,
     )(residual, keep_a, came_a, back_x, grad_y, vec, w_out, attended)
     back_scratch = [
         pltpu.VMEM((keys, 2 * tok), fl),
@@ -1074,65 +1102,66 @@
         ],
         back_scratch + [pltpu.VMEM((2, 2, 8, 24, 5 * width // 2), bf), dma((32,))],
         flops=5 * 10**9,
-        moved=10 * 10**6,
+        vmem=16, moved=10 * 10**6,
     )(coords, start, queries, kv, normed, lse, grad_attended, dw_out)
-    qb_other, qb_mine, p_own, p_y, p_z = call(
+    def across_core(other, mine):
+        came = to_core(other)
+        return came, lambda *index: f32(mine[index]) + f32(came[index])
+
+    def along_z(part, *done):
+        came = [to_z(b16(part(step)), step) for step in (1, 2, 3)]
+        came = lax.optimization_barrier((*came, *done))[:3]
+        return b16(part(0) + f32(came[0]) + f32(came[1]) + f32(came[2]))
+
+    def u_part(*index):
+        return f32(u_terms[(0,) + index]) + f32(u_came[index])
+
+    def d_part(*index):
+        return f32(d_terms[(0,) + index]) + f32(d_came[index])
+
+    qa_came, qa_1 = across_core(qa_other, qa_mine)
+    dq_b, dkv_b, p_own, p_y, p_z, sums = call(
         back_b_kernel,
-        [SM] + [VM] * 15 + [AN] * 9,
-        [AN] * 2 + [VM] * 3,
+        [SM] + [VM] * 14 + [AN] * 13,
+        [VM] * 6,
+        [
+            shape_of((tok, width // 2), bf),
+            shape_of((keys, width), bf),
+            shape_of((tok, width), fl),
+            shape_of((2, tok, width), bf),
+            shape_of((2, tok, width), bf),
+            shape_of((8, 8, 256), fl),
+        ],
+        [pltpu.VMEM((width, 3 * width), bf)] + back_scratch + [dma((1 + 28,))],
+        flops=6 * 10**9,
+        vmem=20, moved=10 * 10**6,
+    )(
+        coords, start, queries, kv, lse, grad_attended, vec_g, upb_g, dq_a, dkv_a,
+        own_tokens, x1, x2, x3, x4, query_key_value_weight, *got_q,
+    )
+    u_sum = along_z(u_part, dkv_b)
+    d_sum = along_z(d_part)
+    qa_x = to_x(b16(qa_1(1)))
+    p_came = to_y(after(p_y, d_came))
+    qb_other, qb_mine = call(
+        back_c_kernel,
+        [SM] + [VM] * 4,
+        [AN] * 2,
         [
             shape_of((2, 2, 4, 32, 3 * width // 2), bf),
             shape_of((2, 2, 4, 32, 3 * width // 2), bf),
-            shape_of((tok, width), fl),
-            shape_of((2, tok, width), bf),
-            shape_of((2, tok, width), bf),
         ],
-        [pltpu.VMEM((width, 3 * width), bf)]
-        + back_scratch
-        + [
-            pltpu.VMEM((tok, width // 2), bf),
-            pltpu.VMEM((keys, width), bf),
-            pltpu.VMEM((2, 2, 8, 32, 3 * width // 2), bf),
-            dma((1 + 56,)),
-            dma((32,)),
-        ],
-        flops=9 * 10**9,
-        moved=14 * 10**6,
-    )(
-        coords, start, queries, kv, normed, lse, grad_attended, vec_g, upb_g, dq_a, dkv_a,
-        own_tokens, x1, x2, x3, x4, query_key_value_weight, *got_a, *got_b,
-    )
-    result = b16(
-        residual + vec[7:8] + keep_a[1] + f32(came_a[1]) + f32(back_y)
-    )
-
-    def across_core(other, mine):
-        came = to_core(other)
-        return lambda *index: f32(mine[index]) + f32(came[index])
-
-    def along_z(part, *done):
-        total = part(0)
-        for step in (1, 2, 3):
-            total = total + f32(to_z(after(b16(part(step)), *done), step))
-        return b16(total)
-
-    def u_part(*index):
-        return f32(u_terms[(0,) + index]) + f32(u_came[index])
-
-    def d_part(*index):
-        return f32(d_terms[(0,) + index]) + f32(d_came[index])
-
-    u_sum = along_z(u_part)
-    d_sum = along_z(d_part, u_sum)
-    qa_1 = across_core(qa_other, qa_mine)
-    qa_x = to_x(b16(qa_1(1)))
-    p_came = to_y(after(p_y, d_came))
-    qb_1 = across_core(qb_other, qb_mine)
+        [pltpu.VMEM((2, 2, 8, 32, 3 * width // 2), bf), dma((32,))],
+        flops=3 * 10**9,
+        vmem=12, moved=6 * 10**6,
+    )(coords, normed, after(dq_b, qa_came), dkv_b, sums)
+    result = b16(residual + vec[7:8] + keep_a[1] + f32(came_a[1]) + f32(back_y))
+    _qb_came, qb_1 = across_core(qb_other, qb_mine)
     qb_x = to_x(after(b16(qb_1(1)), qa_x))
     even = y == 0
     sum_own = p_own + jnp.where(even, f32(p_came[0]), 0.0)
     sum_4 = b16(f32(p_z[1]) + jnp.where(even, 0.0, f32(p_came[1])))
-    hop = to_z(after(sum_4, d_sum), 3)
+    hop = to_z(sum_4, 3)
     sum_2 = b16(f32(p_z[0]) + jnp.where(even, f32(p_came[1]), f32(p_came[0])) + f32(hop))
     back_2 = to_z(sum_2, 3)
 
@@ -1151,36 +1180,34 @@
     def qb_3(*index):
         return qb_2(0, *index) + f32(qb_y[index])
 
-    qa_sum = along_z(qa_3, back_2)
-    qb_sum = along_z(qb_3, qa_sum)
+    qa_sum = along_z(qa_3)
+    qb_sum = along_z(qb_3)
 
     def spread(total, *done):
         over = to_x(after(total, *done))
         return total, over, to_core(total), to_core(over)
 
     done_u = spread(u_sum)
-    done_d = spread(d_sum)
+    done_d = spread(d_sum, qa_x)
     done_a = spread(qa_sum)
     done_b = spread(qb_sum)
     grad_tokens = call(
-        tokens_kernel, [VM] * 6, VM, shape_of((tok, width), fl), vmem=16, moved=3 * 10**6
-    )(sum_own, back_2, jnp.zeros_like(back_2), grad_first, own_tokens, vec)
+        tokens_kernel, [VM] * 5, VM, shape_of((tok, width), fl), vmem=4, moved=3 * 10**6
+    )(sum_own, back_2, grad_first, own_tokens, vec)
     grad_up, grad_down = call(
         finish_f_kernel,
         [SM] + [VM] * 8,
         [VM] * 2,
         [shape_of(up_weight.shape, fl), shape_of(down_weight.shape, fl)],
         [pltpu.VMEM((4, 96, width), bf)],
-        vmem=16,
-        moved=4 * 10**6,
+        vmem=8, moved=4 * 10**6,
     )(coords, *done_u, *done_d)
     grad_qkv, grad_out = call(
         finish_q_kernel,
         [SM] + [VM] * 8,
         [VM] * 2,
         [shape_of(query_key_value_weight.shape, fl), shape_of(output_weight.shape, fl)],
-        vmem=16,
-        moved=3 * 10**6,
+        vmem=8, moved=3 * 10**6,
     )(coords, *done_a, *done_b)
     sums = f32(qb_sum[24:32, :256])
     part = ln_gains.shape[1]

time: 279 us -> 246 us (0.88)
  waiting for transfers between devices: 118 us -> 101 us
  local copies, waits for them, and re-layouts: 13.8 us -> 5.41 us
  starting transfers between devices: 70.2 us -> 62.8 us
    ppermute x28 -> x22, waiting for transfers between devices: 67.2 us -> 25 us  [to_z(): lax.ppermute(value, 'seq', [(k, (k + 2 * steps) % 8) for k in range(8)])]
    ppermute x32 -> x35, waiting for transfers between devices: 18.5 us -> 34.2 us  [swap_rep(): return lax.ppermute(value, 'rep', [(k, k ^ bit) for k in range(4)])]
    ppermute x10 -> x11, waiting for transfers between devices: 32.5 us -> 41.6 us  [to_y(): return lax.ppermute(value, 'seq', [(k, k ^ 1) for k in range(8)])]
    unnamed x64 -> x34, local copies, waits for them, and re-layouts: 11.1 us -> 2.17 us
    ppermute x28 -> x22, starting transfers between devices: 40 us -> 35.2 us  [to_z(): lax.ppermute(value, 'seq', [(k, (k + 2 * steps) % 8) for k in range(8)])]
    ppermute x10 -> x11, starting transfers between devices: 13.8 us -> 11 us  [to_y(): return lax.ppermute(value, 'seq', [(k, k ^ 1) for k in range(8)])]
    pallas_call x7 -> x8, Pallas kernels: 54.2 us -> 54.5 us  [the longest x1 14.6 us: on_device_fast(): call(front_kernel, [SM] + [VM] * 6 + [AN] * 15, [VM] * 11, [shape_of((tok...]
    ppermute x32 -> x35, starting transfers between devices: 16.3 us -> 16.6 us  [swap_rep(): return lax.ppermute(value, 'rep', [(k, k ^ bit) for k in range(4)])]
  transfers between devices with their start and end apart: 70 -> 68, of which waited for: 24 -> 26; matrix products, arithmetic and copies ran while one was open for 3% -> 2% of each run, Pallas kernels for 23% -> 20%
where the time goes in v3:
time: 246 us; the launch traced here: 245 us
  waiting for transfers between devices  101 us (41%)
  Pallas kernels  71.4 us (29%)
  starting transfers between devices  62.8 us (26%)
  local copies, waits for them, and re-layouts  5.41 us (2%)
  other arithmetic  3.62 us (1%)
    ppermute x11, waiting for transfers between devices, to_y(): return lax.ppermute(value, 'seq', [(k, k ^ 1) for k in range(8)])  41.6 us
    ppermute x22, starting transfers between devices, to_z(): lax.ppermute(value, 'seq', [(k, (k + 2 * steps) % 8) for k in range(8)])  35.2 us
    ppermute x35, waiting for transfers between devices, swap_rep(): return lax.ppermute(value, 'rep', [(k, k ^ bit) for k in range(4)])  34.2 us
    ppermute x22, waiting for transfers between devices, to_z(): lax.ppermute(value, 'seq', [(k, (k + 2 * steps) % 8) for k in range(8)])  25 us
    ppermute x35, starting transfers between devices, swap_rep(): return lax.ppermute(value, 'rep', [(k, k ^ bit) for k in range(4)])  16.6 us
    pallas_call x1, Pallas kernels, on_device_fast(): call(front_kernel, [SM] + [VM] * 6 + [AN] * 15, [VM] * 11, [shape_of((tok...  14.6 us
    pallas_call x1, Pallas kernels, on_device_fast(): call(back_b_kernel, [SM] + [VM] * 14 + [AN] * 13, [VM] * 6, [shape_of((to...  11.4 us
    pallas_call x1, Pallas kernels, on_device_fast(): call(back_a_kernel, [SM] + [VM] * 7, [AN] * 2 + [VM] * 2, [shape_of((2, 2...  11.4 us
  transfers between devices with their start and end apart: 68, of which 26 were waited for; matrix products, arithmetic and copies ran while one was open for 2% of the time, Pallas kernels for 20%

profile of v3, /device:TPU:0, one launch (start us, length us, event | category | flops | bytes accessed | tf_op | source)
XLA Modules:
  0.0 245.3 jit_solution(15040587972562014474)
XLA Ops:
  2.6 3.2 %shard_map.186 = (bf16[200,768]{1,0:T(8,128)(2,1)}, bf16[56,1536]{1,0:T(8,128)(2,1)}, bf16[192,768]{1,0:T(8,128)(2,1)}) custom-call(s32[4]{0:T(128)} %pad_add_fusion.1.coords, bf16[1,192,768]{2,1,0:T(8,128)(2,1)} %tokens.1, s32[1,192]{1,0:T(1,128)} %segs.1, bf16[96,2304]{1,0:T(8,128)(2,1)} %own.3, bf16[96,768]{1,0:T(8,128)(2,1)} %own_o.1, ...), custom_call_target="tpu_custom_call" | custom-call | bytes 200000 | tf_op jit(solution)/shard_map/pallas_call | solution.py:948
  5.9 3.1 %collective-permute-start = (bf16[56,1536]{1,0:T(8,128)(2,1)}, bf16[56,1536]{1,0:T(8,128)(2,1)S(1)}, u32[]{:S(2)}, u32[]{:S(2)}) collective-permute-start(bf16[56,1536]{1,0:T(8,128)(2,1)} %get-tuple-element.102.first), channel_id=1, source_target_pairs={{0,2},{1,3},{2,4},{3,5},{4,6},{5,7},{6,0},{7,1},{8,10},{9,11},{10,... | collective-permute-start | bytes 516104 | tf_op jit(solution)/shard_map/ppermute | solution.py:919
  21.4 4.9 %collective-permute-done.2 = bf16[56,1536]{1,0:T(8,128)(2,1)S(1)} collective-permute-done((bf16[56,1536]{1,0:T(8,128)(2,1)S(1)}, bf16[56,1536]{1,0:T(8,128)(2,1)S(1)}, u32[]{:S(2)}, u32[]{:S(2)}) %collective-permute-start.2) | collective-permute-done | bytes 172064 | tf_op jit(solution)/shard_map/ppermute | solution.py:919
  30.6 8.0 %collective-permute-done.12 = bf16[168,1536]{1,0:T(8,128)(2,1)S(1)} collective-permute-done((bf16[168,1536]{1,0:T(8,128)(2,1)S(1)}, bf16[168,1536]{1,0:T(8,128)(2,1)S(1)}, u32[]{:S(2)}, u32[]{:S(2)}) %collective-permute-start.12) | collective-permute-done | bytes 516128 | tf_op jit(solution)/shard_map/ppermute | solution.py:903
  38.6 5.1 %collective-permute-done.4.z1 = bf16[192,768]{1,0:T(8,128)(2,1)S(1)} collective-permute-done((bf16[192,768]{1,0:T(8,128)(2,1)}, bf16[192,768]{1,0:T(8,128)(2,1)S(1)}, u32[]{:S(2)}, u32[]{:S(2)}) %collective-permute-start.4) | collective-permute-done | bytes 294944 | tf_op jit(solution)/shard_map/ppermute | solution.py:919
  47.8 5.2 %collective-permute-done.5.x4 = bf16[200,768]{1,0:T(8,128)(2,1)S(1)} collective-permute-done((bf16[200,768]{1,0:T(8,128)(2,1)S(1)}, bf16[200,768]{1,0:T(8,128)(2,1)S(1)}, u32[]{:S(2)}, u32[]{:S(2)}) %collective-permute-start.5) | collective-permute-done | bytes 307232 | tf_op jit(solution)/shard_map/ppermute | solution.py:919
  53.1 3.0 %collective-permute-done.8 = bf16[168,1536]{1,0:T(8,128)(2,1)S(1)} collective-permute-done((bf16[168,1536]{1,0:T(8,128)(2,1)S(1)}, bf16[168,1536]{1,0:T(8,128)(2,1)S(1)}, u32[]{:S(2)}, u32[]{:S(2)}) %collective-permute-start.8) | collective-permute-done | bytes 516128 | tf_op jit(solution)/shard_map/ppermute | solution.py:915
  58.9 3.5 %collective-permute-start.22 = (bf16[192,768]{1,0:T(8,128)(2,1)S(1)}, bf16[192,768]{1,0:T(8,128)(2,1)S(1)}, u32[]{:S(2)}, u32[]{:S(2)}) collective-permute-start(bf16[192,768]{1,0:T(8,128)(2,1)S(1)} %copy-done.10), channel_id=1, source_target_pairs={{0,6},{1,7},{2,0},{3,1},{4,2},{5,3},{6,4},{7,5},{8,14},{9,15},{10,... | collective-permute-start | bytes 884744 | tf_op jit(solution)/shard_map/ppermute | solution.py:919
  62.5 3.8 %collective-permute-done.13 = bf16[168,1536]{1,0:T(8,128)(2,1)S(1)} collective-permute-done((bf16[168,1536]{1,0:T(8,128)(2,1)S(1)}, bf16[168,1536]{1,0:T(8,128)(2,1)S(1)}, u32[]{:S(2)}, u32[]{:S(2)}) %collective-permute-start.13) | collective-permute-done | bytes 516128 | tf_op jit(solution)/shard_map/ppermute | solution.py:903
  66.3 2.4 collective-permute-done.22.z3
  68.7 4.5 %collective-permute-done.9 = bf16[2,200,768]{2,1,0:T(8,128)(2,1)S(1)} collective-permute-done((bf16[2,200,768]{2,1,0:T(8,128)(2,1)S(1)}, bf16[2,200,768]{2,1,0:T(8,128)(2,1)S(1)}, u32[]{:S(2)}, u32[]{:S(2)}) %collective-permute-start.9) | collective-permute-done | bytes 614432 | tf_op jit(solution)/shard_map/ppermute | solution.py:915
  75.1 14.6 %shard_map.187 = (bf16[192,768]{1,0:T(8,128)(2,1)S(1)}, bf16[960,1536]{1,0:T(8,128)(2,1)S(1)}, bf16[960,768]{1,0:T(8,128)(2,1)S(1)}, bf16[192,768]{1,0:T(8,128)(...) custom-call(s32[4]{0:T(128)S(1)} %copy-done.14, ...), custom_call_target="tpu_custom_call" | custom-call | flops 350000000 | bytes 600000 | tf_op jit(solution)/shard_map/pallas_call | solution.py:1008
  92.4 5.3 %collective-permute-done.27.h_x = bf16[192,768]{1,0:T(8,128)(2,1)S(1)} collective-permute-done((bf16[192,768]{1,0:T(8,128)(2,1)S(1)}, bf16[192,768]{1,0:T(8,128)(2,1)S(1)}, u32[]{:S(2)}, u32[]{:S(2)}) %collective-permute-start.27) | collective-permute-done | bytes 294944 | tf_op jit(solution)/shard_map/ppermute | solution.py:903
  97.7 3.1 %collective-permute-done.25.y2 = bf16[192,768]{1,0:T(8,128)(2,1)S(1)} collective-permute-done((bf16[192,768]{1,0:T(8,128)(2,1)S(1)}, bf16[192,768]{1,0:T(8,128)(2,1)S(1)}, u32[]{:S(2)}, u32[]{:S(2)}) %collective-permute-start.25) | collective-permute-done | bytes 294944 | tf_op jit(solution)/shard_map/ppermute | solution.py:915
  100.7 7.0 %shard_map.188 = (bf16[384,768]{1,0:T(8,128)(2,1)S(1)}, bf16[384,768]{1,0:T(8,128)(2,1)S(1)}, bf16[384,768]{1,0:T(8,128)(2,1)S(1)}, bf16[384,768]{1,0:T(8,128)(2...) custom-call(s32[4]{0:T(128)S(1)} %copy-done.14, ...), custom_call_target="tpu_custom_call" | custom-call | flops 150000000 | bytes 300000 | tf_op jit(solution)/shard_map/pallas_call | solution.py:1043
  107.8 4.6 %shard_map.189 = (bf16[768,768]{1,0:T(8,128)(2,1)S(1)}, bf16[768,768]{1,0:T(8,128)(2,1)S(1)}, bf16[768,768]{1,0:T(8,128)(2,1)S(1)}, bf16[768,768]{1,0:T(8,128)(2...) custom-call(bf16[192,768]{1,0:T(8,128)(2,1)S(1)} %collective-permute-done.27.h_x, ...), custom_call_target="tpu_custom_call" | custom-call | flops 150000000 | bytes 300000 | tf_op jit(solution)/shard_map/pallas_call | solution.py:1054
  115.2 6.4 %shard_map.191 = (bf16[2,4,96,768]{3,2,1,0:T(8,128)(2,1)S(1)}, bf16[2,4,96,768]{3,2,1,0:T(8,128)(2,1)S(1)}, f32[1,768]{1,0:T(1,128)S(1)}) custom-call(s32[4]{0:T(128)S(1)} %copy-done.14, bf16[768,768]{1,0:T(8,128)(2,1)S(1)} %get-tuple-element.147.hs, bf16[768,768]{1,0:T(8,128)(2,1)S(1)} %get-tuple-element.148.dys, ...), custom_call_target="tpu_custom_call" | custom-call | flops 150000000 | bytes 300000 | tf_op jit(solution)/shard_map/pallas_call | solution.py:1065
  125.0 11.4 %shard_map.192 = (bf16[2,2,4,24,1920]{4,3,2,1,0:T(8,128)(2,1)S(1)}, bf16[2,2,4,24,1920]{4,3,2,1,0:T(8,128)(2,1)S(1)}, bf16[192,384]{1,0:T(8,128)(2,1)S(1)}, bf16[960,768]{1,0:T(8,128)(2,1)S(1)}) custom-call(s32[4]{0:T(128)S(1)} %copy-done.14, s32[1,384]{1,0:T(1,128)S(1)} %get-tuple-element.139.start_in, bf16[192,768]{1,0:T(8,128)(2,1)S(1)} %get-tuple-element.140.q_in, ...), custom_call_target="tpu_custom_call" | custom-call | flops 250000000 | bytes 500000 | tf_op jit(solution)/shard_map/pallas_call | solution.py:1093
  137.2 15.2 %collective-permute-done.33 = bf16[4,96,768]{2,1,0:T(8,128)(2,1)S(1)} collective-permute-done((bf16[4,96,768]{2,1,0:T(8,128)(2,1)S(1)}, bf16[4,96,768]{2,1,0:T(8,128)(2,1)S(1)}, u32[]{:S(2)}, u32[]{:S(2)}) %collective-permute-start.33) | collective-permute-done | bytes 589856 | tf_op jit(solution)/shard_map/ppermute | solution.py:915
  153.5 3.9 %collective-permute-start.57 = (bf16[96,768]{1,0:T(8,128)(2,1)S(1)}, bf16[96,768]{1,0:T(8,128)(2,1)S(1)}, u32[]{:S(2)}, u32[]{:S(2)}) collective-permute-start(bf16[96,768]{1,0:T(8,128)(2,1)S(1)} %get-tuple-element.202), channel_id=1, source_target_pairs={{0,4},{1,5},{2,6},{3,7},{4,0},{5,1},{6,2},{7,3},{8,12},{9,13},{10,... | collective-permute-start | bytes 442376 | tf_op jit(solution)/shard_map/ppermute | solution.py:919
  157.4 2.6 %collective-permute-start.58 = (bf16[96,768]{1,0:T(8,128)(2,1)S(1)}, bf16[96,768]{1,0:T(8,128)(2,1)S(1)}, u32[]{:S(2)}, u32[]{:S(2)}) collective-permute-start(bf16[96,768]{1,0:T(8,128)(2,1)S(1)} %get-tuple-element.201), channel_id=1, source_target_pairs={{0,6},{1,7},{2,0},{3,1},{4,2},{5,3},{6,4},{7,5},{8,14},{9,15},{10,... | collective-permute-start | bytes 442376 | tf_op jit(solution)/shard_map/ppermute | solution.py:919
  160.1 11.4 %shard_map.193 = (bf16[192,384]{1,0:T(8,128)(2,1)S(1)}, bf16[960,768]{1,0:T(8,128)(2,1)S(1)}, f32[192,768]{1,0:T(8,128)S(1)}, bf16[2,192,768]{2,1,0:T(8,128)(2,1...) custom-call(s32[4]{0:T(128)S(1)} %copy-done.14, s32[1,384]{1,0:T(1,128)S(1)} %get-tuple-element.139.start_in, ...), custom_call_target="tpu_custom_call" | custom-call | flops 300000000 | bytes 500000 | tf_op jit(solution)/shard_map/pallas_call | solution.py:1123
  177.9 5.9 %shard_map.195 = (bf16[2,2,4,32,1152]{4,3,2,1,0:T(8,128)(2,1)S(1)}, bf16[2,2,4,32,1152]{4,3,2,1,0:T(8,128)(2,1)S(1)}) custom-call(s32[4]{0:T(128)S(1)} %copy-done.14, bf16[960,768]{1,0:T(8,128)(2,1)S(1)} %get-tuple-element.152.h_in, bf16[192,384]{1,0:T(8,128)(2,1)S(1)} %get-tuple-element.171.dq, bf16[960,768]{1,0:T(8,128)(2,1)S(1)} %get-tuple-element.172.dkv, ...), custom_call_target="tpu_custom_call" | custom-call | flops 150000000 | bytes 300000 | tf_op jit(solution)/shard_map/pallas_call | solution.py:1146
  185.7 3.2 %collective-permute-done.35 = bf16[2,192,768]{2,1,0:T(8,128)(2,1)S(1)} collective-permute-done((bf16[2,192,768]{2,1,0:T(8,128)(2,1)S(1)}, bf16[2,192,768]{2,1,0:T(8,128)(2,1)S(1)}, u32[]{:S(2)}, u32[]{:S(2)}) %collective-permute-start.35) | collective-permute-done | bytes 589856 | tf_op jit(solution)/shard_map/ppermute | solution.py:915
  189.9 6.6 %collective-permute-done.39 = bf16[2,4,24,1920]{3,2,1,0:T(8,128)(2,1)S(1)} collective-permute-done((bf16[2,4,24,1920]{3,2,1,0:T(8,128)(2,1)S(1)}, bf16[2,4,24,1920]{3,2,1,0:T(8,128)(2,1)S(1)}, u32[]{:S(2)}, u32[]{:S(2)}) %collective-permute-start.39) | collective-permute-done | bytes 737312 | tf_op jit(solution)/shard_map/ppermute | solution.py:903
  197.5 6.7 %collective-permute-done.40 = bf16[4,24,1920]{2,1,0:T(8,128)(2,1)S(1)} collective-permute-done((bf16[4,24,1920]{2,1,0:T(8,128)(2,1)S(1)}, bf16[4,24,1920]{2,1,0:T(8,128)(2,1)S(1)}, u32[]{:S(2)}, u32[]{:S(2)}) %collective-permute-start.40) | collective-permute-done | bytes 368672 | tf_op jit(solution)/shard_map/ppermute | solution.py:915
  206.5 2.8 %collective-permute-start.43 = (bf16[24,1920]{1,0:T(8,128)(2,1)S(1)}, bf16[24,1920]{1,0:T(8,128)(2,1)S(1)}, u32[]{:S(2)}, u32[]{:S(2)}) collective-permute-start(bf16[24,1920]{1,0:T(8,128)(2,1)S(1)} %get-tuple-element.192), channel_id=1, source_target_pairs={{0,6},{1,7},{2,0},{3,1},{4,2},{5,3},{6,4},{7,5},{8,14},{9,15},{10,... | collective-permute-start | bytes 276488 | tf_op jit(solution)/shard_map/ppermute | solution.py:919
  213.2 2.9 %collective-permute-start.37 = (bf16[192,768]{1,0:T(8,128)(2,1)S(1)}, bf16[192,768]{1,0:T(8,128)(2,1)S(1)}, u32[]{:S(2)}, u32[]{:S(2)}) collective-permute-start(bf16[192,768]{1,0:T(8,128)(2,1)S(1)} %get-tuple-element.208), channel_id=1, source_target_pairs={{0,6},{1,7},{2,0},{3,1},{4,2},{5,3},{6,4},{7,5},{8,14},{9,15},{10,... | collective-permute-start | bytes 884744 | tf_op jit(solution)/shard_map/ppermute | solution.py:919
  216.1 5.9 %collective-permute-done.49 = bf16[4,32,1152]{2,1,0:T(8,128)(2,1)S(1)} collective-permute-done((bf16[4,32,1152]{2,1,0:T(8,128)(2,1)S(1)}, bf16[4,32,1152]{2,1,0:T(8,128)(2,1)S(1)}, u32[]{:S(2)}, u32[]{:S(2)}) %collective-permute-start.49) | collective-permute-done | bytes 294944 | tf_op jit(solution)/shard_map/ppermute | solution.py:915
  222.8 4.4 %collective-permute-done.65.dx = bf16[96,768]{1,0:T(8,128)(2,1)S(1)} collective-permute-done((bf16[96,768]{1,0:T(8,128)(2,1)S(1)}, bf16[96,768]{1,0:T(8,128)(2,1)S(1)}, u32[]{:S(2)}, u32[]{:S(2)}) %collective-permute-start.65) | collective-permute-done | bytes 147488 | tf_op jit(solution)/shard_map/ppermute | solution.py:903
  234.2 2.5 %shard_map.197 = (f32[96,3072]{1,0:T(8,128)}, f32[384,768]{1,0:T(8,128)}) custom-call(s32[4]{0:T(128)S(1)} %copy-done.14, bf16[96,768]{1,0:T(8,128)(2,1)S(1)} %fusion.31.u0, bf16[96,768]{1,0:T(8,128)(2,1)S(1)} %collective-permute-done.59.ux, bf16[96,768]{1,0:T(8,128)(2,1)S(1)} %collective-permute-done.60.uc, ...), custom_call_target="tpu_custom_call" | custom-call | bytes 200000 | tf_op jit(solution)/shard_map/pallas_call | solution.py:1197
  239.9 2.5 %collective-permute-done.53.bx = bf16[32,1152]{1,0:T(8,128)(2,1)S(1)} collective-permute-done((bf16[32,1152]{1,0:T(8,128)(2,1)S(1)}, bf16[32,1152]{1,0:T(8,128)(2,1)S(1)}, u32[]{:S(2)}, u32[]{:S(2)}) %collective-permute-start.53) | collective-permute-done | bytes 73760 | tf_op jit(solution)/shard_map/ppermute | solution.py:903
  (181 shorter events, 68.3 us)
Async XLA Ops:
  5.9 10.6 %collective-permute-start = (bf16[56,1536]{1,0:T(8,128)(2,1)}, bf16[56,1536]{1,0:T(8,128)(2,1)S(1)}, u32[]{:S(2)}, u32[]{:S(2)}) collective-permute-start(bf16[56,1536]{1,0:T(8,128)(2,1)} %get-tuple-element.102.first), channel_id=1, source_target_pairs={{0,2},{1,3},{2,4},{3,5},{4,6},{5,7},{6,0},{7,1},{8,10},{9,11},{10,... | collective-permute-start | bytes 516104 | tf_op jit(solution)/shard_map/ppermute | solution.py:919
  26.3 12.3 %collective-permute-start.12 = (bf16[168,1536]{1,0:T(8,128)(2,1)S(1)}, bf16[168,1536]{1,0:T(8,128)(2,1)S(1)}, u32[]{:S(2)}, u32[]{:S(2)}) collective-permute-start(bf16[168,1536]{1,0:T(8,128)(2,1)S(1)} %constant_dynamic-update-slice_fusion), channel_id=1, source_target_pairs={{0,16},{8,24},{16,0},{24,8},{1,17},{9,25},{17,1},{25,9},{2,18},{10... | collective-permute-start | bytes 1548296 | tf_op jit(solution)/shard_map/ppermute | solution.py:903
  27.9 16.5 %collective-permute-start.3 = (bf16[200,768]{1,0:T(8,128)(2,1)}, bf16[200,768]{1,0:T(8,128)(2,1)S(1)}, u32[]{:S(2)}, u32[]{:S(2)}) collective-permute-start(bf16[200,768]{1,0:T(8,128)(2,1)} %get-tuple-element.104.xo), channel_id=1, source_target_pairs={{0,2},{1,3},{2,4},{3,5},{4,6},{5,7},{6,0},{7,1},{8,10},{9,11},{10,... | collective-permute-start | bytes 921608 | tf_op jit(solution)/shard_map/ppermute | solution.py:919
  27.9 15.8 %collective-permute-start.4 = (bf16[192,768]{1,0:T(8,128)(2,1)}, bf16[192,768]{1,0:T(8,128)(2,1)S(1)}, u32[]{:S(2)}, u32[]{:S(2)}) collective-permute-start(bf16[192,768]{1,0:T(8,128)(2,1)} %get-tuple-element.124.own), channel_id=1, source_target_pairs={{0,2},{1,3},{2,4},{3,5},{4,6},{5,7},{6,0},{7,1},{8,10},{9,11},{10,... | collective-permute-start | bytes 884744 | tf_op jit(solution)/shard_map/ppermute | solution.py:919
  29.1 15.3 %collective-permute-start.7 = (bf16[192,768]{1,0:T(8,128)(2,1)}, bf16[192,768]{1,0:T(8,128)(2,1)S(1)}, u32[]{:S(2)}, u32[]{:S(2)}) collective-permute-start(bf16[192,768]{1,0:T(8,128)(2,1)} %get-tuple-element.124.own), channel_id=1, source_target_pairs={{0,1},{1,0},{2,3},{3,2},{4,5},{5,4},{6,7},{7,6},{8,9},{9,8},{10,11... | collective-permute-start | bytes 884744 | tf_op jit(solution)/shard_map/ppermute | solution.py:915
  45.1 11.0 %collective-permute-start.8 = (bf16[168,1536]{1,0:T(8,128)(2,1)S(1)}, bf16[168,1536]{1,0:T(8,128)(2,1)S(1)}, u32[]{:S(2)}, u32[]{:S(2)}) collective-permute-start(bf16[168,1536]{1,0:T(8,128)(2,1)S(1)} %constant_dynamic-update-slice_fusion), channel_id=1, source_target_pairs={{0,1},{1,0},{2,3},{3,2},{4,5},{5,4},{6,7},{7,6},{8,9},{9,8},{10,11... | collective-permute-start | bytes 1548296 | tf_op jit(solution)/shard_map/ppermute | solution.py:915
  56.1 10.1 %collective-permute-start.13 = (bf16[168,1536]{1,0:T(8,128)(2,1)S(1)}, bf16[168,1536]{1,0:T(8,128)(2,1)S(1)}, u32[]{:S(2)}, u32[]{:S(2)}) collective-permute-start(bf16[168,1536]{1,0:T(8,128)(2,1)S(1)} %collective-permute-done.8), channel_id=1, source_target_pairs={{0,16},{8,24},{16,0},{24,8},{1,17},{9,25},{17,1},{25,9},{2,18},{10... | collective-permute-start | bytes 1548296 | tf_op jit(solution)/shard_map/ppermute | solution.py:903
  57.3 15.9 %collective-permute-start.9 = (bf16[2,200,768]{2,1,0:T(8,128)(2,1)S(1)}, bf16[2,200,768]{2,1,0:T(8,128)(2,1)S(1)}, u32[]{:S(2)}, u32[]{:S(2)}) collective-permute-start(bf16[2,200,768]{2,1,0:T(8,128)(2,1)S(1)} %pad_maximum_fusion), channel_id=1, source_target_pairs={{0,1},{1,0},{2,3},{3,2},{4,5},{5,4},{6,7},{7,6},{8,9},{9,8},{10,11... | collective-permute-start | bytes 1843208 | tf_op jit(solution)/shard_map/ppermute | solution.py:915
  58.9 9.8 %collective-permute-start.22 = (bf16[192,768]{1,0:T(8,128)(2,1)S(1)}, bf16[192,768]{1,0:T(8,128)(2,1)S(1)}, u32[]{:S(2)}, u32[]{:S(2)}) collective-permute-start(bf16[192,768]{1,0:T(8,128)(2,1)S(1)} %copy-done.10), channel_id=1, source_target_pairs={{0,6},{1,7},{2,0},{3,1},{4,2},{5,3},{6,4},{7,5},{8,14},{9,15},{10,... | collective-permute-start | bytes 884744 | tf_op jit(solution)/shard_map/ppermute | solution.py:919
  73.2 18.1 %collective-permute-start.24 = (bf16[384,768]{1,0:T(8,128)(2,1)S(1)}, bf16[384,768]{1,0:T(8,128)(2,1)S(1)}, u32[]{:S(2)}, u32[]{:S(2)}) collective-permute-start(bf16[384,768]{1,0:T(8,128)(2,1)S(1)} %pad_maximum_fusion.1), channel_id=1, source_target_pairs={{0,1},{1,0},{2,3},{3,2},{4,5},{5,4},{6,7},{7,6},{8,9},{9,8},{10,11... | collective-permute-start | bytes 1769480 | tf_op jit(solution)/shard_map/ppermute | solution.py:915
  74.8 16.5 %collective-permute-start.23 = (bf16[192,768]{1,0:T(8,128)(2,1)S(1)}, bf16[192,768]{1,0:T(8,128)(2,1)S(1)}, u32[]{:S(2)}, u32[]{:S(2)}) collective-permute-start(bf16[192,768]{1,0:T(8,128)(2,1)S(1)} %copy-done.4), channel_id=1, source_target_pairs={{0,2},{1,3},{2,4},{3,5},{4,6},{5,7},{6,0},{7,1},{8,10},{9,11},{10,... | collective-permute-start | bytes 884744 | tf_op jit(solution)/shard_map/ppermute | solution.py:919
  92.0 15.7 %collective-permute-start.29 = (bf16[192,768]{1,0:T(8,128)(2,1)}, bf16[192,768]{1,0:T(8,128)(2,1)S(1)}, u32[]{:S(2)}, u32[]{:S(2)}) collective-permute-start(bf16[192,768]{1,0:T(8,128)(2,1)} %collective-permute-done.10.dy_x), channel_id=1, source_target_pairs={{0,8},{8,0},{16,24},{24,16},{1,9},{9,1},{17,25},{25,17},{2,10},{10... | collective-permute-start | bytes 884744 | tf_op jit(solution)/shard_map/ppermute | solution.py:903
  97.7 10.1 %collective-permute-start.28 = (bf16[192,768]{1,0:T(8,128)(2,1)S(1)}, bf16[192,768]{1,0:T(8,128)(2,1)S(1)}, u32[]{:S(2)}, u32[]{:S(2)}) collective-permute-start(bf16[192,768]{1,0:T(8,128)(2,1)S(1)} %collective-permute-done.27.h_x), channel_id=1, source_target_pairs={{0,8},{8,0},{16,24},{24,16},{1,9},{9,1},{17,25},{25,17},{2,10},{10... | collective-permute-start | bytes 884744 | tf_op jit(solution)/shard_map/ppermute | solution.py:903
  136.5 40.6 %collective-permute-start.38 = (bf16[2,2,4,24,1920]{4,3,2,1,0:T(8,128)(2,1)S(1)}, bf16[2,2,4,24,1920]{4,3,2,1,0:T(8,128)(2,1)S(1)}, u32[]{:S(2)}, u32[]{:S(2)}) collective-permute-start(bf16[2,2,4,24,1920]{4,3,2,1,0:T(8,128)(2,1)S(1)} %get-tuple-element.165), channel_id=1, source_target_pairs={{0,8},{8,0},{16,24},{24,16},{1,9},{9,1},{17,25},{25,17},{2,10},{10... | collective-permute-start | bytes 4423688 | tf_op jit(solution)/shard_map/ppermute | solution.py:903
  136.6 15.8 %collective-permute-start.33 = (bf16[4,96,768]{2,1,0:T(8,128)(2,1)S(1)}, bf16[4,96,768]{2,1,0:T(8,128)(2,1)S(1)}, u32[]{:S(2)}, u32[]{:S(2)}) collective-permute-start(bf16[4,96,768]{2,1,0:T(8,128)(2,1)S(1)} %slice_bitcast_fusion), channel_id=1, source_target_pairs={{0,1},{1,0},{2,3},{3,2},{4,5},{5,4},{6,7},{7,6},{8,9},{9,8},{10,11... | collective-permute-start | bytes 1769480 | tf_op jit(solution)/shard_map/ppermute | solution.py:915
  152.4 19.2 %collective-permute-start.34 = (bf16[4,96,768]{2,1,0:T(8,128)(2,1)S(1)}, bf16[4,96,768]{2,1,0:T(8,128)(2,1)S(1)}, u32[]{:S(2)}, u32[]{:S(2)}) collective-permute-start(bf16[4,96,768]{2,1,0:T(8,128)(2,1)S(1)} %slice_bitcast_fusion.1), channel_id=1, source_target_pairs={{0,1},{1,0},{2,3},{3,2},{4,5},{5,4},{6,7},{7,6},{8,9},{9,8},{10,11... | collective-permute-start | bytes 1769480 | tf_op jit(solution)/shard_map/ppermute | solution.py:915
  153.0 18.5 %collective-permute-start.56 = (bf16[96,768]{1,0:T(8,128)(2,1)S(1)}, bf16[96,768]{1,0:T(8,128)(2,1)S(1)}, u32[]{:S(2)}, u32[]{:S(2)}) collective-permute-start(bf16[96,768]{1,0:T(8,128)(2,1)S(1)} %get-tuple-element.203), channel_id=1, source_target_pairs={{0,2},{1,3},{2,4},{3,5},{4,6},{5,7},{6,0},{7,1},{8,10},{9,11},{10,... | collective-permute-start | bytes 442376 | tf_op jit(solution)/shard_map/ppermute | solution.py:919
  153.5 18.0 %collective-permute-start.57 = (bf16[96,768]{1,0:T(8,128)(2,1)S(1)}, bf16[96,768]{1,0:T(8,128)(2,1)S(1)}, u32[]{:S(2)}, u32[]{:S(2)}) collective-permute-start(bf16[96,768]{1,0:T(8,128)(2,1)S(1)} %get-tuple-element.202), channel_id=1, source_target_pairs={{0,4},{1,5},{2,6},{3,7},{4,0},{5,1},{6,2},{7,3},{8,12},{9,13},{10,... | collective-permute-start | bytes 442376 | tf_op jit(solution)/shard_map/ppermute | solution.py:919
  157.4 14.1 %collective-permute-start.58 = (bf16[96,768]{1,0:T(8,128)(2,1)S(1)}, bf16[96,768]{1,0:T(8,128)(2,1)S(1)}, u32[]{:S(2)}, u32[]{:S(2)}) collective-permute-start(bf16[96,768]{1,0:T(8,128)(2,1)S(1)} %get-tuple-element.201), channel_id=1, source_target_pairs={{0,6},{1,7},{2,0},{3,1},{4,2},{5,3},{6,4},{7,5},{8,14},{9,15},{10,... | collective-permute-start | bytes 442376 | tf_op jit(solution)/shard_map/ppermute | solution.py:919
  171.7 12.1 %collective-permute-start.62 = (bf16[96,768]{1,0:T(8,128)(2,1)S(1)}, bf16[96,768]{1,0:T(8,128)(2,1)S(1)}, u32[]{:S(2)}, u32[]{:S(2)}) collective-permute-start(bf16[96,768]{1,0:T(8,128)(2,1)S(1)} %get-tuple-element.200), channel_id=1, source_target_pairs={{0,2},{1,3},{2,4},{3,5},{4,6},{5,7},{6,0},{7,1},{8,10},{9,11},{10,... | collective-permute-start | bytes 442376 | tf_op jit(solution)/shard_map/ppermute | solution.py:919
  171.8 12.6 %collective-permute-start.63 = (bf16[96,768]{1,0:T(8,128)(2,1)S(1)}, bf16[96,768]{1,0:T(8,128)(2,1)S(1)}, u32[]{:S(2)}, u32[]{:S(2)}) collective-permute-start(bf16[96,768]{1,0:T(8,128)(2,1)S(1)} %get-tuple-element.199), channel_id=1, source_target_pairs={{0,4},{1,5},{2,6},{3,7},{4,0},{5,1},{6,2},{7,3},{8,12},{9,13},{10,... | collective-permute-start | bytes 442376 | tf_op jit(solution)/shard_map/ppermute | solution.py:919
  173.5 12.1 %collective-permute-start.64 = (bf16[96,768]{1,0:T(8,128)(2,1)S(1)}, bf16[96,768]{1,0:T(8,128)(2,1)S(1)}, u32[]{:S(2)}, u32[]{:S(2)}) collective-permute-start(bf16[96,768]{1,0:T(8,128)(2,1)S(1)} %get-tuple-element.198), channel_id=1, source_target_pairs={{0,6},{1,7},{2,0},{3,1},{4,2},{5,3},{6,4},{7,5},{8,14},{9,15},{10,... | collective-permute-start | bytes 442376 | tf_op jit(solution)/shard_map/ppermute | solution.py:919
  175.6 13.3 %collective-permute-start.35 = (bf16[2,192,768]{2,1,0:T(8,128)(2,1)S(1)}, bf16[2,192,768]{2,1,0:T(8,128)(2,1)S(1)}, u32[]{:S(2)}, u32[]{:S(2)}) collective-permute-start(bf16[2,192,768]{2,1,0:T(8,128)(2,1)S(1)} %get-tuple-element.161), channel_id=1, source_target_pairs={{0,1},{1,0},{2,3},{3,2},{4,5},{5,4},{6,7},{7,6},{8,9},{9,8},{10,11... | collective-permute-start | bytes 1769480 | tf_op jit(solution)/shard_map/ppermute | solution.py:915
  177.3 19.2 %collective-permute-start.39 = (bf16[2,4,24,1920]{3,2,1,0:T(8,128)(2,1)S(1)}, bf16[2,4,24,1920]{3,2,1,0:T(8,128)(2,1)S(1)}, u32[]{:S(2)}, u32[]{:S(2)}) collective-permute-start(bf16[2,4,24,1920]{3,2,1,0:T(8,128)(2,1)S(1)} %fusion), channel_id=1, source_target_pairs={{0,16},{8,24},{16,0},{24,8},{1,17},{9,25},{17,1},{25,9},{2,18},{10... | collective-permute-start | bytes 2211848 | tf_op jit(solution)/shard_map/ppermute | solution.py:903
  183.8 12.9 %collective-permute-start.47 = (bf16[2,2,4,32,1152]{4,3,2,1,0:T(8,128)(2,1)S(1)}, bf16[2,2,4,32,1152]{4,3,2,1,0:T(8,128)(2,1)S(1)}, u32[]{:S(2)}, u32[]{:S(2)}) collective-permute-start(bf16[2,2,4,32,1152]{4,3,2,1,0:T(8,128)(2,1)S(1)} %get-tuple-element.175), channel_id=1, source_target_pairs={{0,8},{8,0},{16,24},{24,16},{1,9},{9,1},{17,25},{25,17},{2,10},{10... | collective-permute-start | bytes 3538952 | tf_op jit(solution)/shard_map/ppermute | solution.py:903
  184.4 25.1 %collective-permute-start.59 = (bf16[96,768]{1,0:T(8,128)(2,1)S(1)}, bf16[96,768]{1,0:T(8,128)(2,1)S(1)}, u32[]{:S(2)}, u32[]{:S(2)}) collective-permute-start(bf16[96,768]{1,0:T(8,128)(2,1)S(1)} %fusion.31.u0), channel_id=1, source_target_pairs={{0,16},{8,24},{16,0},{24,8},{1,17},{9,25},{17,1},{25,9},{2,18},{10... | collective-permute-start | bytes 442376 | tf_op jit(solution)/shard_map/ppermute | solution.py:903
  188.9 17.6 %collective-permute-start.36 = (bf16[192,768]{1,0:T(8,128)(2,1)S(1)}, bf16[192,768]{1,0:T(8,128)(2,1)S(1)}, u32[]{:S(2)}, u32[]{:S(2)}) collective-permute-start(bf16[192,768]{1,0:T(8,128)(2,1)S(1)} %fusion.17), channel_id=1, source_target_pairs={{0,6},{1,7},{2,0},{3,1},{4,2},{5,3},{6,4},{7,5},{8,14},{9,15},{10,... | collective-permute-start | bytes 884744 | tf_op jit(solution)/shard_map/ppermute | solution.py:919
  196.9 16.0 %collective-permute-start.48 = (bf16[2,4,32,1152]{3,2,1,0:T(8,128)(2,1)S(1)}, bf16[2,4,32,1152]{3,2,1,0:T(8,128)(2,1)S(1)}, u32[]{:S(2)}, u32[]{:S(2)}) collective-permute-start(bf16[2,4,32,1152]{3,2,1,0:T(8,128)(2,1)S(1)} %fusion.10), channel_id=1, source_target_pairs={{0,16},{8,24},{16,0},{24,8},{1,17},{9,25},{17,1},{25,9},{2,18},{10... | collective-permute-start | bytes 1769480 | tf_op jit(solution)/shard_map/ppermute | solution.py:903
  210.9 16.9 %collective-permute-start.32 = (bf16[192,768]{1,0:T(8,128)(2,1)S(1)}, bf16[192,768]{1,0:T(8,128)(2,1)S(1)}, u32[]{:S(2)}, u32[]{:S(2)}) collective-permute-start(bf16[192,768]{1,0:T(8,128)(2,1)S(1)} %get-tuple-element.138), channel_id=1, source_target_pairs={{0,16},{8,24},{16,0},{24,8},{1,17},{9,25},{17,1},{25,9},{2,18},{10... | collective-permute-start | bytes 884744 | tf_op jit(solution)/shard_map/ppermute | solution.py:903
  212.4 14.8 %collective-permute-start.61 = (bf16[96,768]{1,0:T(8,128)(2,1)S(1)}, bf16[96,768]{1,0:T(8,128)(2,1)S(1)}, u32[]{:S(2)}, u32[]{:S(2)}) collective-permute-start(bf16[96,768]{1,0:T(8,128)(2,1)S(1)} %collective-permute-done.59.ux), channel_id=1, source_target_pairs={{0,8},{8,0},{16,24},{24,16},{1,9},{9,1},{17,25},{25,17},{2,10},{10... | collective-permute-start | bytes 442376 | tf_op jit(solution)/shard_map/ppermute | solution.py:903
  212.4 17.2 %collective-permute-start.66 = (bf16[96,768]{1,0:T(8,128)(2,1)S(1)}, bf16[96,768]{1,0:T(8,128)(2,1)S(1)}, u32[]{:S(2)}, u32[]{:S(2)}) collective-permute-start(bf16[96,768]{1,0:T(8,128)(2,1)S(1)} %fusion.24.d0), channel_id=1, source_target_pairs={{0,8},{8,0},{16,24},{24,16},{1,9},{9,1},{17,25},{25,17},{2,10},{10... | collective-permute-start | bytes 442376 | tf_op jit(solution)/shard_map/ppermute | solution.py:903
  213.2 18.7 %collective-permute-start.37 = (bf16[192,768]{1,0:T(8,128)(2,1)S(1)}, bf16[192,768]{1,0:T(8,128)(2,1)S(1)}, u32[]{:S(2)}, u32[]{:S(2)}) collective-permute-start(bf16[192,768]{1,0:T(8,128)(2,1)S(1)} %get-tuple-element.208), channel_id=1, source_target_pairs={{0,6},{1,7},{2,0},{3,1},{4,2},{5,3},{6,4},{7,5},{8,14},{9,15},{10,... | collective-permute-start | bytes 884744 | tf_op jit(solution)/shard_map/ppermute | solution.py:919
  (52 other events, 529.4 us)

commit v4 on v3

--- a/solution.py
+++ b/solution.py
@@ -848,13 +848,13 @@
     grad_out[...] = dr[...] + norm_back(grad, hat, rate, vec_in[0:1, :])
 
 
-def finish_f_kernel(coords, u0, ux, uc, ucx, d0, dx, dc, dcx, up, down, held):
+def finish_f_kernel(coords, f0, fx, fc, fcx, up, down, held):
     x, c, _y, _z = place(coords)
-    rows = u0.shape[0]
-    for (xx, cc), u, d in zip(corners(x, c), (u0, ux, uc, ucx), (d0, dx, dc, dcx), strict=True):
+    rows = f0.shape[0] // 2
+    for (xx, cc), f in zip(corners(x, c), (f0, fx, fc, fcx), strict=True):
         p = 2 * xx + cc
-        held[p] = u[...]
-        down[pl.ds(pl.multiple_of(rows * p, 16), rows), :] = f32(d[...])
+        held[p] = f[pl.ds(0, rows), :]
+        down[pl.ds(pl.multiple_of(rows * p, 16), rows), :] = f32(f[pl.ds(rows, rows), :])
     for group in range(2):
         parts = [unpack96(f32(held[k, :, pl.ds(384 * group, 384)])) for k in range(4)]
         for shard in range(4):
@@ -891,12 +891,12 @@
         out_shape=out_shape,
         scratch_shapes=list(scratch),
         compiler_params=pltpu.CompilerParams(vmem_limit_bytes=vmem << 20),
-        cost_estimate=pl.CostEstimate(flops=flops // 20, bytes_accessed=moved // 20, transcendentals=0),
-    )
-
-
-def after(value, *done):
-    return lax.optimization_barrier((value,) + done)[0]
+        cost_estimate=pl.CostEstimate(flops=flops, bytes_accessed=moved, transcendentals=0),
+    )
+
+
+def fence(*values):
+    return lax.optimization_barrier(values)
 
 
 def swap_rep(value, bit):
@@ -970,31 +970,23 @@
         ln_gains, ln_biases, biases, up_projection_bias[None],
     )
 
-    q1, q3 = to_z(piece_q, 1), to_z(piece_q, 3)
-    q_y0 = to_y(piece_q)
-    dy_x = to_x(grad_y)
-    f_y0 = to_y(after(piece_f, q_y0))
-    q2 = to_z(after(q1, q3), 1)
-    q_xy0 = to_x(after(q_y0, dy_x))
-    x2 = to_z(after(own_tokens, q2), 1)
+    q1, q3, q_y0, dy_x = fence(to_z(piece_q, 1), to_z(piece_q, 3), to_y(piece_q), to_x(grad_y))
+    own_tokens, piece_f, q1, q_y0 = fence(own_tokens, piece_f, q1, q_y0, q3, dy_x)[:4]
+    q2, x2, q_xy0, f_y0 = fence(to_z(q1, 1), to_z(own_tokens, 1), to_x(q_y0), to_y(piece_f))
     q_z = join(q1, q2, q3)
-    q_y = to_y(after(q_z, f_y0))
-    q_xz = to_x(after(q_z, q_xy0))
-    f1 = to_z(after(piece_f, q2), 1)
-    x4 = to_z(after(x2, f1), 1)
+    q_z, x2 = fence(q_z, x2, q_xy0, f_y0)[:2]
+    q_y, q_xz, x4 = fence(to_y(q_z), to_x(q_z), to_z(x2, 1))
     near = jnp.where(y == 0, own_tokens, x2)
     far = jnp.where(y == 0, x2, x4)
-    crossed = to_y(after(jnp.stack([near, far]), q_y))
+    near_far, q_y, piece_f = fence(jnp.stack([near, far]), q_y, piece_f, q_xz)[:3]
+    crossed, q_xy, f1, f3 = fence(to_y(near_far), to_x(q_y), to_z(piece_f, 1), to_z(piece_f, 3))
     x1, x3 = crossed[0], crossed[1]
-    q_xy = to_x(after(q_y, q_xz))
-    f3 = to_z(after(piece_f, x4), 3)
-    f2 = to_z(after(f1, f3), 1)
-    q_cy0, q_cxy0 = to_core(after(q_y0, q_xz)), to_core(after(q_xy0, q_xz))
-    q_cz, q_cxz = to_core(after(q_z, q_cy0)), to_core(after(q_xz, q_cxy0))
-    q_cy = to_core(after(q_y, q_cz))
-    f_y13 = to_y(after(join(f1, f3), crossed))
-    q_cxy = to_core(after(q_xy, q_cy, q_cxz))
-    f_y2 = to_y(after(f2, f_y13))
+    q_z, q_y0, q_y, q_xz, q_xy0, q_xy = fence(q_z, q_y0, q_y, q_xz, q_xy0, q_xy, f1, f3, crossed)[:6]
+    q_cz, q_cy0, q_cy, q_cxz, q_cxy0, q_cxy = fence(
+        *(to_core(v) for v in (q_z, q_y0, q_y, q_xz, q_xy0, q_xy))
+    )
+    f_13, f_1, q_cz = fence(join(f1, f3), f1, q_cz, q_cy0, q_cy, q_cxz, q_cxy0, q_cxy)[:3]
+    f_y13, f2 = to_y(f_13), to_z(f_1, 1)
     dy_c, dy_xc = to_core(grad_y), to_core(dy_x)
 
     def pieces(value):
@@ -1005,7 +997,7 @@
         for v in (q_z, q_y0, q_y, q_xz, q_xy0, q_xy, q_cz, q_cy0, q_cy, q_cxz, q_cxy0, q_cxy)
     ]
     seg = jnp.concatenate([segment_ids, segment_ids], axis=1)
-    queries, kv, normed, attended, lse, start, vec, upb, w_out, residual, hidden_2 = call(
+    front = call(
         front_kernel,
         [SM] + [VM] * 6 + [AN] * 15,
         [VM] * 11,
@@ -1034,8 +1026,9 @@
     )(
         coords, seg, own_tokens, x1, x2, x3, x4, piece_q, query_key_value_weight, output_weight, *got_q,
     )
-    h_x = to_x(hidden_2)
-    h_c = to_core(hidden_2)
+    *front, f_y13, f2, dy_c, dy_xc = fence(*front, f_y13, f2, dy_c, dy_xc)
+    queries, kv, normed, attended, lse, start, vec, upb, w_out, residual, hidden_2 = front
+    h_x, h_c, f_y2 = fence(to_x(hidden_2), to_core(hidden_2), to_y(f2))
     act = shape_of((2 * tok, width), bf)
     acts = shape_of((4 * tok, width), bf)
     feed_shapes = [shape_of((2, tok, width), fl), shape_of((2, tok, width), bf)]
@@ -1049,8 +1042,9 @@
         flops=3 * 10**9,
         vmem=8, moved=6 * 10**6,
     )(coords, hidden_2, h_c, grad_y, dy_c, upb, piece_f, f1, f2, f3, f_y0, f_y13, f_y2)
+    h_xc = to_core(h_x)
+    keep_a, send_a, h_xc, w_up = fence(keep_a, send_a, h_xc, w_up)
     came_a = to_core(send_a)
-    h_xc = to_core(h_x)
     *all_acts, keep_b, send_b = call(
         far_kernel,
         [VM] * 7 + [AN] * 4,
@@ -1060,7 +1054,8 @@
         flops=3 * 10**9,
         vmem=8, moved=6 * 10**6,
     )(h_x, h_xc, dy_x, dy_xc, upb, w_up, w_down, *near_acts)
-    came_b = to_core(send_b)
+    keep_b, send_b, came_a = fence(keep_b, send_b, came_a)
+    keep_b, came_b, *all_acts = fence(keep_b, to_core(send_b), *all_acts)
     back_x = to_x(b16(keep_b[0] + f32(came_b[0])))
     u_terms, d_terms, upb_g = call(
         weights_kernel,
@@ -1071,9 +1066,9 @@
         flops=3 * 10**9,
         vmem=12, moved=6 * 10**6,
     )(coords, *all_acts)
+    back_x, u_terms, d_terms = fence(back_x, u_terms, d_terms)
     u_came = to_y(u_terms[1])
-    d_came = to_y(after(d_terms[1], u_came))
-    back_y = to_x(after(b16(keep_b[1] + f32(came_b[1])), back_x))
+    back_y = to_x(b16(keep_b[1] + f32(came_b[1])))
     grad_first, grad_attended, dw_out, vec_g = call(
         post_kernel,
         [VM] * 8,
@@ -1104,22 +1099,19 @@
         flops=5 * 10**9,
         vmem=16, moved=10 * 10**6,
     )(coords, start, queries, kv, normed, lse, grad_attended, dw_out)
-    def across_core(other, mine):
-        came = to_core(other)
-        return came, lambda *index: f32(mine[index]) + f32(came[index])
-
-    def along_z(part, *done):
-        came = [to_z(b16(part(step)), step) for step in (1, 2, 3)]
-        came = lax.optimization_barrier((*came, *done))[:3]
+    def both(mine, came):
+        return lambda *index: f32(mine[index]) + f32(came[index])
+
+    def along_z(part):
+        return [to_z(b16(part(step)), step) for step in (1, 2, 3)]
+
+    def z_sum(part, came):
         return b16(part(0) + f32(came[0]) + f32(came[1]) + f32(came[2]))
 
-    def u_part(*index):
-        return f32(u_terms[(0,) + index]) + f32(u_came[index])
-
-    def d_part(*index):
-        return f32(d_terms[(0,) + index]) + f32(d_came[index])
-
-    qa_came, qa_1 = across_core(qa_other, qa_mine)
+    dq_a, qa_other, u_came, back_y, d_send = fence(dq_a, qa_other, u_came, back_y, d_terms[1])
+    qa_came, d_came = to_core(qa_other), to_y(d_send)
+    u_part = both(u_terms[0], u_came)
+    u_z = along_z(u_part)
     dq_b, dkv_b, p_own, p_y, p_z, sums = call(
         back_b_kernel,
         [SM] + [VM] * 14 + [AN] * 13,
@@ -1139,10 +1131,11 @@
         coords, start, queries, kv, lse, grad_attended, vec_g, upb_g, dq_a, dkv_a,
         own_tokens, x1, x2, x3, x4, query_key_value_weight, *got_q,
     )
-    u_sum = along_z(u_part, dkv_b)
-    d_sum = along_z(d_part)
-    qa_x = to_x(b16(qa_1(1)))
-    p_came = to_y(after(p_y, d_came))
+    dq_b, qa_came, d_came, p_y, *u_z = fence(dq_b, qa_came, d_came, p_y, *u_z)
+    qa_1 = both(qa_mine, qa_came)
+    d_part = both(d_terms[0], d_came)
+    qa_x, p_came = to_x(b16(qa_1(1))), to_y(p_y)
+    d_z = along_z(d_part)
     qb_other, qb_mine = call(
         back_c_kernel,
         [SM] + [VM] * 4,
@@ -1154,61 +1147,61 @@
         [pltpu.VMEM((2, 2, 8, 32, 3 * width // 2), bf), dma((32,))],
         flops=3 * 10**9,
         vmem=12, moved=6 * 10**6,
-    )(coords, normed, after(dq_b, qa_came), dkv_b, sums)
-    result = b16(residual + vec[7:8] + keep_a[1] + f32(came_a[1]) + f32(back_y))
-    _qb_came, qb_1 = across_core(qb_other, qb_mine)
-    qb_x = to_x(after(b16(qb_1(1)), qa_x))
+    )(coords, normed, dq_b, dkv_b, sums)
+    qb_other, qa_x, p_came, *d_z = fence(qb_other, qa_x, p_came, *d_z)
     even = y == 0
     sum_own = p_own + jnp.where(even, f32(p_came[0]), 0.0)
     sum_4 = b16(f32(p_z[1]) + jnp.where(even, 0.0, f32(p_came[1])))
-    hop = to_z(sum_4, 3)
-    sum_2 = b16(f32(p_z[0]) + jnp.where(even, f32(p_came[1]), f32(p_came[0])) + f32(hop))
-    back_2 = to_z(sum_2, 3)
 
     def qa_2(*index):
         return qa_1(0, *index) + f32(qa_x[index])
 
+    f_tot = join(z_sum(u_part, u_z), z_sum(d_part, d_z))
+    qb_came, qa_y, hop, f_x = fence(
+        to_core(qb_other), to_y(b16(qa_2(1))), to_z(sum_4, 3), to_x(f_tot)
+    )
+    qb_1 = both(qb_mine, qb_came)
+
+    def qa_3(*index):
+        return qa_2(0, *index) + f32(qa_y[index])
+
+    qb_x, *qa_z = fence(to_x(b16(qb_1(1))), *along_z(qa_3))
+    qa_sum = z_sum(qa_3, qa_z)
+
     def qb_2(*index):
         return qb_1(0, *index) + f32(qb_x[index])
 
-    qa_y = to_y(after(b16(qa_2(1)), p_came))
-    qb_y = to_y(after(b16(qb_2(1)), qa_y))
-
-    def qa_3(*index):
-        return qa_2(0, *index) + f32(qa_y[index])
+    sum_2 = b16(f32(p_z[0]) + jnp.where(even, f32(p_came[1]), f32(p_came[0])) + f32(hop))
+    qb_y, back_2, a_x, a_c, a_xc = fence(
+        to_y(b16(qb_2(1))), to_z(sum_2, 3), to_x(qa_sum), to_core(qa_sum), swap_rep(qa_sum, 3)
+    )
 
     def qb_3(*index):
         return qb_2(0, *index) + f32(qb_y[index])
 
-    qa_sum = along_z(qa_3)
-    qb_sum = along_z(qb_3)
-
-    def spread(total, *done):
-        over = to_x(after(total, *done))
-        return total, over, to_core(total), to_core(over)
-
-    done_u = spread(u_sum)
-    done_d = spread(d_sum, qa_x)
-    done_a = spread(qa_sum)
-    done_b = spread(qb_sum)
+    f_tot, f_x = fence(f_tot, f_x, back_2, qb_y)[:2]
+    *qb_z, f_c, f_xc = fence(*along_z(qb_3), to_core(f_tot), to_core(f_x))
+    qb_sum = z_sum(qb_3, qb_z)
+    b_x, b_c, b_xc = to_x(qb_sum), to_core(qb_sum), swap_rep(qb_sum, 3)
+    result = b16(residual + vec[7:8] + keep_a[1] + f32(came_a[1]) + f32(back_y))
     grad_tokens = call(
         tokens_kernel, [VM] * 5, VM, shape_of((tok, width), fl), vmem=4, moved=3 * 10**6
     )(sum_own, back_2, grad_first, own_tokens, vec)
     grad_up, grad_down = call(
         finish_f_kernel,
-        [SM] + [VM] * 8,
+        [SM] + [VM] * 4,
         [VM] * 2,
         [shape_of(up_weight.shape, fl), shape_of(down_weight.shape, fl)],
         [pltpu.VMEM((4, 96, width), bf)],
         vmem=8, moved=4 * 10**6,
-    )(coords, *done_u, *done_d)
+    )(coords, f_tot, f_x, f_c, f_xc)
     grad_qkv, grad_out = call(
         finish_q_kernel,
         [SM] + [VM] * 8,
         [VM] * 2,
         [shape_of(query_key_value_weight.shape, fl), shape_of(output_weight.shape, fl)],
         vmem=8, moved=3 * 10**6,
-    )(coords, *done_a, *done_b)
+    )(coords, qa_sum, a_x, a_c, a_xc, qb_sum, b_x, b_c, b_xc)
     sums = f32(qb_sum[24:32, :256])
     part = ln_gains.shape[1]
     return (

time: 246 us -> 225 us (0.915)
  waiting for transfers between devices: 101 us -> 80.1 us
  starting transfers between devices: 62.8 us -> 66 us
    ppermute x11, waiting for transfers between devices: 41.6 us -> 5.49 us  [to_y(): return lax.ppermute(value, 'seq', [(k, k ^ 1) for k in range(8)])]
    ppermute x22, waiting for transfers between devices: 25 us -> 45.9 us  [to_z(): lax.ppermute(value, 'seq', [(k, (k + 2 * steps) % 8) for k in range(8)])]
    ppermute x35 -> x32, waiting for transfers between devices: 34.2 us -> 28.7 us  [swap_rep(): return lax.ppermute(value, 'rep', [(k, k ^ bit) for k in range(4)])]
    ppermute x35 -> x32, starting transfers between devices: 16.6 us -> 18.5 us  [swap_rep(): return lax.ppermute(value, 'rep', [(k, k ^ bit) for k in range(4)])]
  transfers between devices with their start and end apart: 68 -> 65, of which waited for: 26 -> 31; matrix products, arithmetic and copies ran while one was open for 2% -> 3% of each run, Pallas kernels for 20% -> 31%
where the time goes in v4:
time: 225 us; the launch traced here: 224 us
  waiting for transfers between devices  80.1 us (36%)
  Pallas kernels  70.4 us (31%)
  starting transfers between devices  66 us (29%)
  other arithmetic  3.69 us (2%)
  local copies, waits for them, and re-layouts  3.22 us (1%)
    ppermute x22, waiting for transfers between devices, to_z(): lax.ppermute(value, 'seq', [(k, (k + 2 * steps) % 8) for k in range(8)])  45.9 us
    ppermute x22, starting transfers between devices, to_z(): lax.ppermute(value, 'seq', [(k, (k + 2 * steps) % 8) for k in range(8)])  35.6 us
    ppermute x32, waiting for transfers between devices, swap_rep(): return lax.ppermute(value, 'rep', [(k, k ^ bit) for k in range(4)])  28.7 us
    ppermute x32, starting transfers between devices, swap_rep(): return lax.ppermute(value, 'rep', [(k, k ^ bit) for k in range(4)])  18.5 us
    pallas_call x1, Pallas kernels, on_device_fast(): call(front_kernel, [SM] + [VM] * 6 + [AN] * 15, [VM] * 11, [shape_of((tok...  14.6 us
    ppermute x11, starting transfers between devices, to_y(): return lax.ppermute(value, 'seq', [(k, k ^ 1) for k in range(8)])  11.9 us
    pallas_call x1, Pallas kernels, on_device_fast(): call(back_a_kernel, [SM] + [VM] * 7, [AN] * 2 + [VM] * 2, [shape_of((2, 2...  11.4 us
    pallas_call x1, Pallas kernels, on_device_fast(): call(back_b_kernel, [SM] + [VM] * 14 + [AN] * 13, [VM] * 6, [shape_of((to...  11.4 us
  transfers between devices with their start and end apart: 65, of which 31 were waited for; matrix products, arithmetic and copies ran while one was open for 3% of the time, Pallas kernels for 31%

profile of v4, /device:TPU:0, one launch (start us, length us, event | category | flops | bytes accessed | tf_op | source)
XLA Modules:
  0.0 224.4 jit_solution(13969941104328100113)
XLA Ops:
  0.6 3.0 %collective-permute-start.3 = (bf16[192,768]{1,0:T(8,128)(2,1)}, bf16[192,768]{1,0:T(8,128)(2,1)S(1)}, u32[]{:S(2)}, u32[]{:S(2)}) collective-permute-start(bf16[192,768]{1,0:T(8,128)(2,1)} %bitcast.185), channel_id=1, source_target_pairs={{0,16},{8,24},{16,0},{24,8},{1,17},{9,25},{17,1},{25,9},{2,18},{10... | collective-permute-start | bytes 884744 | tf_op jit(solution)/shard_map/ppermute | solution.py:903
  5.5 3.2 %shard_map.186 = (bf16[200,768]{1,0:T(8,128)(2,1)}, bf16[56,1536]{1,0:T(8,128)(2,1)}, bf16[192,768]{1,0:T(8,128)(2,1)}) custom-call(s32[4]{0:T(128)} %pad_add_fusion.1.coords, bf16[1,192,768]{2,1,0:T(8,128)(2,1)} %tokens.1, s32[1,192]{1,0:T(1,128)} %segs.1, bf16[96,2304]{1,0:T(8,128)(2,1)} %own.3, bf16[96,768]{1,0:T(8,128)(2,1)} %own_o.1, ...), custom_call_target="tpu_custom_call" | custom-call | bytes 4000000 | tf_op jit(solution)/shard_map/pallas_call | solution.py:948
  10.4 2.2 %collective-permute-start.1 = (bf16[56,1536]{1,0:T(8,128)(2,1)}, bf16[56,1536]{1,0:T(8,128)(2,1)S(1)}, u32[]{:S(2)}, u32[]{:S(2)}) collective-permute-start(bf16[56,1536]{1,0:T(8,128)(2,1)} %get-tuple-element.174.first), channel_id=1, source_target_pairs={{0,6},{1,7},{2,0},{3,1},{4,2},{5,3},{6,4},{7,5},{8,14},{9,15},{10,... | collective-permute-start | bytes 516104 | tf_op jit(solution)/shard_map/ppermute | solution.py:919
  14.1 4.0 %collective-permute-done = bf16[56,1536]{1,0:T(8,128)(2,1)S(1)} collective-permute-done((bf16[56,1536]{1,0:T(8,128)(2,1)}, bf16[56,1536]{1,0:T(8,128)(2,1)S(1)}, u32[]{:S(2)}, u32[]{:S(2)}) %collective-permute-start) | collective-permute-done | bytes 172064 | tf_op jit(solution)/shard_map/ppermute | solution.py:919
  23.8 10.3 %collective-permute-done.4 = bf16[56,1536]{1,0:T(8,128)(2,1)S(1)} collective-permute-done((bf16[56,1536]{1,0:T(8,128)(2,1)S(1)}, bf16[56,1536]{1,0:T(8,128)(2,1)S(1)}, u32[]{:S(2)}, u32[]{:S(2)}) %collective-permute-start.4) | collective-permute-done | bytes 172064 | tf_op jit(solution)/shard_map/ppermute | solution.py:919
  36.3 8.9 %collective-permute-done.10.x4 = bf16[200,768]{1,0:T(8,128)(2,1)S(1)} collective-permute-done((bf16[200,768]{1,0:T(8,128)(2,1)S(1)}, bf16[200,768]{1,0:T(8,128)(2,1)S(1)}, u32[]{:S(2)}, u32[]{:S(2)}) %collective-permute-start.10) | collective-permute-done | bytes 307232 | tf_op jit(solution)/shard_map/ppermute | solution.py:919
  49.5 3.1 %collective-permute-start.14 = (bf16[192,768]{1,0:T(8,128)(2,1)S(1)}, bf16[192,768]{1,0:T(8,128)(2,1)S(1)}, u32[]{:S(2)}, u32[]{:S(2)}) collective-permute-start(bf16[192,768]{1,0:T(8,128)(2,1)S(1)} %copy-done.5), channel_id=1, source_target_pairs={{0,6},{1,7},{2,0},{3,1},{4,2},{5,3},{6,4},{7,5},{8,14},{9,15},{10,... | collective-permute-start | bytes 884744 | tf_op jit(solution)/shard_map/ppermute | solution.py:919
  52.6 7.0 %collective-permute-done.13.z1 = bf16[192,768]{1,0:T(8,128)(2,1)S(1)} collective-permute-done((bf16[192,768]{1,0:T(8,128)(2,1)S(1)}, bf16[192,768]{1,0:T(8,128)(2,1)S(1)}, u32[]{:S(2)}, u32[]{:S(2)}) %collective-permute-start.13) | collective-permute-done | bytes 294944 | tf_op jit(solution)/shard_map/ppermute | solution.py:919
  59.6 2.3 %collective-permute-done.14.z3 = bf16[192,768]{1,0:T(8,128)(2,1)S(1)} collective-permute-done((bf16[192,768]{1,0:T(8,128)(2,1)S(1)}, bf16[192,768]{1,0:T(8,128)(2,1)S(1)}, u32[]{:S(2)}, u32[]{:S(2)}) %collective-permute-start.14) | collective-permute-done | bytes 294944 | tf_op jit(solution)/shard_map/ppermute | solution.py:919
  63.7 2.8 %collective-permute-done.19 = bf16[56,1536]{1,0:T(8,128)(2,1)S(1)} collective-permute-done((bf16[56,1536]{1,0:T(8,128)(2,1)S(1)}, bf16[56,1536]{1,0:T(8,128)(2,1)S(1)}, u32[]{:S(2)}, u32[]{:S(2)}) %collective-permute-start.19) | collective-permute-done | bytes 172064 | tf_op jit(solution)/shard_map/ppermute | solution.py:903
  68.9 14.6 %shard_map.187 = (bf16[192,768]{1,0:T(8,128)(2,1)S(1)}, bf16[960,1536]{1,0:T(8,128)(2,1)S(1)}, bf16[960,768]{1,0:T(8,128)(2,1)S(1)}, bf16[192,768]{1,0:T(8,128)(...) custom-call(s32[4]{0:T(128)S(1)} %copy-done.4, ...), custom_call_target="tpu_custom_call" | custom-call | flops 7000000000 | bytes 12000000 | tf_op jit(solution)/shard_map/pallas_call | solution.py:1000
  85.6 6.6 %collective-permute-done.25.h_x = bf16[192,768]{1,0:T(8,128)(2,1)S(1)} collective-permute-done((bf16[192,768]{1,0:T(8,128)(2,1)S(1)}, bf16[192,768]{1,0:T(8,128)(2,1)S(1)}, u32[]{:S(2)}, u32[]{:S(2)}) %collective-permute-start.25) | collective-permute-done | bytes 294944 | tf_op jit(solution)/shard_map/ppermute | solution.py:903
  92.2 2.3 %collective-permute-done.27.y2 = bf16[192,768]{1,0:T(8,128)(2,1)S(1)} collective-permute-done((bf16[192,768]{1,0:T(8,128)(2,1)S(1)}, bf16[192,768]{1,0:T(8,128)(2,1)S(1)}, u32[]{:S(2)}, u32[]{:S(2)}) %collective-permute-start.27) | collective-permute-done | bytes 294944 | tf_op jit(solution)/shard_map/ppermute | solution.py:915
  94.5 7.0 %shard_map.188 = (bf16[384,768]{1,0:T(8,128)(2,1)S(1)}, bf16[384,768]{1,0:T(8,128)(2,1)S(1)}, bf16[384,768]{1,0:T(8,128)(2,1)S(1)}, bf16[384,768]{1,0:T(8,128)(2...) custom-call(s32[4]{0:T(128)S(1)} %copy-done.4, ...), custom_call_target="tpu_custom_call" | custom-call | flops 3000000000 | bytes 6000000 | tf_op jit(solution)/shard_map/pallas_call | solution.py:1036
  102.1 3.7 %shard_map.189 = (bf16[768,768]{1,0:T(8,128)(2,1)S(1)}, bf16[768,768]{1,0:T(8,128)(2,1)S(1)}, bf16[768,768]{1,0:T(8,128)(2,1)S(1)}, bf16[768,768]{1,0:T(8,128)(2...) custom-call(bf16[192,768]{1,0:T(8,128)(2,1)S(1)} %collective-permute-done.25.h_x, ...), custom_call_target="tpu_custom_call" | custom-call | flops 3000000000 | bytes 6000000 | tf_op jit(solution)/shard_map/pallas_call | solution.py:1048
  110.2 6.5 %shard_map.190 = (bf16[2,4,96,768]{3,2,1,0:T(8,128)(2,1)S(1)}, bf16[2,4,96,768]{3,2,1,0:T(8,128)(2,1)S(1)}, f32[1,768]{1,0:T(1,128)S(1)}) custom-call(s32[4]{0:T(128)S(1)} %copy-done.4, bf16[768,768]{1,0:T(8,128)(2,1)S(1)} %get-tuple-element.264.hs, bf16[768,768]{1,0:T(8,128)(2,1)S(1)} %get-tuple-element.265.dys, ...), custom_call_target="tpu_custom_call" | custom-call | flops 3000000000 | bytes 6000000 | tf_op jit(solution)/shard_map/pallas_call | solution.py:1060
  120.0 11.4 %shard_map.192 = (bf16[2,2,4,24,1920]{4,3,2,1,0:T(8,128)(2,1)S(1)}, bf16[2,2,4,24,1920]{4,3,2,1,0:T(8,128)(2,1)S(1)}, bf16[192,384]{1,0:T(8,128)(2,1)S(1)}, bf16[960,768]{1,0:T(8,128)(2,1)S(1)}) custom-call(s32[4]{0:T(128)S(1)} %copy-done.4, s32[1,384]{1,0:T(1,128)S(1)} %get-tuple-element.251.start_in, bf16[192,768]{1,0:T(8,128)(2,1)S(1)} %get-tuple-element.252.q_in, ...), custom_call_target="tpu_custom_call" | custom-call | flops 5000000000 | bytes 10000000 | tf_op jit(solution)/shard_map/pallas_call | solution.py:1088
  134.8 2.5 %collective-permute-start.37 = (bf16[96,768]{1,0:T(8,128)(2,1)S(1)}, bf16[96,768]{1,0:T(8,128)(2,1)S(1)}, u32[]{:S(2)}, u32[]{:S(2)}) collective-permute-start(bf16[96,768]{1,0:T(8,128)(2,1)S(1)} %get-tuple-element.344), channel_id=1, source_target_pairs={{0,4},{1,5},{2,6},{3,7},{4,0},{5,1},{6,2},{7,3},{8,12},{9,13},{10,... | collective-permute-start | bytes 442376 | tf_op jit(solution)/shard_map/ppermute | solution.py:919
  138.5 11.4 %shard_map.193 = (bf16[192,384]{1,0:T(8,128)(2,1)S(1)}, bf16[960,768]{1,0:T(8,128)(2,1)S(1)}, f32[192,768]{1,0:T(8,128)S(1)}, bf16[2,192,768]{2,1,0:T(8,128)(2,1...) custom-call(s32[4]{0:T(128)S(1)} %copy-done.4, s32[1,384]{1,0:T(1,128)S(1)} %get-tuple-element.251.start_in, ...), custom_call_target="tpu_custom_call" | custom-call | flops 6000000000 | bytes 10000000 | tf_op jit(solution)/shard_map/pallas_call | solution.py:1115
  155.5 5.9 %shard_map.194 = (bf16[2,2,4,32,1152]{4,3,2,1,0:T(8,128)(2,1)S(1)}, bf16[2,2,4,32,1152]{4,3,2,1,0:T(8,128)(2,1)S(1)}) custom-call(s32[4]{0:T(128)S(1)} %copy-done.4, bf16[960,768]{1,0:T(8,128)(2,1)S(1)} %get-tuple-element.254.h_in, bf16[192,384]{1,0:T(8,128)(2,1)S(1)} %get-tuple-element.290.dq, bf16[960,768]{1,0:T(8,128)(2,1)S(1)} %get-tuple-element.291.dkv, ...), custom_call_target="tpu_custom_call" | custom-call | flops 3000000000 | bytes 6000000 | tf_op jit(solution)/shard_map/pallas_call | solution.py:1139
  161.5 3.0 %collective-permute-done.42 = bf16[96,768]{1,0:T(8,128)(2,1)S(1)} collective-permute-done((bf16[96,768]{1,0:T(8,128)(2,1)S(1)}, bf16[96,768]{1,0:T(8,128)(2,1)S(1)}, u32[]{:S(2)}, u32[]{:S(2)}) %collective-permute-start.42) | collective-permute-done | bytes 147488 | tf_op jit(solution)/shard_map/ppermute | solution.py:919
  165.0 2.9 %collective-permute-done.39 = bf16[2,4,24,1920]{3,2,1,0:T(8,128)(2,1)S(1)} collective-permute-done((bf16[2,4,24,1920]{3,2,1,0:T(8,128)(2,1)S(1)}, bf16[2,4,24,1920]{3,2,1,0:T(8,128)(2,1)S(1)}, u32[]{:S(2)}, u32[]{:S(2)}) %collective-permute-start.39) | collective-permute-done | bytes 737312 | tf_op jit(solution)/shard_map/ppermute | solution.py:903
  169.8 2.1 collective-permute-start.46
  171.9 5.6 %collective-permute-done.47.fx = bf16[192,768]{1,0:T(8,128)(2,1)S(1)} collective-permute-done((bf16[192,768]{1,0:T(8,128)(2,1)S(1)}, bf16[192,768]{1,0:T(8,128)(2,1)S(1)}, u32[]{:S(2)}, u32[]{:S(2)}) %collective-permute-start.47) | collective-permute-done | bytes 294944 | tf_op jit(solution)/shard_map/ppermute | solution.py:903
  181.5 2.0 collective-permute-start.49
  189.2 2.3 %collective-permute-done.50 = bf16[24,1920]{1,0:T(8,128)(2,1)S(1)} collective-permute-done((bf16[24,1920]{1,0:T(8,128)(2,1)S(1)}, bf16[24,1920]{1,0:T(8,128)(2,1)S(1)}, u32[]{:S(2)}, u32[]{:S(2)}) %collective-permute-start.50) | collective-permute-done | bytes 92192 | tf_op jit(solution)/shard_map/ppermute | solution.py:919
  192.4 2.1 collective-permute-done.48
  197.9 2.5 %collective-permute-done.54.ax = bf16[24,1920]{1,0:T(8,128)(2,1)S(1)} collective-permute-done((bf16[24,1920]{1,0:T(8,128)(2,1)S(1)}, bf16[24,1920]{1,0:T(8,128)(2,1)S(1)}, u32[]{:S(2)}, u32[]{:S(2)}) %collective-permute-start.54) | collective-permute-done | bytes 92192 | tf_op jit(solution)/shard_map/ppermute | solution.py:903
  202.7 4.4 %collective-permute-start.57 = (bf16[32,1152]{1,0:T(8,128)(2,1)S(1)}, bf16[32,1152]{1,0:T(8,128)(2,1)S(1)}, u32[]{:S(2)}, u32[]{:S(2)}) collective-permute-start(bf16[32,1152]{1,0:T(8,128)(2,1)S(1)} %get-tuple-element.339), channel_id=1, source_target_pairs={{0,2},{1,3},{2,4},{3,5},{4,6},{5,7},{6,0},{7,1},{8,10},{9,11},{10,... | collective-permute-start | bytes 221192 | tf_op jit(solution)/shard_map/ppermute | solution.py:919
  207.1 3.5 %collective-permute-start.58 = (bf16[32,1152]{1,0:T(8,128)(2,1)S(1)}, bf16[32,1152]{1,0:T(8,128)(2,1)S(1)}, u32[]{:S(2)}, u32[]{:S(2)}) collective-permute-start(bf16[32,1152]{1,0:T(8,128)(2,1)S(1)} %get-tuple-element.338), channel_id=1, source_target_pairs={{0,4},{1,5},{2,6},{3,7},{4,0},{5,1},{6,2},{7,3},{8,12},{9,13},{10,... | collective-permute-start | bytes 221192 | tf_op jit(solution)/shard_map/ppermute | solution.py:919
  213.2 2.5 %collective-permute-done.58 = bf16[32,1152]{1,0:T(8,128)(2,1)S(1)} collective-permute-done((bf16[32,1152]{1,0:T(8,128)(2,1)S(1)}, bf16[32,1152]{1,0:T(8,128)(2,1)S(1)}, u32[]{:S(2)}, u32[]{:S(2)}) %collective-permute-start.58) | collective-permute-done | bytes 73760 | tf_op jit(solution)/shard_map/ppermute | solution.py:919
  220.3 2.5 %shard_map.197 = (f32[96,3072]{1,0:T(8,128)}, f32[384,768]{1,0:T(8,128)}) custom-call(s32[4]{0:T(128)S(1)} %copy-done.4, bf16[192,768]{1,0:T(8,128)(2,1)S(1)} %pad_maximum_fusion.3.f0, bf16[192,768]{1,0:T(8,128)(2,1)S(1)} %collective-permute-done.47.fx, bf16[192,768]{1,0:T(8,128)(2,1)S(1)} %collective-permute-done.60.fc, ...), custom_call_target="tpu_custom_call" | custom-call | bytes 4000000 | tf_op jit(solution)/shard_map/pallas_call | solution.py:1190
  (158 shorter events, 69.2 us)
Async XLA Ops:
  0.6 19.2 %collective-permute-start.3 = (bf16[192,768]{1,0:T(8,128)(2,1)}, bf16[192,768]{1,0:T(8,128)(2,1)S(1)}, u32[]{:S(2)}, u32[]{:S(2)}) collective-permute-start(bf16[192,768]{1,0:T(8,128)(2,1)} %bitcast.185), channel_id=1, source_target_pairs={{0,16},{8,24},{16,0},{24,8},{1,17},{9,25},{17,1},{25,9},{2,18},{10... | collective-permute-start | bytes 884744 | tf_op jit(solution)/shard_map/ppermute | solution.py:903
  19.8 14.3 %collective-permute-start.5 = (bf16[200,768]{1,0:T(8,128)(2,1)}, bf16[200,768]{1,0:T(8,128)(2,1)S(1)}, u32[]{:S(2)}, u32[]{:S(2)}) collective-permute-start(bf16[200,768]{1,0:T(8,128)(2,1)} %get-tuple-element.179.xo), channel_id=1, source_target_pairs={{0,2},{1,3},{2,4},{3,5},{4,6},{5,7},{6,0},{7,1},{8,10},{9,11},{10,... | collective-permute-start | bytes 921608 | tf_op jit(solution)/shard_map/ppermute | solution.py:919
  20.9 13.1 %collective-permute-start.7 = (bf16[192,768]{1,0:T(8,128)(2,1)}, bf16[192,768]{1,0:T(8,128)(2,1)S(1)}, u32[]{:S(2)}, u32[]{:S(2)}) collective-permute-start(bf16[192,768]{1,0:T(8,128)(2,1)} %get-tuple-element.194.own), channel_id=1, source_target_pairs={{0,1},{1,0},{2,3},{3,2},{4,5},{5,4},{6,7},{7,6},{8,9},{9,8},{10,11... | collective-permute-start | bytes 884744 | tf_op jit(solution)/shard_map/ppermute | solution.py:915
  22.5 11.6 %collective-permute-start.4 = (bf16[56,1536]{1,0:T(8,128)(2,1)S(1)}, bf16[56,1536]{1,0:T(8,128)(2,1)S(1)}, u32[]{:S(2)}, u32[]{:S(2)}) collective-permute-start(bf16[56,1536]{1,0:T(8,128)(2,1)S(1)} %collective-permute-done), channel_id=1, source_target_pairs={{0,2},{1,3},{2,4},{3,5},{4,6},{5,7},{6,0},{7,1},{8,10},{9,11},{10,... | collective-permute-start | bytes 516104 | tf_op jit(solution)/shard_map/ppermute | solution.py:919
  23.3 10.8 %collective-permute-start.6 = (bf16[56,1536]{1,0:T(8,128)(2,1)S(1)}, bf16[56,1536]{1,0:T(8,128)(2,1)S(1)}, u32[]{:S(2)}, u32[]{:S(2)}) collective-permute-start(bf16[56,1536]{1,0:T(8,128)(2,1)S(1)} %collective-permute-done.2), channel_id=1, source_target_pairs={{0,16},{8,24},{16,0},{24,8},{1,17},{9,25},{17,1},{25,9},{2,18},{10... | collective-permute-start | bytes 516104 | tf_op jit(solution)/shard_map/ppermute | solution.py:903
  34.1 12.2 %collective-permute-start.8 = (bf16[168,1536]{1,0:T(8,128)(2,1)S(1)}, bf16[168,1536]{1,0:T(8,128)(2,1)S(1)}, u32[]{:S(2)}, u32[]{:S(2)}) collective-permute-start(bf16[168,1536]{1,0:T(8,128)(2,1)S(1)} %pad_maximum_fusion.2), channel_id=1, source_target_pairs={{0,1},{1,0},{2,3},{3,2},{4,5},{5,4},{6,7},{7,6},{8,9},{9,8},{10,11... | collective-permute-start | bytes 1548296 | tf_op jit(solution)/shard_map/ppermute | solution.py:915
  35.7 11.8 %collective-permute-start.9 = (bf16[168,1536]{1,0:T(8,128)(2,1)S(1)}, bf16[168,1536]{1,0:T(8,128)(2,1)S(1)}, u32[]{:S(2)}, u32[]{:S(2)}) collective-permute-start(bf16[168,1536]{1,0:T(8,128)(2,1)S(1)} %pad_maximum_fusion.2), channel_id=1, source_target_pairs={{0,16},{8,24},{16,0},{24,8},{1,17},{9,25},{17,1},{25,9},{2,18},{10... | collective-permute-start | bytes 1548296 | tf_op jit(solution)/shard_map/ppermute | solution.py:903
  47.7 14.2 %collective-permute-start.11 = (bf16[2,200,768]{2,1,0:T(8,128)(2,1)S(1)}, bf16[2,200,768]{2,1,0:T(8,128)(2,1)S(1)}, u32[]{:S(2)}, u32[]{:S(2)}) collective-permute-start(bf16[2,200,768]{2,1,0:T(8,128)(2,1)S(1)} %pad_maximum_fusion), channel_id=1, source_target_pairs={{0,1},{1,0},{2,3},{3,2},{4,5},{5,4},{6,7},{7,6},{8,9},{9,8},{10,11... | collective-permute-start | bytes 1843208 | tf_op jit(solution)/shard_map/ppermute | solution.py:915
  48.2 13.7 %collective-permute-start.12 = (bf16[168,1536]{1,0:T(8,128)(2,1)S(1)}, bf16[168,1536]{1,0:T(8,128)(2,1)S(1)}, u32[]{:S(2)}, u32[]{:S(2)}) collective-permute-start(bf16[168,1536]{1,0:T(8,128)(2,1)S(1)} %collective-permute-done.8), channel_id=1, source_target_pairs={{0,16},{8,24},{16,0},{24,8},{1,17},{9,25},{17,1},{25,9},{2,18},{10... | collective-permute-start | bytes 1548296 | tf_op jit(solution)/shard_map/ppermute | solution.py:903
  48.8 10.8 %collective-permute-start.13 = (bf16[192,768]{1,0:T(8,128)(2,1)S(1)}, bf16[192,768]{1,0:T(8,128)(2,1)S(1)}, u32[]{:S(2)}, u32[]{:S(2)}) collective-permute-start(bf16[192,768]{1,0:T(8,128)(2,1)S(1)} %copy-done.5), channel_id=1, source_target_pairs={{0,2},{1,3},{2,4},{3,5},{4,6},{5,7},{6,0},{7,1},{8,10},{9,11},{10,... | collective-permute-start | bytes 884744 | tf_op jit(solution)/shard_map/ppermute | solution.py:919
  49.5 12.4 %collective-permute-start.14 = (bf16[192,768]{1,0:T(8,128)(2,1)S(1)}, bf16[192,768]{1,0:T(8,128)(2,1)S(1)}, u32[]{:S(2)}, u32[]{:S(2)}) collective-permute-start(bf16[192,768]{1,0:T(8,128)(2,1)S(1)} %copy-done.5), channel_id=1, source_target_pairs={{0,6},{1,7},{2,0},{3,1},{4,2},{5,3},{6,4},{7,5},{8,14},{9,15},{10,... | collective-permute-start | bytes 884744 | tf_op jit(solution)/shard_map/ppermute | solution.py:919
  66.5 17.0 %collective-permute-start.23 = (bf16[192,768]{1,0:T(8,128)(2,1)S(1)}, bf16[192,768]{1,0:T(8,128)(2,1)S(1)}, u32[]{:S(2)}, u32[]{:S(2)}) collective-permute-start(bf16[192,768]{1,0:T(8,128)(2,1)S(1)} %bitcast.186), channel_id=1, source_target_pairs={{0,8},{8,0},{16,24},{24,16},{1,9},{9,1},{17,25},{25,17},{2,10},{10... | collective-permute-start | bytes 884744 | tf_op jit(solution)/shard_map/ppermute | solution.py:903
  66.8 16.7 %collective-permute-start.24 = (bf16[192,768]{1,0:T(8,128)(2,1)S(1)}, bf16[192,768]{1,0:T(8,128)(2,1)S(1)}, u32[]{:S(2)}, u32[]{:S(2)}) collective-permute-start(bf16[192,768]{1,0:T(8,128)(2,1)S(1)} %collective-permute-done.3.dy_x), channel_id=1, source_target_pairs={{0,8},{8,0},{16,24},{24,16},{1,9},{9,1},{17,25},{25,17},{2,10},{10... | collective-permute-start | bytes 884744 | tf_op jit(solution)/shard_map/ppermute | solution.py:903
  67.0 16.5 %collective-permute-start.21 = (bf16[384,768]{1,0:T(8,128)(2,1)S(1)}, bf16[384,768]{1,0:T(8,128)(2,1)S(1)}, u32[]{:S(2)}, u32[]{:S(2)}) collective-permute-start(bf16[384,768]{1,0:T(8,128)(2,1)S(1)} %pad_maximum_fusion.1), channel_id=1, source_target_pairs={{0,1},{1,0},{2,3},{3,2},{4,5},{5,4},{6,7},{7,6},{8,9},{9,8},{10,11... | collective-permute-start | bytes 1769480 | tf_op jit(solution)/shard_map/ppermute | solution.py:915
  68.6 14.9 %collective-permute-start.22 = (bf16[192,768]{1,0:T(8,128)(2,1)S(1)}, bf16[192,768]{1,0:T(8,128)(2,1)S(1)}, u32[]{:S(2)}, u32[]{:S(2)}) collective-permute-start(bf16[192,768]{1,0:T(8,128)(2,1)S(1)} %collective-permute-done.13.z1), channel_id=1, source_target_pairs={{0,2},{1,3},{2,4},{3,5},{4,6},{5,7},{6,0},{7,1},{8,10},{9,11},{10,... | collective-permute-start | bytes 884744 | tf_op jit(solution)/shard_map/ppermute | solution.py:919
  108.7 22.8 %collective-permute-start.33 = (bf16[192,768]{1,0:T(8,128)(2,1)S(1)}, bf16[192,768]{1,0:T(8,128)(2,1)S(1)}, u32[]{:S(2)}, u32[]{:S(2)}) collective-permute-start(bf16[192,768]{1,0:T(8,128)(2,1)S(1)} %get-tuple-element.346), channel_id=1, source_target_pairs={{0,16},{8,24},{16,0},{24,8},{1,17},{9,25},{17,1},{25,9},{2,18},{10... | collective-permute-start | bytes 884744 | tf_op jit(solution)/shard_map/ppermute | solution.py:903
  118.0 13.7 %collective-permute-start.32 = (bf16[4,96,768]{2,1,0:T(8,128)(2,1)S(1)}, bf16[4,96,768]{2,1,0:T(8,128)(2,1)S(1)}, u32[]{:S(2)}, u32[]{:S(2)}) collective-permute-start(bf16[4,96,768]{2,1,0:T(8,128)(2,1)S(1)} %slice_bitcast_fusion.1), channel_id=1, source_target_pairs={{0,1},{1,0},{2,3},{3,2},{4,5},{5,4},{6,7},{7,6},{8,9},{9,8},{10,11... | collective-permute-start | bytes 1769480 | tf_op jit(solution)/shard_map/ppermute | solution.py:915
  131.8 18.1 %collective-permute-start.34 = (bf16[2,2,4,24,1920]{4,3,2,1,0:T(8,128)(2,1)S(1)}, bf16[2,2,4,24,1920]{4,3,2,1,0:T(8,128)(2,1)S(1)}, u32[]{:S(2)}, u32[]{:S(2)}) collective-permute-start(bf16[2,2,4,24,1920]{4,3,2,1,0:T(8,128)(2,1)S(1)} %get-tuple-element.286), channel_id=1, source_target_pairs={{0,8},{8,0},{16,24},{24,16},{1,9},{9,1},{17,25},{25,17},{2,10},{10... | collective-permute-start | bytes 4423688 | tf_op jit(solution)/shard_map/ppermute | solution.py:903
  131.8 18.1 %collective-permute-start.35 = (bf16[4,96,768]{2,1,0:T(8,128)(2,1)S(1)}, bf16[4,96,768]{2,1,0:T(8,128)(2,1)S(1)}, u32[]{:S(2)}, u32[]{:S(2)}) collective-permute-start(bf16[4,96,768]{2,1,0:T(8,128)(2,1)S(1)} %slice_bitcast_fusion), channel_id=1, source_target_pairs={{0,1},{1,0},{2,3},{3,2},{4,5},{5,4},{6,7},{7,6},{8,9},{9,8},{10,11... | collective-permute-start | bytes 1769480 | tf_op jit(solution)/shard_map/ppermute | solution.py:915
  133.2 16.7 %collective-permute-start.36 = (bf16[96,768]{1,0:T(8,128)(2,1)S(1)}, bf16[96,768]{1,0:T(8,128)(2,1)S(1)}, u32[]{:S(2)}, u32[]{:S(2)}) collective-permute-start(bf16[96,768]{1,0:T(8,128)(2,1)S(1)} %get-tuple-element.345), channel_id=1, source_target_pairs={{0,2},{1,3},{2,4},{3,5},{4,6},{5,7},{6,0},{7,1},{8,10},{9,11},{10,... | collective-permute-start | bytes 442376 | tf_op jit(solution)/shard_map/ppermute | solution.py:919
  134.8 15.1 %collective-permute-start.37 = (bf16[96,768]{1,0:T(8,128)(2,1)S(1)}, bf16[96,768]{1,0:T(8,128)(2,1)S(1)}, u32[]{:S(2)}, u32[]{:S(2)}) collective-permute-start(bf16[96,768]{1,0:T(8,128)(2,1)S(1)} %get-tuple-element.344), channel_id=1, source_target_pairs={{0,4},{1,5},{2,6},{3,7},{4,0},{5,1},{6,2},{7,3},{8,12},{9,13},{10,... | collective-permute-start | bytes 442376 | tf_op jit(solution)/shard_map/ppermute | solution.py:919
  137.3 12.6 %collective-permute-start.38 = (bf16[96,768]{1,0:T(8,128)(2,1)S(1)}, bf16[96,768]{1,0:T(8,128)(2,1)S(1)}, u32[]{:S(2)}, u32[]{:S(2)}) collective-permute-start(bf16[96,768]{1,0:T(8,128)(2,1)S(1)} %get-tuple-element.343), channel_id=1, source_target_pairs={{0,6},{1,7},{2,0},{3,1},{4,2},{5,3},{6,4},{7,5},{8,14},{9,15},{10,... | collective-permute-start | bytes 442376 | tf_op jit(solution)/shard_map/ppermute | solution.py:919
  150.1 17.8 %collective-permute-start.39 = (bf16[2,4,24,1920]{3,2,1,0:T(8,128)(2,1)S(1)}, bf16[2,4,24,1920]{3,2,1,0:T(8,128)(2,1)S(1)}, u32[]{:S(2)}, u32[]{:S(2)}) collective-permute-start(bf16[2,4,24,1920]{3,2,1,0:T(8,128)(2,1)S(1)} %fusion), channel_id=1, source_target_pairs={{0,16},{8,24},{16,0},{24,8},{1,17},{9,25},{17,1},{25,9},{2,18},{10... | collective-permute-start | bytes 2211848 | tf_op jit(solution)/shard_map/ppermute | solution.py:903
  150.7 14.3 %collective-permute-start.40 = (bf16[2,192,768]{2,1,0:T(8,128)(2,1)S(1)}, bf16[2,192,768]{2,1,0:T(8,128)(2,1)S(1)}, u32[]{:S(2)}, u32[]{:S(2)}) collective-permute-start(bf16[2,192,768]{2,1,0:T(8,128)(2,1)S(1)} %get-tuple-element.296), channel_id=1, source_target_pairs={{0,1},{1,0},{2,3},{3,2},{4,5},{5,4},{6,7},{7,6},{8,9},{9,8},{10,11... | collective-permute-start | bytes 1769480 | tf_op jit(solution)/shard_map/ppermute | solution.py:915
  152.8 11.7 %collective-permute-start.42 = (bf16[96,768]{1,0:T(8,128)(2,1)S(1)}, bf16[96,768]{1,0:T(8,128)(2,1)S(1)}, u32[]{:S(2)}, u32[]{:S(2)}) collective-permute-start(bf16[96,768]{1,0:T(8,128)(2,1)S(1)} %get-tuple-element.341), channel_id=1, source_target_pairs={{0,4},{1,5},{2,6},{3,7},{4,0},{5,1},{6,2},{7,3},{8,12},{9,13},{10,... | collective-permute-start | bytes 442376 | tf_op jit(solution)/shard_map/ppermute | solution.py:919
  167.9 11.6 %collective-permute-start.44 = (bf16[2,2,4,32,1152]{4,3,2,1,0:T(8,128)(2,1)S(1)}, bf16[2,2,4,32,1152]{4,3,2,1,0:T(8,128)(2,1)S(1)}, u32[]{:S(2)}, u32[]{:S(2)}) collective-permute-start(bf16[2,2,4,32,1152]{4,3,2,1,0:T(8,128)(2,1)S(1)} %get-tuple-element.300), channel_id=1, source_target_pairs={{0,8},{8,0},{16,24},{24,16},{1,9},{9,1},{17,25},{25,17},{2,10},{10... | collective-permute-start | bytes 3538952 | tf_op jit(solution)/shard_map/ppermute | solution.py:903
  168.8 10.8 %collective-permute-start.45 = (bf16[4,24,1920]{2,1,0:T(8,128)(2,1)S(1)}, bf16[4,24,1920]{2,1,0:T(8,128)(2,1)S(1)}, u32[]{:S(2)}, u32[]{:S(2)}) collective-permute-start(bf16[4,24,1920]{2,1,0:T(8,128)(2,1)S(1)} %fusion.1), channel_id=1, source_target_pairs={{0,1},{1,0},{2,3},{3,2},{4,5},{5,4},{6,7},{7,6},{8,9},{9,8},{10,11... | collective-permute-start | bytes 1105928 | tf_op jit(solution)/shard_map/ppermute | solution.py:915
  179.7 14.7 %collective-permute-start.48 = (bf16[2,4,32,1152]{3,2,1,0:T(8,128)(2,1)S(1)}, bf16[2,4,32,1152]{3,2,1,0:T(8,128)(2,1)S(1)}, u32[]{:S(2)}, u32[]{:S(2)}) collective-permute-start(bf16[2,4,32,1152]{3,2,1,0:T(8,128)(2,1)S(1)} %fusion.10), channel_id=1, source_target_pairs={{0,16},{8,24},{16,0},{24,8},{1,17},{9,25},{17,1},{25,9},{2,18},{10... | collective-permute-start | bytes 1769480 | tf_op jit(solution)/shard_map/ppermute | solution.py:903
  186.2 11.7 %collective-permute-start.53 = (bf16[192,768]{1,0:T(8,128)(2,1)S(1)}, bf16[192,768]{1,0:T(8,128)(2,1)S(1)}, u32[]{:S(2)}, u32[]{:S(2)}) collective-permute-start(bf16[192,768]{1,0:T(8,128)(2,1)S(1)} %get-tuple-element.350), channel_id=1, source_target_pairs={{0,6},{1,7},{2,0},{3,1},{4,2},{5,3},{6,4},{7,5},{8,14},{9,15},{10,... | collective-permute-start | bytes 884744 | tf_op jit(solution)/shard_map/ppermute | solution.py:919
  202.0 14.1 %collective-permute-start.60 = (bf16[192,768]{1,0:T(8,128)(2,1)S(1)}, bf16[192,768]{1,0:T(8,128)(2,1)S(1)}, u32[]{:S(2)}, u32[]{:S(2)}) collective-permute-start(bf16[192,768]{1,0:T(8,128)(2,1)S(1)} %pad_maximum_fusion.3.f0), channel_id=1, source_target_pairs={{0,8},{8,0},{16,24},{24,16},{1,9},{9,1},{17,25},{25,17},{2,10},{10... | collective-permute-start | bytes 884744 | tf_op jit(solution)/shard_map/ppermute | solution.py:903
  202.2 14.0 %collective-permute-start.61 = (bf16[192,768]{1,0:T(8,128)(2,1)S(1)}, bf16[192,768]{1,0:T(8,128)(2,1)S(1)}, u32[]{:S(2)}, u32[]{:S(2)}) collective-permute-start(bf16[192,768]{1,0:T(8,128)(2,1)S(1)} %collective-permute-done.47.fx), channel_id=1, source_target_pairs={{0,8},{8,0},{16,24},{24,16},{1,9},{9,1},{17,25},{25,17},{2,10},{10... | collective-permute-start | bytes 884744 | tf_op jit(solution)/shard_map/ppermute | solution.py:903
  202.7 10.5 %collective-permute-start.57 = (bf16[32,1152]{1,0:T(8,128)(2,1)S(1)}, bf16[32,1152]{1,0:T(8,128)(2,1)S(1)}, u32[]{:S(2)}, u32[]{:S(2)}) collective-permute-start(bf16[32,1152]{1,0:T(8,128)(2,1)S(1)} %get-tuple-element.339), channel_id=1, source_target_pairs={{0,2},{1,3},{2,4},{3,5},{4,6},{5,7},{6,0},{7,1},{8,10},{9,11},{10,... | collective-permute-start | bytes 221192 | tf_op jit(solution)/shard_map/ppermute | solution.py:919
  (41 other events, 325.0 us)

commit v5 on v4

--- a/solution.py
+++ b/solution.py
@@ -333,8 +333,9 @@
     )
 
 
-def place(coords):
-    return coords[0], coords[1], coords[2], coords[3]
+def place():
+    rep, seq = lax.axis_index("rep"), lax.axis_index("seq")
+    return lax.div(rep, 2), lax.rem(rep, 2), lax.rem(seq, 2), lax.div(seq, 2)
 
 
 def piece_shard(number, y, z):
@@ -395,8 +396,8 @@
     return ((x, c), (1 - x, c), (x, 1 - c), (1 - x, 1 - c))
 
 
-def fetch_qkv(copies, coords, own, groups, full, full_out=None, own_out=None):
-    x, c, y, z = place(coords)
+def fetch_qkv(copies, own, groups, full, full_out=None, own_out=None):
+    x, c, y, z = place()
     rows = own.shape[0]
     half, width = rows // 2, own.shape[1] // 3
     row = pl.multiple_of((2 * z + y) * rows, 16)
@@ -448,11 +449,11 @@
 
 
 def prep_kernel(
-    coords, tokens, segs, qkv, out, up, down, gains, shifts, biases, up_bias,
+    tokens, segs, qkv, out, up, down, gains, shifts, biases, up_bias,
     t_out, q_out, f_out,
     scratch, wide, held_g, held_s, held_b, ids, line, sems,
 ):
-    x, c, _y, _z = place(coords)
+    x, c, _y, _z = place()
     tok, width = tokens.shape[1:]
     rows = qkv.shape[0]
     half, side = rows // 2, width // 2
@@ -479,9 +480,15 @@
     scratch[...] = jnp.zeros_like(scratch)
     for first, held in ((0, held_g), (2, held_s), (4, held_b)):
         scratch[pl.ds(first, held.shape[0]), pl.ds(0, rows)] = f32(held[...])
-    scratch[pl.ds(0, 1), pl.ds(128, 384)] = f32(line[...])
-    q_out[pl.ds(half, 8), pl.ds(0, width)] = b16(scratch[...])
-    q_out[pl.ds(half, 8), pl.ds(width, width)] = jnp.zeros((8, width), jnp.bfloat16)
+    parts = unpack96(jnp.broadcast_to(f32(line[...]).reshape(1, line.shape[0]), (8, line.shape[0])))
+    lane = lax.broadcasted_iota(jnp.int32, (8, 128), 1)
+    row = lax.broadcasted_iota(jnp.int32, (8, 128), 0)
+    ups = jnp.zeros((8, 128), jnp.float32)
+    for number in range(4):
+        ups = jnp.where((row == number) & (lane < rows), parts[number], ups)
+    smalls = b16(jnp.concatenate([scratch[:, pl.ds(0, 128)], ups], axis=0))
+    q_out[pl.ds(0, 16), pl.ds(2 * width, 128)] = smalls
+    q_out[pl.ds(16, half - 16), pl.ds(2 * width, 128)] = jnp.zeros((half - 16, 128), jnp.bfloat16)
     scratch[...] = jnp.zeros_like(scratch)
     scratch[pl.ds(0, 1), pl.ds(0, tok)] = f32(ids[...])
     t_out[pl.ds(tok, 8), :] = b16(scratch[...])
@@ -494,22 +501,22 @@
 
 
 def front_kernel(
-    coords, seg, xo, x1, x2, x3, x4, first, own, own_o,
+    seg, xo, x1, x2, x3, x4, first, own, own_o,
     g0, g1, g2, g3, g4, g5, g6, g7, g8, g9, g10, g11,
     q_out, kv_out, h_out, a_out, lse_out, start_out, vec_out, upb_out, wo_out, r_out, h2_out,
     full, small, bias, sems, vsems,
 ):
-    x, c, y, z = place(coords)
+    x, c, y, z = place()
     me = 2 * z + y
     p = 2 * x + c
     tok, width = q_out.shape
     copies, vcopies = Copies(sems), Copies(vsems)
-    vcopies.add(first.at[pl.ds(48, 8), pl.ds(0, 512)], small.at[me])
+    vcopies.add(first.at[pl.ds(0, 16), pl.ds(2 * width, 128)], small.at[me])
     for number in range(7):
         source = piece_of((g0, g1, g2), number)
-        vcopies.add(source.at[pl.ds(48, 8), pl.ds(0, 512)], small.at[piece_shard(number, y, z)])
+        vcopies.add(source.at[pl.ds(0, 16), pl.ds(2 * width, 128)], small.at[piece_shard(number, y, z)])
     groups = ((g0, g1, g2), (g3, g4, g5), (g6, g7, g8), (g9, g10, g11))
-    fetch_qkv(copies, coords, own, groups, full, wo_out, own_o)
+    fetch_qkv(copies, own, groups, full, wo_out, own_o)
     blocks = (xo, x1, x2, x3, x4)
     lane1 = lax.broadcasted_iota(jnp.int32, (1, tok), 1)
     start = jnp.full(seg.shape, 1 << 30, jnp.int32)
@@ -528,9 +535,9 @@
     vcopies.wait()
     for group in range(2):
         held = [f32(small[4 * group + k]) for k in range(4)]
-        vec_out[:, pl.ds(384 * group, 384)] = pack96([block[:, :128] for block in held])
+        vec_out[:, pl.ds(384 * group, 384)] = pack96([block[:8] for block in held])
         upb_out[:, pl.ds(384 * group, 384)] = pack96(
-            [choose(unpack96(block[:, 128:512]), p) for block in held]
+            [choose([jnp.broadcast_to(block[k : k + 1], (8, 128)) for k in range(8, 12)], p) for block in held]
         )
     vec = vec_out[...]
     for back in range(5):
@@ -593,23 +600,34 @@
     y_acc[...] = dot_nn(act_out[...], w_down[...])
 
 
+def assemble_kernel(own, z1, z2, z3, y0, y13, wu_out, wd_out, sems):
+    _x, _c, y, z = place()
+    rows = own.shape[0] // 2
+    copies = Copies(sems)
+    pieces = [(own, 2 * z + y)]
+    for number, ref in ((0, z1), (1, z2), (2, z3), (3, y0)):
+        pieces.append((ref, piece_shard(number, y, z)))
+    for number, first in ((4, 0), (6, 2 * rows)):
+        pieces.append((y13.at[pl.ds(first, 2 * rows), :], piece_shard(number, y, z)))
+    for ref, shard in pieces:
+        at = pl.ds(pl.multiple_of(shard * rows, 16), rows)
+        copies.add(ref.at[pl.ds(0, rows), :], wu_out.at[at, :])
+        copies.add(ref.at[pl.ds(rows, rows), :], wd_out.at[at, :])
+    copies.wait()
+
+
 def near_kernel(
-    coords, h_own, h_c, dy_own, dy_c, upb, own, z1, z2, z3, y0, y13, y2,
+    h_own, h_c, dy_own, dy_c, upb, y2, _wu, _wd,
     h2, dy, act_out, du_out, keep_out, send_out, wu_out, wd_out,
     y_acc, dh_acc, sems,
 ):
-    _x, _c, y, z = place(coords)
+    _x, _c, y, z = place()
     tok, width = h_own.shape
     rows = width // 8
     copies = Copies(sems)
-    across = (y0, y13.at[pl.ds(0, 2 * rows), :], y2, y13.at[pl.ds(2 * rows, 2 * rows), :])
-    shards = [(own, 2 * z + y)] + [
-        (ref, piece_shard(number, y, z)) for number, ref in enumerate((z1, z2, z3) + across)
-    ]
-    for ref, shard in shards:
-        at = pl.ds(pl.multiple_of(shard * rows, 16), rows)
-        copies.add(ref.at[pl.ds(0, rows), :], wu_out.at[at, :])
-        copies.add(ref.at[pl.ds(rows, rows), :], wd_out.at[at, :])
+    at = pl.ds(pl.multiple_of(piece_shard(5, y, z) * rows, 16), rows)
+    copies.add(y2.at[pl.ds(0, rows), :], wu_out.at[at, :])
+    copies.add(y2.at[pl.ds(rows, rows), :], wd_out.at[at, :])
     h2[pl.ds(0, tok), :] = h_own[...]
     h2[pl.ds(tok, tok), :] = h_c[...]
     dy[pl.ds(0, tok), :] = dy_own[...]
@@ -646,8 +664,8 @@
     copies.wait()
 
 
-def weights_kernel(coords, hs, dys, acts, dus, u_out, d_out, upb_out, stage, sems):
-    _x, _c, y, z = place(coords)
+def weights_kernel(hs, dys, acts, dus, u_out, d_out, upb_out, stage, sems):
+    _x, _c, y, z = place()
     width = hs.shape[1]
     rows = width // 8
     upb_out[...] = jnp.sum(f32(dus[...]), axis=0, keepdims=True)
@@ -668,7 +686,23 @@
     outs.wait()
 
 
-def post_kernel(residual, own, near, across, dy_in, vec_in, w_out, a_in, dr_out, da_out, dw_out, vec_out):
+def scatter(stage, other, mine, sems):
+    x, c, y, z = place()
+    outs = Copies(sems)
+    for shard in range(8):
+        zz = lax.rem(shard // 2 + 4 - z, 4)
+        yy = jnp.where(y == shard % 2, 0, 1)
+        for xx in range(2):
+            far = jnp.where(x == xx, 0, 1)
+            outs.add(stage.at[1 - c, xx, shard], other.at[far, yy, zz])
+            outs.add(stage.at[c, xx, shard], mine.at[far, yy, zz])
+    outs.wait()
+
+
+def post_kernel(
+    residual, own, near, across, dy_in, vec_in, w_out, a_in,
+    dr_out, da_out, dw_out, vec_out,
+):
     vec = vec_in[...]
     grad_hidden = own[0] + f32(near[0]) + f32(across[...])
     hat, rate = norm_parts(residual[...])
@@ -677,7 +711,7 @@
     dr_out[...] = grad_first
     low = b16(grad_first)
     da_out[...] = b16(dot_nt(low, w_out[...]))
-    dw_out[...] = b16(dot_tn(a_in[...], low))
+    dw_out[...] = dot_tn(a_in[...], low)
     zero = jnp.zeros((1, dy.shape[1]), jnp.float32)
     vec_out[...] = jnp.concatenate(
         [
@@ -715,7 +749,7 @@
     lax.fori_loop(0, 3, pair, 0)
 
 
-def qkv_weight(h_in, dq, dkv, stage):
+def qkv_weight(h_in, dq, dkv, stage, tail):
     tok, part = dq.shape
     keys = h_in.shape[0]
 
@@ -726,53 +760,45 @@
         for shard in range(4):
             for cc in range(2):
                 for xx in range(2):
-                    row = 96 * shard + 48 * cc + 24 * xx
-                    stage[cc, xx, 4 * number + shard, pl.ds(0, 24), pl.ds(0, part)] = b16(query[row : row + 24])
-                    stage[cc, xx, 4 * number + shard, pl.ds(0, 24), pl.ds(part, 2 * part)] = b16(key[row : row + 24])
+                    rows = slice(96 * shard + 48 * cc + 24 * xx, 96 * shard + 48 * cc + 24 * xx + 24)
+                    blocks = [query[rows], key[rows, :part], key[rows, part:]] + tail(4 * number + shard, 48 * cc + 24 * xx)
+                    stage[cc, xx, 4 * number + shard] = b16(jnp.concatenate(blocks, axis=0))
         return carry
 
     lax.fori_loop(0, 2, weight, 0)
 
 
 def back_a_kernel(
-    coords, start_in, q_in, kv_in, h_in, lse_in, da_in, dw_in,
+    start_in, q_in, kv_in, h_in, lse_in, da_in, dw_in,
     other, mine, dq_out, dkv_out,
     bias, stage, sems,
 ):
-    x, c, y, z = place(coords)
-    tok, width = q_in.shape
-    mask_bias(start_in[...], 2 * z + y, tok, bias)
-    for shard in range(8):
-        for cc in range(2):
-            block = f32(dw_in[pl.ds(96 * shard + 48 * cc, 48), :])
-            for xx in range(2):
-                stage[cc, xx, shard, :, pl.ds(3 * width // 2, width)] = b16(block[24 * xx : 24 * xx + 24])
+    _x, _c, y, z = place()
+    mask_bias(start_in[...], 2 * z + y, q_in.shape[0], bias)
     back_pairs(0, q_in, kv_in, lse_in, da_in, bias, dq_out, dkv_out)
-    qkv_weight(h_in, dq_out, dkv_out, stage)
-    outs = Copies(sems)
-    for shard in range(8):
-        zz = lax.rem(shard // 2 + 4 - z, 4)
-        yy = jnp.where(y == shard % 2, 0, 1)
-        for xx in range(2):
-            far = jnp.where(x == xx, 0, 1)
-            outs.add(stage.at[1 - c, xx, shard], other.at[far, yy, zz])
-            outs.add(stage.at[c, xx, shard], mine.at[far, yy, zz])
-    outs.wait()
+    side = q_in.shape[1] // 2
+
+    def out_rows(shard, row):
+        rows = dw_in[pl.ds(pl.multiple_of(96 * shard + row, 8), 24), :]
+        return [rows[:, :side], rows[:, side:]]
+
+    qkv_weight(h_in, dq_out, dkv_out, stage, out_rows)
+    scatter(stage, other, mine, sems)
 
 
 def back_b_kernel(
-    coords, start_in, q_in, kv_in, lse_in, da_in, vec_in, upb_in, dq_a, dkv_a, xo, x1, x2, x3, x4,
+    start_in, q_in, kv_in, lse_in, da_in, vec_in, upb_in, dq_a, dkv_a, xo, x1, x2, x3, x4,
     own, g0, g1, g2, g3, g4, g5, g6, g7, g8, g9, g10, g11,
     dq_out, dkv_out, p_own, p_y, p_z, sums_out,
     full, bias, sems,
 ):
-    x, c, y, z = place(coords)
+    x, c, y, z = place()
     p = 2 * x + c
     tok, width = q_in.shape
     side = width // 2
     copies = Copies(sems)
     groups = ((g0, g1, g2), (g3, g4, g5), (g6, g7, g8), (g9, g10, g11))
-    fetch_qkv(copies, coords, own, groups, full)
+    fetch_qkv(copies, own, groups, full)
     mask_bias(start_in[...], 2 * z + y, tok, bias)
     back_pairs(3, q_in, kv_in, lse_in, da_in, bias, dq_out, dkv_out)
     copies.wait()
@@ -820,25 +846,12 @@
             )
 
 
-def back_c_kernel(coords, h_in, dq, dkv, sums_in, other, mine, stage, sems):
-    x, c, y, z = place(coords)
-    qkv_weight(h_in, dq, dkv, stage)
-    for shard in range(8):
-        row = b16(
-            jnp.concatenate([sums_in[shard], jnp.zeros((8, stage.shape[4] - 256), jnp.float32)], axis=1)
-        )
-        for cc in range(2):
-            for xx in range(2):
-                stage[cc, xx, shard, pl.ds(24, 8), :] = row
-    outs = Copies(sems)
-    for shard in range(8):
-        zz = lax.rem(shard // 2 + 4 - z, 4)
-        yy = jnp.where(y == shard % 2, 0, 1)
-        for xx in range(2):
-            far = jnp.where(x == xx, 0, 1)
-            outs.add(stage.at[1 - c, xx, shard], other.at[far, yy, zz])
-            outs.add(stage.at[c, xx, shard], mine.at[far, yy, zz])
-    outs.wait()
+def back_c_kernel(h_in, dq, dkv, sums_in, other, mine, stage, sems):
+    blank = jnp.zeros((8, 128), jnp.float32)
+    qkv_weight(
+        h_in, dq, dkv, stage, lambda shard, _row: [jnp.concatenate([sums_in[shard], blank], axis=1)]
+    )
+    scatter(stage, other, mine, sems)
 
 
 def tokens_kernel(own, near, dr, xo, vec_in, grad_out):
@@ -848,8 +861,8 @@
     grad_out[...] = dr[...] + norm_back(grad, hat, rate, vec_in[0:1, :])
 
 
-def finish_f_kernel(coords, f0, fx, fc, fcx, up, down, held):
-    x, c, _y, _z = place(coords)
+def finish_f_kernel(f0, fx, fc, fcx, up, down, held):
+    x, c, _y, _z = place()
     rows = f0.shape[0] // 2
     for (xx, cc), f in zip(corners(x, c), (f0, fx, fc, fcx), strict=True):
         p = 2 * xx + cc
@@ -861,21 +874,22 @@
             up[:, pl.ds(384 * (4 * group + shard), 384)] = pack96([part[shard] for part in parts])
 
 
-def finish_q_kernel(coords, a0, ax, ac, acx, b0, bx, bc, bcx, qkv, out):
-    x, c, _y, _z = place(coords)
+def finish_q_kernel(f0, fx, fc, fcx, qkv, out):
+    x, c, _y, _z = place()
     side = out.shape[1] // 2
-    for (xx, cc), a, b in zip(corners(x, c), (a0, ax, ac, acx), (b0, bx, bc, bcx), strict=True):
+    for (xx, cc), piece in zip(corners(x, c), (f0, fx, fc, fcx), strict=True):
         rows = pl.ds(pl.multiple_of(48 * cc + 24 * xx, 8), 24)
-        first, second = f32(a[...]), f32(b[...])[:24]
+        blocks = f32(piece[...])
         for number in range(3):
-            qkv[rows, pl.ds(2 * side * number, side)] = first[:, side * number : side * (number + 1)]
-            qkv[rows, pl.ds(2 * side * number + side, side)] = second[:, side * number : side * (number + 1)]
-        out[rows, :] = first[:, 3 * side :]
+            first, second = 24 * number, 24 * (number + 5)
+            qkv[rows, pl.ds(2 * side * number, side)] = blocks[first : first + 24]
+            qkv[rows, pl.ds(2 * side * number + side, side)] = blocks[second : second + 24]
+        out[rows, pl.ds(0, side)] = blocks[72:96]
+        out[rows, pl.ds(side, side)] = blocks[96:120]
 
 
 HB = pl.BlockSpec(memory_space=pltpu.HBM)
 VM = pl.BlockSpec(memory_space=pltpu.VMEM)
-SM = pl.BlockSpec(memory_space=pltpu.SMEM)
 AN = pl.BlockSpec(memory_space=pl.ANY)
 
 
@@ -883,13 +897,14 @@
     return jax.ShapeDtypeStruct(shape, dtype)
 
 
-def call(kernel, ins, outs, out_shape, scratch=(), vmem=40, flops=0, moved=0):
+def call(kernel, ins, outs, out_shape, scratch=(), vmem=40, flops=0, moved=0, aliases=None):
     return pl.pallas_call(
         kernel,
         in_specs=ins,
         out_specs=outs,
         out_shape=out_shape,
         scratch_shapes=list(scratch),
+        input_output_aliases=aliases or {},
         compiler_params=pltpu.CompilerParams(vmem_limit_bytes=vmem << 20),
         cost_estimate=pl.CostEstimate(flops=flops, bytes_accessed=moved, transcendentals=0),
     )
@@ -936,9 +951,8 @@
     up_projection_bias,
     cotangent,
 ):
-    rep, seq = lax.axis_index("rep"), lax.axis_index("seq")
-    x, c, z, y = rep // 2, rep % 2, seq // 2, seq % 2
-    coords = jnp.stack([x, c, y, z]).astype(jnp.int32)
+    seq = lax.axis_index("seq")
+    y = seq % 2
     tok, width = tokens.shape[1:]
     hidden = up_weight.shape[1]
     keys = 5 * tok
@@ -947,11 +961,11 @@
     grad_y = cotangent[0]
     own_tokens, piece_q, piece_f = call(
         prep_kernel,
-        [SM] + [HB] * 10,
+        [HB] * 10,
         [VM] * 3,
         [
             shape_of((tok + 8, width), bf),
-            shape_of((56, 2 * width), bf),
+            shape_of((48, 2 * width + 128), bf),
             shape_of((192, width), bf),
         ],
         [
@@ -961,13 +975,13 @@
             pltpu.VMEM((2, 96), bf),
             pltpu.VMEM((4, 96), bf),
             pltpu.VMEM((1, tok), jnp.int32),
-            pltpu.VMEM((1, 384), bf),
+            pltpu.VMEM((384,), bf),
             dma((10,)),
         ],
         vmem=60, moved=4 * 10**6,
     )(
-        coords, tokens, segment_ids, query_key_value_weight, output_weight, up_weight, down_weight,
-        ln_gains, ln_biases, biases, up_projection_bias[None],
+        tokens, segment_ids, query_key_value_weight, output_weight, up_weight, down_weight,
+        ln_gains, ln_biases, biases, up_projection_bias,
     )
 
     q1, q3, q_y0, dy_x = fence(to_z(piece_q, 1), to_z(piece_q, 3), to_y(piece_q), to_x(grad_y))
@@ -990,7 +1004,7 @@
     dy_c, dy_xc = to_core(grad_y), to_core(dy_x)
 
     def pieces(value):
-        return value.reshape(value.shape[0] // 56, 56, value.shape[1])
+        return value.reshape(value.shape[0] // 48, 48, value.shape[1])
 
     got_q = [
         pieces(v)
@@ -999,7 +1013,7 @@
     seg = jnp.concatenate([segment_ids, segment_ids], axis=1)
     front = call(
         front_kernel,
-        [SM] + [VM] * 6 + [AN] * 15,
+        [VM] * 6 + [AN] * 15,
         [VM] * 11,
         [
             shape_of((tok, width), bf),
@@ -1016,7 +1030,7 @@
         ],
         [
             pltpu.VMEM((width, 3 * width), bf),
-            pltpu.VMEM((8, 8, 512), bf),
+            pltpu.VMEM((8, 16, 128), bf),
             pltpu.VMEM((keys, 2 * tok), fl),
             dma((2 + 56,)),
             dma((8,)),
@@ -1024,24 +1038,35 @@
         flops=7 * 10**9,
         vmem=16, moved=12 * 10**6,
     )(
-        coords, seg, own_tokens, x1, x2, x3, x4, piece_q, query_key_value_weight, output_weight, *got_q,
+        seg, own_tokens, x1, x2, x3, x4, piece_q, query_key_value_weight, output_weight, *got_q,
     )
     *front, f_y13, f2, dy_c, dy_xc = fence(*front, f_y13, f2, dy_c, dy_xc)
     queries, kv, normed, attended, lse, start, vec, upb, w_out, residual, hidden_2 = front
-    h_x, h_c, f_y2 = fence(to_x(hidden_2), to_core(hidden_2), to_y(f2))
+    w_half = call(
+        assemble_kernel,
+        [AN] * 6,
+        [VM] * 2,
+        [shape_of((width, width), bf)] * 2,
+        [dma((14,))],
+        vmem=4,
+        moved=5 * 10**6,
+    )(piece_f, f1, f2, f3, f_y0, f_y13)
+    h_x, h_c, f_y2, *w_half = fence(to_x(hidden_2), to_core(hidden_2), to_y(f2), *w_half)
     act = shape_of((2 * tok, width), bf)
     acts = shape_of((4 * tok, width), bf)
     feed_shapes = [shape_of((2, tok, width), fl), shape_of((2, tok, width), bf)]
     feed_scratch = [pltpu.VMEM((2 * tok, width), fl), pltpu.VMEM((2 * tok, width), fl)]
     *near_acts, keep_a, send_a, w_up, w_down = call(
         near_kernel,
-        [SM] + [VM] * 5 + [AN] * 7,
+        [VM] * 5 + [AN] + [VM] * 2,
         [VM] * 8,
         [act] * 4 + feed_shapes + [shape_of((width, width), bf)] * 2,
-        feed_scratch + [dma((16,))],
+        feed_scratch + [dma((2,))],
         flops=3 * 10**9,
-        vmem=8, moved=6 * 10**6,
-    )(coords, hidden_2, h_c, grad_y, dy_c, upb, piece_f, f1, f2, f3, f_y0, f_y13, f_y2)
+        vmem=8,
+        moved=6 * 10**6,
+        aliases={6: 6, 7: 7},
+    )(hidden_2, h_c, grad_y, dy_c, upb, f_y2, *w_half)
     h_xc = to_core(h_x)
     keep_a, send_a, h_xc, w_up = fence(keep_a, send_a, h_xc, w_up)
     came_a = to_core(send_a)
@@ -1059,14 +1084,14 @@
     back_x = to_x(b16(keep_b[0] + f32(came_b[0])))
     u_terms, d_terms, upb_g = call(
         weights_kernel,
-        [SM] + [VM] * 4,
+        [VM] * 4,
         [AN, AN, VM],
         [shape_of((2, 4, 96, width), bf), shape_of((2, 4, 96, width), bf), shape_of((1, width), fl)],
         [pltpu.VMEM((2, width, width), bf), dma((16,))],
         flops=3 * 10**9,
         vmem=12, moved=6 * 10**6,
-    )(coords, *all_acts)
-    back_x, u_terms, d_terms = fence(back_x, u_terms, d_terms)
+    )(*all_acts)
+    back_x, u_terms, d_terms, keep_b = fence(back_x, u_terms, d_terms, keep_b)
     u_came = to_y(u_terms[1])
     back_y = to_x(b16(keep_b[1] + f32(came_b[1])))
     grad_first, grad_attended, dw_out, vec_g = call(
@@ -1076,45 +1101,49 @@
         [
             shape_of((tok, width), fl),
             shape_of((tok, width), bf),
-            shape_of((width, width), bf),
+            shape_of((width, width), fl),
             shape_of((8, width), fl),
         ],
+        vmem=12,
         flops=10**9,
-        vmem=10, moved=4 * 10**6,
+        moved=4 * 10**6,
     )(residual, keep_a, came_a, back_x, grad_y, vec, w_out, attended)
     back_scratch = [
         pltpu.VMEM((keys, 2 * tok), fl),
     ]
     qa_other, qa_mine, dq_a, dkv_a = call(
         back_a_kernel,
-        [SM] + [VM] * 7,
+        [VM] * 7,
         [AN] * 2 + [VM] * 2,
         [
-            shape_of((2, 2, 4, 24, 5 * width // 2), bf),
-            shape_of((2, 2, 4, 24, 5 * width // 2), bf),
+            shape_of((2, 2, 4, 120, width // 2), bf),
+            shape_of((2, 2, 4, 120, width // 2), bf),
             shape_of((tok, width // 2), bf),
             shape_of((keys, width), bf),
         ],
-        back_scratch + [pltpu.VMEM((2, 2, 8, 24, 5 * width // 2), bf), dma((32,))],
+        back_scratch + [pltpu.VMEM((2, 2, 8, 120, width // 2), bf), dma((32,))],
         flops=5 * 10**9,
         vmem=16, moved=10 * 10**6,
-    )(coords, start, queries, kv, normed, lse, grad_attended, dw_out)
+    )(start, queries, kv, normed, lse, grad_attended, dw_out)
+
     def both(mine, came):
         return lambda *index: f32(mine[index]) + f32(came[index])
 
-    def along_z(part):
-        return [to_z(b16(part(step)), step) for step in (1, 2, 3)]
-
-    def z_sum(part, came):
-        return b16(part(0) + f32(came[0]) + f32(came[1]) + f32(came[2]))
-
-    dq_a, qa_other, u_came, back_y, d_send = fence(dq_a, qa_other, u_came, back_y, d_terms[1])
-    qa_came, d_came = to_core(qa_other), to_y(d_send)
+    def z_far(part):
+        return to_z(b16(part(2)), 1), to_z(b16(part(3)), 3)
+
+    def z_sum(part, *came):
+        return b16(part(0) + sum(f32(v) for v in came))
+
+    dq_a, qa_other, u_came, back_y, d_send = fence(
+        dq_a, qa_other, u_came, back_y, d_terms[1]
+    )
+    d_came, qa_came = to_y(d_send), to_core(qa_other)
     u_part = both(u_terms[0], u_came)
-    u_z = along_z(u_part)
+    u_z2, u_z3 = z_far(u_part)
     dq_b, dkv_b, p_own, p_y, p_z, sums = call(
         back_b_kernel,
-        [SM] + [VM] * 14 + [AN] * 13,
+        [VM] * 14 + [AN] * 13,
         [VM] * 6,
         [
             shape_of((tok, width // 2), bf),
@@ -1128,81 +1157,85 @@
         flops=6 * 10**9,
         vmem=20, moved=10 * 10**6,
     )(
-        coords, start, queries, kv, lse, grad_attended, vec_g, upb_g, dq_a, dkv_a,
+        start, queries, kv, lse, grad_attended, vec_g, upb_g, dq_a, dkv_a,
         own_tokens, x1, x2, x3, x4, query_key_value_weight, *got_q,
     )
-    dq_b, qa_came, d_came, p_y, *u_z = fence(dq_b, qa_came, d_came, p_y, *u_z)
+    dq_b, qa_came, d_came, p_y, u_z2, u_z3 = fence(
+        dq_b, qa_came, d_came, p_y, u_z2, u_z3
+    )
+    p_came = to_y(p_y)
     qa_1 = both(qa_mine, qa_came)
+    qa_send = b16(qa_1(1))
+    qa_x = to_x(qa_send[:, :, :96])
     d_part = both(d_terms[0], d_came)
-    qa_x, p_came = to_x(b16(qa_1(1))), to_y(p_y)
-    d_z = along_z(d_part)
+    d_z2, d_z3 = z_far(d_part)
+    u_z1 = to_z(b16(u_part(1) + f32(u_z2)), 1)
     qb_other, qb_mine = call(
         back_c_kernel,
-        [SM] + [VM] * 4,
+        [VM] * 4,
         [AN] * 2,
         [
-            shape_of((2, 2, 4, 32, 3 * width // 2), bf),
-            shape_of((2, 2, 4, 32, 3 * width // 2), bf),
+            shape_of((2, 2, 4, 80, width // 2), bf),
+            shape_of((2, 2, 4, 80, width // 2), bf),
         ],
-        [pltpu.VMEM((2, 2, 8, 32, 3 * width // 2), bf), dma((32,))],
+        [pltpu.VMEM((2, 2, 8, 80, width // 2), bf), dma((32,))],
         flops=3 * 10**9,
         vmem=12, moved=6 * 10**6,
-    )(coords, normed, dq_b, dkv_b, sums)
-    qb_other, qa_x, p_came, *d_z = fence(qb_other, qa_x, p_came, *d_z)
+    )(normed, dq_b, dkv_b, sums)
+    qb_other, qa_x, p_came, d_z2, d_z3, u_z1, qa_rest = fence(
+        qb_other, qa_x, p_came, d_z2, d_z3, u_z1, qa_send[:, :, 96:]
+    )
+    qb_came, qa_x2 = to_core(qb_other), to_x(qa_rest)
     even = y == 0
     sum_own = p_own + jnp.where(even, f32(p_came[0]), 0.0)
     sum_4 = b16(f32(p_z[1]) + jnp.where(even, 0.0, f32(p_came[1])))
+    sum_2 = f32(p_z[0]) + jnp.where(even, f32(p_came[1]), f32(p_came[0]))
+    qb_came, qa_x, qa_x2, sum_4, d_z2 = fence(qb_came, qa_x, qa_x2, sum_4, d_z2)
 
     def qa_2(*index):
-        return qa_1(0, *index) + f32(qa_x[index])
-
-    f_tot = join(z_sum(u_part, u_z), z_sum(d_part, d_z))
-    qb_came, qa_y, hop, f_x = fence(
-        to_core(qb_other), to_y(b16(qa_2(1))), to_z(sum_4, 3), to_x(f_tot)
-    )
+        return qa_1(0, *index) + jnp.concatenate([f32(qa_x[index]), f32(qa_x2[index])], axis=-2)
+
     qb_1 = both(qb_mine, qb_came)
-
-    def qa_3(*index):
-        return qa_2(0, *index) + f32(qa_y[index])
-
-    qb_x, *qa_z = fence(to_x(b16(qb_1(1))), *along_z(qa_3))
-    qa_sum = z_sum(qa_3, qa_z)
+    qb_x, qa_y, hop, d_z1 = fence(
+        to_x(b16(qb_1(1))), to_y(b16(qa_2(1))), to_z(sum_4, 3), to_z(b16(d_part(1) + f32(d_z2)), 1)
+    )
 
     def qb_2(*index):
         return qb_1(0, *index) + f32(qb_x[index])
 
-    sum_2 = b16(f32(p_z[0]) + jnp.where(even, f32(p_came[1]), f32(p_came[0])) + f32(hop))
-    qb_y, back_2, a_x, a_c, a_xc = fence(
-        to_y(b16(qb_2(1))), to_z(sum_2, 3), to_x(qa_sum), to_core(qa_sum), swap_rep(qa_sum, 3)
-    )
-
-    def qb_3(*index):
-        return qb_2(0, *index) + f32(qb_y[index])
-
-    f_tot, f_x = fence(f_tot, f_x, back_2, qb_y)[:2]
-    *qb_z, f_c, f_xc = fence(*along_z(qb_3), to_core(f_tot), to_core(f_x))
-    qb_sum = z_sum(qb_3, qb_z)
-    b_x, b_c, b_xc = to_x(qb_sum), to_core(qb_sum), swap_rep(qb_sum, 3)
+    f_tot = join(z_sum(u_part, u_z1, u_z3), z_sum(d_part, d_z1, d_z3))
+    f_tot, hop = fence(f_tot, hop)
+    qb_y, back_2, f_x = fence(to_y(b16(qb_2(1))), to_z(b16(sum_2 + f32(hop)), 3), to_x(f_tot))
+
+    def q_3(*index):
+        first = qa_2(0, *index) + f32(qa_y[index])
+        return jnp.concatenate([first, qb_2(0, *index) + f32(qb_y[index])], axis=-2)
+
+    f_tot, f_x, back_2, qb_y = fence(f_tot, f_x, back_2, qb_y)
+    *q_z, f_tot, f_x = fence(*(to_z(b16(q_3(step)), step) for step in (1, 2, 3)), f_tot, f_x)
+    f_c, f_xc = to_core(f_tot), to_core(f_x)
+    q_sum = z_sum(q_3, *q_z)
+    q_fx, q_fc, q_fxc = to_x(q_sum), to_core(q_sum), swap_rep(q_sum, 3)
     result = b16(residual + vec[7:8] + keep_a[1] + f32(came_a[1]) + f32(back_y))
     grad_tokens = call(
         tokens_kernel, [VM] * 5, VM, shape_of((tok, width), fl), vmem=4, moved=3 * 10**6
     )(sum_own, back_2, grad_first, own_tokens, vec)
     grad_up, grad_down = call(
         finish_f_kernel,
-        [SM] + [VM] * 4,
+        [VM] * 4,
         [VM] * 2,
         [shape_of(up_weight.shape, fl), shape_of(down_weight.shape, fl)],
         [pltpu.VMEM((4, 96, width), bf)],
         vmem=8, moved=4 * 10**6,
-    )(coords, f_tot, f_x, f_c, f_xc)
+    )(f_tot, f_x, f_c, f_xc)
     grad_qkv, grad_out = call(
         finish_q_kernel,
-        [SM] + [VM] * 8,
+        [VM] * 4,
         [VM] * 2,
         [shape_of(query_key_value_weight.shape, fl), shape_of(output_weight.shape, fl)],
         vmem=8, moved=3 * 10**6,
-    )(coords, qa_sum, a_x, a_c, a_xc, qb_sum, b_x, b_c, b_xc)
-    sums = f32(qb_sum[24:32, :256])
+    )(q_sum, q_fx, q_fc, q_fxc)
+    sums = f32(q_sum[192:200, :256])
     part = ln_gains.shape[1]
     return (
         result[None],

time: 225 us -> 213 us (0.947)
  starting transfers between devices: 66 us -> 57.7 us
  Pallas kernels: 70.4 us -> 64.8 us
  waiting for transfers between devices: 80.1 us -> 83.2 us
    ppermute x22 -> x19, waiting for transfers between devices: 45.9 us -> 56.4 us  [to_z(): lax.ppermute(value, 'seq', [(k, (k + 2 * steps) % 8) for k in range(8)])]
    ppermute x22 -> x19, starting transfers between devices: 35.6 us -> 27.3 us  [to_z(): lax.ppermute(value, 'seq', [(k, (k + 2 * steps) % 8) for k in range(8)])]
    ppermute x32 -> x30, waiting for transfers between devices: 28.7 us -> 22 us  [swap_rep(): return lax.ppermute(value, 'rep', [(k, k ^ bit) for k in range(4)])]
    pallas_call x9 -> x10, Pallas kernels: 64.2 us -> 58.5 us  [the longest x1 14 us: on_device_fast(): call(front_kernel, [VM] * 6 + [AN] * 15, [VM] * 11, [shape_of((tok, width...]
    ppermute x32 -> x30, starting transfers between devices: 18.5 us -> 16.8 us  [swap_rep(): return lax.ppermute(value, 'rep', [(k, k ^ bit) for k in range(4)])]
  transfers between devices with their start and end apart: 65 -> 60, of which waited for: 31 -> 27; matrix products, arithmetic and copies ran while one was open for 3% -> 2% of each run, Pallas kernels for 31% -> 30%
where the time goes in v5:
time: 213 us; the launch traced here: 212 us
  waiting for transfers between devices  83.2 us (39%)
  Pallas kernels  64.8 us (30%)
  starting transfers between devices  57.7 us (27%)
  other arithmetic  3.01 us (1%)
  local copies, waits for them, and re-layouts  2.13 us (1%)
    ppermute x19, waiting for transfers between devices, to_z(): lax.ppermute(value, 'seq', [(k, (k + 2 * steps) % 8) for k in range(8)])  56.4 us
    ppermute x19, starting transfers between devices, to_z(): lax.ppermute(value, 'seq', [(k, (k + 2 * steps) % 8) for k in range(8)])  27.3 us
    ppermute x30, waiting for transfers between devices, swap_rep(): return lax.ppermute(value, 'rep', [(k, k ^ bit) for k in range(4)])  22 us
    ppermute x30, starting transfers between devices, swap_rep(): return lax.ppermute(value, 'rep', [(k, k ^ bit) for k in range(4)])  16.8 us
    pallas_call x1, Pallas kernels, on_device_fast(): call(front_kernel, [VM] * 6 + [AN] * 15, [VM] * 11, [shape_of((tok, width...  14 us
    ppermute x11, starting transfers between devices, to_y(): return lax.ppermute(value, 'seq', [(k, k ^ 1) for k in range(8)])  13.6 us
    pallas_call x1, Pallas kernels, on_device_fast(): call(back_a_kernel, [VM] * 7, [AN] * 2 + [VM] * 2, [shape_of((2, 2, 4, 12...  10.9 us
    pallas_call x1, Pallas kernels, on_device_fast(): call(back_b_kernel, [VM] * 14 + [AN] * 13, [VM] * 6, [shape_of((tok, widt...  10.8 us
  transfers between devices with their start and end apart: 60, of which 27 were waited for; matrix products, arithmetic and copies ran while one was open for 2% of the time, Pallas kernels for 30%

profile of v5, /device:TPU:0, one launch (start us, length us, event | category | flops | bytes accessed | tf_op | source)
XLA Modules:
  0.0 211.9 jit_solution(11600988664703056)
XLA Ops:
  0.6 3.0 %collective-permute-start.3 = (bf16[192,768]{1,0:T(8,128)(2,1)}, bf16[192,768]{1,0:T(8,128)(2,1)S(1)}, u32[]{:S(2)}, u32[]{:S(2)}) collective-permute-start(bf16[192,768]{1,0:T(8,128)(2,1)} %bitcast.196), channel_id=1, source_target_pairs={{0,16},{8,24},{16,0},{24,8},{1,17},{9,25},{17,1},{25,9},{2,18},{10... | collective-permute-start | bytes 884744 | tf_op jit(solution)/shard_map/ppermute | solution.py:918
  3.6 2.6 %shard_map.186 = (bf16[200,768]{1,0:T(8,128)(2,1)}, bf16[48,1664]{1,0:T(8,128)(2,1)}, bf16[192,768]{1,0:T(8,128)(2,1)}) custom-call(bf16[1,192,768]{2,1,0:T(8,128)(2,1)} %tokens.1, s32[1,192]{1,0:T(1,128)} %segs.1, bf16[96,2304]{1,0:T(8,128)(2,1)} %own.3, bf16[96,768]{1,0:T(8,128)(2,1)} %own_o.1, bf16[96,3072]{1,0:T(8,128)(2,1)} %up.1, ...), custom_call_target="tpu_custom_call" | custom-call | bytes 4000000 | tf_op jit(solution)/shard_map/pallas_call | solution.py:962
  7.9 2.2 %collective-permute-start.1 = (bf16[48,1664]{1,0:T(8,128)(2,1)}, bf16[48,1664]{1,0:T(8,128)(2,1)S(1)}, u32[]{:S(2)}, u32[]{:S(2)}) collective-permute-start(bf16[48,1664]{1,0:T(8,128)(2,1)} %get-tuple-element.182.first), channel_id=1, source_target_pairs={{0,6},{1,7},{2,0},{3,1},{4,2},{5,3},{6,4},{7,5},{8,14},{9,15},{10,... | collective-permute-start | bytes 479240 | tf_op jit(solution)/shard_map/ppermute | solution.py:934
  11.6 3.7 %collective-permute-done = bf16[48,1664]{1,0:T(8,128)(2,1)S(1)} collective-permute-done((bf16[48,1664]{1,0:T(8,128)(2,1)}, bf16[48,1664]{1,0:T(8,128)(2,1)S(1)}, u32[]{:S(2)}, u32[]{:S(2)}) %collective-permute-start) | collective-permute-done | bytes 159776 | tf_op jit(solution)/shard_map/ppermute | solution.py:934
  20.8 10.0 %collective-permute-done.4 = bf16[48,1664]{1,0:T(8,128)(2,1)S(1)} collective-permute-done((bf16[48,1664]{1,0:T(8,128)(2,1)S(1)}, bf16[48,1664]{1,0:T(8,128)(2,1)S(1)}, u32[]{:S(2)}, u32[]{:S(2)}) %collective-permute-start.4) | collective-permute-done | bytes 159776 | tf_op jit(solution)/shard_map/ppermute | solution.py:934
  33.0 8.9 %collective-permute-done.10.x4 = bf16[200,768]{1,0:T(8,128)(2,1)S(1)} collective-permute-done((bf16[200,768]{1,0:T(8,128)(2,1)S(1)}, bf16[200,768]{1,0:T(8,128)(2,1)S(1)}, u32[]{:S(2)}, u32[]{:S(2)}) %collective-permute-start.10) | collective-permute-done | bytes 307232 | tf_op jit(solution)/shard_map/ppermute | solution.py:934
  45.4 3.1 %collective-permute-start.14 = (bf16[192,768]{1,0:T(8,128)(2,1)S(1)}, bf16[192,768]{1,0:T(8,128)(2,1)S(1)}, u32[]{:S(2)}, u32[]{:S(2)}) collective-permute-start(bf16[192,768]{1,0:T(8,128)(2,1)S(1)} %copy-done.3), channel_id=1, source_target_pairs={{0,6},{1,7},{2,0},{3,1},{4,2},{5,3},{6,4},{7,5},{8,14},{9,15},{10,... | collective-permute-start | bytes 884744 | tf_op jit(solution)/shard_map/ppermute | solution.py:934
  48.5 7.0 %collective-permute-done.13.z1 = bf16[192,768]{1,0:T(8,128)(2,1)S(1)} collective-permute-done((bf16[192,768]{1,0:T(8,128)(2,1)S(1)}, bf16[192,768]{1,0:T(8,128)(2,1)S(1)}, u32[]{:S(2)}, u32[]{:S(2)}) %collective-permute-start.13) | collective-permute-done | bytes 294944 | tf_op jit(solution)/shard_map/ppermute | solution.py:934
  55.5 2.3 %collective-permute-done.14.z3 = bf16[192,768]{1,0:T(8,128)(2,1)S(1)} collective-permute-done((bf16[192,768]{1,0:T(8,128)(2,1)S(1)}, bf16[192,768]{1,0:T(8,128)(2,1)S(1)}, u32[]{:S(2)}, u32[]{:S(2)}) %collective-permute-start.14) | collective-permute-done | bytes 294944 | tf_op jit(solution)/shard_map/ppermute | solution.py:934
  59.6 2.6 %collective-permute-done.19 = bf16[48,1664]{1,0:T(8,128)(2,1)S(1)} collective-permute-done((bf16[48,1664]{1,0:T(8,128)(2,1)S(1)}, bf16[48,1664]{1,0:T(8,128)(2,1)S(1)}, u32[]{:S(2)}, u32[]{:S(2)}) %collective-permute-start.19) | collective-permute-done | bytes 159776 | tf_op jit(solution)/shard_map/ppermute | solution.py:918
  64.5 14.0 %shard_map.187 = (bf16[192,768]{1,0:T(8,128)(2,1)S(1)}, bf16[960,1536]{1,0:T(8,128)(2,1)S(1)}, bf16[960,768]{1,0:T(8,128)(2,1)S(1)}, bf16[192,768]{1,0:T(8,128)(...) custom-call(s32[1,384]{1,0:T(1,128)S(1)} %pad_add_fusion.seg, ...), custom_call_target="tpu_custom_call" | custom-call | flops 7000000000 | bytes 12000000 | tf_op jit(solution)/shard_map/pallas_call | solution.py:1014
  81.3 2.8 %shard_map.188 = (bf16[768,768]{1,0:T(8,128)(2,1)S(1)}, bf16[768,768]{1,0:T(8,128)(2,1)S(1)}) custom-call(bf16[192,768]{1,0:T(8,128)(2,1)S(1)} %copy-done.3, bf16[192,768]{1,0:T(8,128)(2,1)S(1)} %collective-permute-done.13.z1, bf16[192,768]{1,0:T(8,128)(2,1)S(1)} %collective-permute-done.22.z2, bf16[192,768]{1,0:T(8,128)(2,1)S(1)} %collective-permute-done.14.z3, ...), custom_call_target="tpu_custom_call" | custom-call | bytes 5000000 | tf_op jit(solution)/shard_map/pallas_call | solution.py:1045
  84.0 3.3 %collective-permute-done.25.h_x = bf16[192,768]{1,0:T(8,128)(2,1)S(1)} collective-permute-done((bf16[192,768]{1,0:T(8,128)(2,1)S(1)}, bf16[192,768]{1,0:T(8,128)(2,1)S(1)}, u32[]{:S(2)}, u32[]{:S(2)}) %collective-permute-start.25) | collective-permute-done | bytes 294944 | tf_op jit(solution)/shard_map/ppermute | solution.py:918
  87.3 2.3 %collective-permute-done.27.y2 = bf16[192,768]{1,0:T(8,128)(2,1)S(1)} collective-permute-done((bf16[192,768]{1,0:T(8,128)(2,1)S(1)}, bf16[192,768]{1,0:T(8,128)(2,1)S(1)}, u32[]{:S(2)}, u32[]{:S(2)}) %collective-permute-start.27) | collective-permute-done | bytes 294944 | tf_op jit(solution)/shard_map/ppermute | solution.py:930
  89.6 3.6 %shard_map.189 = (bf16[384,768]{1,0:T(8,128)(2,1)S(1)}, bf16[384,768]{1,0:T(8,128)(2,1)S(1)}, bf16[384,768]{1,0:T(8,128)(2,1)S(1)}, bf16[384,768]{1,0:T(8,128)(2...) custom-call(bf16[192,768]{1,0:T(8,128)(2,1)S(1)} %get-tuple-element., ...), custom_call_target="tpu_custom_call", output_to_operand_aliasing={{6}: (6, {}), {7}: (7, {})} | custom-call | flops 3000000000 | bytes 6000000 | tf_op jit(solution)/shard_map/pallas_call | solution.py:1059
  93.7 3.7 %shard_map.190 = (bf16[768,768]{1,0:T(8,128)(2,1)S(1)}, bf16[768,768]{1,0:T(8,128)(2,1)S(1)}, bf16[768,768]{1,0:T(8,128)(2,1)S(1)}, bf16[768,768]{1,0:T(8,128)(2...) custom-call(bf16[192,768]{1,0:T(8,128)(2,1)S(1)} %collective-permute-done.25.h_x, ...), custom_call_target="tpu_custom_call" | custom-call | flops 3000000000 | bytes 6000000 | tf_op jit(solution)/shard_map/pallas_call | solution.py:1073
  100.1 5.9 %shard_map.191 = (bf16[2,4,96,768]{3,2,1,0:T(8,128)(2,1)S(1)}, bf16[2,4,96,768]{3,2,1,0:T(8,128)(2,1)S(1)}, f32[1,768]{1,0:T(1,128)S(1)}) custom-call(bf16[768,768]{1,0:T(8,128)(2,1)S(1)} %get-tuple-element.276.hs, bf16[768,768]{1,0:T(8,128)(2,1)S(1)} %get-tuple-element.277.dys, bf16[768,768]{1,0:T(8,128)(2,1)S(1)} %get-tuple-element.278.acts, ...), custom_call_target="tpu_custom_call" | custom-call | flops 3000000000 | bytes 6000000 | tf_op jit(solution)/shard_map/pallas_call | solution.py:1085
  106.1 2.6 %collective-permute-done.31.across = bf16[192,768]{1,0:T(8,128)(2,1)S(1)} collective-permute-done((bf16[192,768]{1,0:T(8,128)(2,1)S(1)}, bf16[192,768]{1,0:T(8,128)(2,1)S(1)}, u32[]{:S(2)}, u32[]{:S(2)}) %collective-permute-start.31) | collective-permute-done | bytes 294944 | tf_op jit(solution)/shard_map/ppermute | solution.py:918
  111.8 10.9 %shard_map.193 = (bf16[2,2,4,120,384]{4,3,2,1,0:T(8,128)(2,1)S(1)}, bf16[2,2,4,120,384]{4,3,2,1,0:T(8,128)(2,1)S(1)}, bf16[192,384]{1,0:T(8,128)(2,1)S(1)}, bf16[960,768]{1,0:T(8,128)(2,1)S(1)}) custom-call(s32[1,384]{1,0:T(1,128)S(1)} %get-tuple-element.263.start_in, bf16[192,768]{1,0:T(8,128)(2,1)S(1)} %get-tuple-element.264.q_in, ...), custom_call_target="tpu_custom_call" | custom-call | flops 5000000000 | bytes 10000000 | tf_op jit(solution)/shard_map/pallas_call | solution.py:1114
  126.0 2.7 %collective-permute-start.37 = (bf16[96,768]{1,0:T(8,128)(2,1)S(1)}, bf16[96,768]{1,0:T(8,128)(2,1)S(1)}, u32[]{:S(2)}, u32[]{:S(2)}) collective-permute-start(bf16[96,768]{1,0:T(8,128)(2,1)S(1)} %get-tuple-element.359), channel_id=1, source_target_pairs={{0,6},{1,7},{2,0},{3,1},{4,2},{5,3},{6,4},{7,5},{8,14},{9,15},{10,... | collective-permute-start | bytes 442376 | tf_op jit(solution)/shard_map/ppermute | solution.py:934
  128.7 10.8 %shard_map.194 = (bf16[192,384]{1,0:T(8,128)(2,1)S(1)}, bf16[960,768]{1,0:T(8,128)(2,1)S(1)}, f32[192,768]{1,0:T(8,128)S(1)}, bf16[2,192,768]{2,1,0:T(8,128)(2,1...) custom-call(s32[1,384]{1,0:T(1,128)S(1)} %get-tuple-element.263.start_in, ...), custom_call_target="tpu_custom_call" | custom-call | flops 6000000000 | bytes 10000000 | tf_op jit(solution)/shard_map/pallas_call | solution.py:1144
  145.0 2.5 %collective-permute-start.41 = (bf16[96,768]{1,0:T(8,128)(2,1)S(1)}, bf16[96,768]{1,0:T(8,128)(2,1)S(1)}, u32[]{:S(2)}, u32[]{:S(2)}) collective-permute-start(bf16[96,768]{1,0:T(8,128)(2,1)S(1)} %get-tuple-element.357), channel_id=1, source_target_pairs={{0,6},{1,7},{2,0},{3,1},{4,2},{5,3},{6,4},{7,5},{8,14},{9,15},{10,... | collective-permute-start | bytes 442376 | tf_op jit(solution)/shard_map/ppermute | solution.py:934
  147.5 4.8 %shard_map.195 = (bf16[2,2,4,80,384]{4,3,2,1,0:T(8,128)(2,1)S(1)}, bf16[2,2,4,80,384]{4,3,2,1,0:T(8,128)(2,1)S(1)}) custom-call(bf16[960,768]{1,0:T(8,128)(2,1)S(1)} %get-tuple-element.266.h_in, bf16[192,384]{1,0:T(8,128)(2,1)S(1)} %get-tuple-element.303.dq, bf16[960,768]{1,0:T(8,128)(2,1)S(1)} %get-tuple-element.304.dkv, ...), custom_call_target="tpu_custom_call" | custom-call | flops 3000000000 | bytes 6000000 | tf_op jit(solution)/shard_map/pallas_call | solution.py:1173
  157.6 5.5 %collective-permute-done.44 = bf16[2,4,24,384]{3,2,1,0:T(8,128)(2,1)S(1)} collective-permute-done((bf16[2,4,24,384]{3,2,1,0:T(8,128)(2,1)S(1)}, bf16[2,4,24,384]{3,2,1,0:T(8,128)(2,1)S(1)}, u32[]{:S(2)}, u32[]{:S(2)}) %collective-permute-start.44) | collective-permute-done | bytes 147488 | tf_op jit(solution)/shard_map/ppermute | solution.py:918
  165.2 3.0 %collective-permute-start.47 = (bf16[192,768]{1,0:T(8,128)(2,1)S(1)}, bf16[192,768]{1,0:T(8,128)(2,1)S(1)}, u32[]{:S(2)}, u32[]{:S(2)}) collective-permute-start(bf16[192,768]{1,0:T(8,128)(2,1)S(1)} %fusion.18), channel_id=1, source_target_pairs={{0,6},{1,7},{2,0},{3,1},{4,2},{5,3},{6,4},{7,5},{8,14},{9,15},{10,... | collective-permute-start | bytes 884744 | tf_op jit(solution)/shard_map/ppermute | solution.py:934
  168.4 9.3 %collective-permute-done.48 = bf16[96,768]{1,0:T(8,128)(2,1)S(1)} collective-permute-done((bf16[96,768]{1,0:T(8,128)(2,1)S(1)}, bf16[96,768]{1,0:T(8,128)(2,1)S(1)}, u32[]{:S(2)}, u32[]{:S(2)}) %collective-permute-start.48) | collective-permute-done | bytes 147488 | tf_op jit(solution)/shard_map/ppermute | solution.py:934
  179.7 2.1 collective-permute-start.50
  184.1 2.4 %collective-permute-done.50.near = bf16[192,768]{1,0:T(8,128)(2,1)S(1)} collective-permute-done((bf16[192,768]{1,0:T(8,128)(2,1)S(1)}, bf16[192,768]{1,0:T(8,128)(2,1)S(1)}, u32[]{:S(2)}, u32[]{:S(2)}) %collective-permute-start.50) | collective-permute-done | bytes 294944 | tf_op jit(solution)/shard_map/ppermute | solution.py:934
  186.4 2.0 collective-permute-done.51.fx
  193.4 2.6 %collective-permute-done.54 = bf16[200,384]{1,0:T(8,128)(2,1)S(1)} collective-permute-done((bf16[200,384]{1,0:T(8,128)(2,1)S(1)}, bf16[200,384]{1,0:T(8,128)(2,1)S(1)}, u32[]{:S(2)}, u32[]{:S(2)}) %collective-permute-start.54) | collective-permute-done | bytes 153632 | tf_op jit(solution)/shard_map/ppermute | solution.py:934
  196.0 5.6 %collective-permute-done.53 = bf16[200,384]{1,0:T(8,128)(2,1)S(1)} collective-permute-done((bf16[200,384]{1,0:T(8,128)(2,1)S(1)}, bf16[200,384]{1,0:T(8,128)(2,1)S(1)}, u32[]{:S(2)}, u32[]{:S(2)}) %collective-permute-start.53) | collective-permute-done | bytes 153632 | tf_op jit(solution)/shard_map/ppermute | solution.py:934
  206.3 2.3 %collective-permute-done.55.fx = bf16[200,384]{1,0:T(8,128)(2,1)S(1)} collective-permute-done((bf16[200,384]{1,0:T(8,128)(2,1)S(1)}, bf16[200,384]{1,0:T(8,128)(2,1)S(1)}, u32[]{:S(2)}, u32[]{:S(2)}) %collective-permute-start.55) | collective-permute-done | bytes 153632 | tf_op jit(solution)/shard_map/ppermute | solution.py:918
  (157 shorter events, 60.7 us)
Async XLA Ops:
  0.6 16.2 %collective-permute-start.3 = (bf16[192,768]{1,0:T(8,128)(2,1)}, bf16[192,768]{1,0:T(8,128)(2,1)S(1)}, u32[]{:S(2)}, u32[]{:S(2)}) collective-permute-start(bf16[192,768]{1,0:T(8,128)(2,1)} %bitcast.196), channel_id=1, source_target_pairs={{0,16},{8,24},{16,0},{24,8},{1,17},{9,25},{17,1},{25,9},{2,18},{10... | collective-permute-start | bytes 884744 | tf_op jit(solution)/shard_map/ppermute | solution.py:918
  16.8 14.0 %collective-permute-start.5 = (bf16[200,768]{1,0:T(8,128)(2,1)}, bf16[200,768]{1,0:T(8,128)(2,1)S(1)}, u32[]{:S(2)}, u32[]{:S(2)}) collective-permute-start(bf16[200,768]{1,0:T(8,128)(2,1)} %get-tuple-element.187.xo), channel_id=1, source_target_pairs={{0,2},{1,3},{2,4},{3,5},{4,6},{5,7},{6,0},{7,1},{8,10},{9,11},{10,... | collective-permute-start | bytes 921608 | tf_op jit(solution)/shard_map/ppermute | solution.py:934
  17.9 12.9 %collective-permute-start.7 = (bf16[192,768]{1,0:T(8,128)(2,1)}, bf16[192,768]{1,0:T(8,128)(2,1)S(1)}, u32[]{:S(2)}, u32[]{:S(2)}) collective-permute-start(bf16[192,768]{1,0:T(8,128)(2,1)} %get-tuple-element.202.own), channel_id=1, source_target_pairs={{0,1},{1,0},{2,3},{3,2},{4,5},{5,4},{6,7},{7,6},{8,9},{9,8},{10,11... | collective-permute-start | bytes 884744 | tf_op jit(solution)/shard_map/ppermute | solution.py:930
  19.5 11.3 %collective-permute-start.4 = (bf16[48,1664]{1,0:T(8,128)(2,1)S(1)}, bf16[48,1664]{1,0:T(8,128)(2,1)S(1)}, u32[]{:S(2)}, u32[]{:S(2)}) collective-permute-start(bf16[48,1664]{1,0:T(8,128)(2,1)S(1)} %collective-permute-done), channel_id=1, source_target_pairs={{0,2},{1,3},{2,4},{3,5},{4,6},{5,7},{6,0},{7,1},{8,10},{9,11},{10,... | collective-permute-start | bytes 479240 | tf_op jit(solution)/shard_map/ppermute | solution.py:934
  20.2 10.6 %collective-permute-start.6 = (bf16[48,1664]{1,0:T(8,128)(2,1)S(1)}, bf16[48,1664]{1,0:T(8,128)(2,1)S(1)}, u32[]{:S(2)}, u32[]{:S(2)}) collective-permute-start(bf16[48,1664]{1,0:T(8,128)(2,1)S(1)} %collective-permute-done.2), channel_id=1, source_target_pairs={{0,16},{8,24},{16,0},{24,8},{1,17},{9,25},{17,1},{25,9},{2,18},{10... | collective-permute-start | bytes 479240 | tf_op jit(solution)/shard_map/ppermute | solution.py:918
  30.8 11.4 %collective-permute-start.8 = (bf16[144,1664]{1,0:T(8,128)(2,1)S(1)}, bf16[144,1664]{1,0:T(8,128)(2,1)S(1)}, u32[]{:S(2)}, u32[]{:S(2)}) collective-permute-start(bf16[144,1664]{1,0:T(8,128)(2,1)S(1)} %pad_maximum_fusion.2), channel_id=1, source_target_pairs={{0,1},{1,0},{2,3},{3,2},{4,5},{5,4},{6,7},{7,6},{8,9},{9,8},{10,11... | collective-permute-start | bytes 1437704 | tf_op jit(solution)/shard_map/ppermute | solution.py:930
  32.4 11.0 %collective-permute-start.9 = (bf16[144,1664]{1,0:T(8,128)(2,1)S(1)}, bf16[144,1664]{1,0:T(8,128)(2,1)S(1)}, u32[]{:S(2)}, u32[]{:S(2)}) collective-permute-start(bf16[144,1664]{1,0:T(8,128)(2,1)S(1)} %pad_maximum_fusion.2), channel_id=1, source_target_pairs={{0,16},{8,24},{16,0},{24,8},{1,17},{9,25},{17,1},{25,9},{2,18},{10... | collective-permute-start | bytes 1437704 | tf_op jit(solution)/shard_map/ppermute | solution.py:918
  43.6 14.2 %collective-permute-start.11 = (bf16[2,200,768]{2,1,0:T(8,128)(2,1)S(1)}, bf16[2,200,768]{2,1,0:T(8,128)(2,1)S(1)}, u32[]{:S(2)}, u32[]{:S(2)}) collective-permute-start(bf16[2,200,768]{2,1,0:T(8,128)(2,1)S(1)} %pad_maximum_fusion), channel_id=1, source_target_pairs={{0,1},{1,0},{2,3},{3,2},{4,5},{5,4},{6,7},{7,6},{8,9},{9,8},{10,11... | collective-permute-start | bytes 1843208 | tf_op jit(solution)/shard_map/ppermute | solution.py:930
  44.2 13.7 %collective-permute-start.12 = (bf16[144,1664]{1,0:T(8,128)(2,1)S(1)}, bf16[144,1664]{1,0:T(8,128)(2,1)S(1)}, u32[]{:S(2)}, u32[]{:S(2)}) collective-permute-start(bf16[144,1664]{1,0:T(8,128)(2,1)S(1)} %collective-permute-done.8), channel_id=1, source_target_pairs={{0,16},{8,24},{16,0},{24,8},{1,17},{9,25},{17,1},{25,9},{2,18},{10... | collective-permute-start | bytes 1437704 | tf_op jit(solution)/shard_map/ppermute | solution.py:918
  44.7 10.8 %collective-permute-start.13 = (bf16[192,768]{1,0:T(8,128)(2,1)S(1)}, bf16[192,768]{1,0:T(8,128)(2,1)S(1)}, u32[]{:S(2)}, u32[]{:S(2)}) collective-permute-start(bf16[192,768]{1,0:T(8,128)(2,1)S(1)} %copy-done.3), channel_id=1, source_target_pairs={{0,2},{1,3},{2,4},{3,5},{4,6},{5,7},{6,0},{7,1},{8,10},{9,11},{10,... | collective-permute-start | bytes 884744 | tf_op jit(solution)/shard_map/ppermute | solution.py:934
  45.4 12.4 %collective-permute-start.14 = (bf16[192,768]{1,0:T(8,128)(2,1)S(1)}, bf16[192,768]{1,0:T(8,128)(2,1)S(1)}, u32[]{:S(2)}, u32[]{:S(2)}) collective-permute-start(bf16[192,768]{1,0:T(8,128)(2,1)S(1)} %copy-done.3), channel_id=1, source_target_pairs={{0,6},{1,7},{2,0},{3,1},{4,2},{5,3},{6,4},{7,5},{8,14},{9,15},{10,... | collective-permute-start | bytes 884744 | tf_op jit(solution)/shard_map/ppermute | solution.py:934
  62.2 16.4 %collective-permute-start.23 = (bf16[192,768]{1,0:T(8,128)(2,1)S(1)}, bf16[192,768]{1,0:T(8,128)(2,1)S(1)}, u32[]{:S(2)}, u32[]{:S(2)}) collective-permute-start(bf16[192,768]{1,0:T(8,128)(2,1)S(1)} %bitcast.197), channel_id=1, source_target_pairs={{0,8},{8,0},{16,24},{24,16},{1,9},{9,1},{17,25},{25,17},{2,10},{10... | collective-permute-start | bytes 884744 | tf_op jit(solution)/shard_map/ppermute | solution.py:918
  62.5 16.1 %collective-permute-start.24 = (bf16[192,768]{1,0:T(8,128)(2,1)S(1)}, bf16[192,768]{1,0:T(8,128)(2,1)S(1)}, u32[]{:S(2)}, u32[]{:S(2)}) collective-permute-start(bf16[192,768]{1,0:T(8,128)(2,1)S(1)} %collective-permute-done.3.dy_x), channel_id=1, source_target_pairs={{0,8},{8,0},{16,24},{24,16},{1,9},{9,1},{17,25},{25,17},{2,10},{10... | collective-permute-start | bytes 884744 | tf_op jit(solution)/shard_map/ppermute | solution.py:918
  62.7 15.9 %collective-permute-start.21 = (bf16[384,768]{1,0:T(8,128)(2,1)S(1)}, bf16[384,768]{1,0:T(8,128)(2,1)S(1)}, u32[]{:S(2)}, u32[]{:S(2)}) collective-permute-start(bf16[384,768]{1,0:T(8,128)(2,1)S(1)} %pad_maximum_fusion.1), channel_id=1, source_target_pairs={{0,1},{1,0},{2,3},{3,2},{4,5},{5,4},{6,7},{7,6},{8,9},{9,8},{10,11... | collective-permute-start | bytes 1769480 | tf_op jit(solution)/shard_map/ppermute | solution.py:930
  64.2 14.4 %collective-permute-start.22 = (bf16[192,768]{1,0:T(8,128)(2,1)S(1)}, bf16[192,768]{1,0:T(8,128)(2,1)S(1)}, u32[]{:S(2)}, u32[]{:S(2)}) collective-permute-start(bf16[192,768]{1,0:T(8,128)(2,1)S(1)} %collective-permute-done.13.z1), channel_id=1, source_target_pairs={{0,2},{1,3},{2,4},{3,5},{4,6},{5,7},{6,0},{7,1},{8,10},{9,11},{10,... | collective-permute-start | bytes 884744 | tf_op jit(solution)/shard_map/ppermute | solution.py:934
  108.7 14.1 %collective-permute-start.33 = (bf16[192,768]{1,0:T(8,128)(2,1)S(1)}, bf16[192,768]{1,0:T(8,128)(2,1)S(1)}, u32[]{:S(2)}, u32[]{:S(2)}) collective-permute-start(bf16[192,768]{1,0:T(8,128)(2,1)S(1)} %fusion.16), channel_id=1, source_target_pairs={{0,16},{8,24},{16,0},{24,8},{1,17},{9,25},{17,1},{25,9},{2,18},{10... | collective-permute-start | bytes 884744 | tf_op jit(solution)/shard_map/ppermute | solution.py:918
  109.4 14.3 %collective-permute-start.32 = (bf16[4,96,768]{2,1,0:T(8,128)(2,1)S(1)}, bf16[4,96,768]{2,1,0:T(8,128)(2,1)S(1)}, u32[]{:S(2)}, u32[]{:S(2)}) collective-permute-start(bf16[4,96,768]{2,1,0:T(8,128)(2,1)S(1)} %slice_bitcast_fusion.1), channel_id=1, source_target_pairs={{0,1},{1,0},{2,3},{3,2},{4,5},{5,4},{6,7},{7,6},{8,9},{9,8},{10,11... | collective-permute-start | bytes 1769480 | tf_op jit(solution)/shard_map/ppermute | solution.py:930
  123.7 15.9 %collective-permute-start.34 = (bf16[2,2,4,120,384]{4,3,2,1,0:T(8,128)(2,1)S(1)}, bf16[2,2,4,120,384]{4,3,2,1,0:T(8,128)(2,1)S(1)}, u32[]{:S(2)}, u32[]{:S(2)}) collective-permute-start(bf16[2,2,4,120,384]{4,3,2,1,0:T(8,128)(2,1)S(1)} %get-tuple-element.299), channel_id=1, source_target_pairs={{0,8},{8,0},{16,24},{24,16},{1,9},{9,1},{17,25},{25,17},{2,10},{10... | collective-permute-start | bytes 4423688 | tf_op jit(solution)/shard_map/ppermute | solution.py:918
  123.7 15.9 %collective-permute-start.35 = (bf16[4,96,768]{2,1,0:T(8,128)(2,1)S(1)}, bf16[4,96,768]{2,1,0:T(8,128)(2,1)S(1)}, u32[]{:S(2)}, u32[]{:S(2)}) collective-permute-start(bf16[4,96,768]{2,1,0:T(8,128)(2,1)S(1)} %slice_bitcast_fusion), channel_id=1, source_target_pairs={{0,1},{1,0},{2,3},{3,2},{4,5},{5,4},{6,7},{7,6},{8,9},{9,8},{10,11... | collective-permute-start | bytes 1769480 | tf_op jit(solution)/shard_map/ppermute | solution.py:930
  124.8 14.7 %collective-permute-start.36 = (bf16[96,768]{1,0:T(8,128)(2,1)S(1)}, bf16[96,768]{1,0:T(8,128)(2,1)S(1)}, u32[]{:S(2)}, u32[]{:S(2)}) collective-permute-start(bf16[96,768]{1,0:T(8,128)(2,1)S(1)} %get-tuple-element.360), channel_id=1, source_target_pairs={{0,2},{1,3},{2,4},{3,5},{4,6},{5,7},{6,0},{7,1},{8,10},{9,11},{10,... | collective-permute-start | bytes 442376 | tf_op jit(solution)/shard_map/ppermute | solution.py:934
  126.0 13.6 %collective-permute-start.37 = (bf16[96,768]{1,0:T(8,128)(2,1)S(1)}, bf16[96,768]{1,0:T(8,128)(2,1)S(1)}, u32[]{:S(2)}, u32[]{:S(2)}) collective-permute-start(bf16[96,768]{1,0:T(8,128)(2,1)S(1)} %get-tuple-element.359), channel_id=1, source_target_pairs={{0,6},{1,7},{2,0},{3,1},{4,2},{5,3},{6,4},{7,5},{8,14},{9,15},{10,... | collective-permute-start | bytes 442376 | tf_op jit(solution)/shard_map/ppermute | solution.py:934
  139.9 15.7 %collective-permute-start.38 = (bf16[2,4,96,384]{3,2,1,0:T(8,128)(2,1)S(1)}, bf16[2,4,96,384]{3,2,1,0:T(8,128)(2,1)S(1)}, u32[]{:S(2)}, u32[]{:S(2)}) collective-permute-start(bf16[2,4,96,384]{3,2,1,0:T(8,128)(2,1)S(1)} %slice.360), channel_id=1, source_target_pairs={{0,16},{8,24},{16,0},{24,8},{1,17},{9,25},{17,1},{25,9},{2,18},{10... | collective-permute-start | bytes 1769480 | tf_op jit(solution)/shard_map/ppermute | solution.py:918
  141.4 14.6 %collective-permute-start.39 = (bf16[2,192,768]{2,1,0:T(8,128)(2,1)S(1)}, bf16[2,192,768]{2,1,0:T(8,128)(2,1)S(1)}, u32[]{:S(2)}, u32[]{:S(2)}) collective-permute-start(bf16[2,192,768]{2,1,0:T(8,128)(2,1)S(1)} %get-tuple-element.309), channel_id=1, source_target_pairs={{0,1},{1,0},{2,3},{3,2},{4,5},{5,4},{6,7},{7,6},{8,9},{9,8},{10,11... | collective-permute-start | bytes 1769480 | tf_op jit(solution)/shard_map/ppermute | solution.py:930
  142.4 9.9 %collective-permute-start.42 = (bf16[96,768]{1,0:T(8,128)(2,1)S(1)}, bf16[96,768]{1,0:T(8,128)(2,1)S(1)}, u32[]{:S(2)}, u32[]{:S(2)}) collective-permute-start(bf16[96,768]{1,0:T(8,128)(2,1)S(1)} %fusion.26), channel_id=1, source_target_pairs={{0,2},{1,3},{2,4},{3,5},{4,6},{5,7},{6,0},{7,1},{8,10},{9,11},{10,... | collective-permute-start | bytes 442376 | tf_op jit(solution)/shard_map/ppermute | solution.py:934
  143.6 10.4 %collective-permute-start.40 = (bf16[96,768]{1,0:T(8,128)(2,1)S(1)}, bf16[96,768]{1,0:T(8,128)(2,1)S(1)}, u32[]{:S(2)}, u32[]{:S(2)}) collective-permute-start(bf16[96,768]{1,0:T(8,128)(2,1)S(1)} %get-tuple-element.358), channel_id=1, source_target_pairs={{0,2},{1,3},{2,4},{3,5},{4,6},{5,7},{6,0},{7,1},{8,10},{9,11},{10,... | collective-permute-start | bytes 442376 | tf_op jit(solution)/shard_map/ppermute | solution.py:934
  145.0 10.5 %collective-permute-start.41 = (bf16[96,768]{1,0:T(8,128)(2,1)S(1)}, bf16[96,768]{1,0:T(8,128)(2,1)S(1)}, u32[]{:S(2)}, u32[]{:S(2)}) collective-permute-start(bf16[96,768]{1,0:T(8,128)(2,1)S(1)} %get-tuple-element.357), channel_id=1, source_target_pairs={{0,6},{1,7},{2,0},{3,1},{4,2},{5,3},{6,4},{7,5},{8,14},{9,15},{10,... | collective-permute-start | bytes 442376 | tf_op jit(solution)/shard_map/ppermute | solution.py:934
  163.4 14.3 %collective-permute-start.45 = (bf16[2,4,80,384]{3,2,1,0:T(8,128)(2,1)S(1)}, bf16[2,4,80,384]{3,2,1,0:T(8,128)(2,1)S(1)}, u32[]{:S(2)}, u32[]{:S(2)}) collective-permute-start(bf16[2,4,80,384]{3,2,1,0:T(8,128)(2,1)S(1)} %fusion.12), channel_id=1, source_target_pairs={{0,16},{8,24},{16,0},{24,8},{1,17},{9,25},{17,1},{25,9},{2,18},{10... | collective-permute-start | bytes 1474568 | tf_op jit(solution)/shard_map/ppermute | solution.py:918
  164.1 13.6 %collective-permute-start.46 = (bf16[4,120,384]{2,1,0:T(8,128)(2,1)S(1)}, bf16[4,120,384]{2,1,0:T(8,128)(2,1)S(1)}, u32[]{:S(2)}, u32[]{:S(2)}) collective-permute-start(bf16[4,120,384]{2,1,0:T(8,128)(2,1)S(1)} %fusion.1), channel_id=1, source_target_pairs={{0,1},{1,0},{2,3},{3,2},{4,5},{5,4},{6,7},{7,6},{8,9},{9,8},{10,11... | collective-permute-start | bytes 1105928 | tf_op jit(solution)/shard_map/ppermute | solution.py:930
  165.2 12.5 %collective-permute-start.47 = (bf16[192,768]{1,0:T(8,128)(2,1)S(1)}, bf16[192,768]{1,0:T(8,128)(2,1)S(1)}, u32[]{:S(2)}, u32[]{:S(2)}) collective-permute-start(bf16[192,768]{1,0:T(8,128)(2,1)S(1)} %fusion.18), channel_id=1, source_target_pairs={{0,6},{1,7},{2,0},{3,1},{4,2},{5,3},{6,4},{7,5},{8,14},{9,15},{10,... | collective-permute-start | bytes 884744 | tf_op jit(solution)/shard_map/ppermute | solution.py:934
  168.2 9.4 %collective-permute-start.48 = (bf16[96,768]{1,0:T(8,128)(2,1)S(1)}, bf16[96,768]{1,0:T(8,128)(2,1)S(1)}, u32[]{:S(2)}, u32[]{:S(2)}) collective-permute-start(bf16[96,768]{1,0:T(8,128)(2,1)S(1)} %fusion.20), channel_id=1, source_target_pairs={{0,2},{1,3},{2,4},{3,5},{4,6},{5,7},{6,0},{7,1},{8,10},{9,11},{10,... | collective-permute-start | bytes 442376 | tf_op jit(solution)/shard_map/ppermute | solution.py:934
  190.5 11.2 %collective-permute-start.53 = (bf16[200,384]{1,0:T(8,128)(2,1)S(1)}, bf16[200,384]{1,0:T(8,128)(2,1)S(1)}, u32[]{:S(2)}, u32[]{:S(2)}) collective-permute-start(bf16[200,384]{1,0:T(8,128)(2,1)S(1)} %pad_maximum_fusion.5), channel_id=1, source_target_pairs={{0,4},{1,5},{2,6},{3,7},{4,0},{5,1},{6,2},{7,3},{8,12},{9,13},{10,... | collective-permute-start | bytes 460808 | tf_op jit(solution)/shard_map/ppermute | solution.py:934
  190.6 11.1 %collective-permute-start.52 = (bf16[200,384]{1,0:T(8,128)(2,1)S(1)}, bf16[200,384]{1,0:T(8,128)(2,1)S(1)}, u32[]{:S(2)}, u32[]{:S(2)}) collective-permute-start(bf16[200,384]{1,0:T(8,128)(2,1)S(1)} %pad_maximum_fusion.4), channel_id=1, source_target_pairs={{0,2},{1,3},{2,4},{3,5},{4,6},{5,7},{6,0},{7,1},{8,10},{9,11},{10,... | collective-permute-start | bytes 460808 | tf_op jit(solution)/shard_map/ppermute | solution.py:934
  (35 other events, 265.6 us)

commit v6 on v5

--- a/solution.py
+++ b/solution.py
@@ -1129,9 +1129,6 @@
     def both(mine, came):
         return lambda *index: f32(mine[index]) + f32(came[index])
 
-    def z_far(part):
-        return to_z(b16(part(2)), 1), to_z(b16(part(3)), 3)
-
     def z_sum(part, *came):
         return b16(part(0) + sum(f32(v) for v in came))
 
@@ -1140,7 +1137,7 @@
     )
     d_came, qa_came = to_y(d_send), to_core(qa_other)
     u_part = both(u_terms[0], u_came)
-    u_z2, u_z3 = z_far(u_part)
+    u_z = [to_z(b16(u_part(step)), step) for step in (1, 2, 3)]
     dq_b, dkv_b, p_own, p_y, p_z, sums = call(
         back_b_kernel,
         [VM] * 14 + [AN] * 13,
@@ -1160,16 +1157,12 @@
         start, queries, kv, lse, grad_attended, vec_g, upb_g, dq_a, dkv_a,
         own_tokens, x1, x2, x3, x4, query_key_value_weight, *got_q,
     )
-    dq_b, qa_came, d_came, p_y, u_z2, u_z3 = fence(
-        dq_b, qa_came, d_came, p_y, u_z2, u_z3
-    )
+    dq_b, qa_came, d_came, p_y, *u_z = fence(dq_b, qa_came, d_came, p_y, *u_z)
     p_came = to_y(p_y)
     qa_1 = both(qa_mine, qa_came)
-    qa_send = b16(qa_1(1))
-    qa_x = to_x(qa_send[:, :, :96])
+    qa_x = to_x(b16(qa_1(1)))
     d_part = both(d_terms[0], d_came)
-    d_z2, d_z3 = z_far(d_part)
-    u_z1 = to_z(b16(u_part(1) + f32(u_z2)), 1)
+    d_z2 = to_z(b16(d_part(2)), 1)
     qb_other, qb_mine = call(
         back_c_kernel,
         [VM] * 4,
@@ -1182,28 +1175,30 @@
         flops=3 * 10**9,
         vmem=12, moved=6 * 10**6,
     )(normed, dq_b, dkv_b, sums)
-    qb_other, qa_x, p_came, d_z2, d_z3, u_z1, qa_rest = fence(
-        qb_other, qa_x, p_came, d_z2, d_z3, u_z1, qa_send[:, :, 96:]
-    )
-    qb_came, qa_x2 = to_core(qb_other), to_x(qa_rest)
+    qb_came = [to_core(qb_other[k]) for k in range(2)]
+    *qb_came, qa_x, p_came, d_z2 = fence(*qb_came, qa_x, p_came, d_z2)
     even = y == 0
     sum_own = p_own + jnp.where(even, f32(p_came[0]), 0.0)
     sum_4 = b16(f32(p_z[1]) + jnp.where(even, 0.0, f32(p_came[1])))
     sum_2 = f32(p_z[0]) + jnp.where(even, f32(p_came[1]), f32(p_came[0]))
-    qb_came, qa_x, qa_x2, sum_4, d_z2 = fence(qb_came, qa_x, qa_x2, sum_4, d_z2)
-
     def qa_2(*index):
-        return qa_1(0, *index) + jnp.concatenate([f32(qa_x[index]), f32(qa_x2[index])], axis=-2)
-
-    qb_1 = both(qb_mine, qb_came)
-    qb_x, qa_y, hop, d_z1 = fence(
-        to_x(b16(qb_1(1))), to_y(b16(qa_2(1))), to_z(sum_4, 3), to_z(b16(d_part(1) + f32(d_z2)), 1)
+        return qa_1(0, *index) + f32(qa_x[index])
+
+    def qb_1(side, *index):
+        return f32(qb_mine[(side,) + index]) + f32(qb_came[side][index])
+
+    qb_x, qa_y, hop, d_z1, d_z3 = fence(
+        to_x(b16(qb_1(1))),
+        to_y(b16(qa_2(1))),
+        to_z(sum_4, 3),
+        to_z(b16(d_part(1) + f32(d_z2)), 1),
+        to_z(b16(d_part(3)), 3),
     )
 
     def qb_2(*index):
         return qb_1(0, *index) + f32(qb_x[index])
 
-    f_tot = join(z_sum(u_part, u_z1, u_z3), z_sum(d_part, d_z1, d_z3))
+    f_tot = join(z_sum(u_part, *u_z), z_sum(d_part, d_z1, d_z3))
     f_tot, hop = fence(f_tot, hop)
     qb_y, back_2, f_x = fence(to_y(b16(qb_2(1))), to_z(b16(sum_2 + f32(hop)), 3), to_x(f_tot))
 
@@ -1212,22 +1207,23 @@
         return jnp.concatenate([first, qb_2(0, *index) + f32(qb_y[index])], axis=-2)
 
     f_tot, f_x, back_2, qb_y = fence(f_tot, f_x, back_2, qb_y)
-    *q_z, f_tot, f_x = fence(*(to_z(b16(q_3(step)), step) for step in (1, 2, 3)), f_tot, f_x)
-    f_c, f_xc = to_core(f_tot), to_core(f_x)
-    q_sum = z_sum(q_3, *q_z)
-    q_fx, q_fc, q_fxc = to_x(q_sum), to_core(q_sum), swap_rep(q_sum, 3)
-    result = b16(residual + vec[7:8] + keep_a[1] + f32(came_a[1]) + f32(back_y))
     grad_tokens = call(
         tokens_kernel, [VM] * 5, VM, shape_of((tok, width), fl), vmem=4, moved=3 * 10**6
     )(sum_own, back_2, grad_first, own_tokens, vec)
+    *q_z, f_tot, f_x = fence(*(to_z(b16(q_3(step)), step) for step in (1, 2, 3)), f_tot, f_x)
+    q_sum = z_sum(q_3, *q_z)
+    q_fx, q_fc, q_fxc = to_x(q_sum), to_core(q_sum), swap_rep(q_sum, 3)
     grad_up, grad_down = call(
         finish_f_kernel,
         [VM] * 4,
         [VM] * 2,
         [shape_of(up_weight.shape, fl), shape_of(down_weight.shape, fl)],
         [pltpu.VMEM((4, 96, width), bf)],
-        vmem=8, moved=4 * 10**6,
-    )(f_tot, f_x, f_c, f_xc)
+        vmem=8,
+        moved=4 * 10**6,
+    )(f_tot, f_x, to_core(f_tot), to_core(f_x))
+    q_fx, q_fc, q_fxc, grad_up, grad_down = fence(q_fx, q_fc, q_fxc, grad_up, grad_down)
+    result = b16(residual + vec[7:8] + keep_a[1] + f32(came_a[1]) + f32(back_y))
     grad_qkv, grad_out = call(
         finish_q_kernel,
         [VM] * 4,

time: 213 us -> 208 us (0.977)
  waiting for transfers between devices: 83.2 us -> 76.2 us
  starting transfers between devices: 57.7 us -> 61.1 us
    ppermute x30, waiting for transfers between devices: 22 us -> 17.1 us  [swap_rep(): return lax.ppermute(value, 'rep', [(k, k ^ bit) for k in range(4)])]
  transfers between devices with their start and end apart: 60 -> 60, of which waited for: 27 -> 24; matrix products, arithmetic and copies ran while one was open for 2% -> 2% of each run, Pallas kernels for 30% -> 31%
where the time goes in v6:
time: 208 us
  waiting for transfers between devices  76.2 us (37%)
  Pallas kernels  64.7 us (31%)
  starting transfers between devices  61.1 us (29%)
  other arithmetic  2.99 us (1%)
    ppermute x19, waiting for transfers between devices, to_z(): lax.ppermute(value, 'seq', [(k, (k + 2 * steps) % 8) for k in range(8)])  55.5 us
    ppermute x19, starting transfers between devices, to_z(): lax.ppermute(value, 'seq', [(k, (k + 2 * steps) % 8) for k in range(8)])  29.1 us
    ppermute x30, starting transfers between devices, swap_rep(): return lax.ppermute(value, 'rep', [(k, k ^ bit) for k in range(4)])  17.8 us
    ppermute x30, waiting for transfers between devices, swap_rep(): return lax.ppermute(value, 'rep', [(k, k ^ bit) for k in range(4)])  17.1 us
    ppermute x11, starting transfers between devices, to_y(): return lax.ppermute(value, 'seq', [(k, k ^ 1) for k in range(8)])  14.2 us
    pallas_call x1, Pallas kernels, on_device_fast(): call(front_kernel, [VM] * 6 + [AN] * 15, [VM] * 11, [shape_of((tok, width...  14 us
    pallas_call x1, Pallas kernels, on_device_fast(): call(back_a_kernel, [VM] * 7, [AN] * 2 + [VM] * 2, [shape_of((2, 2, 4, 12...  10.9 us
    pallas_call x1, Pallas kernels, on_device_fast(): call(back_b_kernel, [VM] * 14 + [AN] * 13, [VM] * 6, [shape_of((tok, widt...  10.8 us
  transfers between devices with their start and end apart: 60, of which 24 were waited for; matrix products, arithmetic and copies ran while one was open for 2% of the time, Pallas kernels for 31%

profile of v6, /device:TPU:0, one launch (start us, length us, event | category | flops | bytes accessed | tf_op | source)
XLA Modules:
  0.0 208.2 jit_solution(11104988546864875059)
XLA Ops:
  0.6 3.0 %collective-permute-start.3 = (bf16[192,768]{1,0:T(8,128)(2,1)}, bf16[192,768]{1,0:T(8,128)(2,1)S(1)}, u32[]{:S(2)}, u32[]{:S(2)}) collective-permute-start(bf16[192,768]{1,0:T(8,128)(2,1)} %bitcast.206), channel_id=1, source_target_pairs={{0,16},{8,24},{16,0},{24,8},{1,17},{9,25},{17,1},{25,9},{2,18},{10... | collective-permute-start | bytes 884744 | tf_op jit(solution)/shard_map/ppermute | solution.py:918
  3.6 2.6 %shard_map.186 = (bf16[200,768]{1,0:T(8,128)(2,1)}, bf16[48,1664]{1,0:T(8,128)(2,1)}, bf16[192,768]{1,0:T(8,128)(2,1)}) custom-call(bf16[1,192,768]{2,1,0:T(8,128)(2,1)} %tokens.1, s32[1,192]{1,0:T(1,128)} %segs.1, bf16[96,2304]{1,0:T(8,128)(2,1)} %own.3, bf16[96,768]{1,0:T(8,128)(2,1)} %own_o.1, bf16[96,3072]{1,0:T(8,128)(2,1)} %up.1, ...), custom_call_target="tpu_custom_call" | custom-call | bytes 4000000 | tf_op jit(solution)/shard_map/pallas_call | solution.py:962
  7.9 2.2 %collective-permute-start.1 = (bf16[48,1664]{1,0:T(8,128)(2,1)}, bf16[48,1664]{1,0:T(8,128)(2,1)S(1)}, u32[]{:S(2)}, u32[]{:S(2)}) collective-permute-start(bf16[48,1664]{1,0:T(8,128)(2,1)} %get-tuple-element.182.first), channel_id=1, source_target_pairs={{0,6},{1,7},{2,0},{3,1},{4,2},{5,3},{6,4},{7,5},{8,14},{9,15},{10,... | collective-permute-start | bytes 479240 | tf_op jit(solution)/shard_map/ppermute | solution.py:934
  11.6 3.7 %collective-permute-done = bf16[48,1664]{1,0:T(8,128)(2,1)S(1)} collective-permute-done((bf16[48,1664]{1,0:T(8,128)(2,1)}, bf16[48,1664]{1,0:T(8,128)(2,1)S(1)}, u32[]{:S(2)}, u32[]{:S(2)}) %collective-permute-start) | collective-permute-done | bytes 159776 | tf_op jit(solution)/shard_map/ppermute | solution.py:934
  20.8 10.0 %collective-permute-done.4 = bf16[48,1664]{1,0:T(8,128)(2,1)S(1)} collective-permute-done((bf16[48,1664]{1,0:T(8,128)(2,1)S(1)}, bf16[48,1664]{1,0:T(8,128)(2,1)S(1)}, u32[]{:S(2)}, u32[]{:S(2)}) %collective-permute-start.4) | collective-permute-done | bytes 159776 | tf_op jit(solution)/shard_map/ppermute | solution.py:934
  33.0 8.9 %collective-permute-done.10.x4 = bf16[200,768]{1,0:T(8,128)(2,1)S(1)} collective-permute-done((bf16[200,768]{1,0:T(8,128)(2,1)S(1)}, bf16[200,768]{1,0:T(8,128)(2,1)S(1)}, u32[]{:S(2)}, u32[]{:S(2)}) %collective-permute-start.10) | collective-permute-done | bytes 307232 | tf_op jit(solution)/shard_map/ppermute | solution.py:934
  45.4 3.1 %collective-permute-start.14 = (bf16[192,768]{1,0:T(8,128)(2,1)S(1)}, bf16[192,768]{1,0:T(8,128)(2,1)S(1)}, u32[]{:S(2)}, u32[]{:S(2)}) collective-permute-start(bf16[192,768]{1,0:T(8,128)(2,1)S(1)} %copy-done.3), channel_id=1, source_target_pairs={{0,6},{1,7},{2,0},{3,1},{4,2},{5,3},{6,4},{7,5},{8,14},{9,15},{10,... | collective-permute-start | bytes 884744 | tf_op jit(solution)/shard_map/ppermute | solution.py:934
  48.5 7.0 %collective-permute-done.13.z1 = bf16[192,768]{1,0:T(8,128)(2,1)S(1)} collective-permute-done((bf16[192,768]{1,0:T(8,128)(2,1)S(1)}, bf16[192,768]{1,0:T(8,128)(2,1)S(1)}, u32[]{:S(2)}, u32[]{:S(2)}) %collective-permute-start.13) | collective-permute-done | bytes 294944 | tf_op jit(solution)/shard_map/ppermute | solution.py:934
  55.5 2.3 %collective-permute-done.14.z3 = bf16[192,768]{1,0:T(8,128)(2,1)S(1)} collective-permute-done((bf16[192,768]{1,0:T(8,128)(2,1)S(1)}, bf16[192,768]{1,0:T(8,128)(2,1)S(1)}, u32[]{:S(2)}, u32[]{:S(2)}) %collective-permute-start.14) | collective-permute-done | bytes 294944 | tf_op jit(solution)/shard_map/ppermute | solution.py:934
  59.6 2.6 %collective-permute-done.19 = bf16[48,1664]{1,0:T(8,128)(2,1)S(1)} collective-permute-done((bf16[48,1664]{1,0:T(8,128)(2,1)S(1)}, bf16[48,1664]{1,0:T(8,128)(2,1)S(1)}, u32[]{:S(2)}, u32[]{:S(2)}) %collective-permute-start.19) | collective-permute-done | bytes 159776 | tf_op jit(solution)/shard_map/ppermute | solution.py:918
  64.5 14.0 %shard_map.187 = (bf16[192,768]{1,0:T(8,128)(2,1)S(1)}, bf16[960,1536]{1,0:T(8,128)(2,1)S(1)}, bf16[960,768]{1,0:T(8,128)(2,1)S(1)}, bf16[192,768]{1,0:T(8,128)(...) custom-call(s32[1,384]{1,0:T(1,128)S(1)} %pad_add_fusion.seg, ...), custom_call_target="tpu_custom_call" | custom-call | flops 7000000000 | bytes 12000000 | tf_op jit(solution)/shard_map/pallas_call | solution.py:1014
  81.3 2.8 %shard_map.188 = (bf16[768,768]{1,0:T(8,128)(2,1)S(1)}, bf16[768,768]{1,0:T(8,128)(2,1)S(1)}) custom-call(bf16[192,768]{1,0:T(8,128)(2,1)S(1)} %copy-done.3, bf16[192,768]{1,0:T(8,128)(2,1)S(1)} %collective-permute-done.13.z1, bf16[192,768]{1,0:T(8,128)(2,1)S(1)} %collective-permute-done.22.z2, bf16[192,768]{1,0:T(8,128)(2,1)S(1)} %collective-permute-done.14.z3, ...), custom_call_target="tpu_custom_call" | custom-call | bytes 5000000 | tf_op jit(solution)/shard_map/pallas_call | solution.py:1045
  84.0 3.3 %collective-permute-done.25.h_x = bf16[192,768]{1,0:T(8,128)(2,1)S(1)} collective-permute-done((bf16[192,768]{1,0:T(8,128)(2,1)S(1)}, bf16[192,768]{1,0:T(8,128)(2,1)S(1)}, u32[]{:S(2)}, u32[]{:S(2)}) %collective-permute-start.25) | collective-permute-done | bytes 294944 | tf_op jit(solution)/shard_map/ppermute | solution.py:918
  87.3 2.3 %collective-permute-done.27.y2 = bf16[192,768]{1,0:T(8,128)(2,1)S(1)} collective-permute-done((bf16[192,768]{1,0:T(8,128)(2,1)S(1)}, bf16[192,768]{1,0:T(8,128)(2,1)S(1)}, u32[]{:S(2)}, u32[]{:S(2)}) %collective-permute-start.27) | collective-permute-done | bytes 294944 | tf_op jit(solution)/shard_map/ppermute | solution.py:930
  89.6 3.6 %shard_map.189 = (bf16[384,768]{1,0:T(8,128)(2,1)S(1)}, bf16[384,768]{1,0:T(8,128)(2,1)S(1)}, bf16[384,768]{1,0:T(8,128)(2,1)S(1)}, bf16[384,768]{1,0:T(8,128)(2...) custom-call(bf16[192,768]{1,0:T(8,128)(2,1)S(1)} %get-tuple-element., ...), custom_call_target="tpu_custom_call", output_to_operand_aliasing={{6}: (6, {}), {7}: (7, {})} | custom-call | flops 3000000000 | bytes 6000000 | tf_op jit(solution)/shard_map/pallas_call | solution.py:1059
  93.7 3.7 %shard_map.190 = (bf16[768,768]{1,0:T(8,128)(2,1)S(1)}, bf16[768,768]{1,0:T(8,128)(2,1)S(1)}, bf16[768,768]{1,0:T(8,128)(2,1)S(1)}, bf16[768,768]{1,0:T(8,128)(2...) custom-call(bf16[192,768]{1,0:T(8,128)(2,1)S(1)} %collective-permute-done.25.h_x, ...), custom_call_target="tpu_custom_call" | custom-call | flops 3000000000 | bytes 6000000 | tf_op jit(solution)/shard_map/pallas_call | solution.py:1073
  100.1 5.9 %shard_map.191 = (bf16[2,4,96,768]{3,2,1,0:T(8,128)(2,1)S(1)}, bf16[2,4,96,768]{3,2,1,0:T(8,128)(2,1)S(1)}, f32[1,768]{1,0:T(1,128)S(1)}) custom-call(bf16[768,768]{1,0:T(8,128)(2,1)S(1)} %get-tuple-element.276.hs, bf16[768,768]{1,0:T(8,128)(2,1)S(1)} %get-tuple-element.277.dys, bf16[768,768]{1,0:T(8,128)(2,1)S(1)} %get-tuple-element.278.acts, ...), custom_call_target="tpu_custom_call" | custom-call | flops 3000000000 | bytes 6000000 | tf_op jit(solution)/shard_map/pallas_call | solution.py:1085
  106.1 2.6 %collective-permute-done.31.across = bf16[192,768]{1,0:T(8,128)(2,1)S(1)} collective-permute-done((bf16[192,768]{1,0:T(8,128)(2,1)S(1)}, bf16[192,768]{1,0:T(8,128)(2,1)S(1)}, u32[]{:S(2)}, u32[]{:S(2)}) %collective-permute-start.31) | collective-permute-done | bytes 294944 | tf_op jit(solution)/shard_map/ppermute | solution.py:918
  111.8 10.9 %shard_map.193 = (bf16[2,2,4,120,384]{4,3,2,1,0:T(8,128)(2,1)S(1)}, bf16[2,2,4,120,384]{4,3,2,1,0:T(8,128)(2,1)S(1)}, bf16[192,384]{1,0:T(8,128)(2,1)S(1)}, bf16[960,768]{1,0:T(8,128)(2,1)S(1)}) custom-call(s32[1,384]{1,0:T(1,128)S(1)} %get-tuple-element.263.start_in, bf16[192,768]{1,0:T(8,128)(2,1)S(1)} %get-tuple-element.264.q_in, ...), custom_call_target="tpu_custom_call" | custom-call | flops 5000000000 | bytes 10000000 | tf_op jit(solution)/shard_map/pallas_call | solution.py:1114
  126.0 2.5 %collective-permute-start.37 = (bf16[96,768]{1,0:T(8,128)(2,1)S(1)}, bf16[96,768]{1,0:T(8,128)(2,1)S(1)}, u32[]{:S(2)}, u32[]{:S(2)}) collective-permute-start(bf16[96,768]{1,0:T(8,128)(2,1)S(1)} %get-tuple-element.361), channel_id=1, source_target_pairs={{0,4},{1,5},{2,6},{3,7},{4,0},{5,1},{6,2},{7,3},{8,12},{9,13},{10,... | collective-permute-start | bytes 442376 | tf_op jit(solution)/shard_map/ppermute | solution.py:934
  129.7 10.8 %shard_map.194 = (bf16[192,384]{1,0:T(8,128)(2,1)S(1)}, bf16[960,768]{1,0:T(8,128)(2,1)S(1)}, f32[192,768]{1,0:T(8,128)S(1)}, bf16[2,192,768]{2,1,0:T(8,128)(2,1...) custom-call(s32[1,384]{1,0:T(1,128)S(1)} %get-tuple-element.263.start_in, ...), custom_call_target="tpu_custom_call" | custom-call | flops 6000000000 | bytes 10000000 | tf_op jit(solution)/shard_map/pallas_call | solution.py:1141
  143.8 4.8 %shard_map.195 = (bf16[2,2,4,80,384]{4,3,2,1,0:T(8,128)(2,1)S(1)}, bf16[2,2,4,80,384]{4,3,2,1,0:T(8,128)(2,1)S(1)}) custom-call(bf16[960,768]{1,0:T(8,128)(2,1)S(1)} %get-tuple-element.266.h_in, bf16[192,384]{1,0:T(8,128)(2,1)S(1)} %get-tuple-element.303.dq, bf16[960,768]{1,0:T(8,128)(2,1)S(1)} %get-tuple-element.304.dkv, ...), custom_call_target="tpu_custom_call" | custom-call | flops 3000000000 | bytes 6000000 | tf_op jit(solution)/shard_map/pallas_call | solution.py:1166
  151.1 6.0 %collective-permute-done.43 = bf16[96,768]{1,0:T(8,128)(2,1)S(1)} collective-permute-done((bf16[96,768]{1,0:T(8,128)(2,1)S(1)}, bf16[96,768]{1,0:T(8,128)(2,1)S(1)}, u32[]{:S(2)}, u32[]{:S(2)}) %collective-permute-start.43) | collective-permute-done | bytes 147488 | tf_op jit(solution)/shard_map/ppermute | solution.py:934
  158.7 2.8 %collective-permute-start.46 = (bf16[192,768]{1,0:T(8,128)(2,1)S(1)}, bf16[192,768]{1,0:T(8,128)(2,1)S(1)}, u32[]{:S(2)}, u32[]{:S(2)}) collective-permute-start(bf16[192,768]{1,0:T(8,128)(2,1)S(1)} %fusion.18), channel_id=1, source_target_pairs={{0,6},{1,7},{2,0},{3,1},{4,2},{5,3},{6,4},{7,5},{8,14},{9,15},{10,... | collective-permute-start | bytes 884744 | tf_op jit(solution)/shard_map/ppermute | solution.py:934
  164.9 3.8 %collective-permute-start.48 = (bf16[96,768]{1,0:T(8,128)(2,1)S(1)}, bf16[96,768]{1,0:T(8,128)(2,1)S(1)}, u32[]{:S(2)}, u32[]{:S(2)}) collective-permute-start(bf16[96,768]{1,0:T(8,128)(2,1)S(1)} %get-tuple-element.358), channel_id=1, source_target_pairs={{0,6},{1,7},{2,0},{3,1},{4,2},{5,3},{6,4},{7,5},{8,14},{9,15},{10,... | collective-permute-start | bytes 442376 | tf_op jit(solution)/shard_map/ppermute | solution.py:934
  168.8 3.7 %collective-permute-done.47 = bf16[96,768]{1,0:T(8,128)(2,1)S(1)} collective-permute-done((bf16[96,768]{1,0:T(8,128)(2,1)S(1)}, bf16[96,768]{1,0:T(8,128)(2,1)S(1)}, u32[]{:S(2)}, u32[]{:S(2)}) %collective-permute-start.47) | collective-permute-done | bytes 147488 | tf_op jit(solution)/shard_map/ppermute | solution.py:934
  175.7 3.2 %collective-permute-start.50 = (bf16[192,768]{1,0:T(8,128)(2,1)S(1)}, bf16[192,768]{1,0:T(8,128)(2,1)S(1)}, u32[]{:S(2)}, u32[]{:S(2)}) collective-permute-start(bf16[192,768]{1,0:T(8,128)(2,1)S(1)} %get-tuple-element.367), channel_id=1, source_target_pairs={{0,6},{1,7},{2,0},{3,1},{4,2},{5,3},{6,4},{7,5},{8,14},{9,15},{10,... | collective-permute-start | bytes 884744 | tf_op jit(solution)/shard_map/ppermute | solution.py:934
  180.7 2.7 %collective-permute-done.50.near = bf16[192,768]{1,0:T(8,128)(2,1)S(1)} collective-permute-done((bf16[192,768]{1,0:T(8,128)(2,1)S(1)}, bf16[192,768]{1,0:T(8,128)(2,1)S(1)}, u32[]{:S(2)}, u32[]{:S(2)}) %collective-permute-start.50) | collective-permute-done | bytes 294944 | tf_op jit(solution)/shard_map/ppermute | solution.py:934
  183.4 2.3 %collective-permute-done.51.fx = bf16[192,768]{1,0:T(8,128)(2,1)S(1)} collective-permute-done((bf16[192,768]{1,0:T(8,128)(2,1)S(1)}, bf16[192,768]{1,0:T(8,128)(2,1)S(1)}, u32[]{:S(2)}, u32[]{:S(2)}) %collective-permute-start.51) | collective-permute-done | bytes 294944 | tf_op jit(solution)/shard_map/ppermute | solution.py:918
  185.8 2.1 collective-permute-start.54
  190.8 2.6 %collective-permute-done.54 = bf16[200,384]{1,0:T(8,128)(2,1)S(1)} collective-permute-done((bf16[200,384]{1,0:T(8,128)(2,1)S(1)}, bf16[200,384]{1,0:T(8,128)(2,1)S(1)}, u32[]{:S(2)}, u32[]{:S(2)}) %collective-permute-start.54) | collective-permute-done | bytes 153632 | tf_op jit(solution)/shard_map/ppermute | solution.py:934
  193.4 5.6 %collective-permute-done.53 = bf16[200,384]{1,0:T(8,128)(2,1)S(1)} collective-permute-done((bf16[200,384]{1,0:T(8,128)(2,1)S(1)}, bf16[200,384]{1,0:T(8,128)(2,1)S(1)}, u32[]{:S(2)}, u32[]{:S(2)}) %collective-permute-start.53) | collective-permute-done | bytes 153632 | tf_op jit(solution)/shard_map/ppermute | solution.py:934
  (150 shorter events, 59.7 us)
Async XLA Ops:
  0.6 16.2 %collective-permute-start.3 = (bf16[192,768]{1,0:T(8,128)(2,1)}, bf16[192,768]{1,0:T(8,128)(2,1)S(1)}, u32[]{:S(2)}, u32[]{:S(2)}) collective-permute-start(bf16[192,768]{1,0:T(8,128)(2,1)} %bitcast.206), channel_id=1, source_target_pairs={{0,16},{8,24},{16,0},{24,8},{1,17},{9,25},{17,1},{25,9},{2,18},{10... | collective-permute-start | bytes 884744 | tf_op jit(solution)/shard_map/ppermute | solution.py:918
  6.2 9.1 %collective-permute-start = (bf16[48,1664]{1,0:T(8,128)(2,1)}, bf16[48,1664]{1,0:T(8,128)(2,1)S(1)}, u32[]{:S(2)}, u32[]{:S(2)}) collective-permute-start(bf16[48,1664]{1,0:T(8,128)(2,1)} %get-tuple-element.182.first), channel_id=1, source_target_pairs={{0,2},{1,3},{2,4},{3,5},{4,6},{5,7},{6,0},{7,1},{8,10},{9,11},{10,... | collective-permute-start | bytes 479240 | tf_op jit(solution)/shard_map/ppermute | solution.py:934
  16.8 14.0 %collective-permute-start.5 = (bf16[200,768]{1,0:T(8,128)(2,1)}, bf16[200,768]{1,0:T(8,128)(2,1)S(1)}, u32[]{:S(2)}, u32[]{:S(2)}) collective-permute-start(bf16[200,768]{1,0:T(8,128)(2,1)} %get-tuple-element.187.xo), channel_id=1, source_target_pairs={{0,2},{1,3},{2,4},{3,5},{4,6},{5,7},{6,0},{7,1},{8,10},{9,11},{10,... | collective-permute-start | bytes 921608 | tf_op jit(solution)/shard_map/ppermute | solution.py:934
  17.9 12.9 %collective-permute-start.7 = (bf16[192,768]{1,0:T(8,128)(2,1)}, bf16[192,768]{1,0:T(8,128)(2,1)S(1)}, u32[]{:S(2)}, u32[]{:S(2)}) collective-permute-start(bf16[192,768]{1,0:T(8,128)(2,1)} %get-tuple-element.202.own), channel_id=1, source_target_pairs={{0,1},{1,0},{2,3},{3,2},{4,5},{5,4},{6,7},{7,6},{8,9},{9,8},{10,11... | collective-permute-start | bytes 884744 | tf_op jit(solution)/shard_map/ppermute | solution.py:930
  19.5 11.3 %collective-permute-start.4 = (bf16[48,1664]{1,0:T(8,128)(2,1)S(1)}, bf16[48,1664]{1,0:T(8,128)(2,1)S(1)}, u32[]{:S(2)}, u32[]{:S(2)}) collective-permute-start(bf16[48,1664]{1,0:T(8,128)(2,1)S(1)} %collective-permute-done), channel_id=1, source_target_pairs={{0,2},{1,3},{2,4},{3,5},{4,6},{5,7},{6,0},{7,1},{8,10},{9,11},{10,... | collective-permute-start | bytes 479240 | tf_op jit(solution)/shard_map/ppermute | solution.py:934
  20.2 10.6 %collective-permute-start.6 = (bf16[48,1664]{1,0:T(8,128)(2,1)S(1)}, bf16[48,1664]{1,0:T(8,128)(2,1)S(1)}, u32[]{:S(2)}, u32[]{:S(2)}) collective-permute-start(bf16[48,1664]{1,0:T(8,128)(2,1)S(1)} %collective-permute-done.2), channel_id=1, source_target_pairs={{0,16},{8,24},{16,0},{24,8},{1,17},{9,25},{17,1},{25,9},{2,18},{10... | collective-permute-start | bytes 479240 | tf_op jit(solution)/shard_map/ppermute | solution.py:918
  30.8 11.4 %collective-permute-start.8 = (bf16[144,1664]{1,0:T(8,128)(2,1)S(1)}, bf16[144,1664]{1,0:T(8,128)(2,1)S(1)}, u32[]{:S(2)}, u32[]{:S(2)}) collective-permute-start(bf16[144,1664]{1,0:T(8,128)(2,1)S(1)} %pad_maximum_fusion.2), channel_id=1, source_target_pairs={{0,1},{1,0},{2,3},{3,2},{4,5},{5,4},{6,7},{7,6},{8,9},{9,8},{10,11... | collective-permute-start | bytes 1437704 | tf_op jit(solution)/shard_map/ppermute | solution.py:930
  32.4 11.0 %collective-permute-start.9 = (bf16[144,1664]{1,0:T(8,128)(2,1)S(1)}, bf16[144,1664]{1,0:T(8,128)(2,1)S(1)}, u32[]{:S(2)}, u32[]{:S(2)}) collective-permute-start(bf16[144,1664]{1,0:T(8,128)(2,1)S(1)} %pad_maximum_fusion.2), channel_id=1, source_target_pairs={{0,16},{8,24},{16,0},{24,8},{1,17},{9,25},{17,1},{25,9},{2,18},{10... | collective-permute-start | bytes 1437704 | tf_op jit(solution)/shard_map/ppermute | solution.py:918
  43.6 14.2 %collective-permute-start.11 = (bf16[2,200,768]{2,1,0:T(8,128)(2,1)S(1)}, bf16[2,200,768]{2,1,0:T(8,128)(2,1)S(1)}, u32[]{:S(2)}, u32[]{:S(2)}) collective-permute-start(bf16[2,200,768]{2,1,0:T(8,128)(2,1)S(1)} %pad_maximum_fusion), channel_id=1, source_target_pairs={{0,1},{1,0},{2,3},{3,2},{4,5},{5,4},{6,7},{7,6},{8,9},{9,8},{10,11... | collective-permute-start | bytes 1843208 | tf_op jit(solution)/shard_map/ppermute | solution.py:930
  44.2 13.7 %collective-permute-start.12 = (bf16[144,1664]{1,0:T(8,128)(2,1)S(1)}, bf16[144,1664]{1,0:T(8,128)(2,1)S(1)}, u32[]{:S(2)}, u32[]{:S(2)}) collective-permute-start(bf16[144,1664]{1,0:T(8,128)(2,1)S(1)} %collective-permute-done.8), channel_id=1, source_target_pairs={{0,16},{8,24},{16,0},{24,8},{1,17},{9,25},{17,1},{25,9},{2,18},{10... | collective-permute-start | bytes 1437704 | tf_op jit(solution)/shard_map/ppermute | solution.py:918
  44.7 10.8 %collective-permute-start.13 = (bf16[192,768]{1,0:T(8,128)(2,1)S(1)}, bf16[192,768]{1,0:T(8,128)(2,1)S(1)}, u32[]{:S(2)}, u32[]{:S(2)}) collective-permute-start(bf16[192,768]{1,0:T(8,128)(2,1)S(1)} %copy-done.3), channel_id=1, source_target_pairs={{0,2},{1,3},{2,4},{3,5},{4,6},{5,7},{6,0},{7,1},{8,10},{9,11},{10,... | collective-permute-start | bytes 884744 | tf_op jit(solution)/shard_map/ppermute | solution.py:934
  45.4 12.4 %collective-permute-start.14 = (bf16[192,768]{1,0:T(8,128)(2,1)S(1)}, bf16[192,768]{1,0:T(8,128)(2,1)S(1)}, u32[]{:S(2)}, u32[]{:S(2)}) collective-permute-start(bf16[192,768]{1,0:T(8,128)(2,1)S(1)} %copy-done.3), channel_id=1, source_target_pairs={{0,6},{1,7},{2,0},{3,1},{4,2},{5,3},{6,4},{7,5},{8,14},{9,15},{10,... | collective-permute-start | bytes 884744 | tf_op jit(solution)/shard_map/ppermute | solution.py:934
  62.2 16.4 %collective-permute-start.23 = (bf16[192,768]{1,0:T(8,128)(2,1)S(1)}, bf16[192,768]{1,0:T(8,128)(2,1)S(1)}, u32[]{:S(2)}, u32[]{:S(2)}) collective-permute-start(bf16[192,768]{1,0:T(8,128)(2,1)S(1)} %bitcast.207), channel_id=1, source_target_pairs={{0,8},{8,0},{16,24},{24,16},{1,9},{9,1},{17,25},{25,17},{2,10},{10... | collective-permute-start | bytes 884744 | tf_op jit(solution)/shard_map/ppermute | solution.py:918
  62.5 16.1 %collective-permute-start.24 = (bf16[192,768]{1,0:T(8,128)(2,1)S(1)}, bf16[192,768]{1,0:T(8,128)(2,1)S(1)}, u32[]{:S(2)}, u32[]{:S(2)}) collective-permute-start(bf16[192,768]{1,0:T(8,128)(2,1)S(1)} %collective-permute-done.3.dy_x), channel_id=1, source_target_pairs={{0,8},{8,0},{16,24},{24,16},{1,9},{9,1},{17,25},{25,17},{2,10},{10... | collective-permute-start | bytes 884744 | tf_op jit(solution)/shard_map/ppermute | solution.py:918
  62.7 15.9 %collective-permute-start.21 = (bf16[384,768]{1,0:T(8,128)(2,1)S(1)}, bf16[384,768]{1,0:T(8,128)(2,1)S(1)}, u32[]{:S(2)}, u32[]{:S(2)}) collective-permute-start(bf16[384,768]{1,0:T(8,128)(2,1)S(1)} %pad_maximum_fusion.1), channel_id=1, source_target_pairs={{0,1},{1,0},{2,3},{3,2},{4,5},{5,4},{6,7},{7,6},{8,9},{9,8},{10,11... | collective-permute-start | bytes 1769480 | tf_op jit(solution)/shard_map/ppermute | solution.py:930
  64.2 14.4 %collective-permute-start.22 = (bf16[192,768]{1,0:T(8,128)(2,1)S(1)}, bf16[192,768]{1,0:T(8,128)(2,1)S(1)}, u32[]{:S(2)}, u32[]{:S(2)}) collective-permute-start(bf16[192,768]{1,0:T(8,128)(2,1)S(1)} %collective-permute-done.13.z1), channel_id=1, source_target_pairs={{0,2},{1,3},{2,4},{3,5},{4,6},{5,7},{6,0},{7,1},{8,10},{9,11},{10,... | collective-permute-start | bytes 884744 | tf_op jit(solution)/shard_map/ppermute | solution.py:934
  80.2 9.4 %collective-permute-start.27 = (bf16[192,768]{1,0:T(8,128)(2,1)S(1)}, bf16[192,768]{1,0:T(8,128)(2,1)S(1)}, u32[]{:S(2)}, u32[]{:S(2)}) collective-permute-start(bf16[192,768]{1,0:T(8,128)(2,1)S(1)} %collective-permute-done.22.z2), channel_id=1, source_target_pairs={{0,1},{1,0},{2,3},{3,2},{4,5},{5,4},{6,7},{7,6},{8,9},{9,8},{10,11... | collective-permute-start | bytes 884744 | tf_op jit(solution)/shard_map/ppermute | solution.py:930
  99.6 9.1 %collective-permute-start.31 = (bf16[192,768]{1,0:T(8,128)(2,1)S(1)}, bf16[192,768]{1,0:T(8,128)(2,1)S(1)}, u32[]{:S(2)}, u32[]{:S(2)}) collective-permute-start(bf16[192,768]{1,0:T(8,128)(2,1)S(1)} %fusion.15), channel_id=1, source_target_pairs={{0,16},{8,24},{16,0},{24,8},{1,17},{9,25},{17,1},{25,9},{2,18},{10... | collective-permute-start | bytes 884744 | tf_op jit(solution)/shard_map/ppermute | solution.py:918
  108.7 14.1 %collective-permute-start.33 = (bf16[192,768]{1,0:T(8,128)(2,1)S(1)}, bf16[192,768]{1,0:T(8,128)(2,1)S(1)}, u32[]{:S(2)}, u32[]{:S(2)}) collective-permute-start(bf16[192,768]{1,0:T(8,128)(2,1)S(1)} %fusion.16), channel_id=1, source_target_pairs={{0,16},{8,24},{16,0},{24,8},{1,17},{9,25},{17,1},{25,9},{2,18},{10... | collective-permute-start | bytes 884744 | tf_op jit(solution)/shard_map/ppermute | solution.py:918
  109.4 14.3 %collective-permute-start.32 = (bf16[4,96,768]{2,1,0:T(8,128)(2,1)S(1)}, bf16[4,96,768]{2,1,0:T(8,128)(2,1)S(1)}, u32[]{:S(2)}, u32[]{:S(2)}) collective-permute-start(bf16[4,96,768]{2,1,0:T(8,128)(2,1)S(1)} %slice_bitcast_fusion.1), channel_id=1, source_target_pairs={{0,1},{1,0},{2,3},{3,2},{4,5},{5,4},{6,7},{7,6},{8,9},{9,8},{10,11... | collective-permute-start | bytes 1769480 | tf_op jit(solution)/shard_map/ppermute | solution.py:930
  123.7 16.9 %collective-permute-start.34 = (bf16[2,2,4,120,384]{4,3,2,1,0:T(8,128)(2,1)S(1)}, bf16[2,2,4,120,384]{4,3,2,1,0:T(8,128)(2,1)S(1)}, u32[]{:S(2)}, u32[]{:S(2)}) collective-permute-start(bf16[2,2,4,120,384]{4,3,2,1,0:T(8,128)(2,1)S(1)} %get-tuple-element.299), channel_id=1, source_target_pairs={{0,8},{8,0},{16,24},{24,16},{1,9},{9,1},{17,25},{25,17},{2,10},{10... | collective-permute-start | bytes 4423688 | tf_op jit(solution)/shard_map/ppermute | solution.py:918
  123.7 16.9 %collective-permute-start.35 = (bf16[4,96,768]{2,1,0:T(8,128)(2,1)S(1)}, bf16[4,96,768]{2,1,0:T(8,128)(2,1)S(1)}, u32[]{:S(2)}, u32[]{:S(2)}) collective-permute-start(bf16[4,96,768]{2,1,0:T(8,128)(2,1)S(1)} %slice_bitcast_fusion), channel_id=1, source_target_pairs={{0,1},{1,0},{2,3},{3,2},{4,5},{5,4},{6,7},{7,6},{8,9},{9,8},{10,11... | collective-permute-start | bytes 1769480 | tf_op jit(solution)/shard_map/ppermute | solution.py:930
  124.9 15.6 %collective-permute-start.36 = (bf16[96,768]{1,0:T(8,128)(2,1)S(1)}, bf16[96,768]{1,0:T(8,128)(2,1)S(1)}, u32[]{:S(2)}, u32[]{:S(2)}) collective-permute-start(bf16[96,768]{1,0:T(8,128)(2,1)S(1)} %get-tuple-element.362), channel_id=1, source_target_pairs={{0,2},{1,3},{2,4},{3,5},{4,6},{5,7},{6,0},{7,1},{8,10},{9,11},{10,... | collective-permute-start | bytes 442376 | tf_op jit(solution)/shard_map/ppermute | solution.py:934
  126.0 14.5 %collective-permute-start.37 = (bf16[96,768]{1,0:T(8,128)(2,1)S(1)}, bf16[96,768]{1,0:T(8,128)(2,1)S(1)}, u32[]{:S(2)}, u32[]{:S(2)}) collective-permute-start(bf16[96,768]{1,0:T(8,128)(2,1)S(1)} %get-tuple-element.361), channel_id=1, source_target_pairs={{0,4},{1,5},{2,6},{3,7},{4,0},{5,1},{6,2},{7,3},{8,12},{9,13},{10,... | collective-permute-start | bytes 442376 | tf_op jit(solution)/shard_map/ppermute | solution.py:934
  128.5 12.0 %collective-permute-start.38 = (bf16[96,768]{1,0:T(8,128)(2,1)S(1)}, bf16[96,768]{1,0:T(8,128)(2,1)S(1)}, u32[]{:S(2)}, u32[]{:S(2)}) collective-permute-start(bf16[96,768]{1,0:T(8,128)(2,1)S(1)} %get-tuple-element.360), channel_id=1, source_target_pairs={{0,6},{1,7},{2,0},{3,1},{4,2},{5,3},{6,4},{7,5},{8,14},{9,15},{10,... | collective-permute-start | bytes 442376 | tf_op jit(solution)/shard_map/ppermute | solution.py:934
  140.8 17.8 %collective-permute-start.41 = (bf16[2,4,120,384]{3,2,1,0:T(8,128)(2,1)S(1)}, bf16[2,4,120,384]{3,2,1,0:T(8,128)(2,1)S(1)}, u32[]{:S(2)}, u32[]{:S(2)}) collective-permute-start(bf16[2,4,120,384]{3,2,1,0:T(8,128)(2,1)S(1)} %fusion.1), channel_id=1, source_target_pairs={{0,16},{8,24},{16,0},{24,8},{1,17},{9,25},{17,1},{25,9},{2,18},{10... | collective-permute-start | bytes 2211848 | tf_op jit(solution)/shard_map/ppermute | solution.py:918
  142.3 14.7 %collective-permute-start.42 = (bf16[2,192,768]{2,1,0:T(8,128)(2,1)S(1)}, bf16[2,192,768]{2,1,0:T(8,128)(2,1)S(1)}, u32[]{:S(2)}, u32[]{:S(2)}) collective-permute-start(bf16[2,192,768]{2,1,0:T(8,128)(2,1)S(1)} %get-tuple-element.309), channel_id=1, source_target_pairs={{0,1},{1,0},{2,3},{3,2},{4,5},{5,4},{6,7},{7,6},{8,9},{9,8},{10,11... | collective-permute-start | bytes 1769480 | tf_op jit(solution)/shard_map/ppermute | solution.py:930
  158.7 15.2 %collective-permute-start.46 = (bf16[192,768]{1,0:T(8,128)(2,1)S(1)}, bf16[192,768]{1,0:T(8,128)(2,1)S(1)}, u32[]{:S(2)}, u32[]{:S(2)}) collective-permute-start(bf16[192,768]{1,0:T(8,128)(2,1)S(1)} %fusion.18), channel_id=1, source_target_pairs={{0,6},{1,7},{2,0},{3,1},{4,2},{5,3},{6,4},{7,5},{8,14},{9,15},{10,... | collective-permute-start | bytes 884744 | tf_op jit(solution)/shard_map/ppermute | solution.py:934
  161.6 12.3 %collective-permute-start.44 = (bf16[2,4,80,384]{3,2,1,0:T(8,128)(2,1)S(1)}, bf16[2,4,80,384]{3,2,1,0:T(8,128)(2,1)S(1)}, u32[]{:S(2)}, u32[]{:S(2)}) collective-permute-start(bf16[2,4,80,384]{3,2,1,0:T(8,128)(2,1)S(1)} %fusion), channel_id=1, source_target_pairs={{0,16},{8,24},{16,0},{24,8},{1,17},{9,25},{17,1},{25,9},{2,18},{10... | collective-permute-start | bytes 1474568 | tf_op jit(solution)/shard_map/ppermute | solution.py:918
  163.3 10.6 %collective-permute-start.45 = (bf16[4,120,384]{2,1,0:T(8,128)(2,1)S(1)}, bf16[4,120,384]{2,1,0:T(8,128)(2,1)S(1)}, u32[]{:S(2)}, u32[]{:S(2)}) collective-permute-start(bf16[4,120,384]{2,1,0:T(8,128)(2,1)S(1)} %fusion.2), channel_id=1, source_target_pairs={{0,1},{1,0},{2,3},{3,2},{4,5},{5,4},{6,7},{7,6},{8,9},{9,8},{10,11... | collective-permute-start | bytes 1105928 | tf_op jit(solution)/shard_map/ppermute | solution.py:930
  187.9 11.1 %collective-permute-start.53 = (bf16[200,384]{1,0:T(8,128)(2,1)S(1)}, bf16[200,384]{1,0:T(8,128)(2,1)S(1)}, u32[]{:S(2)}, u32[]{:S(2)}) collective-permute-start(bf16[200,384]{1,0:T(8,128)(2,1)S(1)} %pad_maximum_fusion.5), channel_id=1, source_target_pairs={{0,4},{1,5},{2,6},{3,7},{4,0},{5,1},{6,2},{7,3},{8,12},{9,13},{10,... | collective-permute-start | bytes 460808 | tf_op jit(solution)/shard_map/ppermute | solution.py:934
  188.0 11.0 %collective-permute-start.52 = (bf16[200,384]{1,0:T(8,128)(2,1)S(1)}, bf16[200,384]{1,0:T(8,128)(2,1)S(1)}, u32[]{:S(2)}, u32[]{:S(2)}) collective-permute-start(bf16[200,384]{1,0:T(8,128)(2,1)S(1)} %pad_maximum_fusion.4), channel_id=1, source_target_pairs={{0,2},{1,3},{2,4},{3,5},{4,6},{5,7},{6,0},{7,1},{8,10},{9,11},{10,... | collective-permute-start | bytes 460808 | tf_op jit(solution)/shard_map/ppermute | solution.py:934
  (35 other events, 258.4 us)

commit v7 on v6

--- a/solution.py
+++ b/solution.py
@@ -450,7 +450,7 @@
 
 def prep_kernel(
     tokens, segs, qkv, out, up, down, gains, shifts, biases, up_bias,
-    t_out, q_out, f_out,
+    t_out, q_out, f_out, fu_out, fd_out,
     scratch, wide, held_g, held_s, held_b, ids, line, sems,
 ):
     x, c, _y, _z = place()
@@ -475,7 +475,9 @@
         q_out.at[pl.ds(0, half), pl.ds(wide_cols, side)],
     )
     others.add(tokens.at[0], t_out.at[pl.ds(0, tok), :])
-    others.add(down.at[pl.ds(pl.multiple_of(rows * p, 16), rows), :], f_out.at[pl.ds(rows, rows), :])
+    own_rows = down.at[pl.ds(pl.multiple_of(rows * p, 16), rows), :]
+    others.add(own_rows, f_out.at[pl.ds(rows, rows), :])
+    others.add(own_rows, fd_out)
     copies.wait()
     scratch[...] = jnp.zeros_like(scratch)
     for first, held in ((0, held_g), (2, held_s), (4, held_b)):
@@ -497,7 +499,9 @@
         parts = []
         for shard in range(4 * group, 4 * group + 4):
             parts.append(choose(unpack96(f32(wide[:, pl.ds(384 * shard, 384)])), p))
-        f_out[pl.ds(0, rows), pl.ds(384 * group, 384)] = b16(pack96(parts))
+        packed = b16(pack96(parts))
+        f_out[pl.ds(0, rows), pl.ds(384 * group, 384)] = packed
+        fu_out[:, pl.ds(384 * group, 384)] = packed
 
 
 def front_kernel(
@@ -600,12 +604,12 @@
     y_acc[...] = dot_nn(act_out[...], w_down[...])
 
 
-def assemble_kernel(own, z1, z2, z3, y0, y13, wu_out, wd_out, sems):
+def assemble_kernel(own, z1, z2, z3u, z3d, y0, y13, wu_out, wd_out, sems):
     _x, _c, y, z = place()
     rows = own.shape[0] // 2
     copies = Copies(sems)
     pieces = [(own, 2 * z + y)]
-    for number, ref in ((0, z1), (1, z2), (2, z3), (3, y0)):
+    for number, ref in ((0, z1), (1, z2), (3, y0)):
         pieces.append((ref, piece_shard(number, y, z)))
     for number, first in ((4, 0), (6, 2 * rows)):
         pieces.append((y13.at[pl.ds(first, 2 * rows), :], piece_shard(number, y, z)))
@@ -613,6 +617,9 @@
         at = pl.ds(pl.multiple_of(shard * rows, 16), rows)
         copies.add(ref.at[pl.ds(0, rows), :], wu_out.at[at, :])
         copies.add(ref.at[pl.ds(rows, rows), :], wd_out.at[at, :])
+    at = pl.ds(pl.multiple_of(piece_shard(2, y, z) * rows, 16), rows)
+    copies.add(z3u, wu_out.at[at, :])
+    copies.add(z3d, wd_out.at[at, :])
     copies.wait()
 
 
@@ -645,7 +652,7 @@
     hs, dys, acts, dus, keep_out, send_out,
     y_acc, dh_acc, sems,
 ):
-    tok = h_x.shape[0]
+    tok = dy_x.shape[0]
     copies = Copies(sems)
     for source, target in ((h_near, hs), (dy_near, dys), (act_near, acts), (du_near, dus)):
         copies.add(source, target.at[pl.ds(0, 2 * tok), :])
@@ -746,7 +753,7 @@
         dq[:, pl.ds(to, 128)] = b16(pair_join(dot_tn(keys, low)) * 0.125)
         return carry
 
-    lax.fori_loop(0, 3, pair, 0)
+    lax.fori_loop(0, 3, pair, 0, unroll=first == 0)
 
 
 def qkv_weight(h_in, dq, dkv, stage, tail):
@@ -959,14 +966,16 @@
     bf, fl = jnp.bfloat16, jnp.float32
     dma = pltpu.SemaphoreType.DMA
     grad_y = cotangent[0]
-    own_tokens, piece_q, piece_f = call(
+    own_tokens, piece_q, piece_f, piece_u, piece_d = call(
         prep_kernel,
         [HB] * 10,
-        [VM] * 3,
+        [VM] * 5,
         [
             shape_of((tok + 8, width), bf),
             shape_of((48, 2 * width + 128), bf),
             shape_of((192, width), bf),
+            shape_of((96, width), bf),
+            shape_of((96, width), bf),
         ],
         [
             pltpu.VMEM((8, width), fl),
@@ -976,7 +985,7 @@
             pltpu.VMEM((4, 96), bf),
             pltpu.VMEM((1, tok), jnp.int32),
             pltpu.VMEM((384,), bf),
-            dma((10,)),
+            dma((11,)),
         ],
         vmem=60, moved=4 * 10**6,
     )(
@@ -988,18 +997,20 @@
     own_tokens, piece_f, q1, q_y0 = fence(own_tokens, piece_f, q1, q_y0, q3, dy_x)[:4]
     q2, x2, q_xy0, f_y0 = fence(to_z(q1, 1), to_z(own_tokens, 1), to_x(q_y0), to_y(piece_f))
     q_z = join(q1, q2, q3)
-    q_z, x2 = fence(q_z, x2, q_xy0, f_y0)[:2]
-    q_y, q_xz, x4 = fence(to_y(q_z), to_x(q_z), to_z(x2, 1))
+    q_z, x2, piece_d = fence(q_z, x2, piece_d, q_xy0, f_y0)[:3]
+    q_y, q_xz, x4, f3d = fence(to_y(q_z), to_x(q_z), to_z(x2, 1), to_z(piece_d, 3))
     near = jnp.where(y == 0, own_tokens, x2)
     far = jnp.where(y == 0, x2, x4)
-    near_far, q_y, piece_f = fence(jnp.stack([near, far]), q_y, piece_f, q_xz)[:3]
-    crossed, q_xy, f1, f3 = fence(to_y(near_far), to_x(q_y), to_z(piece_f, 1), to_z(piece_f, 3))
+    near_far, q_y, piece_f, piece_u = fence(
+        jnp.stack([near, far]), q_y, piece_f, piece_u, q_xz, f3d
+    )[:4]
+    crossed, q_xy, f1, f3u = fence(to_y(near_far), to_x(q_y), to_z(piece_f, 1), to_z(piece_u, 3))
     x1, x3 = crossed[0], crossed[1]
-    q_z, q_y0, q_y, q_xz, q_xy0, q_xy = fence(q_z, q_y0, q_y, q_xz, q_xy0, q_xy, f1, f3, crossed)[:6]
+    q_z, q_y0, q_y, q_xz, q_xy0, q_xy = fence(q_z, q_y0, q_y, q_xz, q_xy0, q_xy, f1, f3u, crossed)[:6]
     q_cz, q_cy0, q_cy, q_cxz, q_cxy0, q_cxy = fence(
         *(to_core(v) for v in (q_z, q_y0, q_y, q_xz, q_xy0, q_xy))
     )
-    f_13, f_1, q_cz = fence(join(f1, f3), f1, q_cz, q_cy0, q_cy, q_cxz, q_cxy0, q_cxy)[:3]
+    f_13, f_1, q_cz = fence(join(f1, f3u, f3d), f1, q_cz, q_cy0, q_cy, q_cxz, q_cxy0, q_cxy)[:3]
     f_y13, f2 = to_y(f_13), to_z(f_1, 1)
     dy_c, dy_xc = to_core(grad_y), to_core(dy_x)
 
@@ -1044,13 +1055,13 @@
     queries, kv, normed, attended, lse, start, vec, upb, w_out, residual, hidden_2 = front
     w_half = call(
         assemble_kernel,
-        [AN] * 6,
+        [AN] * 7,
         [VM] * 2,
         [shape_of((width, width), bf)] * 2,
         [dma((14,))],
         vmem=4,
         moved=5 * 10**6,
-    )(piece_f, f1, f2, f3, f_y0, f_y13)
+    )(piece_f, f1, f2, f3u, f3d, f_y0, f_y13)
     h_x, h_c, f_y2, *w_half = fence(to_x(hidden_2), to_core(hidden_2), to_y(f2), *w_half)
     act = shape_of((2 * tok, width), bf)
     acts = shape_of((4 * tok, width), bf)
@@ -1199,18 +1210,16 @@
         return qb_1(0, *index) + f32(qb_x[index])
 
     f_tot = join(z_sum(u_part, *u_z), z_sum(d_part, d_z1, d_z3))
-    f_tot, hop = fence(f_tot, hop)
-    qb_y, back_2, f_x = fence(to_y(b16(qb_2(1))), to_z(b16(sum_2 + f32(hop)), 3), to_x(f_tot))
+    qb_y, back_2, f_tot = fence(to_y(b16(qb_2(1))), to_z(b16(sum_2 + f32(hop)), 3), f_tot)
 
     def q_3(*index):
         first = qa_2(0, *index) + f32(qa_y[index])
         return jnp.concatenate([first, qb_2(0, *index) + f32(qb_y[index])], axis=-2)
 
-    f_tot, f_x, back_2, qb_y = fence(f_tot, f_x, back_2, qb_y)
     grad_tokens = call(
         tokens_kernel, [VM] * 5, VM, shape_of((tok, width), fl), vmem=4, moved=3 * 10**6
     )(sum_own, back_2, grad_first, own_tokens, vec)
-    *q_z, f_tot, f_x = fence(*(to_z(b16(q_3(step)), step) for step in (1, 2, 3)), f_tot, f_x)
+    *q_z, f_x, f_tot = fence(*(to_z(b16(q_3(step)), step) for step in (1, 2, 3)), to_x(f_tot), f_tot)
     q_sum = z_sum(q_3, *q_z)
     q_fx, q_fc, q_fxc = to_x(q_sum), to_core(q_sum), swap_rep(q_sum, 3)
     grad_up, grad_down = call(

time: 208 us -> 206 us (level)
  waiting for transfers between devices: 76.2 us -> 68.8 us
  starting transfers between devices: 61.1 us -> 66.8 us
    ppermute x19 -> x20, waiting for transfers between devices: 55.5 us -> 47.3 us  [to_z(): lax.ppermute(value, 'seq', [(k, (k + 2 * steps) % 8) for k in range(8)])]
    ppermute x19 -> x20, starting transfers between devices: 29.1 us -> 35.2 us  [to_z(): lax.ppermute(value, 'seq', [(k, (k + 2 * steps) % 8) for k in range(8)])]
    ppermute x11, waiting for transfers between devices: 3.58 us -> 7.82 us  [to_y(): return lax.ppermute(value, 'seq', [(k, k ^ 1) for k in range(8)])]
    ppermute x30, waiting for transfers between devices: 17.1 us -> 13.7 us  [swap_rep(): return lax.ppermute(value, 'rep', [(k, k ^ bit) for k in range(4)])]
    ppermute x11, starting transfers between devices: 14.2 us -> 11.8 us  [to_y(): return lax.ppermute(value, 'seq', [(k, k ^ 1) for k in range(8)])]
  transfers between devices with their start and end apart: 60 -> 61, of which waited for: 24 -> 22; matrix products, arithmetic and copies ran while one was open for 2% -> 2% of each run, Pallas kernels for 31% -> 31%
where the time goes in v7:
time: 206 us
  waiting for transfers between devices  68.8 us (33%)
  starting transfers between devices  66.8 us (32%)
  Pallas kernels  64.1 us (31%)
  other arithmetic  2.99 us (1%)
  local copies, waits for them, and re-layouts  2.08 us (1%)
    ppermute x20, waiting for transfers between devices, to_z(): lax.ppermute(value, 'seq', [(k, (k + 2 * steps) % 8) for k in range(8)])  47.3 us
    ppermute x20, starting transfers between devices, to_z(): lax.ppermute(value, 'seq', [(k, (k + 2 * steps) % 8) for k in range(8)])  35.2 us
    ppermute x30, starting transfers between devices, swap_rep(): return lax.ppermute(value, 'rep', [(k, k ^ bit) for k in range(4)])  19.7 us
    pallas_call x1, Pallas kernels, on_device_fast(): call(front_kernel, [VM] * 6 + [AN] * 15, [VM] * 11, [shape_of((tok, width...  13.9 us
    ppermute x30, waiting for transfers between devices, swap_rep(): return lax.ppermute(value, 'rep', [(k, k ^ bit) for k in range(4)])  13.7 us
    ppermute x11, starting transfers between devices, to_y(): return lax.ppermute(value, 'seq', [(k, k ^ 1) for k in range(8)])  11.8 us
    pallas_call x1, Pallas kernels, on_device_fast(): call(back_b_kernel, [VM] * 14 + [AN] * 13, [VM] * 6, [shape_of((tok, widt...  10.8 us
    pallas_call x1, Pallas kernels, on_device_fast(): call(back_a_kernel, [VM] * 7, [AN] * 2 + [VM] * 2, [shape_of((2, 2, 4, 12...  9.98 us
  transfers between devices with their start and end apart: 61, of which 22 were waited for; matrix products, arithmetic and copies ran while one was open for 2% of the time, Pallas kernels for 31%

profile of v7, /device:TPU:0, one launch (start us, length us, event | category | flops | bytes accessed | tf_op | source)
XLA Modules:
  0.0 205.8 jit_solution(16562663735690963311)
XLA Ops:
  0.6 3.0 %collective-permute-start.3 = (bf16[192,768]{1,0:T(8,128)(2,1)}, bf16[192,768]{1,0:T(8,128)(2,1)S(1)}, u32[]{:S(2)}, u32[]{:S(2)}) collective-permute-start(bf16[192,768]{1,0:T(8,128)(2,1)} %bitcast.206), channel_id=1, source_target_pairs={{0,16},{8,24},{16,0},{24,8},{1,17},{9,25},{17,1},{25,9},{2,18},{10... | collective-permute-start | bytes 884744 | tf_op jit(solution)/shard_map/ppermute | solution.py:925
  3.6 2.7 %shard_map.186 = (bf16[200,768]{1,0:T(8,128)(2,1)}, bf16[48,1664]{1,0:T(8,128)(2,1)}, bf16[192,768]{1,0:T(8,128)(2,1)}, bf16[96,768]{1,0:T(8,128)(2,1)}, bf16[96,768]{1,0:T(8,128)(2,1)}) custom-call(bf16[1,192,768]{2,1,0:T(8,128)(2,1)} %tokens.1, s32[1,192]{1,0:T(1,128)} %segs.1, bf16[96,2304]{1,0:T(8,128)(2,1)} %own.3, bf16[96,768]{1,0:T(8,128)(2,1)} %own_o.1, ...), custom_call_target="tpu_custom_call" | custom-call | bytes 4000000 | tf_op jit(solution)/shard_map/pallas_call | solution.py:969
  8.0 2.2 %collective-permute-start.1 = (bf16[48,1664]{1,0:T(8,128)(2,1)}, bf16[48,1664]{1,0:T(8,128)(2,1)S(1)}, u32[]{:S(2)}, u32[]{:S(2)}) collective-permute-start(bf16[48,1664]{1,0:T(8,128)(2,1)} %get-tuple-element.181.first), channel_id=1, source_target_pairs={{0,6},{1,7},{2,0},{3,1},{4,2},{5,3},{6,4},{7,5},{8,14},{9,15},{10,... | collective-permute-start | bytes 479240 | tf_op jit(solution)/shard_map/ppermute | solution.py:941
  11.8 3.7 %collective-permute-done = bf16[48,1664]{1,0:T(8,128)(2,1)S(1)} collective-permute-done((bf16[48,1664]{1,0:T(8,128)(2,1)}, bf16[48,1664]{1,0:T(8,128)(2,1)S(1)}, u32[]{:S(2)}, u32[]{:S(2)}) %collective-permute-start) | collective-permute-done | bytes 159776 | tf_op jit(solution)/shard_map/ppermute | solution.py:941
  20.9 10.0 %collective-permute-done.4 = bf16[48,1664]{1,0:T(8,128)(2,1)S(1)} collective-permute-done((bf16[48,1664]{1,0:T(8,128)(2,1)S(1)}, bf16[48,1664]{1,0:T(8,128)(2,1)S(1)}, u32[]{:S(2)}, u32[]{:S(2)}) %collective-permute-start.4) | collective-permute-done | bytes 159776 | tf_op jit(solution)/shard_map/ppermute | solution.py:941
  33.1 3.8 %collective-permute-start.11 = (bf16[96,768]{1,0:T(8,128)(2,1)}, bf16[96,768]{1,0:T(8,128)(2,1)S(1)}, u32[]{:S(2)}, u32[]{:S(2)}) collective-permute-start(bf16[96,768]{1,0:T(8,128)(2,1)} %get-tuple-element.197), channel_id=1, source_target_pairs={{0,6},{1,7},{2,0},{3,1},{4,2},{5,3},{6,4},{7,5},{8,14},{9,15},{10,... | collective-permute-start | bytes 442376 | tf_op jit(solution)/shard_map/ppermute | solution.py:941
  36.9 7.0 %collective-permute-done.11.z3d = bf16[96,768]{1,0:T(8,128)(2,1)S(1)} collective-permute-done((bf16[96,768]{1,0:T(8,128)(2,1)}, bf16[96,768]{1,0:T(8,128)(2,1)S(1)}, u32[]{:S(2)}, u32[]{:S(2)}) %collective-permute-start.11) | collective-permute-done | bytes 147488 | tf_op jit(solution)/shard_map/ppermute | solution.py:941
  46.5 3.5 %collective-permute-start.15 = (bf16[96,768]{1,0:T(8,128)(2,1)S(1)}, bf16[96,768]{1,0:T(8,128)(2,1)S(1)}, u32[]{:S(2)}, u32[]{:S(2)}) collective-permute-start(bf16[96,768]{1,0:T(8,128)(2,1)S(1)} %copy-done.7), channel_id=1, source_target_pairs={{0,6},{1,7},{2,0},{3,1},{4,2},{5,3},{6,4},{7,5},{8,14},{9,15},{10,... | collective-permute-start | bytes 442376 | tf_op jit(solution)/shard_map/ppermute | solution.py:941
  50.0 4.9 %collective-permute-done.15.z3u = bf16[96,768]{1,0:T(8,128)(2,1)S(1)} collective-permute-done((bf16[96,768]{1,0:T(8,128)(2,1)S(1)}, bf16[96,768]{1,0:T(8,128)(2,1)S(1)}, u32[]{:S(2)}, u32[]{:S(2)}) %collective-permute-start.15) | collective-permute-done | bytes 147488 | tf_op jit(solution)/shard_map/ppermute | solution.py:941
  54.9 1.9 collective-permute-done.12
  58.6 2.6 %collective-permute-done.20 = bf16[48,1664]{1,0:T(8,128)(2,1)S(1)} collective-permute-done((bf16[48,1664]{1,0:T(8,128)(2,1)S(1)}, bf16[48,1664]{1,0:T(8,128)(2,1)S(1)}, u32[]{:S(2)}, u32[]{:S(2)}) %collective-permute-start.20) | collective-permute-done | bytes 159776 | tf_op jit(solution)/shard_map/ppermute | solution.py:925
  63.8 13.9 %shard_map.187 = (bf16[192,768]{1,0:T(8,128)(2,1)S(1)}, bf16[960,1536]{1,0:T(8,128)(2,1)S(1)}, bf16[960,768]{1,0:T(8,128)(2,1)S(1)}, bf16[192,768]{1,0:T(8,128)(...) custom-call(s32[1,384]{1,0:T(1,128)S(1)} %pad_add_fusion.seg, ...), custom_call_target="tpu_custom_call" | custom-call | flops 7000000000 | bytes 12000000 | tf_op jit(solution)/shard_map/pallas_call | solution.py:1025
  79.7 2.9 %shard_map.188 = (bf16[768,768]{1,0:T(8,128)(2,1)S(1)}, bf16[768,768]{1,0:T(8,128)(2,1)S(1)}) custom-call(bf16[192,768]{1,0:T(8,128)(2,1)S(1)} %copy-done.3, bf16[192,768]{1,0:T(8,128)(2,1)S(1)} %collective-permute-done.14.z1, bf16[192,768]{1,0:T(8,128)(2,1)S(1)} %collective-permute-done.23.z2, bf16[96,768]{1,0:T(8,128)(2,1)S(1)} %collective-permute-done.15.z3u, ...), custom_call_target="tpu_custom_call" | custom-call | bytes 5000000 | tf_op jit(solution)/shard_map/pallas_call | solution.py:1056
  82.6 3.8 %collective-permute-done.26.h_x = bf16[192,768]{1,0:T(8,128)(2,1)S(1)} collective-permute-done((bf16[192,768]{1,0:T(8,128)(2,1)S(1)}, bf16[192,768]{1,0:T(8,128)(2,1)S(1)}, u32[]{:S(2)}, u32[]{:S(2)}) %collective-permute-start.26) | collective-permute-done | bytes 294944 | tf_op jit(solution)/shard_map/ppermute | solution.py:925
  87.7 3.5 %shard_map.189 = (bf16[384,768]{1,0:T(8,128)(2,1)S(1)}, bf16[384,768]{1,0:T(8,128)(2,1)S(1)}, bf16[384,768]{1,0:T(8,128)(2,1)S(1)}, bf16[384,768]{1,0:T(8,128)(2...) custom-call(bf16[192,768]{1,0:T(8,128)(2,1)S(1)} %get-tuple-element., ...), custom_call_target="tpu_custom_call", output_to_operand_aliasing={{6}: (6, {}), {7}: (7, {})} | custom-call | flops 3000000000 | bytes 6000000 | tf_op jit(solution)/shard_map/pallas_call | solution.py:1070
  91.8 3.7 %shard_map.190 = (bf16[768,768]{1,0:T(8,128)(2,1)S(1)}, bf16[768,768]{1,0:T(8,128)(2,1)S(1)}, bf16[768,768]{1,0:T(8,128)(2,1)S(1)}, bf16[768,768]{1,0:T(8,128)(2...) custom-call(bf16[192,768]{1,0:T(8,128)(2,1)S(1)} %collective-permute-done.26.h_x, ...), custom_call_target="tpu_custom_call" | custom-call | flops 3000000000 | bytes 6000000 | tf_op jit(solution)/shard_map/pallas_call | solution.py:1084
  95.6 2.0 collective-permute-done.31
  99.2 6.1 %shard_map.191 = (bf16[2,4,96,768]{3,2,1,0:T(8,128)(2,1)S(1)}, bf16[2,4,96,768]{3,2,1,0:T(8,128)(2,1)S(1)}, f32[1,768]{1,0:T(1,128)S(1)}) custom-call(bf16[768,768]{1,0:T(8,128)(2,1)S(1)} %get-tuple-element.280.hs, bf16[768,768]{1,0:T(8,128)(2,1)S(1)} %get-tuple-element.281.dys, bf16[768,768]{1,0:T(8,128)(2,1)S(1)} %get-tuple-element.282.acts, ...), custom_call_target="tpu_custom_call" | custom-call | flops 3000000000 | bytes 6000000 | tf_op jit(solution)/shard_map/pallas_call | solution.py:1096
  111.2 10.0 %shard_map.193 = (bf16[2,2,4,120,384]{4,3,2,1,0:T(8,128)(2,1)S(1)}, bf16[2,2,4,120,384]{4,3,2,1,0:T(8,128)(2,1)S(1)}, bf16[192,384]{1,0:T(8,128)(2,1)S(1)}, bf16[960,768]{1,0:T(8,128)(2,1)S(1)}) custom-call(s32[1,384]{1,0:T(1,128)S(1)} %get-tuple-element.267.start_in, bf16[192,768]{1,0:T(8,128)(2,1)S(1)} %get-tuple-element.268.q_in, ...), custom_call_target="tpu_custom_call" | custom-call | flops 5000000000 | bytes 10000000 | tf_op jit(solution)/shard_map/pallas_call | solution.py:1125
  125.5 1.9 collective-permute-start.38
  128.8 10.8 %shard_map.194 = (bf16[192,384]{1,0:T(8,128)(2,1)S(1)}, bf16[960,768]{1,0:T(8,128)(2,1)S(1)}, f32[192,768]{1,0:T(8,128)S(1)}, bf16[2,192,768]{2,1,0:T(8,128)(2,1...) custom-call(s32[1,384]{1,0:T(1,128)S(1)} %get-tuple-element.267.start_in, ...), custom_call_target="tpu_custom_call" | custom-call | flops 6000000000 | bytes 10000000 | tf_op jit(solution)/shard_map/pallas_call | solution.py:1152
  141.9 4.8 %shard_map.195 = (bf16[2,2,4,80,384]{4,3,2,1,0:T(8,128)(2,1)S(1)}, bf16[2,2,4,80,384]{4,3,2,1,0:T(8,128)(2,1)S(1)}) custom-call(bf16[960,768]{1,0:T(8,128)(2,1)S(1)} %get-tuple-element.270.h_in, bf16[192,384]{1,0:T(8,128)(2,1)S(1)} %get-tuple-element.307.dq, bf16[960,768]{1,0:T(8,128)(2,1)S(1)} %get-tuple-element.308.dkv, ...), custom_call_target="tpu_custom_call" | custom-call | flops 3000000000 | bytes 6000000 | tf_op jit(solution)/shard_map/pallas_call | solution.py:1177
  149.2 6.0 %collective-permute-done.44 = bf16[96,768]{1,0:T(8,128)(2,1)S(1)} collective-permute-done((bf16[96,768]{1,0:T(8,128)(2,1)S(1)}, bf16[96,768]{1,0:T(8,128)(2,1)S(1)}, u32[]{:S(2)}, u32[]{:S(2)}) %collective-permute-start.44) | collective-permute-done | bytes 147488 | tf_op jit(solution)/shard_map/ppermute | solution.py:941
  155.8 1.9 collective-permute-done.42
  157.8 2.6 %collective-permute-start.47 = (bf16[192,768]{1,0:T(8,128)(2,1)S(1)}, bf16[192,768]{1,0:T(8,128)(2,1)S(1)}, u32[]{:S(2)}, u32[]{:S(2)}) collective-permute-start(bf16[192,768]{1,0:T(8,128)(2,1)S(1)} %fusion.18), channel_id=1, source_target_pairs={{0,6},{1,7},{2,0},{3,1},{4,2},{5,3},{6,4},{7,5},{8,14},{9,15},{10,... | collective-permute-start | bytes 884744 | tf_op jit(solution)/shard_map/ppermute | solution.py:941
  163.0 3.8 %collective-permute-start.49 = (bf16[96,768]{1,0:T(8,128)(2,1)S(1)}, bf16[96,768]{1,0:T(8,128)(2,1)S(1)}, u32[]{:S(2)}, u32[]{:S(2)}) collective-permute-start(bf16[96,768]{1,0:T(8,128)(2,1)S(1)} %get-tuple-element.356), channel_id=1, source_target_pairs={{0,6},{1,7},{2,0},{3,1},{4,2},{5,3},{6,4},{7,5},{8,14},{9,15},{10,... | collective-permute-start | bytes 442376 | tf_op jit(solution)/shard_map/ppermute | solution.py:941
  166.9 5.2 %collective-permute-done.48 = bf16[96,768]{1,0:T(8,128)(2,1)S(1)} collective-permute-done((bf16[96,768]{1,0:T(8,128)(2,1)S(1)}, bf16[96,768]{1,0:T(8,128)(2,1)S(1)}, u32[]{:S(2)}, u32[]{:S(2)}) %collective-permute-start.48) | collective-permute-done | bytes 147488 | tf_op jit(solution)/shard_map/ppermute | solution.py:941
  174.2 2.8 %collective-permute-start.51 = (bf16[192,768]{1,0:T(8,128)(2,1)S(1)}, bf16[192,768]{1,0:T(8,128)(2,1)S(1)}, u32[]{:S(2)}, u32[]{:S(2)}) collective-permute-start(bf16[192,768]{1,0:T(8,128)(2,1)S(1)} %get-tuple-element.365), channel_id=1, source_target_pairs={{0,6},{1,7},{2,0},{3,1},{4,2},{5,3},{6,4},{7,5},{8,14},{9,15},{10,... | collective-permute-start | bytes 884744 | tf_op jit(solution)/shard_map/ppermute | solution.py:941
  177.3 2.5 %collective-permute-done.50 = bf16[4,80,384]{2,1,0:T(8,128)(2,1)S(1)} collective-permute-done((bf16[4,80,384]{2,1,0:T(8,128)(2,1)S(1)}, bf16[4,80,384]{2,1,0:T(8,128)(2,1)S(1)}, u32[]{:S(2)}, u32[]{:S(2)}) %collective-permute-start.50) | collective-permute-done | bytes 245792 | tf_op jit(solution)/shard_map/ppermute | solution.py:937
  181.4 4.3 %collective-permute-start.54 = (bf16[200,384]{1,0:T(8,128)(2,1)S(1)}, bf16[200,384]{1,0:T(8,128)(2,1)S(1)}, u32[]{:S(2)}, u32[]{:S(2)}) collective-permute-start(bf16[200,384]{1,0:T(8,128)(2,1)S(1)} %pad_maximum_fusion.6), channel_id=1, source_target_pairs={{0,6},{1,7},{2,0},{3,1},{4,2},{5,3},{6,4},{7,5},{8,14},{9,15},{10,... | collective-permute-start | bytes 460808 | tf_op jit(solution)/shard_map/ppermute | solution.py:941
  190.2 6.3 %collective-permute-done.53 = bf16[200,384]{1,0:T(8,128)(2,1)S(1)} collective-permute-done((bf16[200,384]{1,0:T(8,128)(2,1)S(1)}, bf16[200,384]{1,0:T(8,128)(2,1)S(1)}, u32[]{:S(2)}, u32[]{:S(2)}) %collective-permute-start.53) | collective-permute-done | bytes 153632 | tf_op jit(solution)/shard_map/ppermute | solution.py:941
  201.1 2.0 shard_map.197
  (154 shorter events, 58.5 us)
Async XLA Ops:
  0.6 16.3 %collective-permute-start.3 = (bf16[192,768]{1,0:T(8,128)(2,1)}, bf16[192,768]{1,0:T(8,128)(2,1)S(1)}, u32[]{:S(2)}, u32[]{:S(2)}) collective-permute-start(bf16[192,768]{1,0:T(8,128)(2,1)} %bitcast.206), channel_id=1, source_target_pairs={{0,16},{8,24},{16,0},{24,8},{1,17},{9,25},{17,1},{25,9},{2,18},{10... | collective-permute-start | bytes 884744 | tf_op jit(solution)/shard_map/ppermute | solution.py:925
  16.9 14.0 %collective-permute-start.5 = (bf16[200,768]{1,0:T(8,128)(2,1)}, bf16[200,768]{1,0:T(8,128)(2,1)S(1)}, u32[]{:S(2)}, u32[]{:S(2)}) collective-permute-start(bf16[200,768]{1,0:T(8,128)(2,1)} %get-tuple-element.186.xo), channel_id=1, source_target_pairs={{0,2},{1,3},{2,4},{3,5},{4,6},{5,7},{6,0},{7,1},{8,10},{9,11},{10,... | collective-permute-start | bytes 921608 | tf_op jit(solution)/shard_map/ppermute | solution.py:941
  18.1 12.9 %collective-permute-start.7 = (bf16[192,768]{1,0:T(8,128)(2,1)}, bf16[192,768]{1,0:T(8,128)(2,1)S(1)}, u32[]{:S(2)}, u32[]{:S(2)}) collective-permute-start(bf16[192,768]{1,0:T(8,128)(2,1)} %get-tuple-element.205.own), channel_id=1, source_target_pairs={{0,1},{1,0},{2,3},{3,2},{4,5},{5,4},{6,7},{7,6},{8,9},{9,8},{10,11... | collective-permute-start | bytes 884744 | tf_op jit(solution)/shard_map/ppermute | solution.py:937
  19.6 11.3 %collective-permute-start.4 = (bf16[48,1664]{1,0:T(8,128)(2,1)S(1)}, bf16[48,1664]{1,0:T(8,128)(2,1)S(1)}, u32[]{:S(2)}, u32[]{:S(2)}) collective-permute-start(bf16[48,1664]{1,0:T(8,128)(2,1)S(1)} %collective-permute-done), channel_id=1, source_target_pairs={{0,2},{1,3},{2,4},{3,5},{4,6},{5,7},{6,0},{7,1},{8,10},{9,11},{10,... | collective-permute-start | bytes 479240 | tf_op jit(solution)/shard_map/ppermute | solution.py:941
  20.4 10.6 %collective-permute-start.6 = (bf16[48,1664]{1,0:T(8,128)(2,1)S(1)}, bf16[48,1664]{1,0:T(8,128)(2,1)S(1)}, u32[]{:S(2)}, u32[]{:S(2)}) collective-permute-start(bf16[48,1664]{1,0:T(8,128)(2,1)S(1)} %collective-permute-done.2), channel_id=1, source_target_pairs={{0,16},{8,24},{16,0},{24,8},{1,17},{9,25},{17,1},{25,9},{2,18},{10... | collective-permute-start | bytes 479240 | tf_op jit(solution)/shard_map/ppermute | solution.py:925
  31.0 13.0 %collective-permute-start.8 = (bf16[144,1664]{1,0:T(8,128)(2,1)S(1)}, bf16[144,1664]{1,0:T(8,128)(2,1)S(1)}, u32[]{:S(2)}, u32[]{:S(2)}) collective-permute-start(bf16[144,1664]{1,0:T(8,128)(2,1)S(1)} %pad_maximum_fusion.2), channel_id=1, source_target_pairs={{0,1},{1,0},{2,3},{3,2},{4,5},{5,4},{6,7},{7,6},{8,9},{9,8},{10,11... | collective-permute-start | bytes 1437704 | tf_op jit(solution)/shard_map/ppermute | solution.py:937
  32.6 11.4 %collective-permute-start.9 = (bf16[144,1664]{1,0:T(8,128)(2,1)S(1)}, bf16[144,1664]{1,0:T(8,128)(2,1)S(1)}, u32[]{:S(2)}, u32[]{:S(2)}) collective-permute-start(bf16[144,1664]{1,0:T(8,128)(2,1)S(1)} %pad_maximum_fusion.2), channel_id=1, source_target_pairs={{0,16},{8,24},{16,0},{24,8},{1,17},{9,25},{17,1},{25,9},{2,18},{10... | collective-permute-start | bytes 1437704 | tf_op jit(solution)/shard_map/ppermute | solution.py:925
  33.1 10.9 %collective-permute-start.10 = (bf16[200,768]{1,0:T(8,128)(2,1)S(1)}, bf16[200,768]{1,0:T(8,128)(2,1)S(1)}, u32[]{:S(2)}, u32[]{:S(2)}) collective-permute-start(bf16[200,768]{1,0:T(8,128)(2,1)S(1)} %collective-permute-done.5.x2), channel_id=1, source_target_pairs={{0,2},{1,3},{2,4},{3,5},{4,6},{5,7},{6,0},{7,1},{8,10},{9,11},{10,... | collective-permute-start | bytes 921608 | tf_op jit(solution)/shard_map/ppermute | solution.py:941
  33.1 10.8 %collective-permute-start.11 = (bf16[96,768]{1,0:T(8,128)(2,1)}, bf16[96,768]{1,0:T(8,128)(2,1)S(1)}, u32[]{:S(2)}, u32[]{:S(2)}) collective-permute-start(bf16[96,768]{1,0:T(8,128)(2,1)} %get-tuple-element.197), channel_id=1, source_target_pairs={{0,6},{1,7},{2,0},{3,1},{4,2},{5,3},{6,4},{7,5},{8,14},{9,15},{10,... | collective-permute-start | bytes 442376 | tf_op jit(solution)/shard_map/ppermute | solution.py:941
  44.1 12.7 %collective-permute-start.12 = (bf16[2,200,768]{2,1,0:T(8,128)(2,1)S(1)}, bf16[2,200,768]{2,1,0:T(8,128)(2,1)S(1)}, u32[]{:S(2)}, u32[]{:S(2)}) collective-permute-start(bf16[2,200,768]{2,1,0:T(8,128)(2,1)S(1)} %pad_maximum_fusion), channel_id=1, source_target_pairs={{0,1},{1,0},{2,3},{3,2},{4,5},{5,4},{6,7},{7,6},{8,9},{9,8},{10,11... | collective-permute-start | bytes 1843208 | tf_op jit(solution)/shard_map/ppermute | solution.py:937
  44.7 10.2 %collective-permute-start.13 = (bf16[144,1664]{1,0:T(8,128)(2,1)S(1)}, bf16[144,1664]{1,0:T(8,128)(2,1)S(1)}, u32[]{:S(2)}, u32[]{:S(2)}) collective-permute-start(bf16[144,1664]{1,0:T(8,128)(2,1)S(1)} %collective-permute-done.8), channel_id=1, source_target_pairs={{0,16},{8,24},{16,0},{24,8},{1,17},{9,25},{17,1},{25,9},{2,18},{10... | collective-permute-start | bytes 1437704 | tf_op jit(solution)/shard_map/ppermute | solution.py:925
  61.2 16.4 %collective-permute-start.24 = (bf16[192,768]{1,0:T(8,128)(2,1)S(1)}, bf16[192,768]{1,0:T(8,128)(2,1)S(1)}, u32[]{:S(2)}, u32[]{:S(2)}) collective-permute-start(bf16[192,768]{1,0:T(8,128)(2,1)S(1)} %bitcast.207), channel_id=1, source_target_pairs={{0,8},{8,0},{16,24},{24,16},{1,9},{9,1},{17,25},{25,17},{2,10},{10... | collective-permute-start | bytes 884744 | tf_op jit(solution)/shard_map/ppermute | solution.py:925
  61.5 16.2 %collective-permute-start.25 = (bf16[192,768]{1,0:T(8,128)(2,1)S(1)}, bf16[192,768]{1,0:T(8,128)(2,1)S(1)}, u32[]{:S(2)}, u32[]{:S(2)}) collective-permute-start(bf16[192,768]{1,0:T(8,128)(2,1)S(1)} %collective-permute-done.3.dy_x), channel_id=1, source_target_pairs={{0,8},{8,0},{16,24},{24,16},{1,9},{9,1},{17,25},{25,17},{2,10},{10... | collective-permute-start | bytes 884744 | tf_op jit(solution)/shard_map/ppermute | solution.py:925
  61.7 15.9 %collective-permute-start.22 = (bf16[384,768]{1,0:T(8,128)(2,1)S(1)}, bf16[384,768]{1,0:T(8,128)(2,1)S(1)}, u32[]{:S(2)}, u32[]{:S(2)}) collective-permute-start(bf16[384,768]{1,0:T(8,128)(2,1)S(1)} %pad_maximum_fusion.1), channel_id=1, source_target_pairs={{0,1},{1,0},{2,3},{3,2},{4,5},{5,4},{6,7},{7,6},{8,9},{9,8},{10,11... | collective-permute-start | bytes 1769480 | tf_op jit(solution)/shard_map/ppermute | solution.py:937
  62.3 15.3 %collective-permute-start.23 = (bf16[192,768]{1,0:T(8,128)(2,1)S(1)}, bf16[192,768]{1,0:T(8,128)(2,1)S(1)}, u32[]{:S(2)}, u32[]{:S(2)}) collective-permute-start(bf16[192,768]{1,0:T(8,128)(2,1)S(1)} %collective-permute-done.14.z1), channel_id=1, source_target_pairs={{0,2},{1,3},{2,4},{3,5},{4,6},{5,7},{6,0},{7,1},{8,10},{9,11},{10,... | collective-permute-start | bytes 884744 | tf_op jit(solution)/shard_map/ppermute | solution.py:941
  78.3 9.4 %collective-permute-start.28 = (bf16[192,768]{1,0:T(8,128)(2,1)S(1)}, bf16[192,768]{1,0:T(8,128)(2,1)S(1)}, u32[]{:S(2)}, u32[]{:S(2)}) collective-permute-start(bf16[192,768]{1,0:T(8,128)(2,1)S(1)} %collective-permute-done.23.z2), channel_id=1, source_target_pairs={{0,1},{1,0},{2,3},{3,2},{4,5},{5,4},{6,7},{7,6},{8,9},{9,8},{10,11... | collective-permute-start | bytes 884744 | tf_op jit(solution)/shard_map/ppermute | solution.py:937
  106.8 14.5 %collective-permute-start.34 = (bf16[192,768]{1,0:T(8,128)(2,1)S(1)}, bf16[192,768]{1,0:T(8,128)(2,1)S(1)}, u32[]{:S(2)}, u32[]{:S(2)}) collective-permute-start(bf16[192,768]{1,0:T(8,128)(2,1)S(1)} %fusion.16), channel_id=1, source_target_pairs={{0,16},{8,24},{16,0},{24,8},{1,17},{9,25},{17,1},{25,9},{2,18},{10... | collective-permute-start | bytes 884744 | tf_op jit(solution)/shard_map/ppermute | solution.py:925
  108.4 14.3 %collective-permute-start.33 = (bf16[4,96,768]{2,1,0:T(8,128)(2,1)S(1)}, bf16[4,96,768]{2,1,0:T(8,128)(2,1)S(1)}, u32[]{:S(2)}, u32[]{:S(2)}) collective-permute-start(bf16[4,96,768]{2,1,0:T(8,128)(2,1)S(1)} %slice_bitcast_fusion.1), channel_id=1, source_target_pairs={{0,1},{1,0},{2,3},{3,2},{4,5},{5,4},{6,7},{7,6},{8,9},{9,8},{10,11... | collective-permute-start | bytes 1769480 | tf_op jit(solution)/shard_map/ppermute | solution.py:937
  122.7 16.9 %collective-permute-start.35 = (bf16[2,2,4,120,384]{4,3,2,1,0:T(8,128)(2,1)S(1)}, bf16[2,2,4,120,384]{4,3,2,1,0:T(8,128)(2,1)S(1)}, u32[]{:S(2)}, u32[]{:S(2)}) collective-permute-start(bf16[2,2,4,120,384]{4,3,2,1,0:T(8,128)(2,1)S(1)} %get-tuple-element.303), channel_id=1, source_target_pairs={{0,8},{8,0},{16,24},{24,16},{1,9},{9,1},{17,25},{25,17},{2,10},{10... | collective-permute-start | bytes 4423688 | tf_op jit(solution)/shard_map/ppermute | solution.py:925
  122.7 16.9 %collective-permute-start.36 = (bf16[4,96,768]{2,1,0:T(8,128)(2,1)S(1)}, bf16[4,96,768]{2,1,0:T(8,128)(2,1)S(1)}, u32[]{:S(2)}, u32[]{:S(2)}) collective-permute-start(bf16[4,96,768]{2,1,0:T(8,128)(2,1)S(1)} %slice_bitcast_fusion), channel_id=1, source_target_pairs={{0,1},{1,0},{2,3},{3,2},{4,5},{5,4},{6,7},{7,6},{8,9},{9,8},{10,11... | collective-permute-start | bytes 1769480 | tf_op jit(solution)/shard_map/ppermute | solution.py:937
  124.3 15.3 %collective-permute-start.37 = (bf16[96,768]{1,0:T(8,128)(2,1)S(1)}, bf16[96,768]{1,0:T(8,128)(2,1)S(1)}, u32[]{:S(2)}, u32[]{:S(2)}) collective-permute-start(bf16[96,768]{1,0:T(8,128)(2,1)S(1)} %get-tuple-element.360), channel_id=1, source_target_pairs={{0,2},{1,3},{2,4},{3,5},{4,6},{5,7},{6,0},{7,1},{8,10},{9,11},{10,... | collective-permute-start | bytes 442376 | tf_op jit(solution)/shard_map/ppermute | solution.py:941
  125.5 14.2 %collective-permute-start.38 = (bf16[96,768]{1,0:T(8,128)(2,1)S(1)}, bf16[96,768]{1,0:T(8,128)(2,1)S(1)}, u32[]{:S(2)}, u32[]{:S(2)}) collective-permute-start(bf16[96,768]{1,0:T(8,128)(2,1)S(1)} %get-tuple-element.359), channel_id=1, source_target_pairs={{0,4},{1,5},{2,6},{3,7},{4,0},{5,1},{6,2},{7,3},{8,12},{9,13},{10,... | collective-permute-start | bytes 442376 | tf_op jit(solution)/shard_map/ppermute | solution.py:941
  127.4 12.3 %collective-permute-start.39 = (bf16[96,768]{1,0:T(8,128)(2,1)S(1)}, bf16[96,768]{1,0:T(8,128)(2,1)S(1)}, u32[]{:S(2)}, u32[]{:S(2)}) collective-permute-start(bf16[96,768]{1,0:T(8,128)(2,1)S(1)} %get-tuple-element.358), channel_id=1, source_target_pairs={{0,6},{1,7},{2,0},{3,1},{4,2},{5,3},{6,4},{7,5},{8,14},{9,15},{10,... | collective-permute-start | bytes 442376 | tf_op jit(solution)/shard_map/ppermute | solution.py:941
  139.9 17.8 %collective-permute-start.42 = (bf16[2,4,120,384]{3,2,1,0:T(8,128)(2,1)S(1)}, bf16[2,4,120,384]{3,2,1,0:T(8,128)(2,1)S(1)}, u32[]{:S(2)}, u32[]{:S(2)}) collective-permute-start(bf16[2,4,120,384]{3,2,1,0:T(8,128)(2,1)S(1)} %fusion.1), channel_id=1, source_target_pairs={{0,16},{8,24},{16,0},{24,8},{1,17},{9,25},{17,1},{25,9},{2,18},{10... | collective-permute-start | bytes 2211848 | tf_op jit(solution)/shard_map/ppermute | solution.py:925
  141.4 14.3 %collective-permute-start.43 = (bf16[2,192,768]{2,1,0:T(8,128)(2,1)S(1)}, bf16[2,192,768]{2,1,0:T(8,128)(2,1)S(1)}, u32[]{:S(2)}, u32[]{:S(2)}) collective-permute-start(bf16[2,192,768]{2,1,0:T(8,128)(2,1)S(1)} %get-tuple-element.313), channel_id=1, source_target_pairs={{0,1},{1,0},{2,3},{3,2},{4,5},{5,4},{6,7},{7,6},{8,9},{9,8},{10,11... | collective-permute-start | bytes 1769480 | tf_op jit(solution)/shard_map/ppermute | solution.py:937
  157.8 15.6 %collective-permute-start.47 = (bf16[192,768]{1,0:T(8,128)(2,1)S(1)}, bf16[192,768]{1,0:T(8,128)(2,1)S(1)}, u32[]{:S(2)}, u32[]{:S(2)}) collective-permute-start(bf16[192,768]{1,0:T(8,128)(2,1)S(1)} %fusion.18), channel_id=1, source_target_pairs={{0,6},{1,7},{2,0},{3,1},{4,2},{5,3},{6,4},{7,5},{8,14},{9,15},{10,... | collective-permute-start | bytes 884744 | tf_op jit(solution)/shard_map/ppermute | solution.py:941
  160.6 12.8 %collective-permute-start.45 = (bf16[2,4,80,384]{3,2,1,0:T(8,128)(2,1)S(1)}, bf16[2,4,80,384]{3,2,1,0:T(8,128)(2,1)S(1)}, u32[]{:S(2)}, u32[]{:S(2)}) collective-permute-start(bf16[2,4,80,384]{3,2,1,0:T(8,128)(2,1)S(1)} %fusion), channel_id=1, source_target_pairs={{0,16},{8,24},{16,0},{24,8},{1,17},{9,25},{17,1},{25,9},{2,18},{10... | collective-permute-start | bytes 1474568 | tf_op jit(solution)/shard_map/ppermute | solution.py:925
  162.3 11.1 %collective-permute-start.46 = (bf16[4,120,384]{2,1,0:T(8,128)(2,1)S(1)}, bf16[4,120,384]{2,1,0:T(8,128)(2,1)S(1)}, u32[]{:S(2)}, u32[]{:S(2)}) collective-permute-start(bf16[4,120,384]{2,1,0:T(8,128)(2,1)S(1)} %fusion.2), channel_id=1, source_target_pairs={{0,1},{1,0},{2,3},{3,2},{4,5},{5,4},{6,7},{7,6},{8,9},{9,8},{10,11... | collective-permute-start | bytes 1105928 | tf_op jit(solution)/shard_map/ppermute | solution.py:937
  163.0 9.2 %collective-permute-start.48 = (bf16[96,768]{1,0:T(8,128)(2,1)S(1)}, bf16[96,768]{1,0:T(8,128)(2,1)S(1)}, u32[]{:S(2)}, u32[]{:S(2)}) collective-permute-start(bf16[96,768]{1,0:T(8,128)(2,1)S(1)} %get-tuple-element.357), channel_id=1, source_target_pairs={{0,2},{1,3},{2,4},{3,5},{4,6},{5,7},{6,0},{7,1},{8,10},{9,11},{10,... | collective-permute-start | bytes 442376 | tf_op jit(solution)/shard_map/ppermute | solution.py:941
  163.0 10.4 %collective-permute-start.49 = (bf16[96,768]{1,0:T(8,128)(2,1)S(1)}, bf16[96,768]{1,0:T(8,128)(2,1)S(1)}, u32[]{:S(2)}, u32[]{:S(2)}) collective-permute-start(bf16[96,768]{1,0:T(8,128)(2,1)S(1)} %get-tuple-element.356), channel_id=1, source_target_pairs={{0,6},{1,7},{2,0},{3,1},{4,2},{5,3},{6,4},{7,5},{8,14},{9,15},{10,... | collective-permute-start | bytes 442376 | tf_op jit(solution)/shard_map/ppermute | solution.py:941
  185.8 10.7 %collective-permute-start.53 = (bf16[200,384]{1,0:T(8,128)(2,1)S(1)}, bf16[200,384]{1,0:T(8,128)(2,1)S(1)}, u32[]{:S(2)}, u32[]{:S(2)}) collective-permute-start(bf16[200,384]{1,0:T(8,128)(2,1)S(1)} %pad_maximum_fusion.5), channel_id=1, source_target_pairs={{0,4},{1,5},{2,6},{3,7},{4,0},{5,1},{6,2},{7,3},{8,12},{9,13},{10,... | collective-permute-start | bytes 460808 | tf_op jit(solution)/shard_map/ppermute | solution.py:941
  185.9 10.6 %collective-permute-start.55 = (bf16[192,768]{1,0:T(8,128)(2,1)S(1)}, bf16[192,768]{1,0:T(8,128)(2,1)S(1)}, u32[]{:S(2)}, u32[]{:S(2)}) collective-permute-start(bf16[192,768]{1,0:T(8,128)(2,1)S(1)} %pad_maximum_fusion.3.f0), channel_id=1, source_target_pairs={{0,16},{8,24},{16,0},{24,8},{1,17},{9,25},{17,1},{25,9},{2,18},{10... | collective-permute-start | bytes 884744 | tf_op jit(solution)/shard_map/ppermute | solution.py:925
  (37 other events, 274.5 us)

commit v8 on v7

--- a/solution.py
+++ b/solution.py
@@ -581,7 +581,7 @@
     h2_out[...] = b16(hat * vec[1:2] + vec[3:4])
 
 
-def feed_tokens(h2, dy, w_up, w_down, upb, act_out, du_out, y_acc, dh_acc):
+def feed_tokens(h2, dy, w_up, w_down, upb, act_out, du_out):
     root = math.sqrt(2.0 / math.pi)
     chunk = 256
 
@@ -600,8 +600,7 @@
         return carry
 
     lax.fori_loop(0, w_up.shape[1] // chunk, feed, 0)
-    dh_acc[...] = dot_nt(du_out[...], w_up[...])
-    y_acc[...] = dot_nn(act_out[...], w_down[...])
+    return dot_nt(du_out[...], w_up[...])
 
 
 def assemble_kernel(own, z1, z2, z3u, z3d, y0, y13, wu_out, wd_out, sems):
@@ -626,7 +625,7 @@
 def near_kernel(
     h_own, h_c, dy_own, dy_c, upb, y2, _wu, _wd,
     h2, dy, act_out, du_out, keep_out, send_out, wu_out, wd_out,
-    y_acc, dh_acc, sems,
+    sems,
 ):
     _x, _c, y, z = place()
     tok, width = h_own.shape
@@ -640,38 +639,45 @@
     dy[pl.ds(0, tok), :] = dy_own[...]
     dy[pl.ds(tok, tok), :] = dy_c[...]
     copies.wait()
-    feed_tokens(h2, dy, wu_out, wd_out, upb, act_out, du_out, y_acc, dh_acc)
-    keep_out[0] = dh_acc[pl.ds(0, tok), :]
-    keep_out[1] = y_acc[pl.ds(0, tok), :]
-    send_out[0] = b16(dh_acc[pl.ds(tok, tok), :])
-    send_out[1] = b16(y_acc[pl.ds(tok, tok), :])
-
-
-def far_kernel(
-    h_x, h_xc, dy_x, dy_xc, upb, w_up, w_down, h_near, dy_near, act_near, du_near,
-    hs, dys, acts, dus, keep_out, send_out,
-    y_acc, dh_acc, sems,
+    grad = feed_tokens(h2, dy, wu_out, wd_out, upb, act_out, du_out)
+    keep_out[...] = grad[:tok]
+    send_out[...] = b16(grad[tok:])
+
+
+def far_c_kernel(
+    h_xc, dy_xc, upb, w_up, w_down, h_near, dy_near, act_near, du_near,
+    hs, dys, acts, dus, send_out,
+    sems,
 ):
-    tok = dy_x.shape[0]
+    tok = dy_xc.shape[0]
     copies = Copies(sems)
     for source, target in ((h_near, hs), (dy_near, dys), (act_near, acts), (du_near, dus)):
         copies.add(source, target.at[pl.ds(0, 2 * tok), :])
-    later = pl.ds(2 * tok, 2 * tok)
-    hs[pl.ds(2 * tok, tok), :] = h_x[...]
-    hs[pl.ds(3 * tok, tok), :] = h_xc[...]
-    dys[pl.ds(2 * tok, tok), :] = dy_x[...]
-    dys[pl.ds(3 * tok, tok), :] = dy_xc[...]
-    feed_tokens(
-        hs.at[later, :], dys.at[later, :], w_up, w_down, upb, acts.at[later, :], dus.at[later, :], y_acc, dh_acc
-    )
-    keep_out[0] = dh_acc[pl.ds(0, tok), :]
-    keep_out[1] = y_acc[pl.ds(0, tok), :]
-    send_out[0] = b16(dh_acc[pl.ds(tok, tok), :])
-    send_out[1] = b16(y_acc[pl.ds(tok, tok), :])
+    last = pl.ds(3 * tok, tok)
+    hs[last, :] = h_xc[...]
+    dys[last, :] = dy_xc[...]
+    send_out[...] = b16(
+        feed_tokens(h_xc, dy_xc, w_up, w_down, upb, acts.at[last, :], dus.at[last, :])
+    )
     copies.wait()
 
 
-def weights_kernel(hs, dys, acts, dus, u_out, d_out, upb_out, stage, sems):
+def far_x_kernel(
+    h_x, dy_x, upb, w_up, w_down, _hs, _dys, _acts, _dus,
+    hs, dys, acts, dus, keep_out,
+):
+    tok = dy_x.shape[0]
+    third = pl.ds(2 * tok, tok)
+    hs[third, :] = h_x[...]
+    dys[third, :] = dy_x[...]
+    keep_out[...] = feed_tokens(h_x, dy_x, w_up, w_down, upb, acts.at[third, :], dus.at[third, :])
+
+
+def weights_kernel(
+    hs, dys, acts, dus, w_down,
+    u_out, d_out, upb_out, keep_out, send_out,
+    stage, sems,
+):
     _x, _c, y, z = place()
     width = hs.shape[1]
     rows = width // 8
@@ -690,6 +696,13 @@
         yy = jnp.where(y == shard % 2, 0, 1)
         outs.add(stage.at[0, pl.ds(shard * rows, rows), :], u_out.at[yy, zz])
         outs.add(stage.at[1, pl.ds(shard * rows, rows), :], d_out.at[yy, zz])
+    tok = hs.shape[0] // 4
+    for number in range(4):
+        part = dot_nn(acts[pl.ds(number * tok, tok), :], w_down[...])
+        if number % 2:
+            send_out[number // 2] = b16(part)
+        else:
+            keep_out[number // 2] = part
     outs.wait()
 
 
@@ -711,7 +724,7 @@
     dr_out, da_out, dw_out, vec_out,
 ):
     vec = vec_in[...]
-    grad_hidden = own[0] + f32(near[0]) + f32(across[...])
+    grad_hidden = own[...] + f32(near[...]) + f32(across[...])
     hat, rate = norm_parts(residual[...])
     dy = f32(dy_in[...])
     grad_first = dy + norm_back(grad_hidden, hat, rate, vec[1:2])
@@ -1065,14 +1078,13 @@
     h_x, h_c, f_y2, *w_half = fence(to_x(hidden_2), to_core(hidden_2), to_y(f2), *w_half)
     act = shape_of((2 * tok, width), bf)
     acts = shape_of((4 * tok, width), bf)
-    feed_shapes = [shape_of((2, tok, width), fl), shape_of((2, tok, width), bf)]
-    feed_scratch = [pltpu.VMEM((2 * tok, width), fl), pltpu.VMEM((2 * tok, width), fl)]
+    feed_shapes = [shape_of((tok, width), fl), shape_of((tok, width), bf)]
     *near_acts, keep_a, send_a, w_up, w_down = call(
         near_kernel,
         [VM] * 5 + [AN] + [VM] * 2,
         [VM] * 8,
         [act] * 4 + feed_shapes + [shape_of((width, width), bf)] * 2,
-        feed_scratch + [dma((2,))],
+        [dma((2,))],
         flops=3 * 10**9,
         vmem=8,
         moved=6 * 10**6,
@@ -1081,30 +1093,49 @@
     h_xc = to_core(h_x)
     keep_a, send_a, h_xc, w_up = fence(keep_a, send_a, h_xc, w_up)
     came_a = to_core(send_a)
-    *all_acts, keep_b, send_b = call(
-        far_kernel,
-        [VM] * 7 + [AN] * 4,
-        [VM] * 6,
-        [acts] * 4 + feed_shapes,
-        feed_scratch + [dma((4,))],
+    *all_acts, send_b = call(
+        far_c_kernel,
+        [VM] * 5 + [AN] * 4,
+        [VM] * 5,
+        [acts] * 4 + feed_shapes[1:],
+        [dma((4,))],
+        flops=15 * 10**8,
+        vmem=8,
+        moved=6 * 10**6,
+    )(h_xc, dy_xc, upb, w_up, w_down, *near_acts)
+    send_b, came_a, h_x = fence(send_b, came_a, h_x)
+    came_b = to_core(send_b)
+    *all_acts, keep_b = call(
+        far_x_kernel,
+        [VM] * 9,
+        [VM] * 5,
+        [acts] * 4 + feed_shapes[:1],
         flops=3 * 10**9,
-        vmem=8, moved=6 * 10**6,
-    )(h_x, h_xc, dy_x, dy_xc, upb, w_up, w_down, *near_acts)
-    keep_b, send_b, came_a = fence(keep_b, send_b, came_a)
-    keep_b, came_b, *all_acts = fence(keep_b, to_core(send_b), *all_acts)
-    back_x = to_x(b16(keep_b[0] + f32(came_b[0])))
-    u_terms, d_terms, upb_g = call(
+        vmem=8,
+        moved=6 * 10**6,
+        aliases={5: 0, 6: 1, 7: 2, 8: 3},
+    )(h_x, dy_x, upb, w_up, w_down, *all_acts)
+    keep_b, came_b, *all_acts = fence(keep_b, came_b, *all_acts)
+    back_x = to_x(b16(keep_b + f32(came_b)))
+    u_terms, d_terms, upb_g, y_keep, y_send = call(
         weights_kernel,
-        [VM] * 4,
-        [AN, AN, VM],
-        [shape_of((2, 4, 96, width), bf), shape_of((2, 4, 96, width), bf), shape_of((1, width), fl)],
+        [VM] * 5,
+        [AN, AN] + [VM] * 3,
+        [
+            shape_of((2, 4, 96, width), bf),
+            shape_of((2, 4, 96, width), bf),
+            shape_of((1, width), fl),
+            shape_of((2, tok, width), fl),
+            shape_of((2, tok, width), bf),
+        ],
         [pltpu.VMEM((2, width, width), bf), dma((16,))],
         flops=3 * 10**9,
-        vmem=12, moved=6 * 10**6,
-    )(*all_acts)
-    back_x, u_terms, d_terms, keep_b = fence(back_x, u_terms, d_terms, keep_b)
+        vmem=12,
+        moved=6 * 10**6,
+    )(*all_acts, w_down)
+    back_x, u_terms, d_terms, y_send = fence(back_x, u_terms, d_terms, y_send)
     u_came = to_y(u_terms[1])
-    back_y = to_x(b16(keep_b[1] + f32(came_b[1])))
+    came_y = to_core(y_send)
     grad_first, grad_attended, dw_out, vec_g = call(
         post_kernel,
         [VM] * 8,
@@ -1143,8 +1174,8 @@
     def z_sum(part, *came):
         return b16(part(0) + sum(f32(v) for v in came))
 
-    dq_a, qa_other, u_came, back_y, d_send = fence(
-        dq_a, qa_other, u_came, back_y, d_terms[1]
+    dq_a, qa_other, u_came, came_y, d_send = fence(
+        dq_a, qa_other, u_came, came_y, d_terms[1]
     )
     d_came, qa_came = to_y(d_send), to_core(qa_other)
     u_part = both(u_terms[0], u_came)
@@ -1210,7 +1241,10 @@
         return qb_1(0, *index) + f32(qb_x[index])
 
     f_tot = join(z_sum(u_part, *u_z), z_sum(d_part, d_z1, d_z3))
-    qb_y, back_2, f_tot = fence(to_y(b16(qb_2(1))), to_z(b16(sum_2 + f32(hop)), 3), f_tot)
+    fy_tot = join(f_tot, b16(y_keep[1] + f32(came_y[1])))
+    qb_y, back_2, f_tot, fy_tot = fence(
+        to_y(b16(qb_2(1))), to_z(b16(sum_2 + f32(hop)), 3), f_tot, fy_tot
+    )
 
     def q_3(*index):
         first = qa_2(0, *index) + f32(qa_y[index])
@@ -1219,7 +1253,8 @@
     grad_tokens = call(
         tokens_kernel, [VM] * 5, VM, shape_of((tok, width), fl), vmem=4, moved=3 * 10**6
     )(sum_own, back_2, grad_first, own_tokens, vec)
-    *q_z, f_x, f_tot = fence(*(to_z(b16(q_3(step)), step) for step in (1, 2, 3)), to_x(f_tot), f_tot)
+    *q_z, over_x, f_tot = fence(*(to_z(b16(q_3(step)), step) for step in (1, 2, 3)), to_x(fy_tot), f_tot)
+    f_x, back_y = over_x[:tok], over_x[tok:]
     q_sum = z_sum(q_3, *q_z)
     q_fx, q_fc, q_fxc = to_x(q_sum), to_core(q_sum), swap_rep(q_sum, 3)
     grad_up, grad_down = call(
@@ -1232,7 +1267,7 @@
         moved=4 * 10**6,
     )(f_tot, f_x, to_core(f_tot), to_core(f_x))
     q_fx, q_fc, q_fxc, grad_up, grad_down = fence(q_fx, q_fc, q_fxc, grad_up, grad_down)
-    result = b16(residual + vec[7:8] + keep_a[1] + f32(came_a[1]) + f32(back_y))
+    result = b16(residual + vec[7:8] + y_keep[0] + f32(came_y[0]) + f32(back_y))
     grad_qkv, grad_out = call(
         finish_q_kernel,
         [VM] * 4,

time: 206 us -> 205 us (level)
  starting transfers between devices: 66.8 us -> 63.2 us
    ppermute x30, starting transfers between devices: 19.7 us -> 15.3 us  [swap_rep(): return lax.ppermute(value, 'rep', [(k, k ^ bit) for k in range(4)])]
    ppermute x11, waiting for transfers between devices: 7.82 us -> 11.3 us  [to_y(): return lax.ppermute(value, 'seq', [(k, k ^ 1) for k in range(8)])]
    ppermute x30, waiting for transfers between devices: 13.7 us -> 10.4 us  [swap_rep(): return lax.ppermute(value, 'rep', [(k, k ^ bit) for k in range(4)])]
    pallas_call x2 -> x3, Pallas kernels: 9.83 us -> 11.5 us  [the longest x1 7.23 us: on_device_fast(): call(weights_kernel, [VM] * 5, [AN, AN] + [VM] * 3, [shape_of((2, 4, 96,...]
  transfers between devices with their start and end apart: 61 -> 61, of which waited for: 22 -> 21; matrix products, arithmetic and copies ran while one was open for 2% -> 2% of each run, Pallas kernels for 31% -> 31%
where the time goes in v8:
time: 205 us
  waiting for transfers between devices  69.9 us (34%)
  Pallas kernels  65.5 us (32%)
  starting transfers between devices  63.2 us (31%)
  other arithmetic  3.01 us (1%)
  local copies, waits for them, and re-layouts  2.1 us (1%)
    ppermute x20, waiting for transfers between devices, to_z(): lax.ppermute(value, 'seq', [(k, (k + 2 * steps) % 8) for k in range(8)])  48.2 us
    ppermute x20, starting transfers between devices, to_z(): lax.ppermute(value, 'seq', [(k, (k + 2 * steps) % 8) for k in range(8)])  36 us
    ppermute x30, starting transfers between devices, swap_rep(): return lax.ppermute(value, 'rep', [(k, k ^ bit) for k in range(4)])  15.3 us
    pallas_call x1, Pallas kernels, on_device_fast(): call(front_kernel, [VM] * 6 + [AN] * 15, [VM] * 11, [shape_of((tok, width...  13.9 us
    ppermute x11, starting transfers between devices, to_y(): return lax.ppermute(value, 'seq', [(k, k ^ 1) for k in range(8)])  11.9 us
    ppermute x11, waiting for transfers between devices, to_y(): return lax.ppermute(value, 'seq', [(k, k ^ 1) for k in range(8)])  11.3 us
    pallas_call x1, Pallas kernels, on_device_fast(): call(back_b_kernel, [VM] * 14 + [AN] * 13, [VM] * 6, [shape_of((tok, widt...  10.8 us
    ppermute x30, waiting for transfers between devices, swap_rep(): return lax.ppermute(value, 'rep', [(k, k ^ bit) for k in range(4)])  10.4 us
  transfers between devices with their start and end apart: 61, of which 21 were waited for; matrix products, arithmetic and copies ran while one was open for 2% of the time, Pallas kernels for 31%

profile of v8, /device:TPU:0, one launch (start us, length us, event | category | flops | bytes accessed | tf_op | source)
XLA Modules:
  0.0 204.8 jit_solution(2926510940436193933)
XLA Ops:
  0.6 3.0 %collective-permute-start.3 = (bf16[192,768]{1,0:T(8,128)(2,1)}, bf16[192,768]{1,0:T(8,128)(2,1)S(1)}, u32[]{:S(2)}, u32[]{:S(2)}) collective-permute-start(bf16[192,768]{1,0:T(8,128)(2,1)} %bitcast.218), channel_id=1, source_target_pairs={{0,16},{8,24},{16,0},{24,8},{1,17},{9,25},{17,1},{25,9},{2,18},{10... | collective-permute-start | bytes 884744 | tf_op jit(solution)/shard_map/ppermute | solution.py:938
  3.6 2.7 %shard_map.186 = (bf16[200,768]{1,0:T(8,128)(2,1)}, bf16[48,1664]{1,0:T(8,128)(2,1)}, bf16[192,768]{1,0:T(8,128)(2,1)}, bf16[96,768]{1,0:T(8,128)(2,1)}, bf16[96,768]{1,0:T(8,128)(2,1)}) custom-call(bf16[1,192,768]{2,1,0:T(8,128)(2,1)} %tokens.1, s32[1,192]{1,0:T(1,128)} %segs.1, bf16[96,2304]{1,0:T(8,128)(2,1)} %own.3, bf16[96,768]{1,0:T(8,128)(2,1)} %own_o.1, ...), custom_call_target="tpu_custom_call" | custom-call | bytes 4000000 | tf_op jit(solution)/shard_map/pallas_call | solution.py:982
  8.0 2.2 %collective-permute-start.1 = (bf16[48,1664]{1,0:T(8,128)(2,1)}, bf16[48,1664]{1,0:T(8,128)(2,1)S(1)}, u32[]{:S(2)}, u32[]{:S(2)}) collective-permute-start(bf16[48,1664]{1,0:T(8,128)(2,1)} %get-tuple-element.188.first), channel_id=1, source_target_pairs={{0,6},{1,7},{2,0},{3,1},{4,2},{5,3},{6,4},{7,5},{8,14},{9,15},{10,... | collective-permute-start | bytes 479240 | tf_op jit(solution)/shard_map/ppermute | solution.py:954
  11.8 3.7 %collective-permute-done = bf16[48,1664]{1,0:T(8,128)(2,1)S(1)} collective-permute-done((bf16[48,1664]{1,0:T(8,128)(2,1)}, bf16[48,1664]{1,0:T(8,128)(2,1)S(1)}, u32[]{:S(2)}, u32[]{:S(2)}) %collective-permute-start) | collective-permute-done | bytes 159776 | tf_op jit(solution)/shard_map/ppermute | solution.py:954
  20.9 10.0 %collective-permute-done.4 = bf16[48,1664]{1,0:T(8,128)(2,1)S(1)} collective-permute-done((bf16[48,1664]{1,0:T(8,128)(2,1)S(1)}, bf16[48,1664]{1,0:T(8,128)(2,1)S(1)}, u32[]{:S(2)}, u32[]{:S(2)}) %collective-permute-start.4) | collective-permute-done | bytes 159776 | tf_op jit(solution)/shard_map/ppermute | solution.py:954
  33.1 3.8 %collective-permute-start.11 = (bf16[96,768]{1,0:T(8,128)(2,1)}, bf16[96,768]{1,0:T(8,128)(2,1)S(1)}, u32[]{:S(2)}, u32[]{:S(2)}) collective-permute-start(bf16[96,768]{1,0:T(8,128)(2,1)} %get-tuple-element.204), channel_id=1, source_target_pairs={{0,6},{1,7},{2,0},{3,1},{4,2},{5,3},{6,4},{7,5},{8,14},{9,15},{10,... | collective-permute-start | bytes 442376 | tf_op jit(solution)/shard_map/ppermute | solution.py:954
  36.9 7.0 %collective-permute-done.11.z3d = bf16[96,768]{1,0:T(8,128)(2,1)S(1)} collective-permute-done((bf16[96,768]{1,0:T(8,128)(2,1)}, bf16[96,768]{1,0:T(8,128)(2,1)S(1)}, u32[]{:S(2)}, u32[]{:S(2)}) %collective-permute-start.11) | collective-permute-done | bytes 147488 | tf_op jit(solution)/shard_map/ppermute | solution.py:954
  46.5 3.5 %collective-permute-start.15 = (bf16[96,768]{1,0:T(8,128)(2,1)S(1)}, bf16[96,768]{1,0:T(8,128)(2,1)S(1)}, u32[]{:S(2)}, u32[]{:S(2)}) collective-permute-start(bf16[96,768]{1,0:T(8,128)(2,1)S(1)} %copy-done.7), channel_id=1, source_target_pairs={{0,6},{1,7},{2,0},{3,1},{4,2},{5,3},{6,4},{7,5},{8,14},{9,15},{10,... | collective-permute-start | bytes 442376 | tf_op jit(solution)/shard_map/ppermute | solution.py:954
  50.0 4.9 %collective-permute-done.15.z3u = bf16[96,768]{1,0:T(8,128)(2,1)S(1)} collective-permute-done((bf16[96,768]{1,0:T(8,128)(2,1)S(1)}, bf16[96,768]{1,0:T(8,128)(2,1)S(1)}, u32[]{:S(2)}, u32[]{:S(2)}) %collective-permute-start.15) | collective-permute-done | bytes 147488 | tf_op jit(solution)/shard_map/ppermute | solution.py:954
  58.6 2.6 %collective-permute-done.20 = bf16[48,1664]{1,0:T(8,128)(2,1)S(1)} collective-permute-done((bf16[48,1664]{1,0:T(8,128)(2,1)S(1)}, bf16[48,1664]{1,0:T(8,128)(2,1)S(1)}, u32[]{:S(2)}, u32[]{:S(2)}) %collective-permute-start.20) | collective-permute-done | bytes 159776 | tf_op jit(solution)/shard_map/ppermute | solution.py:938
  63.8 13.9 %shard_map.187 = (bf16[192,768]{1,0:T(8,128)(2,1)S(1)}, bf16[960,1536]{1,0:T(8,128)(2,1)S(1)}, bf16[960,768]{1,0:T(8,128)(2,1)S(1)}, bf16[192,768]{1,0:T(8,128)(...) custom-call(s32[1,384]{1,0:T(1,128)S(1)} %pad_add_fusion.seg, ...), custom_call_target="tpu_custom_call" | custom-call | flops 7000000000 | bytes 12000000 | tf_op jit(solution)/shard_map/pallas_call | solution.py:1038
  79.8 2.9 %shard_map.188 = (bf16[768,768]{1,0:T(8,128)(2,1)S(1)}, bf16[768,768]{1,0:T(8,128)(2,1)S(1)}) custom-call(bf16[192,768]{1,0:T(8,128)(2,1)S(1)} %copy-done.2, bf16[192,768]{1,0:T(8,128)(2,1)S(1)} %collective-permute-done.14.z1, bf16[192,768]{1,0:T(8,128)(2,1)S(1)} %collective-permute-done.23.z2, bf16[96,768]{1,0:T(8,128)(2,1)S(1)} %collective-permute-done.15.z3u, ...), custom_call_target="tpu_custom_call" | custom-call | bytes 5000000 | tf_op jit(solution)/shard_map/pallas_call | solution.py:1069
  82.6 3.8 %collective-permute-done.26.h_x = bf16[192,768]{1,0:T(8,128)(2,1)S(1)} collective-permute-done((bf16[192,768]{1,0:T(8,128)(2,1)S(1)}, bf16[192,768]{1,0:T(8,128)(2,1)S(1)}, u32[]{:S(2)}, u32[]{:S(2)}) %collective-permute-start.26) | collective-permute-done | bytes 294944 | tf_op jit(solution)/shard_map/ppermute | solution.py:938
  87.7 3.1 %shard_map.189 = (bf16[384,768]{1,0:T(8,128)(2,1)S(1)}, bf16[384,768]{1,0:T(8,128)(2,1)S(1)}, bf16[384,768]{1,0:T(8,128)(2,1)S(1)}, bf16[384,768]{1,0:T(8,128)(2...) custom-call(bf16[192,768]{1,0:T(8,128)(2,1)S(1)} %get-tuple-element., ...), custom_call_target="tpu_custom_call", output_to_operand_aliasing={{6}: (6, {}), {7}: (7, {})} | custom-call | flops 3000000000 | bytes 6000000 | tf_op jit(solution)/shard_map/pallas_call | solution.py:1082
  91.4 2.4 %shard_map.190 = (bf16[768,768]{1,0:T(8,128)(2,1)S(1)}, bf16[768,768]{1,0:T(8,128)(2,1)S(1)}, bf16[768,768]{1,0:T(8,128)(2,1)S(1)}, bf16[768,768]{1,0:T(8,128)(2,1)S(1)}, bf16[192,768]{1,0:T(8,128)(2,1)S(1)}) custom-call(bf16[192,768]{1,0:T(8,128)(2,1)S(1)} %collective-permute-done.29.h_xc, bf16[192,768]{1,0:T(8,128)(2,1)S(1)} %collective-permute-done.25.dy_xc, ...), custom_call_target="tpu_custom_call" | custom-call | flops 1500000000 | bytes 6000000 | tf_op jit(solution)/shard_map/pallas_call | solution.py:1096
  97.4 7.2 %shard_map.192 = (bf16[2,4,96,768]{3,2,1,0:T(8,128)(2,1)S(1)}, bf16[2,4,96,768]{3,2,1,0:T(8,128)(2,1)S(1)}, f32[1,768]{1,0:T(1,128)S(1)}, f32[2,192,768]{2,1,0:T(8,128)S(1)}, bf16[2,192,768]{2,1,0:T(8,128)(2,1)S(1)}) custom-call(bf16[768,768]{1,0:T(8,128)(2,1)S(1)} %get-tuple-element.282.hs, bf16[768,768]{1,0:T(8,128)(2,1)S(1)} %get-tuple-element.283.dys, ...), custom_call_target="tpu_custom_call" | custom-call | flops 3000000000 | bytes 6000000 | tf_op jit(solution)/shard_map/pallas_call | solution.py:1120
  108.3 10.0 %shard_map.194 = (bf16[2,2,4,120,384]{4,3,2,1,0:T(8,128)(2,1)S(1)}, bf16[2,2,4,120,384]{4,3,2,1,0:T(8,128)(2,1)S(1)}, bf16[192,384]{1,0:T(8,128)(2,1)S(1)}, bf16[960,768]{1,0:T(8,128)(2,1)S(1)}) custom-call(s32[1,384]{1,0:T(1,128)S(1)} %get-tuple-element.287.start_in, bf16[192,768]{1,0:T(8,128)(2,1)S(1)} %get-tuple-element.288.q_in, ...), custom_call_target="tpu_custom_call" | custom-call | flops 5000000000 | bytes 10000000 | tf_op jit(solution)/shard_map/pallas_call | solution.py:1156
  118.3 2.1 %collective-permute-done.33 = bf16[4,96,768]{2,1,0:T(8,128)(2,1)S(1)} collective-permute-done((bf16[4,96,768]{2,1,0:T(8,128)(2,1)S(1)}, bf16[4,96,768]{2,1,0:T(8,128)(2,1)S(1)}, u32[]{:S(2)}, u32[]{:S(2)}) %collective-permute-start.33) | collective-permute-done | bytes 589856 | tf_op jit(solution)/shard_map/ppermute | solution.py:950
  125.3 2.2 %collective-permute-start.39 = (bf16[96,768]{1,0:T(8,128)(2,1)S(1)}, bf16[96,768]{1,0:T(8,128)(2,1)S(1)}, u32[]{:S(2)}, u32[]{:S(2)}) collective-permute-start(bf16[96,768]{1,0:T(8,128)(2,1)S(1)} %get-tuple-element.372), channel_id=1, source_target_pairs={{0,6},{1,7},{2,0},{3,1},{4,2},{5,3},{6,4},{7,5},{8,14},{9,15},{10,... | collective-permute-start | bytes 442376 | tf_op jit(solution)/shard_map/ppermute | solution.py:954
  127.4 10.8 %shard_map.195 = (bf16[192,384]{1,0:T(8,128)(2,1)S(1)}, bf16[960,768]{1,0:T(8,128)(2,1)S(1)}, f32[192,768]{1,0:T(8,128)S(1)}, bf16[2,192,768]{2,1,0:T(8,128)(2,1...) custom-call(s32[1,384]{1,0:T(1,128)S(1)} %get-tuple-element.287.start_in, ...), custom_call_target="tpu_custom_call" | custom-call | flops 6000000000 | bytes 10000000 | tf_op jit(solution)/shard_map/pallas_call | solution.py:1183
  139.6 4.8 %shard_map.196 = (bf16[2,2,4,80,384]{4,3,2,1,0:T(8,128)(2,1)S(1)}, bf16[2,2,4,80,384]{4,3,2,1,0:T(8,128)(2,1)S(1)}) custom-call(bf16[960,768]{1,0:T(8,128)(2,1)S(1)} %get-tuple-element.290.h_in, bf16[192,384]{1,0:T(8,128)(2,1)S(1)} %get-tuple-element.321.dq, bf16[960,768]{1,0:T(8,128)(2,1)S(1)} %get-tuple-element.322.dkv, ...), custom_call_target="tpu_custom_call" | custom-call | flops 3000000000 | bytes 6000000 | tf_op jit(solution)/shard_map/pallas_call | solution.py:1208
  145.2 2.5 %collective-permute-start.44 = (bf16[96,768]{1,0:T(8,128)(2,1)S(1)}, bf16[96,768]{1,0:T(8,128)(2,1)S(1)}, u32[]{:S(2)}, u32[]{:S(2)}) collective-permute-start(bf16[96,768]{1,0:T(8,128)(2,1)S(1)} %fusion.25), channel_id=1, source_target_pairs={{0,2},{1,3},{2,4},{3,5},{4,6},{5,7},{6,0},{7,1},{8,10},{9,11},{10,... | collective-permute-start | bytes 442376 | tf_op jit(solution)/shard_map/ppermute | solution.py:954
  147.7 5.1 %collective-permute-done.44 = bf16[96,768]{1,0:T(8,128)(2,1)S(1)} collective-permute-done((bf16[96,768]{1,0:T(8,128)(2,1)S(1)}, bf16[96,768]{1,0:T(8,128)(2,1)S(1)}, u32[]{:S(2)}, u32[]{:S(2)}) %collective-permute-start.44) | collective-permute-done | bytes 147488 | tf_op jit(solution)/shard_map/ppermute | solution.py:954
  153.5 2.9 %collective-permute-done.42 = bf16[2,4,120,384]{3,2,1,0:T(8,128)(2,1)S(1)} collective-permute-done((bf16[2,4,120,384]{3,2,1,0:T(8,128)(2,1)S(1)}, bf16[2,4,120,384]{3,2,1,0:T(8,128)(2,1)S(1)}, u32[]{:S(2)}, u32[]{:S(2)}) %collective-permute-start.42) | collective-permute-done | bytes 737312 | tf_op jit(solution)/shard_map/ppermute | solution.py:938
  156.5 2.6 %collective-permute-start.47 = (bf16[192,768]{1,0:T(8,128)(2,1)S(1)}, bf16[192,768]{1,0:T(8,128)(2,1)S(1)}, u32[]{:S(2)}, u32[]{:S(2)}) collective-permute-start(bf16[192,768]{1,0:T(8,128)(2,1)S(1)} %fusion.17), channel_id=1, source_target_pairs={{0,6},{1,7},{2,0},{3,1},{4,2},{5,3},{6,4},{7,5},{8,14},{9,15},{10,... | collective-permute-start | bytes 884744 | tf_op jit(solution)/shard_map/ppermute | solution.py:954
  161.0 3.5 %collective-permute-start.49 = (bf16[96,768]{1,0:T(8,128)(2,1)S(1)}, bf16[96,768]{1,0:T(8,128)(2,1)S(1)}, u32[]{:S(2)}, u32[]{:S(2)}) collective-permute-start(bf16[96,768]{1,0:T(8,128)(2,1)S(1)} %get-tuple-element.370), channel_id=1, source_target_pairs={{0,6},{1,7},{2,0},{3,1},{4,2},{5,3},{6,4},{7,5},{8,14},{9,15},{10,... | collective-permute-start | bytes 442376 | tf_op jit(solution)/shard_map/ppermute | solution.py:954
  164.6 5.5 %collective-permute-done.48 = bf16[96,768]{1,0:T(8,128)(2,1)S(1)} collective-permute-done((bf16[96,768]{1,0:T(8,128)(2,1)S(1)}, bf16[96,768]{1,0:T(8,128)(2,1)S(1)}, u32[]{:S(2)}, u32[]{:S(2)}) %collective-permute-start.48) | collective-permute-done | bytes 147488 | tf_op jit(solution)/shard_map/ppermute | solution.py:954
  171.6 3.3 %collective-permute-start.51 = (bf16[192,768]{1,0:T(8,128)(2,1)S(1)}, bf16[192,768]{1,0:T(8,128)(2,1)S(1)}, u32[]{:S(2)}, u32[]{:S(2)}) collective-permute-start(bf16[192,768]{1,0:T(8,128)(2,1)S(1)} %get-tuple-element.380), channel_id=1, source_target_pairs={{0,6},{1,7},{2,0},{3,1},{4,2},{5,3},{6,4},{7,5},{8,14},{9,15},{10,... | collective-permute-start | bytes 884744 | tf_op jit(solution)/shard_map/ppermute | solution.py:954
  175.9 5.4 %collective-permute-done.50 = bf16[4,80,384]{2,1,0:T(8,128)(2,1)S(1)} collective-permute-done((bf16[4,80,384]{2,1,0:T(8,128)(2,1)S(1)}, bf16[4,80,384]{2,1,0:T(8,128)(2,1)S(1)}, u32[]{:S(2)}, u32[]{:S(2)}) %collective-permute-start.50) | collective-permute-done | bytes 245792 | tf_op jit(solution)/shard_map/ppermute | solution.py:950
  181.9 2.8 %collective-permute-start.54 = (bf16[200,384]{1,0:T(8,128)(2,1)S(1)}, bf16[200,384]{1,0:T(8,128)(2,1)S(1)}, u32[]{:S(2)}, u32[]{:S(2)}) collective-permute-start(bf16[200,384]{1,0:T(8,128)(2,1)S(1)} %pad_maximum_fusion.7), channel_id=1, source_target_pairs={{0,6},{1,7},{2,0},{3,1},{4,2},{5,3},{6,4},{7,5},{8,14},{9,15},{10,... | collective-permute-start | bytes 460808 | tf_op jit(solution)/shard_map/ppermute | solution.py:954
  186.8 2.9 %collective-permute-done.54 = bf16[200,384]{1,0:T(8,128)(2,1)S(1)} collective-permute-done((bf16[200,384]{1,0:T(8,128)(2,1)S(1)}, bf16[200,384]{1,0:T(8,128)(2,1)S(1)}, u32[]{:S(2)}, u32[]{:S(2)}) %collective-permute-start.54) | collective-permute-done | bytes 153632 | tf_op jit(solution)/shard_map/ppermute | solution.py:954
  189.7 6.2 %collective-permute-done.53 = bf16[200,384]{1,0:T(8,128)(2,1)S(1)} collective-permute-done((bf16[200,384]{1,0:T(8,128)(2,1)S(1)}, bf16[200,384]{1,0:T(8,128)(2,1)S(1)}, u32[]{:S(2)}, u32[]{:S(2)}) %collective-permute-start.53) | collective-permute-done | bytes 153632 | tf_op jit(solution)/shard_map/ppermute | solution.py:954
  (157 shorter events, 54.3 us)
Async XLA Ops:
  0.6 16.3 %collective-permute-start.3 = (bf16[192,768]{1,0:T(8,128)(2,1)}, bf16[192,768]{1,0:T(8,128)(2,1)S(1)}, u32[]{:S(2)}, u32[]{:S(2)}) collective-permute-start(bf16[192,768]{1,0:T(8,128)(2,1)} %bitcast.218), channel_id=1, source_target_pairs={{0,16},{8,24},{16,0},{24,8},{1,17},{9,25},{17,1},{25,9},{2,18},{10... | collective-permute-start | bytes 884744 | tf_op jit(solution)/shard_map/ppermute | solution.py:938
  16.9 14.0 %collective-permute-start.5 = (bf16[200,768]{1,0:T(8,128)(2,1)}, bf16[200,768]{1,0:T(8,128)(2,1)S(1)}, u32[]{:S(2)}, u32[]{:S(2)}) collective-permute-start(bf16[200,768]{1,0:T(8,128)(2,1)} %get-tuple-element.193.xo), channel_id=1, source_target_pairs={{0,2},{1,3},{2,4},{3,5},{4,6},{5,7},{6,0},{7,1},{8,10},{9,11},{10,... | collective-permute-start | bytes 921608 | tf_op jit(solution)/shard_map/ppermute | solution.py:954
  18.1 12.9 %collective-permute-start.7 = (bf16[192,768]{1,0:T(8,128)(2,1)}, bf16[192,768]{1,0:T(8,128)(2,1)S(1)}, u32[]{:S(2)}, u32[]{:S(2)}) collective-permute-start(bf16[192,768]{1,0:T(8,128)(2,1)} %get-tuple-element.212.own), channel_id=1, source_target_pairs={{0,1},{1,0},{2,3},{3,2},{4,5},{5,4},{6,7},{7,6},{8,9},{9,8},{10,11... | collective-permute-start | bytes 884744 | tf_op jit(solution)/shard_map/ppermute | solution.py:950
  19.6 11.3 %collective-permute-start.4 = (bf16[48,1664]{1,0:T(8,128)(2,1)S(1)}, bf16[48,1664]{1,0:T(8,128)(2,1)S(1)}, u32[]{:S(2)}, u32[]{:S(2)}) collective-permute-start(bf16[48,1664]{1,0:T(8,128)(2,1)S(1)} %collective-permute-done), channel_id=1, source_target_pairs={{0,2},{1,3},{2,4},{3,5},{4,6},{5,7},{6,0},{7,1},{8,10},{9,11},{10,... | collective-permute-start | bytes 479240 | tf_op jit(solution)/shard_map/ppermute | solution.py:954
  20.4 10.6 %collective-permute-start.6 = (bf16[48,1664]{1,0:T(8,128)(2,1)S(1)}, bf16[48,1664]{1,0:T(8,128)(2,1)S(1)}, u32[]{:S(2)}, u32[]{:S(2)}) collective-permute-start(bf16[48,1664]{1,0:T(8,128)(2,1)S(1)} %collective-permute-done.2), channel_id=1, source_target_pairs={{0,16},{8,24},{16,0},{24,8},{1,17},{9,25},{17,1},{25,9},{2,18},{10... | collective-permute-start | bytes 479240 | tf_op jit(solution)/shard_map/ppermute | solution.py:938
  31.0 13.0 %collective-permute-start.8 = (bf16[144,1664]{1,0:T(8,128)(2,1)S(1)}, bf16[144,1664]{1,0:T(8,128)(2,1)S(1)}, u32[]{:S(2)}, u32[]{:S(2)}) collective-permute-start(bf16[144,1664]{1,0:T(8,128)(2,1)S(1)} %pad_maximum_fusion.3), channel_id=1, source_target_pairs={{0,1},{1,0},{2,3},{3,2},{4,5},{5,4},{6,7},{7,6},{8,9},{9,8},{10,11... | collective-permute-start | bytes 1437704 | tf_op jit(solution)/shard_map/ppermute | solution.py:950
  32.6 11.4 %collective-permute-start.9 = (bf16[144,1664]{1,0:T(8,128)(2,1)S(1)}, bf16[144,1664]{1,0:T(8,128)(2,1)S(1)}, u32[]{:S(2)}, u32[]{:S(2)}) collective-permute-start(bf16[144,1664]{1,0:T(8,128)(2,1)S(1)} %pad_maximum_fusion.3), channel_id=1, source_target_pairs={{0,16},{8,24},{16,0},{24,8},{1,17},{9,25},{17,1},{25,9},{2,18},{10... | collective-permute-start | bytes 1437704 | tf_op jit(solution)/shard_map/ppermute | solution.py:938
  33.1 10.9 %collective-permute-start.10 = (bf16[200,768]{1,0:T(8,128)(2,1)S(1)}, bf16[200,768]{1,0:T(8,128)(2,1)S(1)}, u32[]{:S(2)}, u32[]{:S(2)}) collective-permute-start(bf16[200,768]{1,0:T(8,128)(2,1)S(1)} %collective-permute-done.5.x2), channel_id=1, source_target_pairs={{0,2},{1,3},{2,4},{3,5},{4,6},{5,7},{6,0},{7,1},{8,10},{9,11},{10,... | collective-permute-start | bytes 921608 | tf_op jit(solution)/shard_map/ppermute | solution.py:954
  33.1 10.8 %collective-permute-start.11 = (bf16[96,768]{1,0:T(8,128)(2,1)}, bf16[96,768]{1,0:T(8,128)(2,1)S(1)}, u32[]{:S(2)}, u32[]{:S(2)}) collective-permute-start(bf16[96,768]{1,0:T(8,128)(2,1)} %get-tuple-element.204), channel_id=1, source_target_pairs={{0,6},{1,7},{2,0},{3,1},{4,2},{5,3},{6,4},{7,5},{8,14},{9,15},{10,... | collective-permute-start | bytes 442376 | tf_op jit(solution)/shard_map/ppermute | solution.py:954
  44.1 12.7 %collective-permute-start.12 = (bf16[2,200,768]{2,1,0:T(8,128)(2,1)S(1)}, bf16[2,200,768]{2,1,0:T(8,128)(2,1)S(1)}, u32[]{:S(2)}, u32[]{:S(2)}) collective-permute-start(bf16[2,200,768]{2,1,0:T(8,128)(2,1)S(1)} %pad_maximum_fusion), channel_id=1, source_target_pairs={{0,1},{1,0},{2,3},{3,2},{4,5},{5,4},{6,7},{7,6},{8,9},{9,8},{10,11... | collective-permute-start | bytes 1843208 | tf_op jit(solution)/shard_map/ppermute | solution.py:950
  44.7 10.2 %collective-permute-start.13 = (bf16[144,1664]{1,0:T(8,128)(2,1)S(1)}, bf16[144,1664]{1,0:T(8,128)(2,1)S(1)}, u32[]{:S(2)}, u32[]{:S(2)}) collective-permute-start(bf16[144,1664]{1,0:T(8,128)(2,1)S(1)} %collective-permute-done.8), channel_id=1, source_target_pairs={{0,16},{8,24},{16,0},{24,8},{1,17},{9,25},{17,1},{25,9},{2,18},{10... | collective-permute-start | bytes 1437704 | tf_op jit(solution)/shard_map/ppermute | solution.py:938
  61.2 16.5 %collective-permute-start.24 = (bf16[192,768]{1,0:T(8,128)(2,1)S(1)}, bf16[192,768]{1,0:T(8,128)(2,1)S(1)}, u32[]{:S(2)}, u32[]{:S(2)}) collective-permute-start(bf16[192,768]{1,0:T(8,128)(2,1)S(1)} %bitcast.219), channel_id=1, source_target_pairs={{0,8},{8,0},{16,24},{24,16},{1,9},{9,1},{17,25},{25,17},{2,10},{10... | collective-permute-start | bytes 884744 | tf_op jit(solution)/shard_map/ppermute | solution.py:938
  61.5 16.2 %collective-permute-start.25 = (bf16[192,768]{1,0:T(8,128)(2,1)S(1)}, bf16[192,768]{1,0:T(8,128)(2,1)S(1)}, u32[]{:S(2)}, u32[]{:S(2)}) collective-permute-start(bf16[192,768]{1,0:T(8,128)(2,1)S(1)} %collective-permute-done.3.dy_x), channel_id=1, source_target_pairs={{0,8},{8,0},{16,24},{24,16},{1,9},{9,1},{17,25},{25,17},{2,10},{10... | collective-permute-start | bytes 884744 | tf_op jit(solution)/shard_map/ppermute | solution.py:938
  61.7 16.0 %collective-permute-start.22 = (bf16[384,768]{1,0:T(8,128)(2,1)S(1)}, bf16[384,768]{1,0:T(8,128)(2,1)S(1)}, u32[]{:S(2)}, u32[]{:S(2)}) collective-permute-start(bf16[384,768]{1,0:T(8,128)(2,1)S(1)} %pad_maximum_fusion.1), channel_id=1, source_target_pairs={{0,1},{1,0},{2,3},{3,2},{4,5},{5,4},{6,7},{7,6},{8,9},{9,8},{10,11... | collective-permute-start | bytes 1769480 | tf_op jit(solution)/shard_map/ppermute | solution.py:950
  62.3 15.4 %collective-permute-start.23 = (bf16[192,768]{1,0:T(8,128)(2,1)S(1)}, bf16[192,768]{1,0:T(8,128)(2,1)S(1)}, u32[]{:S(2)}, u32[]{:S(2)}) collective-permute-start(bf16[192,768]{1,0:T(8,128)(2,1)S(1)} %collective-permute-done.14.z1), channel_id=1, source_target_pairs={{0,2},{1,3},{2,4},{3,5},{4,6},{5,7},{6,0},{7,1},{8,10},{9,11},{10,... | collective-permute-start | bytes 884744 | tf_op jit(solution)/shard_map/ppermute | solution.py:954
  105.4 15.0 %collective-permute-start.33 = (bf16[4,96,768]{2,1,0:T(8,128)(2,1)S(1)}, bf16[4,96,768]{2,1,0:T(8,128)(2,1)S(1)}, u32[]{:S(2)}, u32[]{:S(2)}) collective-permute-start(bf16[4,96,768]{2,1,0:T(8,128)(2,1)S(1)} %slice_bitcast_fusion.1), channel_id=1, source_target_pairs={{0,1},{1,0},{2,3},{3,2},{4,5},{5,4},{6,7},{7,6},{8,9},{9,8},{10,11... | collective-permute-start | bytes 1769480 | tf_op jit(solution)/shard_map/ppermute | solution.py:950
  106.9 13.5 %collective-permute-start.34 = (bf16[2,192,768]{2,1,0:T(8,128)(2,1)S(1)}, bf16[2,192,768]{2,1,0:T(8,128)(2,1)S(1)}, u32[]{:S(2)}, u32[]{:S(2)}) collective-permute-start(bf16[2,192,768]{2,1,0:T(8,128)(2,1)S(1)} %get-tuple-element.307), channel_id=1, source_target_pairs={{0,8},{8,0},{16,24},{24,16},{1,9},{9,1},{17,25},{25,17},{2,10},{10... | collective-permute-start | bytes 1769480 | tf_op jit(solution)/shard_map/ppermute | solution.py:938
  120.4 17.9 %collective-permute-start.35 = (bf16[2,2,4,120,384]{4,3,2,1,0:T(8,128)(2,1)S(1)}, bf16[2,2,4,120,384]{4,3,2,1,0:T(8,128)(2,1)S(1)}, u32[]{:S(2)}, u32[]{:S(2)}) collective-permute-start(bf16[2,2,4,120,384]{4,3,2,1,0:T(8,128)(2,1)S(1)} %get-tuple-element.316), channel_id=1, source_target_pairs={{0,8},{8,0},{16,24},{24,16},{1,9},{9,1},{17,25},{25,17},{2,10},{10... | collective-permute-start | bytes 4423688 | tf_op jit(solution)/shard_map/ppermute | solution.py:938
  120.4 17.9 %collective-permute-start.36 = (bf16[4,96,768]{2,1,0:T(8,128)(2,1)S(1)}, bf16[4,96,768]{2,1,0:T(8,128)(2,1)S(1)}, u32[]{:S(2)}, u32[]{:S(2)}) collective-permute-start(bf16[4,96,768]{2,1,0:T(8,128)(2,1)S(1)} %slice_bitcast_fusion), channel_id=1, source_target_pairs={{0,1},{1,0},{2,3},{3,2},{4,5},{5,4},{6,7},{7,6},{8,9},{9,8},{10,11... | collective-permute-start | bytes 1769480 | tf_op jit(solution)/shard_map/ppermute | solution.py:950
  122.0 16.3 %collective-permute-start.37 = (bf16[96,768]{1,0:T(8,128)(2,1)S(1)}, bf16[96,768]{1,0:T(8,128)(2,1)S(1)}, u32[]{:S(2)}, u32[]{:S(2)}) collective-permute-start(bf16[96,768]{1,0:T(8,128)(2,1)S(1)} %get-tuple-element.374), channel_id=1, source_target_pairs={{0,2},{1,3},{2,4},{3,5},{4,6},{5,7},{6,0},{7,1},{8,10},{9,11},{10,... | collective-permute-start | bytes 442376 | tf_op jit(solution)/shard_map/ppermute | solution.py:954
  123.9 14.4 %collective-permute-start.38 = (bf16[96,768]{1,0:T(8,128)(2,1)S(1)}, bf16[96,768]{1,0:T(8,128)(2,1)S(1)}, u32[]{:S(2)}, u32[]{:S(2)}) collective-permute-start(bf16[96,768]{1,0:T(8,128)(2,1)S(1)} %get-tuple-element.373), channel_id=1, source_target_pairs={{0,4},{1,5},{2,6},{3,7},{4,0},{5,1},{6,2},{7,3},{8,12},{9,13},{10,... | collective-permute-start | bytes 442376 | tf_op jit(solution)/shard_map/ppermute | solution.py:954
  125.3 13.0 %collective-permute-start.39 = (bf16[96,768]{1,0:T(8,128)(2,1)S(1)}, bf16[96,768]{1,0:T(8,128)(2,1)S(1)}, u32[]{:S(2)}, u32[]{:S(2)}) collective-permute-start(bf16[96,768]{1,0:T(8,128)(2,1)S(1)} %get-tuple-element.372), channel_id=1, source_target_pairs={{0,6},{1,7},{2,0},{3,1},{4,2},{5,3},{6,4},{7,5},{8,14},{9,15},{10,... | collective-permute-start | bytes 442376 | tf_op jit(solution)/shard_map/ppermute | solution.py:954
  138.5 17.8 %collective-permute-start.42 = (bf16[2,4,120,384]{3,2,1,0:T(8,128)(2,1)S(1)}, bf16[2,4,120,384]{3,2,1,0:T(8,128)(2,1)S(1)}, u32[]{:S(2)}, u32[]{:S(2)}) collective-permute-start(bf16[2,4,120,384]{3,2,1,0:T(8,128)(2,1)S(1)} %fusion.1), channel_id=1, source_target_pairs={{0,16},{8,24},{16,0},{24,8},{1,17},{9,25},{17,1},{25,9},{2,18},{10... | collective-permute-start | bytes 2211848 | tf_op jit(solution)/shard_map/ppermute | solution.py:938
  139.1 14.3 %collective-permute-start.43 = (bf16[2,192,768]{2,1,0:T(8,128)(2,1)S(1)}, bf16[2,192,768]{2,1,0:T(8,128)(2,1)S(1)}, u32[]{:S(2)}, u32[]{:S(2)}) collective-permute-start(bf16[2,192,768]{2,1,0:T(8,128)(2,1)S(1)} %get-tuple-element.325), channel_id=1, source_target_pairs={{0,1},{1,0},{2,3},{3,2},{4,5},{5,4},{6,7},{7,6},{8,9},{9,8},{10,11... | collective-permute-start | bytes 1769480 | tf_op jit(solution)/shard_map/ppermute | solution.py:950
  156.5 14.9 %collective-permute-start.47 = (bf16[192,768]{1,0:T(8,128)(2,1)S(1)}, bf16[192,768]{1,0:T(8,128)(2,1)S(1)}, u32[]{:S(2)}, u32[]{:S(2)}) collective-permute-start(bf16[192,768]{1,0:T(8,128)(2,1)S(1)} %fusion.17), channel_id=1, source_target_pairs={{0,6},{1,7},{2,0},{3,1},{4,2},{5,3},{6,4},{7,5},{8,14},{9,15},{10,... | collective-permute-start | bytes 884744 | tf_op jit(solution)/shard_map/ppermute | solution.py:954
  159.2 12.2 %collective-permute-start.45 = (bf16[2,4,80,384]{3,2,1,0:T(8,128)(2,1)S(1)}, bf16[2,4,80,384]{3,2,1,0:T(8,128)(2,1)S(1)}, u32[]{:S(2)}, u32[]{:S(2)}) collective-permute-start(bf16[2,4,80,384]{3,2,1,0:T(8,128)(2,1)S(1)} %fusion), channel_id=1, source_target_pairs={{0,16},{8,24},{16,0},{24,8},{1,17},{9,25},{17,1},{25,9},{2,18},{10... | collective-permute-start | bytes 1474568 | tf_op jit(solution)/shard_map/ppermute | solution.py:938
  160.0 11.4 %collective-permute-start.46 = (bf16[4,120,384]{2,1,0:T(8,128)(2,1)S(1)}, bf16[4,120,384]{2,1,0:T(8,128)(2,1)S(1)}, u32[]{:S(2)}, u32[]{:S(2)}) collective-permute-start(bf16[4,120,384]{2,1,0:T(8,128)(2,1)S(1)} %fusion.2), channel_id=1, source_target_pairs={{0,1},{1,0},{2,3},{3,2},{4,5},{5,4},{6,7},{7,6},{8,9},{9,8},{10,11... | collective-permute-start | bytes 1105928 | tf_op jit(solution)/shard_map/ppermute | solution.py:950
  161.0 10.3 %collective-permute-start.49 = (bf16[96,768]{1,0:T(8,128)(2,1)S(1)}, bf16[96,768]{1,0:T(8,128)(2,1)S(1)}, u32[]{:S(2)}, u32[]{:S(2)}) collective-permute-start(bf16[96,768]{1,0:T(8,128)(2,1)S(1)} %get-tuple-element.370), channel_id=1, source_target_pairs={{0,6},{1,7},{2,0},{3,1},{4,2},{5,3},{6,4},{7,5},{8,14},{9,15},{10,... | collective-permute-start | bytes 442376 | tf_op jit(solution)/shard_map/ppermute | solution.py:954
  171.6 9.7 %collective-permute-start.51 = (bf16[192,768]{1,0:T(8,128)(2,1)S(1)}, bf16[192,768]{1,0:T(8,128)(2,1)S(1)}, u32[]{:S(2)}, u32[]{:S(2)}) collective-permute-start(bf16[192,768]{1,0:T(8,128)(2,1)S(1)} %get-tuple-element.380), channel_id=1, source_target_pairs={{0,6},{1,7},{2,0},{3,1},{4,2},{5,3},{6,4},{7,5},{8,14},{9,15},{10,... | collective-permute-start | bytes 884744 | tf_op jit(solution)/shard_map/ppermute | solution.py:954
  181.2 14.7 %collective-permute-start.55 = (bf16[384,768]{1,0:T(8,128)(2,1)S(1)}, bf16[384,768]{1,0:T(8,128)(2,1)S(1)}, u32[]{:S(2)}, u32[]{:S(2)}) collective-permute-start(bf16[384,768]{1,0:T(8,128)(2,1)S(1)} %pad_maximum_fusion.2), channel_id=1, source_target_pairs={{0,16},{8,24},{16,0},{24,8},{1,17},{9,25},{17,1},{25,9},{2,18},{10... | collective-permute-start | bytes 1769480 | tf_op jit(solution)/shard_map/ppermute | solution.py:938
  184.7 11.2 %collective-permute-start.53 = (bf16[200,384]{1,0:T(8,128)(2,1)S(1)}, bf16[200,384]{1,0:T(8,128)(2,1)S(1)}, u32[]{:S(2)}, u32[]{:S(2)}) collective-permute-start(bf16[200,384]{1,0:T(8,128)(2,1)S(1)} %pad_maximum_fusion.6), channel_id=1, source_target_pairs={{0,4},{1,5},{2,6},{3,7},{4,0},{5,1},{6,2},{7,3},{8,12},{9,13},{10,... | collective-permute-start | bytes 460808 | tf_op jit(solution)/shard_map/ppermute | solution.py:954
  184.8 11.1 %collective-permute-start.52 = (bf16[200,384]{1,0:T(8,128)(2,1)S(1)}, bf16[200,384]{1,0:T(8,128)(2,1)S(1)}, u32[]{:S(2)}, u32[]{:S(2)}) collective-permute-start(bf16[200,384]{1,0:T(8,128)(2,1)S(1)} %pad_maximum_fusion.5), channel_id=1, source_target_pairs={{0,2},{1,3},{2,4},{3,5},{4,6},{5,7},{6,0},{7,1},{8,10},{9,11},{10,... | collective-permute-start | bytes 460808 | tf_op jit(solution)/shard_map/ppermute | solution.py:954
  (37 other events, 279.2 us)

commit v9 on v8

--- a/solution.py
+++ b/solution.py
@@ -599,7 +599,7 @@
         du_out[:, pl.ds(col, chunk)] = low
         return carry
 
-    lax.fori_loop(0, w_up.shape[1] // chunk, feed, 0)
+    lax.fori_loop(0, w_up.shape[1] // chunk, feed, 0, unroll=True)
     return dot_nt(du_out[...], w_up[...])
 
 

time: 205 us -> 203 us (level)
  Pallas kernels: 65.5 us -> 63.3 us
  transfers between devices with their start and end apart: 61 -> 61, of which waited for: 21 -> 22; matrix products, arithmetic and copies ran while one was open for 2% -> 2% of each run, Pallas kernels for 31% -> 31%
where the time goes in v9:
time: 203 us; the launch traced here: 202 us
  waiting for transfers between devices  69.6 us (34%)
  starting transfers between devices  63.3 us (31%)
  Pallas kernels  63.3 us (31%)
  other arithmetic  3.01 us (1%)
  local copies, waits for them, and re-layouts  2.1 us (1%)
    ppermute x20, waiting for transfers between devices, to_z(): lax.ppermute(value, 'seq', [(k, (k + 2 * steps) % 8) for k in range(8)])  48.3 us
    ppermute x20, starting transfers between devices, to_z(): lax.ppermute(value, 'seq', [(k, (k + 2 * steps) % 8) for k in range(8)])  35.5 us
    ppermute x30, starting transfers between devices, swap_rep(): return lax.ppermute(value, 'rep', [(k, k ^ bit) for k in range(4)])  15.9 us
    pallas_call x1, Pallas kernels, on_device_fast(): call(front_kernel, [VM] * 6 + [AN] * 15, [VM] * 11, [shape_of((tok, width...  13.9 us
    ppermute x11, starting transfers between devices, to_y(): return lax.ppermute(value, 'seq', [(k, k ^ 1) for k in range(8)])  11.9 us
    ppermute x11, waiting for transfers between devices, to_y(): return lax.ppermute(value, 'seq', [(k, k ^ 1) for k in range(8)])  11.1 us
    pallas_call x1, Pallas kernels, on_device_fast(): call(back_b_kernel, [VM] * 14 + [AN] * 13, [VM] * 6, [shape_of((tok, widt...  10.8 us
    ppermute x30, waiting for transfers between devices, swap_rep(): return lax.ppermute(value, 'rep', [(k, k ^ bit) for k in range(4)])  10.2 us
  transfers between devices with their start and end apart: 61, of which 22 were waited for; matrix products, arithmetic and copies ran while one was open for 2% of the time, Pallas kernels for 31%

profile of v9, /device:TPU:0, one launch (start us, length us, event | category | flops | bytes accessed | tf_op | source)
XLA Modules:
  0.0 202.4 jit_solution(16382921414950515067)
XLA Ops:
  0.6 3.0 %collective-permute-start.3 = (bf16[192,768]{1,0:T(8,128)(2,1)}, bf16[192,768]{1,0:T(8,128)(2,1)S(1)}, u32[]{:S(2)}, u32[]{:S(2)}) collective-permute-start(bf16[192,768]{1,0:T(8,128)(2,1)} %bitcast.218), channel_id=1, source_target_pairs={{0,16},{8,24},{16,0},{24,8},{1,17},{9,25},{17,1},{25,9},{2,18},{10... | collective-permute-start | bytes 884744 | tf_op jit(solution)/shard_map/ppermute | solution.py:938
  3.6 2.7 %shard_map.186 = (bf16[200,768]{1,0:T(8,128)(2,1)}, bf16[48,1664]{1,0:T(8,128)(2,1)}, bf16[192,768]{1,0:T(8,128)(2,1)}, bf16[96,768]{1,0:T(8,128)(2,1)}, bf16[96,768]{1,0:T(8,128)(2,1)}) custom-call(bf16[1,192,768]{2,1,0:T(8,128)(2,1)} %tokens.1, s32[1,192]{1,0:T(1,128)} %segs.1, bf16[96,2304]{1,0:T(8,128)(2,1)} %own.3, bf16[96,768]{1,0:T(8,128)(2,1)} %own_o.1, ...), custom_call_target="tpu_custom_call" | custom-call | bytes 4000000 | tf_op jit(solution)/shard_map/pallas_call | solution.py:982
  8.0 2.2 %collective-permute-start.1 = (bf16[48,1664]{1,0:T(8,128)(2,1)}, bf16[48,1664]{1,0:T(8,128)(2,1)S(1)}, u32[]{:S(2)}, u32[]{:S(2)}) collective-permute-start(bf16[48,1664]{1,0:T(8,128)(2,1)} %get-tuple-element.188.first), channel_id=1, source_target_pairs={{0,6},{1,7},{2,0},{3,1},{4,2},{5,3},{6,4},{7,5},{8,14},{9,15},{10,... | collective-permute-start | bytes 479240 | tf_op jit(solution)/shard_map/ppermute | solution.py:954
  11.8 3.7 %collective-permute-done = bf16[48,1664]{1,0:T(8,128)(2,1)S(1)} collective-permute-done((bf16[48,1664]{1,0:T(8,128)(2,1)}, bf16[48,1664]{1,0:T(8,128)(2,1)S(1)}, u32[]{:S(2)}, u32[]{:S(2)}) %collective-permute-start) | collective-permute-done | bytes 159776 | tf_op jit(solution)/shard_map/ppermute | solution.py:954
  20.9 10.0 %collective-permute-done.4 = bf16[48,1664]{1,0:T(8,128)(2,1)S(1)} collective-permute-done((bf16[48,1664]{1,0:T(8,128)(2,1)S(1)}, bf16[48,1664]{1,0:T(8,128)(2,1)S(1)}, u32[]{:S(2)}, u32[]{:S(2)}) %collective-permute-start.4) | collective-permute-done | bytes 159776 | tf_op jit(solution)/shard_map/ppermute | solution.py:954
  33.1 3.8 %collective-permute-start.11 = (bf16[96,768]{1,0:T(8,128)(2,1)}, bf16[96,768]{1,0:T(8,128)(2,1)S(1)}, u32[]{:S(2)}, u32[]{:S(2)}) collective-permute-start(bf16[96,768]{1,0:T(8,128)(2,1)} %get-tuple-element.204), channel_id=1, source_target_pairs={{0,6},{1,7},{2,0},{3,1},{4,2},{5,3},{6,4},{7,5},{8,14},{9,15},{10,... | collective-permute-start | bytes 442376 | tf_op jit(solution)/shard_map/ppermute | solution.py:954
  36.9 7.0 %collective-permute-done.11.z3d = bf16[96,768]{1,0:T(8,128)(2,1)S(1)} collective-permute-done((bf16[96,768]{1,0:T(8,128)(2,1)}, bf16[96,768]{1,0:T(8,128)(2,1)S(1)}, u32[]{:S(2)}, u32[]{:S(2)}) %collective-permute-start.11) | collective-permute-done | bytes 147488 | tf_op jit(solution)/shard_map/ppermute | solution.py:954
  46.5 3.5 %collective-permute-start.15 = (bf16[96,768]{1,0:T(8,128)(2,1)S(1)}, bf16[96,768]{1,0:T(8,128)(2,1)S(1)}, u32[]{:S(2)}, u32[]{:S(2)}) collective-permute-start(bf16[96,768]{1,0:T(8,128)(2,1)S(1)} %copy-done.7), channel_id=1, source_target_pairs={{0,6},{1,7},{2,0},{3,1},{4,2},{5,3},{6,4},{7,5},{8,14},{9,15},{10,... | collective-permute-start | bytes 442376 | tf_op jit(solution)/shard_map/ppermute | solution.py:954
  50.0 4.9 %collective-permute-done.15.z3u = bf16[96,768]{1,0:T(8,128)(2,1)S(1)} collective-permute-done((bf16[96,768]{1,0:T(8,128)(2,1)S(1)}, bf16[96,768]{1,0:T(8,128)(2,1)S(1)}, u32[]{:S(2)}, u32[]{:S(2)}) %collective-permute-start.15) | collective-permute-done | bytes 147488 | tf_op jit(solution)/shard_map/ppermute | solution.py:954
  58.6 2.6 %collective-permute-done.20 = bf16[48,1664]{1,0:T(8,128)(2,1)S(1)} collective-permute-done((bf16[48,1664]{1,0:T(8,128)(2,1)S(1)}, bf16[48,1664]{1,0:T(8,128)(2,1)S(1)}, u32[]{:S(2)}, u32[]{:S(2)}) %collective-permute-start.20) | collective-permute-done | bytes 159776 | tf_op jit(solution)/shard_map/ppermute | solution.py:938
  63.8 13.9 %shard_map.187 = (bf16[192,768]{1,0:T(8,128)(2,1)S(1)}, bf16[960,1536]{1,0:T(8,128)(2,1)S(1)}, bf16[960,768]{1,0:T(8,128)(2,1)S(1)}, bf16[192,768]{1,0:T(8,128)(...) custom-call(s32[1,384]{1,0:T(1,128)S(1)} %pad_add_fusion.seg, ...), custom_call_target="tpu_custom_call" | custom-call | flops 7000000000 | bytes 12000000 | tf_op jit(solution)/shard_map/pallas_call | solution.py:1038
  79.8 2.9 %shard_map.188 = (bf16[768,768]{1,0:T(8,128)(2,1)S(1)}, bf16[768,768]{1,0:T(8,128)(2,1)S(1)}) custom-call(bf16[192,768]{1,0:T(8,128)(2,1)S(1)} %copy-done.2, bf16[192,768]{1,0:T(8,128)(2,1)S(1)} %collective-permute-done.14.z1, bf16[192,768]{1,0:T(8,128)(2,1)S(1)} %collective-permute-done.23.z2, bf16[96,768]{1,0:T(8,128)(2,1)S(1)} %collective-permute-done.15.z3u, ...), custom_call_target="tpu_custom_call" | custom-call | bytes 5000000 | tf_op jit(solution)/shard_map/pallas_call | solution.py:1069
  82.6 3.8 %collective-permute-done.26.h_x = bf16[192,768]{1,0:T(8,128)(2,1)S(1)} collective-permute-done((bf16[192,768]{1,0:T(8,128)(2,1)S(1)}, bf16[192,768]{1,0:T(8,128)(2,1)S(1)}, u32[]{:S(2)}, u32[]{:S(2)}) %collective-permute-start.26) | collective-permute-done | bytes 294944 | tf_op jit(solution)/shard_map/ppermute | solution.py:938
  87.7 2.3 %shard_map.189 = (bf16[384,768]{1,0:T(8,128)(2,1)S(1)}, bf16[384,768]{1,0:T(8,128)(2,1)S(1)}, bf16[384,768]{1,0:T(8,128)(2,1)S(1)}, bf16[384,768]{1,0:T(8,128)(2...) custom-call(bf16[192,768]{1,0:T(8,128)(2,1)S(1)} %get-tuple-element., ...), custom_call_target="tpu_custom_call", output_to_operand_aliasing={{6}: (6, {}), {7}: (7, {})} | custom-call | flops 3000000000 | bytes 6000000 | tf_op jit(solution)/shard_map/pallas_call | solution.py:1082
  95.6 7.2 %shard_map.192 = (bf16[2,4,96,768]{3,2,1,0:T(8,128)(2,1)S(1)}, bf16[2,4,96,768]{3,2,1,0:T(8,128)(2,1)S(1)}, f32[1,768]{1,0:T(1,128)S(1)}, f32[2,192,768]{2,1,0:T(8,128)S(1)}, bf16[2,192,768]{2,1,0:T(8,128)(2,1)S(1)}) custom-call(bf16[768,768]{1,0:T(8,128)(2,1)S(1)} %get-tuple-element.282.hs, bf16[768,768]{1,0:T(8,128)(2,1)S(1)} %get-tuple-element.283.dys, ...), custom_call_target="tpu_custom_call" | custom-call | flops 3000000000 | bytes 6000000 | tf_op jit(solution)/shard_map/pallas_call | solution.py:1120
  106.1 10.0 %shard_map.194 = (bf16[2,2,4,120,384]{4,3,2,1,0:T(8,128)(2,1)S(1)}, bf16[2,2,4,120,384]{4,3,2,1,0:T(8,128)(2,1)S(1)}, bf16[192,384]{1,0:T(8,128)(2,1)S(1)}, bf16[960,768]{1,0:T(8,128)(2,1)S(1)}) custom-call(s32[1,384]{1,0:T(1,128)S(1)} %get-tuple-element.287.start_in, bf16[192,768]{1,0:T(8,128)(2,1)S(1)} %get-tuple-element.288.q_in, ...), custom_call_target="tpu_custom_call" | custom-call | flops 5000000000 | bytes 10000000 | tf_op jit(solution)/shard_map/pallas_call | solution.py:1156
  116.2 1.9 collective-permute-done.33
  122.8 2.2 %collective-permute-start.39 = (bf16[96,768]{1,0:T(8,128)(2,1)S(1)}, bf16[96,768]{1,0:T(8,128)(2,1)S(1)}, u32[]{:S(2)}, u32[]{:S(2)}) collective-permute-start(bf16[96,768]{1,0:T(8,128)(2,1)S(1)} %get-tuple-element.372), channel_id=1, source_target_pairs={{0,6},{1,7},{2,0},{3,1},{4,2},{5,3},{6,4},{7,5},{8,14},{9,15},{10,... | collective-permute-start | bytes 442376 | tf_op jit(solution)/shard_map/ppermute | solution.py:954
  125.0 10.8 %shard_map.195 = (bf16[192,384]{1,0:T(8,128)(2,1)S(1)}, bf16[960,768]{1,0:T(8,128)(2,1)S(1)}, f32[192,768]{1,0:T(8,128)S(1)}, bf16[2,192,768]{2,1,0:T(8,128)(2,1...) custom-call(s32[1,384]{1,0:T(1,128)S(1)} %get-tuple-element.287.start_in, ...), custom_call_target="tpu_custom_call" | custom-call | flops 6000000000 | bytes 10000000 | tf_op jit(solution)/shard_map/pallas_call | solution.py:1183
  137.4 4.8 %shard_map.196 = (bf16[2,2,4,80,384]{4,3,2,1,0:T(8,128)(2,1)S(1)}, bf16[2,2,4,80,384]{4,3,2,1,0:T(8,128)(2,1)S(1)}) custom-call(bf16[960,768]{1,0:T(8,128)(2,1)S(1)} %get-tuple-element.290.h_in, bf16[192,384]{1,0:T(8,128)(2,1)S(1)} %get-tuple-element.321.dq, bf16[960,768]{1,0:T(8,128)(2,1)S(1)} %get-tuple-element.322.dkv, ...), custom_call_target="tpu_custom_call" | custom-call | flops 3000000000 | bytes 6000000 | tf_op jit(solution)/shard_map/pallas_call | solution.py:1208
  142.9 2.3 %collective-permute-start.44 = (bf16[96,768]{1,0:T(8,128)(2,1)S(1)}, bf16[96,768]{1,0:T(8,128)(2,1)S(1)}, u32[]{:S(2)}, u32[]{:S(2)}) collective-permute-start(bf16[96,768]{1,0:T(8,128)(2,1)S(1)} %fusion.25), channel_id=1, source_target_pairs={{0,2},{1,3},{2,4},{3,5},{4,6},{5,7},{6,0},{7,1},{8,10},{9,11},{10,... | collective-permute-start | bytes 442376 | tf_op jit(solution)/shard_map/ppermute | solution.py:954
  145.3 5.3 %collective-permute-done.44 = bf16[96,768]{1,0:T(8,128)(2,1)S(1)} collective-permute-done((bf16[96,768]{1,0:T(8,128)(2,1)S(1)}, bf16[96,768]{1,0:T(8,128)(2,1)S(1)}, u32[]{:S(2)}, u32[]{:S(2)}) %collective-permute-start.44) | collective-permute-done | bytes 147488 | tf_op jit(solution)/shard_map/ppermute | solution.py:954
  151.2 2.7 %collective-permute-done.42 = bf16[2,4,120,384]{3,2,1,0:T(8,128)(2,1)S(1)} collective-permute-done((bf16[2,4,120,384]{3,2,1,0:T(8,128)(2,1)S(1)}, bf16[2,4,120,384]{3,2,1,0:T(8,128)(2,1)S(1)}, u32[]{:S(2)}, u32[]{:S(2)}) %collective-permute-start.42) | collective-permute-done | bytes 737312 | tf_op jit(solution)/shard_map/ppermute | solution.py:938
  154.0 2.6 %collective-permute-start.47 = (bf16[192,768]{1,0:T(8,128)(2,1)S(1)}, bf16[192,768]{1,0:T(8,128)(2,1)S(1)}, u32[]{:S(2)}, u32[]{:S(2)}) collective-permute-start(bf16[192,768]{1,0:T(8,128)(2,1)S(1)} %fusion.17), channel_id=1, source_target_pairs={{0,6},{1,7},{2,0},{3,1},{4,2},{5,3},{6,4},{7,5},{8,14},{9,15},{10,... | collective-permute-start | bytes 884744 | tf_op jit(solution)/shard_map/ppermute | solution.py:954
  158.6 3.6 %collective-permute-start.49 = (bf16[96,768]{1,0:T(8,128)(2,1)S(1)}, bf16[96,768]{1,0:T(8,128)(2,1)S(1)}, u32[]{:S(2)}, u32[]{:S(2)}) collective-permute-start(bf16[96,768]{1,0:T(8,128)(2,1)S(1)} %get-tuple-element.370), channel_id=1, source_target_pairs={{0,6},{1,7},{2,0},{3,1},{4,2},{5,3},{6,4},{7,5},{8,14},{9,15},{10,... | collective-permute-start | bytes 442376 | tf_op jit(solution)/shard_map/ppermute | solution.py:954
  162.3 5.5 %collective-permute-done.48 = bf16[96,768]{1,0:T(8,128)(2,1)S(1)} collective-permute-done((bf16[96,768]{1,0:T(8,128)(2,1)S(1)}, bf16[96,768]{1,0:T(8,128)(2,1)S(1)}, u32[]{:S(2)}, u32[]{:S(2)}) %collective-permute-start.48) | collective-permute-done | bytes 147488 | tf_op jit(solution)/shard_map/ppermute | solution.py:954
  169.3 3.1 %collective-permute-start.51 = (bf16[192,768]{1,0:T(8,128)(2,1)S(1)}, bf16[192,768]{1,0:T(8,128)(2,1)S(1)}, u32[]{:S(2)}, u32[]{:S(2)}) collective-permute-start(bf16[192,768]{1,0:T(8,128)(2,1)S(1)} %get-tuple-element.380), channel_id=1, source_target_pairs={{0,6},{1,7},{2,0},{3,1},{4,2},{5,3},{6,4},{7,5},{8,14},{9,15},{10,... | collective-permute-start | bytes 884744 | tf_op jit(solution)/shard_map/ppermute | solution.py:954
  173.4 5.3 %collective-permute-done.50 = bf16[4,80,384]{2,1,0:T(8,128)(2,1)S(1)} collective-permute-done((bf16[4,80,384]{2,1,0:T(8,128)(2,1)S(1)}, bf16[4,80,384]{2,1,0:T(8,128)(2,1)S(1)}, u32[]{:S(2)}, u32[]{:S(2)}) %collective-permute-start.50) | collective-permute-done | bytes 245792 | tf_op jit(solution)/shard_map/ppermute | solution.py:950
  179.6 2.8 %collective-permute-start.54 = (bf16[200,384]{1,0:T(8,128)(2,1)S(1)}, bf16[200,384]{1,0:T(8,128)(2,1)S(1)}, u32[]{:S(2)}, u32[]{:S(2)}) collective-permute-start(bf16[200,384]{1,0:T(8,128)(2,1)S(1)} %pad_maximum_fusion.7), channel_id=1, source_target_pairs={{0,6},{1,7},{2,0},{3,1},{4,2},{5,3},{6,4},{7,5},{8,14},{9,15},{10,... | collective-permute-start | bytes 460808 | tf_op jit(solution)/shard_map/ppermute | solution.py:954
  184.5 2.9 %collective-permute-done.54 = bf16[200,384]{1,0:T(8,128)(2,1)S(1)} collective-permute-done((bf16[200,384]{1,0:T(8,128)(2,1)S(1)}, bf16[200,384]{1,0:T(8,128)(2,1)S(1)}, u32[]{:S(2)}, u32[]{:S(2)}) %collective-permute-start.54) | collective-permute-done | bytes 153632 | tf_op jit(solution)/shard_map/ppermute | solution.py:954
  187.4 6.2 %collective-permute-done.53 = bf16[200,384]{1,0:T(8,128)(2,1)S(1)} collective-permute-done((bf16[200,384]{1,0:T(8,128)(2,1)S(1)}, bf16[200,384]{1,0:T(8,128)(2,1)S(1)}, u32[]{:S(2)}, u32[]{:S(2)}) %collective-permute-start.53) | collective-permute-done | bytes 153632 | tf_op jit(solution)/shard_map/ppermute | solution.py:954
  199.2 2.0 shard_map.198
  (157 shorter events, 53.6 us)
Async XLA Ops:
  0.6 16.3 %collective-permute-start.3 = (bf16[192,768]{1,0:T(8,128)(2,1)}, bf16[192,768]{1,0:T(8,128)(2,1)S(1)}, u32[]{:S(2)}, u32[]{:S(2)}) collective-permute-start(bf16[192,768]{1,0:T(8,128)(2,1)} %bitcast.218), channel_id=1, source_target_pairs={{0,16},{8,24},{16,0},{24,8},{1,17},{9,25},{17,1},{25,9},{2,18},{10... | collective-permute-start | bytes 884744 | tf_op jit(solution)/shard_map/ppermute | solution.py:938
  16.9 14.0 %collective-permute-start.5 = (bf16[200,768]{1,0:T(8,128)(2,1)}, bf16[200,768]{1,0:T(8,128)(2,1)S(1)}, u32[]{:S(2)}, u32[]{:S(2)}) collective-permute-start(bf16[200,768]{1,0:T(8,128)(2,1)} %get-tuple-element.193.xo), channel_id=1, source_target_pairs={{0,2},{1,3},{2,4},{3,5},{4,6},{5,7},{6,0},{7,1},{8,10},{9,11},{10,... | collective-permute-start | bytes 921608 | tf_op jit(solution)/shard_map/ppermute | solution.py:954
  18.1 12.9 %collective-permute-start.7 = (bf16[192,768]{1,0:T(8,128)(2,1)}, bf16[192,768]{1,0:T(8,128)(2,1)S(1)}, u32[]{:S(2)}, u32[]{:S(2)}) collective-permute-start(bf16[192,768]{1,0:T(8,128)(2,1)} %get-tuple-element.212.own), channel_id=1, source_target_pairs={{0,1},{1,0},{2,3},{3,2},{4,5},{5,4},{6,7},{7,6},{8,9},{9,8},{10,11... | collective-permute-start | bytes 884744 | tf_op jit(solution)/shard_map/ppermute | solution.py:950
  19.6 11.3 %collective-permute-start.4 = (bf16[48,1664]{1,0:T(8,128)(2,1)S(1)}, bf16[48,1664]{1,0:T(8,128)(2,1)S(1)}, u32[]{:S(2)}, u32[]{:S(2)}) collective-permute-start(bf16[48,1664]{1,0:T(8,128)(2,1)S(1)} %collective-permute-done), channel_id=1, source_target_pairs={{0,2},{1,3},{2,4},{3,5},{4,6},{5,7},{6,0},{7,1},{8,10},{9,11},{10,... | collective-permute-start | bytes 479240 | tf_op jit(solution)/shard_map/ppermute | solution.py:954
  20.4 10.6 %collective-permute-start.6 = (bf16[48,1664]{1,0:T(8,128)(2,1)S(1)}, bf16[48,1664]{1,0:T(8,128)(2,1)S(1)}, u32[]{:S(2)}, u32[]{:S(2)}) collective-permute-start(bf16[48,1664]{1,0:T(8,128)(2,1)S(1)} %collective-permute-done.2), channel_id=1, source_target_pairs={{0,16},{8,24},{16,0},{24,8},{1,17},{9,25},{17,1},{25,9},{2,18},{10... | collective-permute-start | bytes 479240 | tf_op jit(solution)/shard_map/ppermute | solution.py:938
  31.0 13.0 %collective-permute-start.8 = (bf16[144,1664]{1,0:T(8,128)(2,1)S(1)}, bf16[144,1664]{1,0:T(8,128)(2,1)S(1)}, u32[]{:S(2)}, u32[]{:S(2)}) collective-permute-start(bf16[144,1664]{1,0:T(8,128)(2,1)S(1)} %pad_maximum_fusion.3), channel_id=1, source_target_pairs={{0,1},{1,0},{2,3},{3,2},{4,5},{5,4},{6,7},{7,6},{8,9},{9,8},{10,11... | collective-permute-start | bytes 1437704 | tf_op jit(solution)/shard_map/ppermute | solution.py:950
  32.6 11.4 %collective-permute-start.9 = (bf16[144,1664]{1,0:T(8,128)(2,1)S(1)}, bf16[144,1664]{1,0:T(8,128)(2,1)S(1)}, u32[]{:S(2)}, u32[]{:S(2)}) collective-permute-start(bf16[144,1664]{1,0:T(8,128)(2,1)S(1)} %pad_maximum_fusion.3), channel_id=1, source_target_pairs={{0,16},{8,24},{16,0},{24,8},{1,17},{9,25},{17,1},{25,9},{2,18},{10... | collective-permute-start | bytes 1437704 | tf_op jit(solution)/shard_map/ppermute | solution.py:938
  33.1 10.9 %collective-permute-start.10 = (bf16[200,768]{1,0:T(8,128)(2,1)S(1)}, bf16[200,768]{1,0:T(8,128)(2,1)S(1)}, u32[]{:S(2)}, u32[]{:S(2)}) collective-permute-start(bf16[200,768]{1,0:T(8,128)(2,1)S(1)} %collective-permute-done.5.x2), channel_id=1, source_target_pairs={{0,2},{1,3},{2,4},{3,5},{4,6},{5,7},{6,0},{7,1},{8,10},{9,11},{10,... | collective-permute-start | bytes 921608 | tf_op jit(solution)/shard_map/ppermute | solution.py:954
  33.1 10.8 %collective-permute-start.11 = (bf16[96,768]{1,0:T(8,128)(2,1)}, bf16[96,768]{1,0:T(8,128)(2,1)S(1)}, u32[]{:S(2)}, u32[]{:S(2)}) collective-permute-start(bf16[96,768]{1,0:T(8,128)(2,1)} %get-tuple-element.204), channel_id=1, source_target_pairs={{0,6},{1,7},{2,0},{3,1},{4,2},{5,3},{6,4},{7,5},{8,14},{9,15},{10,... | collective-permute-start | bytes 442376 | tf_op jit(solution)/shard_map/ppermute | solution.py:954
  44.1 12.7 %collective-permute-start.12 = (bf16[2,200,768]{2,1,0:T(8,128)(2,1)S(1)}, bf16[2,200,768]{2,1,0:T(8,128)(2,1)S(1)}, u32[]{:S(2)}, u32[]{:S(2)}) collective-permute-start(bf16[2,200,768]{2,1,0:T(8,128)(2,1)S(1)} %pad_maximum_fusion), channel_id=1, source_target_pairs={{0,1},{1,0},{2,3},{3,2},{4,5},{5,4},{6,7},{7,6},{8,9},{9,8},{10,11... | collective-permute-start | bytes 1843208 | tf_op jit(solution)/shard_map/ppermute | solution.py:950
  44.7 10.2 %collective-permute-start.13 = (bf16[144,1664]{1,0:T(8,128)(2,1)S(1)}, bf16[144,1664]{1,0:T(8,128)(2,1)S(1)}, u32[]{:S(2)}, u32[]{:S(2)}) collective-permute-start(bf16[144,1664]{1,0:T(8,128)(2,1)S(1)} %collective-permute-done.8), channel_id=1, source_target_pairs={{0,16},{8,24},{16,0},{24,8},{1,17},{9,25},{17,1},{25,9},{2,18},{10... | collective-permute-start | bytes 1437704 | tf_op jit(solution)/shard_map/ppermute | solution.py:938
  61.2 16.5 %collective-permute-start.24 = (bf16[192,768]{1,0:T(8,128)(2,1)S(1)}, bf16[192,768]{1,0:T(8,128)(2,1)S(1)}, u32[]{:S(2)}, u32[]{:S(2)}) collective-permute-start(bf16[192,768]{1,0:T(8,128)(2,1)S(1)} %bitcast.219), channel_id=1, source_target_pairs={{0,8},{8,0},{16,24},{24,16},{1,9},{9,1},{17,25},{25,17},{2,10},{10... | collective-permute-start | bytes 884744 | tf_op jit(solution)/shard_map/ppermute | solution.py:938
  61.5 16.2 %collective-permute-start.25 = (bf16[192,768]{1,0:T(8,128)(2,1)S(1)}, bf16[192,768]{1,0:T(8,128)(2,1)S(1)}, u32[]{:S(2)}, u32[]{:S(2)}) collective-permute-start(bf16[192,768]{1,0:T(8,128)(2,1)S(1)} %collective-permute-done.3.dy_x), channel_id=1, source_target_pairs={{0,8},{8,0},{16,24},{24,16},{1,9},{9,1},{17,25},{25,17},{2,10},{10... | collective-permute-start | bytes 884744 | tf_op jit(solution)/shard_map/ppermute | solution.py:938
  61.7 16.0 %collective-permute-start.22 = (bf16[384,768]{1,0:T(8,128)(2,1)S(1)}, bf16[384,768]{1,0:T(8,128)(2,1)S(1)}, u32[]{:S(2)}, u32[]{:S(2)}) collective-permute-start(bf16[384,768]{1,0:T(8,128)(2,1)S(1)} %pad_maximum_fusion.1), channel_id=1, source_target_pairs={{0,1},{1,0},{2,3},{3,2},{4,5},{5,4},{6,7},{7,6},{8,9},{9,8},{10,11... | collective-permute-start | bytes 1769480 | tf_op jit(solution)/shard_map/ppermute | solution.py:950
  62.3 15.4 %collective-permute-start.23 = (bf16[192,768]{1,0:T(8,128)(2,1)S(1)}, bf16[192,768]{1,0:T(8,128)(2,1)S(1)}, u32[]{:S(2)}, u32[]{:S(2)}) collective-permute-start(bf16[192,768]{1,0:T(8,128)(2,1)S(1)} %collective-permute-done.14.z1), channel_id=1, source_target_pairs={{0,2},{1,3},{2,4},{3,5},{4,6},{5,7},{6,0},{7,1},{8,10},{9,11},{10,... | collective-permute-start | bytes 884744 | tf_op jit(solution)/shard_map/ppermute | solution.py:954
  103.3 14.8 %collective-permute-start.33 = (bf16[4,96,768]{2,1,0:T(8,128)(2,1)S(1)}, bf16[4,96,768]{2,1,0:T(8,128)(2,1)S(1)}, u32[]{:S(2)}, u32[]{:S(2)}) collective-permute-start(bf16[4,96,768]{2,1,0:T(8,128)(2,1)S(1)} %slice_bitcast_fusion.1), channel_id=1, source_target_pairs={{0,1},{1,0},{2,3},{3,2},{4,5},{5,4},{6,7},{7,6},{8,9},{9,8},{10,11... | collective-permute-start | bytes 1769480 | tf_op jit(solution)/shard_map/ppermute | solution.py:950
  104.8 13.3 %collective-permute-start.34 = (bf16[2,192,768]{2,1,0:T(8,128)(2,1)S(1)}, bf16[2,192,768]{2,1,0:T(8,128)(2,1)S(1)}, u32[]{:S(2)}, u32[]{:S(2)}) collective-permute-start(bf16[2,192,768]{2,1,0:T(8,128)(2,1)S(1)} %get-tuple-element.307), channel_id=1, source_target_pairs={{0,8},{8,0},{16,24},{24,16},{1,9},{9,1},{17,25},{25,17},{2,10},{10... | collective-permute-start | bytes 1769480 | tf_op jit(solution)/shard_map/ppermute | solution.py:938
  118.1 17.7 %collective-permute-start.35 = (bf16[2,2,4,120,384]{4,3,2,1,0:T(8,128)(2,1)S(1)}, bf16[2,2,4,120,384]{4,3,2,1,0:T(8,128)(2,1)S(1)}, u32[]{:S(2)}, u32[]{:S(2)}) collective-permute-start(bf16[2,2,4,120,384]{4,3,2,1,0:T(8,128)(2,1)S(1)} %get-tuple-element.316), channel_id=1, source_target_pairs={{0,8},{8,0},{16,24},{24,16},{1,9},{9,1},{17,25},{25,17},{2,10},{10... | collective-permute-start | bytes 4423688 | tf_op jit(solution)/shard_map/ppermute | solution.py:938
  118.1 17.7 %collective-permute-start.36 = (bf16[4,96,768]{2,1,0:T(8,128)(2,1)S(1)}, bf16[4,96,768]{2,1,0:T(8,128)(2,1)S(1)}, u32[]{:S(2)}, u32[]{:S(2)}) collective-permute-start(bf16[4,96,768]{2,1,0:T(8,128)(2,1)S(1)} %slice_bitcast_fusion), channel_id=1, source_target_pairs={{0,1},{1,0},{2,3},{3,2},{4,5},{5,4},{6,7},{7,6},{8,9},{9,8},{10,11... | collective-permute-start | bytes 1769480 | tf_op jit(solution)/shard_map/ppermute | solution.py:950
  119.7 16.1 %collective-permute-start.37 = (bf16[96,768]{1,0:T(8,128)(2,1)S(1)}, bf16[96,768]{1,0:T(8,128)(2,1)S(1)}, u32[]{:S(2)}, u32[]{:S(2)}) collective-permute-start(bf16[96,768]{1,0:T(8,128)(2,1)S(1)} %get-tuple-element.374), channel_id=1, source_target_pairs={{0,2},{1,3},{2,4},{3,5},{4,6},{5,7},{6,0},{7,1},{8,10},{9,11},{10,... | collective-permute-start | bytes 442376 | tf_op jit(solution)/shard_map/ppermute | solution.py:954
  121.4 14.4 %collective-permute-start.38 = (bf16[96,768]{1,0:T(8,128)(2,1)S(1)}, bf16[96,768]{1,0:T(8,128)(2,1)S(1)}, u32[]{:S(2)}, u32[]{:S(2)}) collective-permute-start(bf16[96,768]{1,0:T(8,128)(2,1)S(1)} %get-tuple-element.373), channel_id=1, source_target_pairs={{0,4},{1,5},{2,6},{3,7},{4,0},{5,1},{6,2},{7,3},{8,12},{9,13},{10,... | collective-permute-start | bytes 442376 | tf_op jit(solution)/shard_map/ppermute | solution.py:954
  122.8 13.0 %collective-permute-start.39 = (bf16[96,768]{1,0:T(8,128)(2,1)S(1)}, bf16[96,768]{1,0:T(8,128)(2,1)S(1)}, u32[]{:S(2)}, u32[]{:S(2)}) collective-permute-start(bf16[96,768]{1,0:T(8,128)(2,1)S(1)} %get-tuple-element.372), channel_id=1, source_target_pairs={{0,6},{1,7},{2,0},{3,1},{4,2},{5,3},{6,4},{7,5},{8,14},{9,15},{10,... | collective-permute-start | bytes 442376 | tf_op jit(solution)/shard_map/ppermute | solution.py:954
  136.0 17.8 %collective-permute-start.42 = (bf16[2,4,120,384]{3,2,1,0:T(8,128)(2,1)S(1)}, bf16[2,4,120,384]{3,2,1,0:T(8,128)(2,1)S(1)}, u32[]{:S(2)}, u32[]{:S(2)}) collective-permute-start(bf16[2,4,120,384]{3,2,1,0:T(8,128)(2,1)S(1)} %fusion.1), channel_id=1, source_target_pairs={{0,16},{8,24},{16,0},{24,8},{1,17},{9,25},{17,1},{25,9},{2,18},{10... | collective-permute-start | bytes 2211848 | tf_op jit(solution)/shard_map/ppermute | solution.py:938
  136.8 14.3 %collective-permute-start.43 = (bf16[2,192,768]{2,1,0:T(8,128)(2,1)S(1)}, bf16[2,192,768]{2,1,0:T(8,128)(2,1)S(1)}, u32[]{:S(2)}, u32[]{:S(2)}) collective-permute-start(bf16[2,192,768]{2,1,0:T(8,128)(2,1)S(1)} %get-tuple-element.325), channel_id=1, source_target_pairs={{0,1},{1,0},{2,3},{3,2},{4,5},{5,4},{6,7},{7,6},{8,9},{9,8},{10,11... | collective-permute-start | bytes 1769480 | tf_op jit(solution)/shard_map/ppermute | solution.py:950
  154.0 15.1 %collective-permute-start.47 = (bf16[192,768]{1,0:T(8,128)(2,1)S(1)}, bf16[192,768]{1,0:T(8,128)(2,1)S(1)}, u32[]{:S(2)}, u32[]{:S(2)}) collective-permute-start(bf16[192,768]{1,0:T(8,128)(2,1)S(1)} %fusion.17), channel_id=1, source_target_pairs={{0,6},{1,7},{2,0},{3,1},{4,2},{5,3},{6,4},{7,5},{8,14},{9,15},{10,... | collective-permute-start | bytes 884744 | tf_op jit(solution)/shard_map/ppermute | solution.py:954
  156.7 12.4 %collective-permute-start.45 = (bf16[2,4,80,384]{3,2,1,0:T(8,128)(2,1)S(1)}, bf16[2,4,80,384]{3,2,1,0:T(8,128)(2,1)S(1)}, u32[]{:S(2)}, u32[]{:S(2)}) collective-permute-start(bf16[2,4,80,384]{3,2,1,0:T(8,128)(2,1)S(1)} %fusion), channel_id=1, source_target_pairs={{0,16},{8,24},{16,0},{24,8},{1,17},{9,25},{17,1},{25,9},{2,18},{10... | collective-permute-start | bytes 1474568 | tf_op jit(solution)/shard_map/ppermute | solution.py:938
  157.7 11.4 %collective-permute-start.46 = (bf16[4,120,384]{2,1,0:T(8,128)(2,1)S(1)}, bf16[4,120,384]{2,1,0:T(8,128)(2,1)S(1)}, u32[]{:S(2)}, u32[]{:S(2)}) collective-permute-start(bf16[4,120,384]{2,1,0:T(8,128)(2,1)S(1)} %fusion.2), channel_id=1, source_target_pairs={{0,1},{1,0},{2,3},{3,2},{4,5},{5,4},{6,7},{7,6},{8,9},{9,8},{10,11... | collective-permute-start | bytes 1105928 | tf_op jit(solution)/shard_map/ppermute | solution.py:950
  158.3 9.5 %collective-permute-start.48 = (bf16[96,768]{1,0:T(8,128)(2,1)S(1)}, bf16[96,768]{1,0:T(8,128)(2,1)S(1)}, u32[]{:S(2)}, u32[]{:S(2)}) collective-permute-start(bf16[96,768]{1,0:T(8,128)(2,1)S(1)} %get-tuple-element.371), channel_id=1, source_target_pairs={{0,2},{1,3},{2,4},{3,5},{4,6},{5,7},{6,0},{7,1},{8,10},{9,11},{10,... | collective-permute-start | bytes 442376 | tf_op jit(solution)/shard_map/ppermute | solution.py:954
  158.6 10.5 %collective-permute-start.49 = (bf16[96,768]{1,0:T(8,128)(2,1)S(1)}, bf16[96,768]{1,0:T(8,128)(2,1)S(1)}, u32[]{:S(2)}, u32[]{:S(2)}) collective-permute-start(bf16[96,768]{1,0:T(8,128)(2,1)S(1)} %get-tuple-element.370), channel_id=1, source_target_pairs={{0,6},{1,7},{2,0},{3,1},{4,2},{5,3},{6,4},{7,5},{8,14},{9,15},{10,... | collective-permute-start | bytes 442376 | tf_op jit(solution)/shard_map/ppermute | solution.py:954
  178.8 14.9 %collective-permute-start.55 = (bf16[384,768]{1,0:T(8,128)(2,1)S(1)}, bf16[384,768]{1,0:T(8,128)(2,1)S(1)}, u32[]{:S(2)}, u32[]{:S(2)}) collective-permute-start(bf16[384,768]{1,0:T(8,128)(2,1)S(1)} %pad_maximum_fusion.2), channel_id=1, source_target_pairs={{0,16},{8,24},{16,0},{24,8},{1,17},{9,25},{17,1},{25,9},{2,18},{10... | collective-permute-start | bytes 1769480 | tf_op jit(solution)/shard_map/ppermute | solution.py:938
  182.5 11.2 %collective-permute-start.53 = (bf16[200,384]{1,0:T(8,128)(2,1)S(1)}, bf16[200,384]{1,0:T(8,128)(2,1)S(1)}, u32[]{:S(2)}, u32[]{:S(2)}) collective-permute-start(bf16[200,384]{1,0:T(8,128)(2,1)S(1)} %pad_maximum_fusion.6), channel_id=1, source_target_pairs={{0,4},{1,5},{2,6},{3,7},{4,0},{5,1},{6,2},{7,3},{8,12},{9,13},{10,... | collective-permute-start | bytes 460808 | tf_op jit(solution)/shard_map/ppermute | solution.py:954
  182.6 11.1 %collective-permute-start.52 = (bf16[200,384]{1,0:T(8,128)(2,1)S(1)}, bf16[200,384]{1,0:T(8,128)(2,1)S(1)}, u32[]{:S(2)}, u32[]{:S(2)}) collective-permute-start(bf16[200,384]{1,0:T(8,128)(2,1)S(1)} %pad_maximum_fusion.5), channel_id=1, source_target_pairs={{0,2},{1,3},{2,4},{3,5},{4,6},{5,7},{6,0},{7,1},{8,10},{9,11},{10,... | collective-permute-start | bytes 460808 | tf_op jit(solution)/shard_map/ppermute | solution.py:954
  (37 other events, 277.1 us)

commit v10 on v9

--- a/solution.py
+++ b/solution.py
@@ -894,7 +894,7 @@
             up[:, pl.ds(384 * (4 * group + shard), 384)] = pack96([part[shard] for part in parts])
 
 
-def finish_q_kernel(f0, fx, fc, fcx, qkv, out):
+def finish_q_kernel(f0, fx, fc, fcx, qkv, out, gains, shifts, biases, up_bias):
     x, c, _y, _z = place()
     side = out.shape[1] // 2
     for (xx, cc), piece in zip(corners(x, c), (f0, fx, fc, fcx), strict=True):
@@ -906,6 +906,14 @@
             qkv[rows, pl.ds(2 * side * number + side, side)] = blocks[second : second + 24]
         out[rows, pl.ds(0, side)] = blocks[72:96]
         out[rows, pl.ds(side, side)] = blocks[96:120]
+    sums = f32(f0[...])[192:]
+    part = gains.shape[1]
+    gains[...] = sums[0:2, :part]
+    shifts[...] = sums[2:4, :part]
+    biases[...] = sums[4:8, :part]
+    ups = sums[:, 128:256]
+    packed = pack96([jnp.broadcast_to(ups[k : k + 1], (8, 128)) for k in range(4)])
+    up_bias[...] = packed[0]
 
 
 HB = pl.BlockSpec(memory_space=pltpu.HBM)
@@ -1256,7 +1264,7 @@
     *q_z, over_x, f_tot = fence(*(to_z(b16(q_3(step)), step) for step in (1, 2, 3)), to_x(fy_tot), f_tot)
     f_x, back_y = over_x[:tok], over_x[tok:]
     q_sum = z_sum(q_3, *q_z)
-    q_fx, q_fc, q_fxc = to_x(q_sum), to_core(q_sum), swap_rep(q_sum, 3)
+    q_fx, q_fc = to_x(q_sum), to_core(q_sum)
     grad_up, grad_down = call(
         finish_f_kernel,
         [VM] * 4,
@@ -1266,17 +1274,24 @@
         vmem=8,
         moved=4 * 10**6,
     )(f_tot, f_x, to_core(f_tot), to_core(f_x))
-    q_fx, q_fc, q_fxc, grad_up, grad_down = fence(q_fx, q_fc, q_fxc, grad_up, grad_down)
+    q_fx, q_fc, grad_up, grad_down = fence(q_fx, q_fc, grad_up, grad_down)
+    q_fxc = to_core(q_fx)
     result = b16(residual + vec[7:8] + y_keep[0] + f32(came_y[0]) + f32(back_y))
-    grad_qkv, grad_out = call(
+    grad_qkv, grad_out, grad_gains, grad_shifts, grad_biases, grad_up_bias = call(
         finish_q_kernel,
         [VM] * 4,
-        [VM] * 2,
-        [shape_of(query_key_value_weight.shape, fl), shape_of(output_weight.shape, fl)],
-        vmem=8, moved=3 * 10**6,
+        [VM] * 6,
+        [
+            shape_of(query_key_value_weight.shape, fl),
+            shape_of(output_weight.shape, fl),
+            shape_of(ln_gains.shape, fl),
+            shape_of(ln_biases.shape, fl),
+            shape_of(biases.shape, fl),
+            shape_of(up_projection_bias.shape, fl),
+        ],
+        vmem=8,
+        moved=3 * 10**6,
     )(q_sum, q_fx, q_fc, q_fxc)
-    sums = f32(q_sum[192:200, :256])
-    part = ln_gains.shape[1]
     return (
         result[None],
         grad_tokens[None],
@@ -1284,10 +1299,10 @@
         grad_out,
         grad_up,
         grad_down,
-        sums[0:2, :part],
-        sums[2:4, :part],
-        sums[4:8, :part],
-        sums[0:4, 128 : 128 + part].reshape(4 * part),
+        grad_gains,
+        grad_shifts,
+        grad_biases,
+        grad_up_bias,
     )
 
 

time: 203 us -> 203 us (level)
  waiting for transfers between devices: 69.6 us -> 72.7 us
  transfers between devices with their start and end apart: 61 -> 61, of which waited for: 22 -> 23; matrix products, arithmetic and copies ran while one was open for 2% -> 1% of each run, Pallas kernels for 31% -> 31%
where the time goes in v10:
time: 203 us
  waiting for transfers between devices  72.7 us (36%)
  Pallas kernels  63.3 us (31%)
  starting transfers between devices  62.4 us (31%)
  other arithmetic  3.01 us (1%)
    ppermute x20, waiting for transfers between devices, to_z(): lax.ppermute(value, 'seq', [(k, (k + 2 * steps) % 8) for k in range(8)])  49.6 us
    ppermute x20, starting transfers between devices, to_z(): lax.ppermute(value, 'seq', [(k, (k + 2 * steps) % 8) for k in range(8)])  35.5 us
    ppermute x30, starting transfers between devices, swap_rep(): return lax.ppermute(value, 'rep', [(k, k ^ bit) for k in range(4)])  15 us
    pallas_call x1, Pallas kernels, on_device_fast(): call(front_kernel, [VM] * 6 + [AN] * 15, [VM] * 11, [shape_of((tok, width...  13.9 us
    ppermute x30, waiting for transfers between devices, swap_rep(): return lax.ppermute(value, 'rep', [(k, k ^ bit) for k in range(4)])  11.9 us
    ppermute x11, starting transfers between devices, to_y(): return lax.ppermute(value, 'seq', [(k, k ^ 1) for k in range(8)])  11.9 us
    ppermute x11, waiting for transfers between devices, to_y(): return lax.ppermute(value, 'seq', [(k, k ^ 1) for k in range(8)])  11.1 us
    pallas_call x1, Pallas kernels, on_device_fast(): call(back_b_kernel, [VM] * 14 + [AN] * 13, [VM] * 6, [shape_of((tok, widt...  10.8 us
  transfers between devices with their start and end apart: 61, of which 23 were waited for; matrix products, arithmetic and copies ran while one was open for 1% of the time, Pallas kernels for 31%

profile of v10, /device:TPU:0, one launch (start us, length us, event | category | flops | bytes accessed | tf_op | source)
XLA Modules:
  0.0 202.8 jit_solution(15971824038441774289)
XLA Ops:
  0.6 3.0 %collective-permute-start.3 = (bf16[192,768]{1,0:T(8,128)(2,1)}, bf16[192,768]{1,0:T(8,128)(2,1)S(1)}, u32[]{:S(2)}, u32[]{:S(2)}) collective-permute-start(bf16[192,768]{1,0:T(8,128)(2,1)} %bitcast.218), channel_id=1, source_target_pairs={{0,16},{8,24},{16,0},{24,8},{1,17},{9,25},{17,1},{25,9},{2,18},{10... | collective-permute-start | bytes 884744 | tf_op jit(solution)/shard_map/ppermute | solution.py:946
  3.6 2.7 %shard_map.186 = (bf16[200,768]{1,0:T(8,128)(2,1)}, bf16[48,1664]{1,0:T(8,128)(2,1)}, bf16[192,768]{1,0:T(8,128)(2,1)}, bf16[96,768]{1,0:T(8,128)(2,1)}, bf16[96,768]{1,0:T(8,128)(2,1)}) custom-call(bf16[1,192,768]{2,1,0:T(8,128)(2,1)} %tokens.1, s32[1,192]{1,0:T(1,128)} %segs.1, bf16[96,2304]{1,0:T(8,128)(2,1)} %own.3, bf16[96,768]{1,0:T(8,128)(2,1)} %own_o.1, ...), custom_call_target="tpu_custom_call" | custom-call | bytes 4000000 | tf_op jit(solution)/shard_map/pallas_call | solution.py:990
  8.0 2.2 %collective-permute-start.1 = (bf16[48,1664]{1,0:T(8,128)(2,1)}, bf16[48,1664]{1,0:T(8,128)(2,1)S(1)}, u32[]{:S(2)}, u32[]{:S(2)}) collective-permute-start(bf16[48,1664]{1,0:T(8,128)(2,1)} %get-tuple-element.191.first), channel_id=1, source_target_pairs={{0,6},{1,7},{2,0},{3,1},{4,2},{5,3},{6,4},{7,5},{8,14},{9,15},{10,... | collective-permute-start | bytes 479240 | tf_op jit(solution)/shard_map/ppermute | solution.py:962
  11.8 3.7 %collective-permute-done = bf16[48,1664]{1,0:T(8,128)(2,1)S(1)} collective-permute-done((bf16[48,1664]{1,0:T(8,128)(2,1)}, bf16[48,1664]{1,0:T(8,128)(2,1)S(1)}, u32[]{:S(2)}, u32[]{:S(2)}) %collective-permute-start) | collective-permute-done | bytes 159776 | tf_op jit(solution)/shard_map/ppermute | solution.py:962
  20.9 10.0 %collective-permute-done.4 = bf16[48,1664]{1,0:T(8,128)(2,1)S(1)} collective-permute-done((bf16[48,1664]{1,0:T(8,128)(2,1)S(1)}, bf16[48,1664]{1,0:T(8,128)(2,1)S(1)}, u32[]{:S(2)}, u32[]{:S(2)}) %collective-permute-start.4) | collective-permute-done | bytes 159776 | tf_op jit(solution)/shard_map/ppermute | solution.py:962
  33.1 3.8 %collective-permute-start.11 = (bf16[96,768]{1,0:T(8,128)(2,1)}, bf16[96,768]{1,0:T(8,128)(2,1)S(1)}, u32[]{:S(2)}, u32[]{:S(2)}) collective-permute-start(bf16[96,768]{1,0:T(8,128)(2,1)} %get-tuple-element.207), channel_id=1, source_target_pairs={{0,6},{1,7},{2,0},{3,1},{4,2},{5,3},{6,4},{7,5},{8,14},{9,15},{10,... | collective-permute-start | bytes 442376 | tf_op jit(solution)/shard_map/ppermute | solution.py:962
  36.9 7.0 %collective-permute-done.11.z3d = bf16[96,768]{1,0:T(8,128)(2,1)S(1)} collective-permute-done((bf16[96,768]{1,0:T(8,128)(2,1)}, bf16[96,768]{1,0:T(8,128)(2,1)S(1)}, u32[]{:S(2)}, u32[]{:S(2)}) %collective-permute-start.11) | collective-permute-done | bytes 147488 | tf_op jit(solution)/shard_map/ppermute | solution.py:962
  46.5 3.5 %collective-permute-start.15 = (bf16[96,768]{1,0:T(8,128)(2,1)S(1)}, bf16[96,768]{1,0:T(8,128)(2,1)S(1)}, u32[]{:S(2)}, u32[]{:S(2)}) collective-permute-start(bf16[96,768]{1,0:T(8,128)(2,1)S(1)} %copy-done.7), channel_id=1, source_target_pairs={{0,6},{1,7},{2,0},{3,1},{4,2},{5,3},{6,4},{7,5},{8,14},{9,15},{10,... | collective-permute-start | bytes 442376 | tf_op jit(solution)/shard_map/ppermute | solution.py:962
  50.0 4.9 %collective-permute-done.15.z3u = bf16[96,768]{1,0:T(8,128)(2,1)S(1)} collective-permute-done((bf16[96,768]{1,0:T(8,128)(2,1)S(1)}, bf16[96,768]{1,0:T(8,128)(2,1)S(1)}, u32[]{:S(2)}, u32[]{:S(2)}) %collective-permute-start.15) | collective-permute-done | bytes 147488 | tf_op jit(solution)/shard_map/ppermute | solution.py:962
  58.6 2.6 %collective-permute-done.20 = bf16[48,1664]{1,0:T(8,128)(2,1)S(1)} collective-permute-done((bf16[48,1664]{1,0:T(8,128)(2,1)S(1)}, bf16[48,1664]{1,0:T(8,128)(2,1)S(1)}, u32[]{:S(2)}, u32[]{:S(2)}) %collective-permute-start.20) | collective-permute-done | bytes 159776 | tf_op jit(solution)/shard_map/ppermute | solution.py:946
  63.8 13.9 %shard_map.187 = (bf16[192,768]{1,0:T(8,128)(2,1)S(1)}, bf16[960,1536]{1,0:T(8,128)(2,1)S(1)}, bf16[960,768]{1,0:T(8,128)(2,1)S(1)}, bf16[192,768]{1,0:T(8,128)(...) custom-call(s32[1,384]{1,0:T(1,128)S(1)} %pad_add_fusion.seg, ...), custom_call_target="tpu_custom_call" | custom-call | flops 7000000000 | bytes 12000000 | tf_op jit(solution)/shard_map/pallas_call | solution.py:1046
  79.8 2.9 %shard_map.188 = (bf16[768,768]{1,0:T(8,128)(2,1)S(1)}, bf16[768,768]{1,0:T(8,128)(2,1)S(1)}) custom-call(bf16[192,768]{1,0:T(8,128)(2,1)S(1)} %copy-done.2, bf16[192,768]{1,0:T(8,128)(2,1)S(1)} %collective-permute-done.14.z1, bf16[192,768]{1,0:T(8,128)(2,1)S(1)} %collective-permute-done.23.z2, bf16[96,768]{1,0:T(8,128)(2,1)S(1)} %collective-permute-done.15.z3u, ...), custom_call_target="tpu_custom_call" | custom-call | bytes 5000000 | tf_op jit(solution)/shard_map/pallas_call | solution.py:1077
  82.6 3.8 %collective-permute-done.26.h_x = bf16[192,768]{1,0:T(8,128)(2,1)S(1)} collective-permute-done((bf16[192,768]{1,0:T(8,128)(2,1)S(1)}, bf16[192,768]{1,0:T(8,128)(2,1)S(1)}, u32[]{:S(2)}, u32[]{:S(2)}) %collective-permute-start.26) | collective-permute-done | bytes 294944 | tf_op jit(solution)/shard_map/ppermute | solution.py:946
  87.7 2.3 %shard_map.189 = (bf16[384,768]{1,0:T(8,128)(2,1)S(1)}, bf16[384,768]{1,0:T(8,128)(2,1)S(1)}, bf16[384,768]{1,0:T(8,128)(2,1)S(1)}, bf16[384,768]{1,0:T(8,128)(2...) custom-call(bf16[192,768]{1,0:T(8,128)(2,1)S(1)} %get-tuple-element., ...), custom_call_target="tpu_custom_call", output_to_operand_aliasing={{6}: (6, {}), {7}: (7, {})} | custom-call | flops 3000000000 | bytes 6000000 | tf_op jit(solution)/shard_map/pallas_call | solution.py:1090
  95.6 7.2 %shard_map.192 = (bf16[2,4,96,768]{3,2,1,0:T(8,128)(2,1)S(1)}, bf16[2,4,96,768]{3,2,1,0:T(8,128)(2,1)S(1)}, f32[1,768]{1,0:T(1,128)S(1)}, f32[2,192,768]{2,1,0:T(8,128)S(1)}, bf16[2,192,768]{2,1,0:T(8,128)(2,1)S(1)}) custom-call(bf16[768,768]{1,0:T(8,128)(2,1)S(1)} %get-tuple-element.285.hs, bf16[768,768]{1,0:T(8,128)(2,1)S(1)} %get-tuple-element.286.dys, ...), custom_call_target="tpu_custom_call" | custom-call | flops 3000000000 | bytes 6000000 | tf_op jit(solution)/shard_map/pallas_call | solution.py:1128
  106.1 10.0 %shard_map.194 = (bf16[2,2,4,120,384]{4,3,2,1,0:T(8,128)(2,1)S(1)}, bf16[2,2,4,120,384]{4,3,2,1,0:T(8,128)(2,1)S(1)}, bf16[192,384]{1,0:T(8,128)(2,1)S(1)}, bf16[960,768]{1,0:T(8,128)(2,1)S(1)}) custom-call(s32[1,384]{1,0:T(1,128)S(1)} %get-tuple-element.290.start_in, bf16[192,768]{1,0:T(8,128)(2,1)S(1)} %get-tuple-element.291.q_in, ...), custom_call_target="tpu_custom_call" | custom-call | flops 5000000000 | bytes 10000000 | tf_op jit(solution)/shard_map/pallas_call | solution.py:1164
  116.2 1.9 collective-permute-done.33
  122.8 2.2 %collective-permute-start.39 = (bf16[96,768]{1,0:T(8,128)(2,1)S(1)}, bf16[96,768]{1,0:T(8,128)(2,1)S(1)}, u32[]{:S(2)}, u32[]{:S(2)}) collective-permute-start(bf16[96,768]{1,0:T(8,128)(2,1)S(1)} %get-tuple-element.378), channel_id=1, source_target_pairs={{0,6},{1,7},{2,0},{3,1},{4,2},{5,3},{6,4},{7,5},{8,14},{9,15},{10,... | collective-permute-start | bytes 442376 | tf_op jit(solution)/shard_map/ppermute | solution.py:962
  125.0 10.8 %shard_map.195 = (bf16[192,384]{1,0:T(8,128)(2,1)S(1)}, bf16[960,768]{1,0:T(8,128)(2,1)S(1)}, f32[192,768]{1,0:T(8,128)S(1)}, bf16[2,192,768]{2,1,0:T(8,128)(2,1...) custom-call(s32[1,384]{1,0:T(1,128)S(1)} %get-tuple-element.290.start_in, ...), custom_call_target="tpu_custom_call" | custom-call | flops 6000000000 | bytes 10000000 | tf_op jit(solution)/shard_map/pallas_call | solution.py:1191
  137.4 4.8 %shard_map.196 = (bf16[2,2,4,80,384]{4,3,2,1,0:T(8,128)(2,1)S(1)}, bf16[2,2,4,80,384]{4,3,2,1,0:T(8,128)(2,1)S(1)}) custom-call(bf16[960,768]{1,0:T(8,128)(2,1)S(1)} %get-tuple-element.293.h_in, bf16[192,384]{1,0:T(8,128)(2,1)S(1)} %get-tuple-element.324.dq, bf16[960,768]{1,0:T(8,128)(2,1)S(1)} %get-tuple-element.325.dkv, ...), custom_call_target="tpu_custom_call" | custom-call | flops 3000000000 | bytes 6000000 | tf_op jit(solution)/shard_map/pallas_call | solution.py:1216
  142.9 2.3 %collective-permute-start.44 = (bf16[96,768]{1,0:T(8,128)(2,1)S(1)}, bf16[96,768]{1,0:T(8,128)(2,1)S(1)}, u32[]{:S(2)}, u32[]{:S(2)}) collective-permute-start(bf16[96,768]{1,0:T(8,128)(2,1)S(1)} %fusion.25), channel_id=1, source_target_pairs={{0,2},{1,3},{2,4},{3,5},{4,6},{5,7},{6,0},{7,1},{8,10},{9,11},{10,... | collective-permute-start | bytes 442376 | tf_op jit(solution)/shard_map/ppermute | solution.py:962
  145.3 5.3 %collective-permute-done.44 = bf16[96,768]{1,0:T(8,128)(2,1)S(1)} collective-permute-done((bf16[96,768]{1,0:T(8,128)(2,1)S(1)}, bf16[96,768]{1,0:T(8,128)(2,1)S(1)}, u32[]{:S(2)}, u32[]{:S(2)}) %collective-permute-start.44) | collective-permute-done | bytes 147488 | tf_op jit(solution)/shard_map/ppermute | solution.py:962
  151.2 2.7 %collective-permute-done.42 = bf16[2,4,120,384]{3,2,1,0:T(8,128)(2,1)S(1)} collective-permute-done((bf16[2,4,120,384]{3,2,1,0:T(8,128)(2,1)S(1)}, bf16[2,4,120,384]{3,2,1,0:T(8,128)(2,1)S(1)}, u32[]{:S(2)}, u32[]{:S(2)}) %collective-permute-start.42) | collective-permute-done | bytes 737312 | tf_op jit(solution)/shard_map/ppermute | solution.py:946
  154.0 2.6 %collective-permute-start.47 = (bf16[192,768]{1,0:T(8,128)(2,1)S(1)}, bf16[192,768]{1,0:T(8,128)(2,1)S(1)}, u32[]{:S(2)}, u32[]{:S(2)}) collective-permute-start(bf16[192,768]{1,0:T(8,128)(2,1)S(1)} %fusion.17), channel_id=1, source_target_pairs={{0,6},{1,7},{2,0},{3,1},{4,2},{5,3},{6,4},{7,5},{8,14},{9,15},{10,... | collective-permute-start | bytes 884744 | tf_op jit(solution)/shard_map/ppermute | solution.py:962
  158.6 3.6 %collective-permute-start.49 = (bf16[96,768]{1,0:T(8,128)(2,1)S(1)}, bf16[96,768]{1,0:T(8,128)(2,1)S(1)}, u32[]{:S(2)}, u32[]{:S(2)}) collective-permute-start(bf16[96,768]{1,0:T(8,128)(2,1)S(1)} %get-tuple-element.376), channel_id=1, source_target_pairs={{0,6},{1,7},{2,0},{3,1},{4,2},{5,3},{6,4},{7,5},{8,14},{9,15},{10,... | collective-permute-start | bytes 442376 | tf_op jit(solution)/shard_map/ppermute | solution.py:962
  162.3 5.5 %collective-permute-done.48 = bf16[96,768]{1,0:T(8,128)(2,1)S(1)} collective-permute-done((bf16[96,768]{1,0:T(8,128)(2,1)S(1)}, bf16[96,768]{1,0:T(8,128)(2,1)S(1)}, u32[]{:S(2)}, u32[]{:S(2)}) %collective-permute-start.48) | collective-permute-done | bytes 147488 | tf_op jit(solution)/shard_map/ppermute | solution.py:962
  169.3 3.1 %collective-permute-start.51 = (bf16[192,768]{1,0:T(8,128)(2,1)S(1)}, bf16[192,768]{1,0:T(8,128)(2,1)S(1)}, u32[]{:S(2)}, u32[]{:S(2)}) collective-permute-start(bf16[192,768]{1,0:T(8,128)(2,1)S(1)} %get-tuple-element.386), channel_id=1, source_target_pairs={{0,6},{1,7},{2,0},{3,1},{4,2},{5,3},{6,4},{7,5},{8,14},{9,15},{10,... | collective-permute-start | bytes 884744 | tf_op jit(solution)/shard_map/ppermute | solution.py:962
  173.4 5.3 %collective-permute-done.50 = bf16[4,80,384]{2,1,0:T(8,128)(2,1)S(1)} collective-permute-done((bf16[4,80,384]{2,1,0:T(8,128)(2,1)S(1)}, bf16[4,80,384]{2,1,0:T(8,128)(2,1)S(1)}, u32[]{:S(2)}, u32[]{:S(2)}) %collective-permute-start.50) | collective-permute-done | bytes 245792 | tf_op jit(solution)/shard_map/ppermute | solution.py:958
  179.6 2.8 %collective-permute-start.54 = (bf16[200,384]{1,0:T(8,128)(2,1)S(1)}, bf16[200,384]{1,0:T(8,128)(2,1)S(1)}, u32[]{:S(2)}, u32[]{:S(2)}) collective-permute-start(bf16[200,384]{1,0:T(8,128)(2,1)S(1)} %pad_maximum_fusion.7), channel_id=1, source_target_pairs={{0,6},{1,7},{2,0},{3,1},{4,2},{5,3},{6,4},{7,5},{8,14},{9,15},{10,... | collective-permute-start | bytes 460808 | tf_op jit(solution)/shard_map/ppermute | solution.py:962
  183.2 4.2 %collective-permute-done.54 = bf16[200,384]{1,0:T(8,128)(2,1)S(1)} collective-permute-done((bf16[200,384]{1,0:T(8,128)(2,1)S(1)}, bf16[200,384]{1,0:T(8,128)(2,1)S(1)}, u32[]{:S(2)}, u32[]{:S(2)}) %collective-permute-start.54) | collective-permute-done | bytes 153632 | tf_op jit(solution)/shard_map/ppermute | solution.py:962
  187.4 6.2 %collective-permute-done.53 = bf16[200,384]{1,0:T(8,128)(2,1)S(1)} collective-permute-done((bf16[200,384]{1,0:T(8,128)(2,1)S(1)}, bf16[200,384]{1,0:T(8,128)(2,1)S(1)}, u32[]{:S(2)}, u32[]{:S(2)}) %collective-permute-start.53) | collective-permute-done | bytes 153632 | tf_op jit(solution)/shard_map/ppermute | solution.py:962
  197.0 2.0 shard_map.198
  (153 shorter events, 52.7 us)
Async XLA Ops:
  0.6 16.3 %collective-permute-start.3 = (bf16[192,768]{1,0:T(8,128)(2,1)}, bf16[192,768]{1,0:T(8,128)(2,1)S(1)}, u32[]{:S(2)}, u32[]{:S(2)}) collective-permute-start(bf16[192,768]{1,0:T(8,128)(2,1)} %bitcast.218), channel_id=1, source_target_pairs={{0,16},{8,24},{16,0},{24,8},{1,17},{9,25},{17,1},{25,9},{2,18},{10... | collective-permute-start | bytes 884744 | tf_op jit(solution)/shard_map/ppermute | solution.py:946
  16.9 14.0 %collective-permute-start.5 = (bf16[200,768]{1,0:T(8,128)(2,1)}, bf16[200,768]{1,0:T(8,128)(2,1)S(1)}, u32[]{:S(2)}, u32[]{:S(2)}) collective-permute-start(bf16[200,768]{1,0:T(8,128)(2,1)} %get-tuple-element.196.xo), channel_id=1, source_target_pairs={{0,2},{1,3},{2,4},{3,5},{4,6},{5,7},{6,0},{7,1},{8,10},{9,11},{10,... | collective-permute-start | bytes 921608 | tf_op jit(solution)/shard_map/ppermute | solution.py:962
  18.1 12.9 %collective-permute-start.7 = (bf16[192,768]{1,0:T(8,128)(2,1)}, bf16[192,768]{1,0:T(8,128)(2,1)S(1)}, u32[]{:S(2)}, u32[]{:S(2)}) collective-permute-start(bf16[192,768]{1,0:T(8,128)(2,1)} %get-tuple-element.215.own), channel_id=1, source_target_pairs={{0,1},{1,0},{2,3},{3,2},{4,5},{5,4},{6,7},{7,6},{8,9},{9,8},{10,11... | collective-permute-start | bytes 884744 | tf_op jit(solution)/shard_map/ppermute | solution.py:958
  19.6 11.3 %collective-permute-start.4 = (bf16[48,1664]{1,0:T(8,128)(2,1)S(1)}, bf16[48,1664]{1,0:T(8,128)(2,1)S(1)}, u32[]{:S(2)}, u32[]{:S(2)}) collective-permute-start(bf16[48,1664]{1,0:T(8,128)(2,1)S(1)} %collective-permute-done), channel_id=1, source_target_pairs={{0,2},{1,3},{2,4},{3,5},{4,6},{5,7},{6,0},{7,1},{8,10},{9,11},{10,... | collective-permute-start | bytes 479240 | tf_op jit(solution)/shard_map/ppermute | solution.py:962
  20.4 10.6 %collective-permute-start.6 = (bf16[48,1664]{1,0:T(8,128)(2,1)S(1)}, bf16[48,1664]{1,0:T(8,128)(2,1)S(1)}, u32[]{:S(2)}, u32[]{:S(2)}) collective-permute-start(bf16[48,1664]{1,0:T(8,128)(2,1)S(1)} %collective-permute-done.2), channel_id=1, source_target_pairs={{0,16},{8,24},{16,0},{24,8},{1,17},{9,25},{17,1},{25,9},{2,18},{10... | collective-permute-start | bytes 479240 | tf_op jit(solution)/shard_map/ppermute | solution.py:946
  31.0 13.0 %collective-permute-start.8 = (bf16[144,1664]{1,0:T(8,128)(2,1)S(1)}, bf16[144,1664]{1,0:T(8,128)(2,1)S(1)}, u32[]{:S(2)}, u32[]{:S(2)}) collective-permute-start(bf16[144,1664]{1,0:T(8,128)(2,1)S(1)} %pad_maximum_fusion.3), channel_id=1, source_target_pairs={{0,1},{1,0},{2,3},{3,2},{4,5},{5,4},{6,7},{7,6},{8,9},{9,8},{10,11... | collective-permute-start | bytes 1437704 | tf_op jit(solution)/shard_map/ppermute | solution.py:958
  32.6 11.4 %collective-permute-start.9 = (bf16[144,1664]{1,0:T(8,128)(2,1)S(1)}, bf16[144,1664]{1,0:T(8,128)(2,1)S(1)}, u32[]{:S(2)}, u32[]{:S(2)}) collective-permute-start(bf16[144,1664]{1,0:T(8,128)(2,1)S(1)} %pad_maximum_fusion.3), channel_id=1, source_target_pairs={{0,16},{8,24},{16,0},{24,8},{1,17},{9,25},{17,1},{25,9},{2,18},{10... | collective-permute-start | bytes 1437704 | tf_op jit(solution)/shard_map/ppermute | solution.py:946
  33.1 10.9 %collective-permute-start.10 = (bf16[200,768]{1,0:T(8,128)(2,1)S(1)}, bf16[200,768]{1,0:T(8,128)(2,1)S(1)}, u32[]{:S(2)}, u32[]{:S(2)}) collective-permute-start(bf16[200,768]{1,0:T(8,128)(2,1)S(1)} %collective-permute-done.5.x2), channel_id=1, source_target_pairs={{0,2},{1,3},{2,4},{3,5},{4,6},{5,7},{6,0},{7,1},{8,10},{9,11},{10,... | collective-permute-start | bytes 921608 | tf_op jit(solution)/shard_map/ppermute | solution.py:962
  33.1 10.8 %collective-permute-start.11 = (bf16[96,768]{1,0:T(8,128)(2,1)}, bf16[96,768]{1,0:T(8,128)(2,1)S(1)}, u32[]{:S(2)}, u32[]{:S(2)}) collective-permute-start(bf16[96,768]{1,0:T(8,128)(2,1)} %get-tuple-element.207), channel_id=1, source_target_pairs={{0,6},{1,7},{2,0},{3,1},{4,2},{5,3},{6,4},{7,5},{8,14},{9,15},{10,... | collective-permute-start | bytes 442376 | tf_op jit(solution)/shard_map/ppermute | solution.py:962
  44.1 12.7 %collective-permute-start.12 = (bf16[2,200,768]{2,1,0:T(8,128)(2,1)S(1)}, bf16[2,200,768]{2,1,0:T(8,128)(2,1)S(1)}, u32[]{:S(2)}, u32[]{:S(2)}) collective-permute-start(bf16[2,200,768]{2,1,0:T(8,128)(2,1)S(1)} %pad_maximum_fusion), channel_id=1, source_target_pairs={{0,1},{1,0},{2,3},{3,2},{4,5},{5,4},{6,7},{7,6},{8,9},{9,8},{10,11... | collective-permute-start | bytes 1843208 | tf_op jit(solution)/shard_map/ppermute | solution.py:958
  44.7 10.2 %collective-permute-start.13 = (bf16[144,1664]{1,0:T(8,128)(2,1)S(1)}, bf16[144,1664]{1,0:T(8,128)(2,1)S(1)}, u32[]{:S(2)}, u32[]{:S(2)}) collective-permute-start(bf16[144,1664]{1,0:T(8,128)(2,1)S(1)} %collective-permute-done.8), channel_id=1, source_target_pairs={{0,16},{8,24},{16,0},{24,8},{1,17},{9,25},{17,1},{25,9},{2,18},{10... | collective-permute-start | bytes 1437704 | tf_op jit(solution)/shard_map/ppermute | solution.py:946
  61.2 16.5 %collective-permute-start.24 = (bf16[192,768]{1,0:T(8,128)(2,1)S(1)}, bf16[192,768]{1,0:T(8,128)(2,1)S(1)}, u32[]{:S(2)}, u32[]{:S(2)}) collective-permute-start(bf16[192,768]{1,0:T(8,128)(2,1)S(1)} %bitcast.219), channel_id=1, source_target_pairs={{0,8},{8,0},{16,24},{24,16},{1,9},{9,1},{17,25},{25,17},{2,10},{10... | collective-permute-start | bytes 884744 | tf_op jit(solution)/shard_map/ppermute | solution.py:946
  61.5 16.2 %collective-permute-start.25 = (bf16[192,768]{1,0:T(8,128)(2,1)S(1)}, bf16[192,768]{1,0:T(8,128)(2,1)S(1)}, u32[]{:S(2)}, u32[]{:S(2)}) collective-permute-start(bf16[192,768]{1,0:T(8,128)(2,1)S(1)} %collective-permute-done.3.dy_x), channel_id=1, source_target_pairs={{0,8},{8,0},{16,24},{24,16},{1,9},{9,1},{17,25},{25,17},{2,10},{10... | collective-permute-start | bytes 884744 | tf_op jit(solution)/shard_map/ppermute | solution.py:946
  61.7 16.0 %collective-permute-start.22 = (bf16[384,768]{1,0:T(8,128)(2,1)S(1)}, bf16[384,768]{1,0:T(8,128)(2,1)S(1)}, u32[]{:S(2)}, u32[]{:S(2)}) collective-permute-start(bf16[384,768]{1,0:T(8,128)(2,1)S(1)} %pad_maximum_fusion.1), channel_id=1, source_target_pairs={{0,1},{1,0},{2,3},{3,2},{4,5},{5,4},{6,7},{7,6},{8,9},{9,8},{10,11... | collective-permute-start | bytes 1769480 | tf_op jit(solution)/shard_map/ppermute | solution.py:958
  62.3 15.4 %collective-permute-start.23 = (bf16[192,768]{1,0:T(8,128)(2,1)S(1)}, bf16[192,768]{1,0:T(8,128)(2,1)S(1)}, u32[]{:S(2)}, u32[]{:S(2)}) collective-permute-start(bf16[192,768]{1,0:T(8,128)(2,1)S(1)} %collective-permute-done.14.z1), channel_id=1, source_target_pairs={{0,2},{1,3},{2,4},{3,5},{4,6},{5,7},{6,0},{7,1},{8,10},{9,11},{10,... | collective-permute-start | bytes 884744 | tf_op jit(solution)/shard_map/ppermute | solution.py:962
  103.3 14.8 %collective-permute-start.33 = (bf16[4,96,768]{2,1,0:T(8,128)(2,1)S(1)}, bf16[4,96,768]{2,1,0:T(8,128)(2,1)S(1)}, u32[]{:S(2)}, u32[]{:S(2)}) collective-permute-start(bf16[4,96,768]{2,1,0:T(8,128)(2,1)S(1)} %slice_bitcast_fusion.1), channel_id=1, source_target_pairs={{0,1},{1,0},{2,3},{3,2},{4,5},{5,4},{6,7},{7,6},{8,9},{9,8},{10,11... | collective-permute-start | bytes 1769480 | tf_op jit(solution)/shard_map/ppermute | solution.py:958
  104.8 13.3 %collective-permute-start.34 = (bf16[2,192,768]{2,1,0:T(8,128)(2,1)S(1)}, bf16[2,192,768]{2,1,0:T(8,128)(2,1)S(1)}, u32[]{:S(2)}, u32[]{:S(2)}) collective-permute-start(bf16[2,192,768]{2,1,0:T(8,128)(2,1)S(1)} %get-tuple-element.310), channel_id=1, source_target_pairs={{0,8},{8,0},{16,24},{24,16},{1,9},{9,1},{17,25},{25,17},{2,10},{10... | collective-permute-start | bytes 1769480 | tf_op jit(solution)/shard_map/ppermute | solution.py:946
  118.1 17.7 %collective-permute-start.35 = (bf16[2,2,4,120,384]{4,3,2,1,0:T(8,128)(2,1)S(1)}, bf16[2,2,4,120,384]{4,3,2,1,0:T(8,128)(2,1)S(1)}, u32[]{:S(2)}, u32[]{:S(2)}) collective-permute-start(bf16[2,2,4,120,384]{4,3,2,1,0:T(8,128)(2,1)S(1)} %get-tuple-element.319), channel_id=1, source_target_pairs={{0,8},{8,0},{16,24},{24,16},{1,9},{9,1},{17,25},{25,17},{2,10},{10... | collective-permute-start | bytes 4423688 | tf_op jit(solution)/shard_map/ppermute | solution.py:946
  118.1 17.7 %collective-permute-start.36 = (bf16[4,96,768]{2,1,0:T(8,128)(2,1)S(1)}, bf16[4,96,768]{2,1,0:T(8,128)(2,1)S(1)}, u32[]{:S(2)}, u32[]{:S(2)}) collective-permute-start(bf16[4,96,768]{2,1,0:T(8,128)(2,1)S(1)} %slice_bitcast_fusion), channel_id=1, source_target_pairs={{0,1},{1,0},{2,3},{3,2},{4,5},{5,4},{6,7},{7,6},{8,9},{9,8},{10,11... | collective-permute-start | bytes 1769480 | tf_op jit(solution)/shard_map/ppermute | solution.py:958
  119.7 16.1 %collective-permute-start.37 = (bf16[96,768]{1,0:T(8,128)(2,1)S(1)}, bf16[96,768]{1,0:T(8,128)(2,1)S(1)}, u32[]{:S(2)}, u32[]{:S(2)}) collective-permute-start(bf16[96,768]{1,0:T(8,128)(2,1)S(1)} %get-tuple-element.380), channel_id=1, source_target_pairs={{0,2},{1,3},{2,4},{3,5},{4,6},{5,7},{6,0},{7,1},{8,10},{9,11},{10,... | collective-permute-start | bytes 442376 | tf_op jit(solution)/shard_map/ppermute | solution.py:962
  121.4 14.4 %collective-permute-start.38 = (bf16[96,768]{1,0:T(8,128)(2,1)S(1)}, bf16[96,768]{1,0:T(8,128)(2,1)S(1)}, u32[]{:S(2)}, u32[]{:S(2)}) collective-permute-start(bf16[96,768]{1,0:T(8,128)(2,1)S(1)} %get-tuple-element.379), channel_id=1, source_target_pairs={{0,4},{1,5},{2,6},{3,7},{4,0},{5,1},{6,2},{7,3},{8,12},{9,13},{10,... | collective-permute-start | bytes 442376 | tf_op jit(solution)/shard_map/ppermute | solution.py:962
  122.8 13.0 %collective-permute-start.39 = (bf16[96,768]{1,0:T(8,128)(2,1)S(1)}, bf16[96,768]{1,0:T(8,128)(2,1)S(1)}, u32[]{:S(2)}, u32[]{:S(2)}) collective-permute-start(bf16[96,768]{1,0:T(8,128)(2,1)S(1)} %get-tuple-element.378), channel_id=1, source_target_pairs={{0,6},{1,7},{2,0},{3,1},{4,2},{5,3},{6,4},{7,5},{8,14},{9,15},{10,... | collective-permute-start | bytes 442376 | tf_op jit(solution)/shard_map/ppermute | solution.py:962
  136.0 17.8 %collective-permute-start.42 = (bf16[2,4,120,384]{3,2,1,0:T(8,128)(2,1)S(1)}, bf16[2,4,120,384]{3,2,1,0:T(8,128)(2,1)S(1)}, u32[]{:S(2)}, u32[]{:S(2)}) collective-permute-start(bf16[2,4,120,384]{3,2,1,0:T(8,128)(2,1)S(1)} %fusion.1), channel_id=1, source_target_pairs={{0,16},{8,24},{16,0},{24,8},{1,17},{9,25},{17,1},{25,9},{2,18},{10... | collective-permute-start | bytes 2211848 | tf_op jit(solution)/shard_map/ppermute | solution.py:946
  136.8 14.3 %collective-permute-start.43 = (bf16[2,192,768]{2,1,0:T(8,128)(2,1)S(1)}, bf16[2,192,768]{2,1,0:T(8,128)(2,1)S(1)}, u32[]{:S(2)}, u32[]{:S(2)}) collective-permute-start(bf16[2,192,768]{2,1,0:T(8,128)(2,1)S(1)} %get-tuple-element.328), channel_id=1, source_target_pairs={{0,1},{1,0},{2,3},{3,2},{4,5},{5,4},{6,7},{7,6},{8,9},{9,8},{10,11... | collective-permute-start | bytes 1769480 | tf_op jit(solution)/shard_map/ppermute | solution.py:958
  154.0 15.1 %collective-permute-start.47 = (bf16[192,768]{1,0:T(8,128)(2,1)S(1)}, bf16[192,768]{1,0:T(8,128)(2,1)S(1)}, u32[]{:S(2)}, u32[]{:S(2)}) collective-permute-start(bf16[192,768]{1,0:T(8,128)(2,1)S(1)} %fusion.17), channel_id=1, source_target_pairs={{0,6},{1,7},{2,0},{3,1},{4,2},{5,3},{6,4},{7,5},{8,14},{9,15},{10,... | collective-permute-start | bytes 884744 | tf_op jit(solution)/shard_map/ppermute | solution.py:962
  156.7 12.4 %collective-permute-start.45 = (bf16[2,4,80,384]{3,2,1,0:T(8,128)(2,1)S(1)}, bf16[2,4,80,384]{3,2,1,0:T(8,128)(2,1)S(1)}, u32[]{:S(2)}, u32[]{:S(2)}) collective-permute-start(bf16[2,4,80,384]{3,2,1,0:T(8,128)(2,1)S(1)} %fusion), channel_id=1, source_target_pairs={{0,16},{8,24},{16,0},{24,8},{1,17},{9,25},{17,1},{25,9},{2,18},{10... | collective-permute-start | bytes 1474568 | tf_op jit(solution)/shard_map/ppermute | solution.py:946
  157.7 11.4 %collective-permute-start.46 = (bf16[4,120,384]{2,1,0:T(8,128)(2,1)S(1)}, bf16[4,120,384]{2,1,0:T(8,128)(2,1)S(1)}, u32[]{:S(2)}, u32[]{:S(2)}) collective-permute-start(bf16[4,120,384]{2,1,0:T(8,128)(2,1)S(1)} %fusion.2), channel_id=1, source_target_pairs={{0,1},{1,0},{2,3},{3,2},{4,5},{5,4},{6,7},{7,6},{8,9},{9,8},{10,11... | collective-permute-start | bytes 1105928 | tf_op jit(solution)/shard_map/ppermute | solution.py:958
  158.3 9.5 %collective-permute-start.48 = (bf16[96,768]{1,0:T(8,128)(2,1)S(1)}, bf16[96,768]{1,0:T(8,128)(2,1)S(1)}, u32[]{:S(2)}, u32[]{:S(2)}) collective-permute-start(bf16[96,768]{1,0:T(8,128)(2,1)S(1)} %get-tuple-element.377), channel_id=1, source_target_pairs={{0,2},{1,3},{2,4},{3,5},{4,6},{5,7},{6,0},{7,1},{8,10},{9,11},{10,... | collective-permute-start | bytes 442376 | tf_op jit(solution)/shard_map/ppermute | solution.py:962
  158.6 10.5 %collective-permute-start.49 = (bf16[96,768]{1,0:T(8,128)(2,1)S(1)}, bf16[96,768]{1,0:T(8,128)(2,1)S(1)}, u32[]{:S(2)}, u32[]{:S(2)}) collective-permute-start(bf16[96,768]{1,0:T(8,128)(2,1)S(1)} %get-tuple-element.376), channel_id=1, source_target_pairs={{0,6},{1,7},{2,0},{3,1},{4,2},{5,3},{6,4},{7,5},{8,14},{9,15},{10,... | collective-permute-start | bytes 442376 | tf_op jit(solution)/shard_map/ppermute | solution.py:962
  178.8 14.9 %collective-permute-start.55 = (bf16[384,768]{1,0:T(8,128)(2,1)S(1)}, bf16[384,768]{1,0:T(8,128)(2,1)S(1)}, u32[]{:S(2)}, u32[]{:S(2)}) collective-permute-start(bf16[384,768]{1,0:T(8,128)(2,1)S(1)} %pad_maximum_fusion.2), channel_id=1, source_target_pairs={{0,16},{8,24},{16,0},{24,8},{1,17},{9,25},{17,1},{25,9},{2,18},{10... | collective-permute-start | bytes 1769480 | tf_op jit(solution)/shard_map/ppermute | solution.py:946
  182.5 11.2 %collective-permute-start.53 = (bf16[200,384]{1,0:T(8,128)(2,1)S(1)}, bf16[200,384]{1,0:T(8,128)(2,1)S(1)}, u32[]{:S(2)}, u32[]{:S(2)}) collective-permute-start(bf16[200,384]{1,0:T(8,128)(2,1)S(1)} %pad_maximum_fusion.6), channel_id=1, source_target_pairs={{0,4},{1,5},{2,6},{3,7},{4,0},{5,1},{6,2},{7,3},{8,12},{9,13},{10,... | collective-permute-start | bytes 460808 | tf_op jit(solution)/shard_map/ppermute | solution.py:962
  182.6 11.1 %collective-permute-start.52 = (bf16[200,384]{1,0:T(8,128)(2,1)S(1)}, bf16[200,384]{1,0:T(8,128)(2,1)S(1)}, u32[]{:S(2)}, u32[]{:S(2)}) collective-permute-start(bf16[200,384]{1,0:T(8,128)(2,1)S(1)} %pad_maximum_fusion.5), channel_id=1, source_target_pairs={{0,2},{1,3},{2,4},{3,5},{4,6},{5,7},{6,0},{7,1},{8,10},{9,11},{10,... | collective-permute-start | bytes 460808 | tf_op jit(solution)/shard_map/ppermute | solution.py:962
  (37 other events, 269.4 us)

commit v11 on v10

--- a/solution.py
+++ b/solution.py
@@ -623,7 +623,7 @@
 
 
 def near_kernel(
-    h_own, h_c, dy_own, dy_c, upb, y2, _wu, _wd,
+    h_own, h_c, dy_own, dy_c, upb, y2u, y2d, _wu, _wd,
     h2, dy, act_out, du_out, keep_out, send_out, wu_out, wd_out,
     sems,
 ):
@@ -632,8 +632,8 @@
     rows = width // 8
     copies = Copies(sems)
     at = pl.ds(pl.multiple_of(piece_shard(5, y, z) * rows, 16), rows)
-    copies.add(y2.at[pl.ds(0, rows), :], wu_out.at[at, :])
-    copies.add(y2.at[pl.ds(rows, rows), :], wd_out.at[at, :])
+    copies.add(y2u, wu_out.at[at, :])
+    copies.add(y2d, wd_out.at[at, :])
     h2[pl.ds(0, tok), :] = h_own[...]
     h2[pl.ds(tok, tok), :] = h_c[...]
     dy[pl.ds(0, tok), :] = dy_own[...]
@@ -1083,21 +1083,23 @@
         vmem=4,
         moved=5 * 10**6,
     )(piece_f, f1, f2, f3u, f3d, f_y0, f_y13)
-    h_x, h_c, f_y2, *w_half = fence(to_x(hidden_2), to_core(hidden_2), to_y(f2), *w_half)
+    h_x, h_c, f_y2u, f_y2d, *w_half = fence(
+        to_x(hidden_2), to_core(hidden_2), to_y(f2[:96]), to_z(f_y13[96:192], 1), *w_half
+    )
     act = shape_of((2 * tok, width), bf)
     acts = shape_of((4 * tok, width), bf)
     feed_shapes = [shape_of((tok, width), fl), shape_of((tok, width), bf)]
     *near_acts, keep_a, send_a, w_up, w_down = call(
         near_kernel,
-        [VM] * 5 + [AN] + [VM] * 2,
+        [VM] * 5 + [AN] * 2 + [VM] * 2,
         [VM] * 8,
         [act] * 4 + feed_shapes + [shape_of((width, width), bf)] * 2,
         [dma((2,))],
         flops=3 * 10**9,
         vmem=8,
         moved=6 * 10**6,
-        aliases={6: 6, 7: 7},
-    )(hidden_2, h_c, grad_y, dy_c, upb, f_y2, *w_half)
+        aliases={7: 6, 8: 7},
+    )(hidden_2, h_c, grad_y, dy_c, upb, f_y2u, f_y2d, *w_half)
     h_xc = to_core(h_x)
     keep_a, send_a, h_xc, w_up = fence(keep_a, send_a, h_xc, w_up)
     came_a = to_core(send_a)

time: 203 us -> 201 us (level)
  waiting for transfers between devices: 72.7 us -> 68.1 us
  starting transfers between devices: 62.4 us -> 65 us
    ppermute x30, waiting for transfers between devices: 11.9 us -> 8.69 us  [swap_rep(): return lax.ppermute(value, 'rep', [(k, k ^ bit) for k in range(4)])]
    ppermute x20 -> x21, starting transfers between devices: 35.5 us -> 36.8 us  [to_z(): lax.ppermute(value, 'seq', [(k, (k + 2 * steps) % 8) for k in range(8)])]
    ppermute x20 -> x21, waiting for transfers between devices: 49.6 us -> 50.1 us  [to_z(): lax.ppermute(value, 'seq', [(k, (k + 2 * steps) % 8) for k in range(8)])]
  transfers between devices with their start and end apart: 61 -> 62, of which waited for: 23 -> 23; matrix products, arithmetic and copies ran while one was open for 1% -> 1% of each run, Pallas kernels for 31% -> 31%
where the time goes in v11:
time: 201 us
  waiting for transfers between devices  68.1 us (34%)
  starting transfers between devices  65 us (32%)
  Pallas kernels  63.3 us (31%)
  other arithmetic  3.03 us (2%)
    ppermute x21, waiting for transfers between devices, to_z(): lax.ppermute(value, 'seq', [(k, (k + 2 * steps) % 8) for k in range(8)])  50.1 us
    ppermute x21, starting transfers between devices, to_z(): lax.ppermute(value, 'seq', [(k, (k + 2 * steps) % 8) for k in range(8)])  36.8 us
    ppermute x30, starting transfers between devices, swap_rep(): return lax.ppermute(value, 'rep', [(k, k ^ bit) for k in range(4)])  16.3 us
    pallas_call x1, Pallas kernels, on_device_fast(): call(front_kernel, [VM] * 6 + [AN] * 15, [VM] * 11, [shape_of((tok, width...  13.9 us
    ppermute x11, starting transfers between devices, to_y(): return lax.ppermute(value, 'seq', [(k, k ^ 1) for k in range(8)])  12 us
    pallas_call x1, Pallas kernels, on_device_fast(): call(back_b_kernel, [VM] * 14 + [AN] * 13, [VM] * 6, [shape_of((tok, widt...  10.8 us
    pallas_call x1, Pallas kernels, on_device_fast(): call(back_a_kernel, [VM] * 7, [AN] * 2 + [VM] * 2, [shape_of((2, 2, 4, 12...  10.2 us
    ppermute x11, waiting for transfers between devices, to_y(): return lax.ppermute(value, 'seq', [(k, k ^ 1) for k in range(8)])  9.31 us
  transfers between devices with their start and end apart: 62, of which 23 were waited for; matrix products, arithmetic and copies ran while one was open for 1% of the time, Pallas kernels for 31%

profile of v11, /device:TPU:0, one launch (start us, length us, event | category | flops | bytes accessed | tf_op | source)
XLA Modules:
  0.0 200.8 jit_solution(4725254299296103755)
XLA Ops:
  0.6 3.0 %collective-permute-start.3 = (bf16[192,768]{1,0:T(8,128)(2,1)}, bf16[192,768]{1,0:T(8,128)(2,1)S(1)}, u32[]{:S(2)}, u32[]{:S(2)}) collective-permute-start(bf16[192,768]{1,0:T(8,128)(2,1)} %bitcast.218), channel_id=1, source_target_pairs={{0,16},{8,24},{16,0},{24,8},{1,17},{9,25},{17,1},{25,9},{2,18},{10... | collective-permute-start | bytes 884744 | tf_op jit(solution)/shard_map/ppermute | solution.py:946
  3.6 2.7 %shard_map.186 = (bf16[200,768]{1,0:T(8,128)(2,1)}, bf16[48,1664]{1,0:T(8,128)(2,1)}, bf16[192,768]{1,0:T(8,128)(2,1)}, bf16[96,768]{1,0:T(8,128)(2,1)}, bf16[96,768]{1,0:T(8,128)(2,1)}) custom-call(bf16[1,192,768]{2,1,0:T(8,128)(2,1)} %tokens.1, s32[1,192]{1,0:T(1,128)} %segs.1, bf16[96,2304]{1,0:T(8,128)(2,1)} %own.3, bf16[96,768]{1,0:T(8,128)(2,1)} %own_o.1, ...), custom_call_target="tpu_custom_call" | custom-call | bytes 4000000 | tf_op jit(solution)/shard_map/pallas_call | solution.py:990
  8.0 2.2 %collective-permute-start.1 = (bf16[48,1664]{1,0:T(8,128)(2,1)}, bf16[48,1664]{1,0:T(8,128)(2,1)S(1)}, u32[]{:S(2)}, u32[]{:S(2)}) collective-permute-start(bf16[48,1664]{1,0:T(8,128)(2,1)} %get-tuple-element.192.first), channel_id=1, source_target_pairs={{0,6},{1,7},{2,0},{3,1},{4,2},{5,3},{6,4},{7,5},{8,14},{9,15},{10,... | collective-permute-start | bytes 479240 | tf_op jit(solution)/shard_map/ppermute | solution.py:962
  11.8 3.7 %collective-permute-done = bf16[48,1664]{1,0:T(8,128)(2,1)S(1)} collective-permute-done((bf16[48,1664]{1,0:T(8,128)(2,1)}, bf16[48,1664]{1,0:T(8,128)(2,1)S(1)}, u32[]{:S(2)}, u32[]{:S(2)}) %collective-permute-start) | collective-permute-done | bytes 159776 | tf_op jit(solution)/shard_map/ppermute | solution.py:962
  20.9 10.0 %collective-permute-done.4 = bf16[48,1664]{1,0:T(8,128)(2,1)S(1)} collective-permute-done((bf16[48,1664]{1,0:T(8,128)(2,1)S(1)}, bf16[48,1664]{1,0:T(8,128)(2,1)S(1)}, u32[]{:S(2)}, u32[]{:S(2)}) %collective-permute-start.4) | collective-permute-done | bytes 159776 | tf_op jit(solution)/shard_map/ppermute | solution.py:962
  33.1 3.8 %collective-permute-start.11 = (bf16[96,768]{1,0:T(8,128)(2,1)}, bf16[96,768]{1,0:T(8,128)(2,1)S(1)}, u32[]{:S(2)}, u32[]{:S(2)}) collective-permute-start(bf16[96,768]{1,0:T(8,128)(2,1)} %get-tuple-element.208), channel_id=1, source_target_pairs={{0,6},{1,7},{2,0},{3,1},{4,2},{5,3},{6,4},{7,5},{8,14},{9,15},{10,... | collective-permute-start | bytes 442376 | tf_op jit(solution)/shard_map/ppermute | solution.py:962
  36.9 7.0 %collective-permute-done.11.z3d = bf16[96,768]{1,0:T(8,128)(2,1)S(1)} collective-permute-done((bf16[96,768]{1,0:T(8,128)(2,1)}, bf16[96,768]{1,0:T(8,128)(2,1)S(1)}, u32[]{:S(2)}, u32[]{:S(2)}) %collective-permute-start.11) | collective-permute-done | bytes 147488 | tf_op jit(solution)/shard_map/ppermute | solution.py:962
  46.5 3.5 %collective-permute-start.15 = (bf16[96,768]{1,0:T(8,128)(2,1)S(1)}, bf16[96,768]{1,0:T(8,128)(2,1)S(1)}, u32[]{:S(2)}, u32[]{:S(2)}) collective-permute-start(bf16[96,768]{1,0:T(8,128)(2,1)S(1)} %copy-done.7), channel_id=1, source_target_pairs={{0,6},{1,7},{2,0},{3,1},{4,2},{5,3},{6,4},{7,5},{8,14},{9,15},{10,... | collective-permute-start | bytes 442376 | tf_op jit(solution)/shard_map/ppermute | solution.py:962
  50.0 4.9 %collective-permute-done.15.z3u = bf16[96,768]{1,0:T(8,128)(2,1)S(1)} collective-permute-done((bf16[96,768]{1,0:T(8,128)(2,1)S(1)}, bf16[96,768]{1,0:T(8,128)(2,1)S(1)}, u32[]{:S(2)}, u32[]{:S(2)}) %collective-permute-start.15) | collective-permute-done | bytes 147488 | tf_op jit(solution)/shard_map/ppermute | solution.py:962
  58.6 2.6 %collective-permute-done.20 = bf16[48,1664]{1,0:T(8,128)(2,1)S(1)} collective-permute-done((bf16[48,1664]{1,0:T(8,128)(2,1)S(1)}, bf16[48,1664]{1,0:T(8,128)(2,1)S(1)}, u32[]{:S(2)}, u32[]{:S(2)}) %collective-permute-start.20) | collective-permute-done | bytes 159776 | tf_op jit(solution)/shard_map/ppermute | solution.py:946
  63.8 13.9 %shard_map.187 = (bf16[192,768]{1,0:T(8,128)(2,1)S(1)}, bf16[960,1536]{1,0:T(8,128)(2,1)S(1)}, bf16[960,768]{1,0:T(8,128)(2,1)S(1)}, bf16[192,768]{1,0:T(8,128)(...) custom-call(s32[1,384]{1,0:T(1,128)S(1)} %pad_add_fusion.seg, ...), custom_call_target="tpu_custom_call" | custom-call | flops 7000000000 | bytes 12000000 | tf_op jit(solution)/shard_map/pallas_call | solution.py:1046
  79.9 2.1 %collective-permute-start.29 = (bf16[96,768]{1,0:T(8,128)(2,1)S(1)}, bf16[96,768]{1,0:T(8,128)(2,1)S(1)}, u32[]{:S(2)}, u32[]{:S(2)}) collective-permute-start(bf16[96,768]{1,0:T(8,128)(2,1)S(1)} %slice.252), channel_id=1, source_target_pairs={{0,2},{1,3},{2,4},{3,5},{4,6},{5,7},{6,0},{7,1},{8,10},{9,11},{10,... | collective-permute-start | bytes 442376 | tf_op jit(solution)/shard_map/ppermute | solution.py:962
  82.0 2.9 %shard_map.188 = (bf16[768,768]{1,0:T(8,128)(2,1)S(1)}, bf16[768,768]{1,0:T(8,128)(2,1)S(1)}) custom-call(bf16[192,768]{1,0:T(8,128)(2,1)S(1)} %copy-done.2, bf16[192,768]{1,0:T(8,128)(2,1)S(1)} %collective-permute-done.14.z1, bf16[192,768]{1,0:T(8,128)(2,1)S(1)} %collective-permute-done.23.z2, bf16[96,768]{1,0:T(8,128)(2,1)S(1)} %collective-permute-done.15.z3u, ...), custom_call_target="tpu_custom_call" | custom-call | bytes 5000000 | tf_op jit(solution)/shard_map/pallas_call | solution.py:1077
  84.9 3.0 %collective-permute-done.29.y2d = bf16[96,768]{1,0:T(8,128)(2,1)S(1)} collective-permute-done((bf16[96,768]{1,0:T(8,128)(2,1)S(1)}, bf16[96,768]{1,0:T(8,128)(2,1)S(1)}, u32[]{:S(2)}, u32[]{:S(2)}) %collective-permute-start.29) | collective-permute-done | bytes 147488 | tf_op jit(solution)/shard_map/ppermute | solution.py:962
  87.9 2.3 %shard_map.189 = (bf16[384,768]{1,0:T(8,128)(2,1)S(1)}, bf16[384,768]{1,0:T(8,128)(2,1)S(1)}, bf16[384,768]{1,0:T(8,128)(2,1)S(1)}, bf16[384,768]{1,0:T(8,128)(2...) custom-call(bf16[192,768]{1,0:T(8,128)(2,1)S(1)} %get-tuple-element., ...), custom_call_target="tpu_custom_call", output_to_operand_aliasing={{6}: (7, {}), {7}: (8, {})} | custom-call | flops 3000000000 | bytes 6000000 | tf_op jit(solution)/shard_map/pallas_call | solution.py:1092
  95.8 7.0 %shard_map.192 = (bf16[2,4,96,768]{3,2,1,0:T(8,128)(2,1)S(1)}, bf16[2,4,96,768]{3,2,1,0:T(8,128)(2,1)S(1)}, f32[1,768]{1,0:T(1,128)S(1)}, f32[2,192,768]{2,1,0:T(8,128)S(1)}, bf16[2,192,768]{2,1,0:T(8,128)(2,1)S(1)}) custom-call(bf16[768,768]{1,0:T(8,128)(2,1)S(1)} %get-tuple-element.287.hs, bf16[768,768]{1,0:T(8,128)(2,1)S(1)} %get-tuple-element.288.dys, ...), custom_call_target="tpu_custom_call" | custom-call | flops 3000000000 | bytes 6000000 | tf_op jit(solution)/shard_map/pallas_call | solution.py:1130
  105.4 10.2 %shard_map.194 = (bf16[2,2,4,120,384]{4,3,2,1,0:T(8,128)(2,1)S(1)}, bf16[2,2,4,120,384]{4,3,2,1,0:T(8,128)(2,1)S(1)}, bf16[192,384]{1,0:T(8,128)(2,1)S(1)}, bf16[960,768]{1,0:T(8,128)(2,1)S(1)}) custom-call(s32[1,384]{1,0:T(1,128)S(1)} %get-tuple-element.292.start_in, bf16[192,768]{1,0:T(8,128)(2,1)S(1)} %get-tuple-element.293.q_in, ...), custom_call_target="tpu_custom_call" | custom-call | flops 5000000000 | bytes 10000000 | tf_op jit(solution)/shard_map/pallas_call | solution.py:1166
  115.6 2.4 %collective-permute-done.34 = bf16[4,96,768]{2,1,0:T(8,128)(2,1)S(1)} collective-permute-done((bf16[4,96,768]{2,1,0:T(8,128)(2,1)S(1)}, bf16[4,96,768]{2,1,0:T(8,128)(2,1)S(1)}, u32[]{:S(2)}, u32[]{:S(2)}) %collective-permute-start.34) | collective-permute-done | bytes 589856 | tf_op jit(solution)/shard_map/ppermute | solution.py:958
  122.7 10.8 %shard_map.195 = (bf16[192,384]{1,0:T(8,128)(2,1)S(1)}, bf16[960,768]{1,0:T(8,128)(2,1)S(1)}, f32[192,768]{1,0:T(8,128)S(1)}, bf16[2,192,768]{2,1,0:T(8,128)(2,1...) custom-call(s32[1,384]{1,0:T(1,128)S(1)} %get-tuple-element.292.start_in, ...), custom_call_target="tpu_custom_call" | custom-call | flops 6000000000 | bytes 10000000 | tf_op jit(solution)/shard_map/pallas_call | solution.py:1193
  136.7 4.8 %shard_map.196 = (bf16[2,2,4,80,384]{4,3,2,1,0:T(8,128)(2,1)S(1)}, bf16[2,2,4,80,384]{4,3,2,1,0:T(8,128)(2,1)S(1)}) custom-call(bf16[960,768]{1,0:T(8,128)(2,1)S(1)} %get-tuple-element.295.h_in, bf16[192,384]{1,0:T(8,128)(2,1)S(1)} %get-tuple-element.326.dq, bf16[960,768]{1,0:T(8,128)(2,1)S(1)} %get-tuple-element.327.dkv, ...), custom_call_target="tpu_custom_call" | custom-call | flops 3000000000 | bytes 6000000 | tf_op jit(solution)/shard_map/pallas_call | solution.py:1218
  142.3 2.4 %collective-permute-start.45 = (bf16[96,768]{1,0:T(8,128)(2,1)S(1)}, bf16[96,768]{1,0:T(8,128)(2,1)S(1)}, u32[]{:S(2)}, u32[]{:S(2)}) collective-permute-start(bf16[96,768]{1,0:T(8,128)(2,1)S(1)} %fusion.25), channel_id=1, source_target_pairs={{0,2},{1,3},{2,4},{3,5},{4,6},{5,7},{6,0},{7,1},{8,10},{9,11},{10,... | collective-permute-start | bytes 442376 | tf_op jit(solution)/shard_map/ppermute | solution.py:962
  144.7 5.2 %collective-permute-done.45 = bf16[96,768]{1,0:T(8,128)(2,1)S(1)} collective-permute-done((bf16[96,768]{1,0:T(8,128)(2,1)S(1)}, bf16[96,768]{1,0:T(8,128)(2,1)S(1)}, u32[]{:S(2)}, u32[]{:S(2)}) %collective-permute-start.45) | collective-permute-done | bytes 147488 | tf_op jit(solution)/shard_map/ppermute | solution.py:962
  152.3 2.3 %collective-permute-start.48 = (bf16[192,768]{1,0:T(8,128)(2,1)S(1)}, bf16[192,768]{1,0:T(8,128)(2,1)S(1)}, u32[]{:S(2)}, u32[]{:S(2)}) collective-permute-start(bf16[192,768]{1,0:T(8,128)(2,1)S(1)} %fusion.17), channel_id=1, source_target_pairs={{0,6},{1,7},{2,0},{3,1},{4,2},{5,3},{6,4},{7,5},{8,14},{9,15},{10,... | collective-permute-start | bytes 884744 | tf_op jit(solution)/shard_map/ppermute | solution.py:962
  157.6 3.5 %collective-permute-start.50 = (bf16[96,768]{1,0:T(8,128)(2,1)S(1)}, bf16[96,768]{1,0:T(8,128)(2,1)S(1)}, u32[]{:S(2)}, u32[]{:S(2)}) collective-permute-start(bf16[96,768]{1,0:T(8,128)(2,1)S(1)} %get-tuple-element.378), channel_id=1, source_target_pairs={{0,6},{1,7},{2,0},{3,1},{4,2},{5,3},{6,4},{7,5},{8,14},{9,15},{10,... | collective-permute-start | bytes 442376 | tf_op jit(solution)/shard_map/ppermute | solution.py:962
  161.2 4.3 %collective-permute-done.49 = bf16[96,768]{1,0:T(8,128)(2,1)S(1)} collective-permute-done((bf16[96,768]{1,0:T(8,128)(2,1)S(1)}, bf16[96,768]{1,0:T(8,128)(2,1)S(1)}, u32[]{:S(2)}, u32[]{:S(2)}) %collective-permute-start.49) | collective-permute-done | bytes 147488 | tf_op jit(solution)/shard_map/ppermute | solution.py:962
  166.6 4.0 %collective-permute-start.52 = (bf16[192,768]{1,0:T(8,128)(2,1)S(1)}, bf16[192,768]{1,0:T(8,128)(2,1)S(1)}, u32[]{:S(2)}, u32[]{:S(2)}) collective-permute-start(bf16[192,768]{1,0:T(8,128)(2,1)S(1)} %get-tuple-element.388), channel_id=1, source_target_pairs={{0,6},{1,7},{2,0},{3,1},{4,2},{5,3},{6,4},{7,5},{8,14},{9,15},{10,... | collective-permute-start | bytes 884744 | tf_op jit(solution)/shard_map/ppermute | solution.py:962
  172.5 4.4 %collective-permute-done.51 = bf16[4,80,384]{2,1,0:T(8,128)(2,1)S(1)} collective-permute-done((bf16[4,80,384]{2,1,0:T(8,128)(2,1)S(1)}, bf16[4,80,384]{2,1,0:T(8,128)(2,1)S(1)}, u32[]{:S(2)}, u32[]{:S(2)}) %collective-permute-start.51) | collective-permute-done | bytes 245792 | tf_op jit(solution)/shard_map/ppermute | solution.py:958
  178.6 2.7 %collective-permute-start.55 = (bf16[200,384]{1,0:T(8,128)(2,1)S(1)}, bf16[200,384]{1,0:T(8,128)(2,1)S(1)}, u32[]{:S(2)}, u32[]{:S(2)}) collective-permute-start(bf16[200,384]{1,0:T(8,128)(2,1)S(1)} %pad_maximum_fusion.7), channel_id=1, source_target_pairs={{0,6},{1,7},{2,0},{3,1},{4,2},{5,3},{6,4},{7,5},{8,14},{9,15},{10,... | collective-permute-start | bytes 460808 | tf_op jit(solution)/shard_map/ppermute | solution.py:962
  182.1 4.4 %collective-permute-done.55 = bf16[200,384]{1,0:T(8,128)(2,1)S(1)} collective-permute-done((bf16[200,384]{1,0:T(8,128)(2,1)S(1)}, bf16[200,384]{1,0:T(8,128)(2,1)S(1)}, u32[]{:S(2)}, u32[]{:S(2)}) %collective-permute-start.55) | collective-permute-done | bytes 153632 | tf_op jit(solution)/shard_map/ppermute | solution.py:962
  186.6 5.1 %collective-permute-done.54 = bf16[200,384]{1,0:T(8,128)(2,1)S(1)} collective-permute-done((bf16[200,384]{1,0:T(8,128)(2,1)S(1)}, bf16[200,384]{1,0:T(8,128)(2,1)S(1)}, u32[]{:S(2)}, u32[]{:S(2)}) %collective-permute-start.54) | collective-permute-done | bytes 153632 | tf_op jit(solution)/shard_map/ppermute | solution.py:962
  193.9 2.0 shard_map.198
  195.9 2.5 %collective-permute-done.57.fx = bf16[200,384]{1,0:T(8,128)(2,1)S(1)} collective-permute-done((bf16[200,384]{1,0:T(8,128)(2,1)S(1)}, bf16[200,384]{1,0:T(8,128)(2,1)S(1)}, u32[]{:S(2)}, u32[]{:S(2)}) %collective-permute-start.57) | collective-permute-done | bytes 153632 | tf_op jit(solution)/shard_map/ppermute | solution.py:946
  (157 shorter events, 53.9 us)
Async XLA Ops:
  0.6 16.3 %collective-permute-start.3 = (bf16[192,768]{1,0:T(8,128)(2,1)}, bf16[192,768]{1,0:T(8,128)(2,1)S(1)}, u32[]{:S(2)}, u32[]{:S(2)}) collective-permute-start(bf16[192,768]{1,0:T(8,128)(2,1)} %bitcast.218), channel_id=1, source_target_pairs={{0,16},{8,24},{16,0},{24,8},{1,17},{9,25},{17,1},{25,9},{2,18},{10... | collective-permute-start | bytes 884744 | tf_op jit(solution)/shard_map/ppermute | solution.py:946
  16.9 14.0 %collective-permute-start.5 = (bf16[200,768]{1,0:T(8,128)(2,1)}, bf16[200,768]{1,0:T(8,128)(2,1)S(1)}, u32[]{:S(2)}, u32[]{:S(2)}) collective-permute-start(bf16[200,768]{1,0:T(8,128)(2,1)} %get-tuple-element.197.xo), channel_id=1, source_target_pairs={{0,2},{1,3},{2,4},{3,5},{4,6},{5,7},{6,0},{7,1},{8,10},{9,11},{10,... | collective-permute-start | bytes 921608 | tf_op jit(solution)/shard_map/ppermute | solution.py:962
  18.1 12.9 %collective-permute-start.7 = (bf16[192,768]{1,0:T(8,128)(2,1)}, bf16[192,768]{1,0:T(8,128)(2,1)S(1)}, u32[]{:S(2)}, u32[]{:S(2)}) collective-permute-start(bf16[192,768]{1,0:T(8,128)(2,1)} %get-tuple-element.216.own), channel_id=1, source_target_pairs={{0,1},{1,0},{2,3},{3,2},{4,5},{5,4},{6,7},{7,6},{8,9},{9,8},{10,11... | collective-permute-start | bytes 884744 | tf_op jit(solution)/shard_map/ppermute | solution.py:958
  19.6 11.3 %collective-permute-start.4 = (bf16[48,1664]{1,0:T(8,128)(2,1)S(1)}, bf16[48,1664]{1,0:T(8,128)(2,1)S(1)}, u32[]{:S(2)}, u32[]{:S(2)}) collective-permute-start(bf16[48,1664]{1,0:T(8,128)(2,1)S(1)} %collective-permute-done), channel_id=1, source_target_pairs={{0,2},{1,3},{2,4},{3,5},{4,6},{5,7},{6,0},{7,1},{8,10},{9,11},{10,... | collective-permute-start | bytes 479240 | tf_op jit(solution)/shard_map/ppermute | solution.py:962
  20.4 10.6 %collective-permute-start.6 = (bf16[48,1664]{1,0:T(8,128)(2,1)S(1)}, bf16[48,1664]{1,0:T(8,128)(2,1)S(1)}, u32[]{:S(2)}, u32[]{:S(2)}) collective-permute-start(bf16[48,1664]{1,0:T(8,128)(2,1)S(1)} %collective-permute-done.2), channel_id=1, source_target_pairs={{0,16},{8,24},{16,0},{24,8},{1,17},{9,25},{17,1},{25,9},{2,18},{10... | collective-permute-start | bytes 479240 | tf_op jit(solution)/shard_map/ppermute | solution.py:946
  31.0 13.0 %collective-permute-start.8 = (bf16[144,1664]{1,0:T(8,128)(2,1)S(1)}, bf16[144,1664]{1,0:T(8,128)(2,1)S(1)}, u32[]{:S(2)}, u32[]{:S(2)}) collective-permute-start(bf16[144,1664]{1,0:T(8,128)(2,1)S(1)} %pad_maximum_fusion.3), channel_id=1, source_target_pairs={{0,1},{1,0},{2,3},{3,2},{4,5},{5,4},{6,7},{7,6},{8,9},{9,8},{10,11... | collective-permute-start | bytes 1437704 | tf_op jit(solution)/shard_map/ppermute | solution.py:958
  32.6 11.4 %collective-permute-start.9 = (bf16[144,1664]{1,0:T(8,128)(2,1)S(1)}, bf16[144,1664]{1,0:T(8,128)(2,1)S(1)}, u32[]{:S(2)}, u32[]{:S(2)}) collective-permute-start(bf16[144,1664]{1,0:T(8,128)(2,1)S(1)} %pad_maximum_fusion.3), channel_id=1, source_target_pairs={{0,16},{8,24},{16,0},{24,8},{1,17},{9,25},{17,1},{25,9},{2,18},{10... | collective-permute-start | bytes 1437704 | tf_op jit(solution)/shard_map/ppermute | solution.py:946
  33.1 10.9 %collective-permute-start.10 = (bf16[200,768]{1,0:T(8,128)(2,1)S(1)}, bf16[200,768]{1,0:T(8,128)(2,1)S(1)}, u32[]{:S(2)}, u32[]{:S(2)}) collective-permute-start(bf16[200,768]{1,0:T(8,128)(2,1)S(1)} %collective-permute-done.5.x2), channel_id=1, source_target_pairs={{0,2},{1,3},{2,4},{3,5},{4,6},{5,7},{6,0},{7,1},{8,10},{9,11},{10,... | collective-permute-start | bytes 921608 | tf_op jit(solution)/shard_map/ppermute | solution.py:962
  33.1 10.8 %collective-permute-start.11 = (bf16[96,768]{1,0:T(8,128)(2,1)}, bf16[96,768]{1,0:T(8,128)(2,1)S(1)}, u32[]{:S(2)}, u32[]{:S(2)}) collective-permute-start(bf16[96,768]{1,0:T(8,128)(2,1)} %get-tuple-element.208), channel_id=1, source_target_pairs={{0,6},{1,7},{2,0},{3,1},{4,2},{5,3},{6,4},{7,5},{8,14},{9,15},{10,... | collective-permute-start | bytes 442376 | tf_op jit(solution)/shard_map/ppermute | solution.py:962
  44.1 12.7 %collective-permute-start.12 = (bf16[2,200,768]{2,1,0:T(8,128)(2,1)S(1)}, bf16[2,200,768]{2,1,0:T(8,128)(2,1)S(1)}, u32[]{:S(2)}, u32[]{:S(2)}) collective-permute-start(bf16[2,200,768]{2,1,0:T(8,128)(2,1)S(1)} %pad_maximum_fusion), channel_id=1, source_target_pairs={{0,1},{1,0},{2,3},{3,2},{4,5},{5,4},{6,7},{7,6},{8,9},{9,8},{10,11... | collective-permute-start | bytes 1843208 | tf_op jit(solution)/shard_map/ppermute | solution.py:958
  44.7 10.2 %collective-permute-start.13 = (bf16[144,1664]{1,0:T(8,128)(2,1)S(1)}, bf16[144,1664]{1,0:T(8,128)(2,1)S(1)}, u32[]{:S(2)}, u32[]{:S(2)}) collective-permute-start(bf16[144,1664]{1,0:T(8,128)(2,1)S(1)} %collective-permute-done.8), channel_id=1, source_target_pairs={{0,16},{8,24},{16,0},{24,8},{1,17},{9,25},{17,1},{25,9},{2,18},{10... | collective-permute-start | bytes 1437704 | tf_op jit(solution)/shard_map/ppermute | solution.py:946
  61.2 16.5 %collective-permute-start.24 = (bf16[192,768]{1,0:T(8,128)(2,1)S(1)}, bf16[192,768]{1,0:T(8,128)(2,1)S(1)}, u32[]{:S(2)}, u32[]{:S(2)}) collective-permute-start(bf16[192,768]{1,0:T(8,128)(2,1)S(1)} %bitcast.219), channel_id=1, source_target_pairs={{0,8},{8,0},{16,24},{24,16},{1,9},{9,1},{17,25},{25,17},{2,10},{10... | collective-permute-start | bytes 884744 | tf_op jit(solution)/shard_map/ppermute | solution.py:946
  61.5 16.2 %collective-permute-start.25 = (bf16[192,768]{1,0:T(8,128)(2,1)S(1)}, bf16[192,768]{1,0:T(8,128)(2,1)S(1)}, u32[]{:S(2)}, u32[]{:S(2)}) collective-permute-start(bf16[192,768]{1,0:T(8,128)(2,1)S(1)} %collective-permute-done.3.dy_x), channel_id=1, source_target_pairs={{0,8},{8,0},{16,24},{24,16},{1,9},{9,1},{17,25},{25,17},{2,10},{10... | collective-permute-start | bytes 884744 | tf_op jit(solution)/shard_map/ppermute | solution.py:946
  61.7 16.0 %collective-permute-start.22 = (bf16[384,768]{1,0:T(8,128)(2,1)S(1)}, bf16[384,768]{1,0:T(8,128)(2,1)S(1)}, u32[]{:S(2)}, u32[]{:S(2)}) collective-permute-start(bf16[384,768]{1,0:T(8,128)(2,1)S(1)} %pad_maximum_fusion.1), channel_id=1, source_target_pairs={{0,1},{1,0},{2,3},{3,2},{4,5},{5,4},{6,7},{7,6},{8,9},{9,8},{10,11... | collective-permute-start | bytes 1769480 | tf_op jit(solution)/shard_map/ppermute | solution.py:958
  62.3 15.4 %collective-permute-start.23 = (bf16[192,768]{1,0:T(8,128)(2,1)S(1)}, bf16[192,768]{1,0:T(8,128)(2,1)S(1)}, u32[]{:S(2)}, u32[]{:S(2)}) collective-permute-start(bf16[192,768]{1,0:T(8,128)(2,1)S(1)} %collective-permute-done.14.z1), channel_id=1, source_target_pairs={{0,2},{1,3},{2,4},{3,5},{4,6},{5,7},{6,0},{7,1},{8,10},{9,11},{10,... | collective-permute-start | bytes 884744 | tf_op jit(solution)/shard_map/ppermute | solution.py:962
  77.7 10.2 %collective-permute-start.26 = (bf16[192,768]{1,0:T(8,128)(2,1)S(1)}, bf16[192,768]{1,0:T(8,128)(2,1)S(1)}, u32[]{:S(2)}, u32[]{:S(2)}) collective-permute-start(bf16[192,768]{1,0:T(8,128)(2,1)S(1)} %get-tuple-element.250.h_own), channel_id=1, source_target_pairs={{0,16},{8,24},{16,0},{24,8},{1,17},{9,25},{17,1},{25,9},{2,18},{10... | collective-permute-start | bytes 884744 | tf_op jit(solution)/shard_map/ppermute | solution.py:946
  103.4 14.6 %collective-permute-start.34 = (bf16[4,96,768]{2,1,0:T(8,128)(2,1)S(1)}, bf16[4,96,768]{2,1,0:T(8,128)(2,1)S(1)}, u32[]{:S(2)}, u32[]{:S(2)}) collective-permute-start(bf16[4,96,768]{2,1,0:T(8,128)(2,1)S(1)} %slice_bitcast_fusion.1), channel_id=1, source_target_pairs={{0,1},{1,0},{2,3},{3,2},{4,5},{5,4},{6,7},{7,6},{8,9},{9,8},{10,11... | collective-permute-start | bytes 1769480 | tf_op jit(solution)/shard_map/ppermute | solution.py:958
  104.0 14.0 %collective-permute-start.35 = (bf16[2,192,768]{2,1,0:T(8,128)(2,1)S(1)}, bf16[2,192,768]{2,1,0:T(8,128)(2,1)S(1)}, u32[]{:S(2)}, u32[]{:S(2)}) collective-permute-start(bf16[2,192,768]{2,1,0:T(8,128)(2,1)S(1)} %get-tuple-element.312), channel_id=1, source_target_pairs={{0,8},{8,0},{16,24},{24,16},{1,9},{9,1},{17,25},{25,17},{2,10},{10... | collective-permute-start | bytes 1769480 | tf_op jit(solution)/shard_map/ppermute | solution.py:946
  118.1 15.7 %collective-permute-start.36 = (bf16[2,2,4,120,384]{4,3,2,1,0:T(8,128)(2,1)S(1)}, bf16[2,2,4,120,384]{4,3,2,1,0:T(8,128)(2,1)S(1)}, u32[]{:S(2)}, u32[]{:S(2)}) collective-permute-start(bf16[2,2,4,120,384]{4,3,2,1,0:T(8,128)(2,1)S(1)} %get-tuple-element.321), channel_id=1, source_target_pairs={{0,8},{8,0},{16,24},{24,16},{1,9},{9,1},{17,25},{25,17},{2,10},{10... | collective-permute-start | bytes 4423688 | tf_op jit(solution)/shard_map/ppermute | solution.py:946
  118.1 15.7 %collective-permute-start.37 = (bf16[4,96,768]{2,1,0:T(8,128)(2,1)S(1)}, bf16[4,96,768]{2,1,0:T(8,128)(2,1)S(1)}, u32[]{:S(2)}, u32[]{:S(2)}) collective-permute-start(bf16[4,96,768]{2,1,0:T(8,128)(2,1)S(1)} %slice_bitcast_fusion), channel_id=1, source_target_pairs={{0,1},{1,0},{2,3},{3,2},{4,5},{5,4},{6,7},{7,6},{8,9},{9,8},{10,11... | collective-permute-start | bytes 1769480 | tf_op jit(solution)/shard_map/ppermute | solution.py:958
  118.8 14.8 %collective-permute-start.38 = (bf16[96,768]{1,0:T(8,128)(2,1)S(1)}, bf16[96,768]{1,0:T(8,128)(2,1)S(1)}, u32[]{:S(2)}, u32[]{:S(2)}) collective-permute-start(bf16[96,768]{1,0:T(8,128)(2,1)S(1)} %get-tuple-element.382), channel_id=1, source_target_pairs={{0,2},{1,3},{2,4},{3,5},{4,6},{5,7},{6,0},{7,1},{8,10},{9,11},{10,... | collective-permute-start | bytes 442376 | tf_op jit(solution)/shard_map/ppermute | solution.py:962
  119.3 14.2 %collective-permute-start.39 = (bf16[96,768]{1,0:T(8,128)(2,1)S(1)}, bf16[96,768]{1,0:T(8,128)(2,1)S(1)}, u32[]{:S(2)}, u32[]{:S(2)}) collective-permute-start(bf16[96,768]{1,0:T(8,128)(2,1)S(1)} %get-tuple-element.381), channel_id=1, source_target_pairs={{0,4},{1,5},{2,6},{3,7},{4,0},{5,1},{6,2},{7,3},{8,12},{9,13},{10,... | collective-permute-start | bytes 442376 | tf_op jit(solution)/shard_map/ppermute | solution.py:962
  121.2 12.3 %collective-permute-start.40 = (bf16[96,768]{1,0:T(8,128)(2,1)S(1)}, bf16[96,768]{1,0:T(8,128)(2,1)S(1)}, u32[]{:S(2)}, u32[]{:S(2)}) collective-permute-start(bf16[96,768]{1,0:T(8,128)(2,1)S(1)} %get-tuple-element.380), channel_id=1, source_target_pairs={{0,6},{1,7},{2,0},{3,1},{4,2},{5,3},{6,4},{7,5},{8,14},{9,15},{10,... | collective-permute-start | bytes 442376 | tf_op jit(solution)/shard_map/ppermute | solution.py:962
  134.0 18.2 %collective-permute-start.43 = (bf16[2,4,120,384]{3,2,1,0:T(8,128)(2,1)S(1)}, bf16[2,4,120,384]{3,2,1,0:T(8,128)(2,1)S(1)}, u32[]{:S(2)}, u32[]{:S(2)}) collective-permute-start(bf16[2,4,120,384]{3,2,1,0:T(8,128)(2,1)S(1)} %fusion.1), channel_id=1, source_target_pairs={{0,16},{8,24},{16,0},{24,8},{1,17},{9,25},{17,1},{25,9},{2,18},{10... | collective-permute-start | bytes 2211848 | tf_op jit(solution)/shard_map/ppermute | solution.py:946
  135.6 14.7 %collective-permute-start.44 = (bf16[2,192,768]{2,1,0:T(8,128)(2,1)S(1)}, bf16[2,192,768]{2,1,0:T(8,128)(2,1)S(1)}, u32[]{:S(2)}, u32[]{:S(2)}) collective-permute-start(bf16[2,192,768]{2,1,0:T(8,128)(2,1)S(1)} %get-tuple-element.330), channel_id=1, source_target_pairs={{0,1},{1,0},{2,3},{3,2},{4,5},{5,4},{6,7},{7,6},{8,9},{9,8},{10,11... | collective-permute-start | bytes 1769480 | tf_op jit(solution)/shard_map/ppermute | solution.py:958
  152.3 14.1 %collective-permute-start.48 = (bf16[192,768]{1,0:T(8,128)(2,1)S(1)}, bf16[192,768]{1,0:T(8,128)(2,1)S(1)}, u32[]{:S(2)}, u32[]{:S(2)}) collective-permute-start(bf16[192,768]{1,0:T(8,128)(2,1)S(1)} %fusion.17), channel_id=1, source_target_pairs={{0,6},{1,7},{2,0},{3,1},{4,2},{5,3},{6,4},{7,5},{8,14},{9,15},{10,... | collective-permute-start | bytes 884744 | tf_op jit(solution)/shard_map/ppermute | solution.py:962
  154.7 11.7 %collective-permute-start.46 = (bf16[2,4,80,384]{3,2,1,0:T(8,128)(2,1)S(1)}, bf16[2,4,80,384]{3,2,1,0:T(8,128)(2,1)S(1)}, u32[]{:S(2)}, u32[]{:S(2)}) collective-permute-start(bf16[2,4,80,384]{3,2,1,0:T(8,128)(2,1)S(1)} %fusion), channel_id=1, source_target_pairs={{0,16},{8,24},{16,0},{24,8},{1,17},{9,25},{17,1},{25,9},{2,18},{10... | collective-permute-start | bytes 1474568 | tf_op jit(solution)/shard_map/ppermute | solution.py:946
  156.4 10.0 %collective-permute-start.47 = (bf16[4,120,384]{2,1,0:T(8,128)(2,1)S(1)}, bf16[4,120,384]{2,1,0:T(8,128)(2,1)S(1)}, u32[]{:S(2)}, u32[]{:S(2)}) collective-permute-start(bf16[4,120,384]{2,1,0:T(8,128)(2,1)S(1)} %fusion.2), channel_id=1, source_target_pairs={{0,1},{1,0},{2,3},{3,2},{4,5},{5,4},{6,7},{7,6},{8,9},{9,8},{10,11... | collective-permute-start | bytes 1105928 | tf_op jit(solution)/shard_map/ppermute | solution.py:958
  166.6 10.3 %collective-permute-start.52 = (bf16[192,768]{1,0:T(8,128)(2,1)S(1)}, bf16[192,768]{1,0:T(8,128)(2,1)S(1)}, u32[]{:S(2)}, u32[]{:S(2)}) collective-permute-start(bf16[192,768]{1,0:T(8,128)(2,1)S(1)} %get-tuple-element.388), channel_id=1, source_target_pairs={{0,6},{1,7},{2,0},{3,1},{4,2},{5,3},{6,4},{7,5},{8,14},{9,15},{10,... | collective-permute-start | bytes 884744 | tf_op jit(solution)/shard_map/ppermute | solution.py:962
  176.9 14.7 %collective-permute-start.56 = (bf16[384,768]{1,0:T(8,128)(2,1)S(1)}, bf16[384,768]{1,0:T(8,128)(2,1)S(1)}, u32[]{:S(2)}, u32[]{:S(2)}) collective-permute-start(bf16[384,768]{1,0:T(8,128)(2,1)S(1)} %pad_maximum_fusion.2), channel_id=1, source_target_pairs={{0,16},{8,24},{16,0},{24,8},{1,17},{9,25},{17,1},{25,9},{2,18},{10... | collective-permute-start | bytes 1769480 | tf_op jit(solution)/shard_map/ppermute | solution.py:946
  181.4 10.3 %collective-permute-start.54 = (bf16[200,384]{1,0:T(8,128)(2,1)S(1)}, bf16[200,384]{1,0:T(8,128)(2,1)S(1)}, u32[]{:S(2)}, u32[]{:S(2)}) collective-permute-start(bf16[200,384]{1,0:T(8,128)(2,1)S(1)} %pad_maximum_fusion.6), channel_id=1, source_target_pairs={{0,4},{1,5},{2,6},{3,7},{4,0},{5,1},{6,2},{7,3},{8,12},{9,13},{10,... | collective-permute-start | bytes 460808 | tf_op jit(solution)/shard_map/ppermute | solution.py:962
  181.5 10.2 %collective-permute-start.53 = (bf16[200,384]{1,0:T(8,128)(2,1)S(1)}, bf16[200,384]{1,0:T(8,128)(2,1)S(1)}, u32[]{:S(2)}, u32[]{:S(2)}) collective-permute-start(bf16[200,384]{1,0:T(8,128)(2,1)S(1)} %pad_maximum_fusion.5), channel_id=1, source_target_pairs={{0,2},{1,3},{2,4},{3,5},{4,6},{5,7},{6,0},{7,1},{8,10},{9,11},{10,... | collective-permute-start | bytes 460808 | tf_op jit(solution)/shard_map/ppermute | solution.py:962
  (38 other events, 274.0 us)

commit v12 on v11

--- a/solution.py
+++ b/solution.py
@@ -574,7 +574,7 @@
         lse_out[number] = top + jnp.log(total)
         return carry
 
-    lax.fori_loop(0, width // 128, pair, 0)
+    lax.fori_loop(0, width // 128, pair, 0, unroll=2)
     residual = f32(xo[pl.ds(0, tok), :]) + dot_nn(a_out[...], wo_out[...]) + vec[6:7]
     r_out[...] = residual
     hat, _rate = norm_parts(residual)

time: 201 us -> 200 us (level)
  transfers between devices with their start and end apart: 62 -> 62, of which waited for: 23 -> 25; matrix products, arithmetic and copies ran while one was open for 1% -> 1% of each run, Pallas kernels for 31% -> 31%
where the time goes in v12:
time: 200 us
  waiting for transfers between devices  68.8 us (34%)
  starting transfers between devices  64.5 us (32%)
  Pallas kernels  62.1 us (31%)
  other arithmetic  3.03 us (2%)
    ppermute x21, waiting for transfers between devices, to_z(): lax.ppermute(value, 'seq', [(k, (k + 2 * steps) % 8) for k in range(8)])  50 us
    ppermute x21, starting transfers between devices, to_z(): lax.ppermute(value, 'seq', [(k, (k + 2 * steps) % 8) for k in range(8)])  36.9 us
    ppermute x30, starting transfers between devices, swap_rep(): return lax.ppermute(value, 'rep', [(k, k ^ bit) for k in range(4)])  15 us
    pallas_call x1, Pallas kernels, on_device_fast(): call(front_kernel, [VM] * 6 + [AN] * 15, [VM] * 11, [shape_of((tok, width...  12.7 us
    ppermute x11, starting transfers between devices, to_y(): return lax.ppermute(value, 'seq', [(k, k ^ 1) for k in range(8)])  12.6 us
    pallas_call x1, Pallas kernels, on_device_fast(): call(back_b_kernel, [VM] * 14 + [AN] * 13, [VM] * 6, [shape_of((tok, widt...  10.8 us
    ppermute x11, waiting for transfers between devices, to_y(): return lax.ppermute(value, 'seq', [(k, k ^ 1) for k in range(8)])  10.6 us
    pallas_call x1, Pallas kernels, on_device_fast(): call(back_a_kernel, [VM] * 7, [AN] * 2 + [VM] * 2, [shape_of((2, 2, 4, 12...  10.3 us
  transfers between devices with their start and end apart: 62, of which 25 were waited for; matrix products, arithmetic and copies ran while one was open for 1% of the time, Pallas kernels for 31%

profile of v12, /device:TPU:0, one launch (start us, length us, event | category | flops | bytes accessed | tf_op | source)
XLA Modules:
  0.0 199.9 jit_solution(10932347048752951902)
XLA Ops:
  0.6 3.0 %collective-permute-start.3 = (bf16[192,768]{1,0:T(8,128)(2,1)}, bf16[192,768]{1,0:T(8,128)(2,1)S(1)}, u32[]{:S(2)}, u32[]{:S(2)}) collective-permute-start(bf16[192,768]{1,0:T(8,128)(2,1)} %bitcast.218), channel_id=1, source_target_pairs={{0,16},{8,24},{16,0},{24,8},{1,17},{9,25},{17,1},{25,9},{2,18},{10... | collective-permute-start | bytes 884744 | tf_op jit(solution)/shard_map/ppermute | solution.py:946
  3.6 2.7 %shard_map.186 = (bf16[200,768]{1,0:T(8,128)(2,1)}, bf16[48,1664]{1,0:T(8,128)(2,1)}, bf16[192,768]{1,0:T(8,128)(2,1)}, bf16[96,768]{1,0:T(8,128)(2,1)}, bf16[96,768]{1,0:T(8,128)(2,1)}) custom-call(bf16[1,192,768]{2,1,0:T(8,128)(2,1)} %tokens.1, s32[1,192]{1,0:T(1,128)} %segs.1, bf16[96,2304]{1,0:T(8,128)(2,1)} %own.3, bf16[96,768]{1,0:T(8,128)(2,1)} %own_o.1, ...), custom_call_target="tpu_custom_call" | custom-call | bytes 4000000 | tf_op jit(solution)/shard_map/pallas_call | solution.py:990
  8.0 2.2 %collective-permute-start.1 = (bf16[48,1664]{1,0:T(8,128)(2,1)}, bf16[48,1664]{1,0:T(8,128)(2,1)S(1)}, u32[]{:S(2)}, u32[]{:S(2)}) collective-permute-start(bf16[48,1664]{1,0:T(8,128)(2,1)} %get-tuple-element.192.first), channel_id=1, source_target_pairs={{0,6},{1,7},{2,0},{3,1},{4,2},{5,3},{6,4},{7,5},{8,14},{9,15},{10,... | collective-permute-start | bytes 479240 | tf_op jit(solution)/shard_map/ppermute | solution.py:962
  11.8 3.7 %collective-permute-done = bf16[48,1664]{1,0:T(8,128)(2,1)S(1)} collective-permute-done((bf16[48,1664]{1,0:T(8,128)(2,1)}, bf16[48,1664]{1,0:T(8,128)(2,1)S(1)}, u32[]{:S(2)}, u32[]{:S(2)}) %collective-permute-start) | collective-permute-done | bytes 159776 | tf_op jit(solution)/shard_map/ppermute | solution.py:962
  20.9 10.0 %collective-permute-done.4 = bf16[48,1664]{1,0:T(8,128)(2,1)S(1)} collective-permute-done((bf16[48,1664]{1,0:T(8,128)(2,1)S(1)}, bf16[48,1664]{1,0:T(8,128)(2,1)S(1)}, u32[]{:S(2)}, u32[]{:S(2)}) %collective-permute-start.4) | collective-permute-done | bytes 159776 | tf_op jit(solution)/shard_map/ppermute | solution.py:962
  33.1 3.8 %collective-permute-start.11 = (bf16[96,768]{1,0:T(8,128)(2,1)}, bf16[96,768]{1,0:T(8,128)(2,1)S(1)}, u32[]{:S(2)}, u32[]{:S(2)}) collective-permute-start(bf16[96,768]{1,0:T(8,128)(2,1)} %get-tuple-element.208), channel_id=1, source_target_pairs={{0,6},{1,7},{2,0},{3,1},{4,2},{5,3},{6,4},{7,5},{8,14},{9,15},{10,... | collective-permute-start | bytes 442376 | tf_op jit(solution)/shard_map/ppermute | solution.py:962
  36.9 7.0 %collective-permute-done.11.z3d = bf16[96,768]{1,0:T(8,128)(2,1)S(1)} collective-permute-done((bf16[96,768]{1,0:T(8,128)(2,1)}, bf16[96,768]{1,0:T(8,128)(2,1)S(1)}, u32[]{:S(2)}, u32[]{:S(2)}) %collective-permute-start.11) | collective-permute-done | bytes 147488 | tf_op jit(solution)/shard_map/ppermute | solution.py:962
  46.5 3.5 %collective-permute-start.15 = (bf16[96,768]{1,0:T(8,128)(2,1)S(1)}, bf16[96,768]{1,0:T(8,128)(2,1)S(1)}, u32[]{:S(2)}, u32[]{:S(2)}) collective-permute-start(bf16[96,768]{1,0:T(8,128)(2,1)S(1)} %copy-done.7), channel_id=1, source_target_pairs={{0,6},{1,7},{2,0},{3,1},{4,2},{5,3},{6,4},{7,5},{8,14},{9,15},{10,... | collective-permute-start | bytes 442376 | tf_op jit(solution)/shard_map/ppermute | solution.py:962
  50.0 4.9 %collective-permute-done.15.z3u = bf16[96,768]{1,0:T(8,128)(2,1)S(1)} collective-permute-done((bf16[96,768]{1,0:T(8,128)(2,1)S(1)}, bf16[96,768]{1,0:T(8,128)(2,1)S(1)}, u32[]{:S(2)}, u32[]{:S(2)}) %collective-permute-start.15) | collective-permute-done | bytes 147488 | tf_op jit(solution)/shard_map/ppermute | solution.py:962
  58.6 2.6 %collective-permute-done.20 = bf16[48,1664]{1,0:T(8,128)(2,1)S(1)} collective-permute-done((bf16[48,1664]{1,0:T(8,128)(2,1)S(1)}, bf16[48,1664]{1,0:T(8,128)(2,1)S(1)}, u32[]{:S(2)}, u32[]{:S(2)}) %collective-permute-start.20) | collective-permute-done | bytes 159776 | tf_op jit(solution)/shard_map/ppermute | solution.py:946
  63.8 12.7 %shard_map.187 = (bf16[192,768]{1,0:T(8,128)(2,1)S(1)}, bf16[960,1536]{1,0:T(8,128)(2,1)S(1)}, bf16[960,768]{1,0:T(8,128)(2,1)S(1)}, bf16[192,768]{1,0:T(8,128)(...) custom-call(s32[1,384]{1,0:T(1,128)S(1)} %pad_add_fusion.seg, ...), custom_call_target="tpu_custom_call" | custom-call | flops 7000000000 | bytes 12000000 | tf_op jit(solution)/shard_map/pallas_call | solution.py:1046
  78.7 2.1 %collective-permute-start.29 = (bf16[96,768]{1,0:T(8,128)(2,1)S(1)}, bf16[96,768]{1,0:T(8,128)(2,1)S(1)}, u32[]{:S(2)}, u32[]{:S(2)}) collective-permute-start(bf16[96,768]{1,0:T(8,128)(2,1)S(1)} %slice.252), channel_id=1, source_target_pairs={{0,2},{1,3},{2,4},{3,5},{4,6},{5,7},{6,0},{7,1},{8,10},{9,11},{10,... | collective-permute-start | bytes 442376 | tf_op jit(solution)/shard_map/ppermute | solution.py:962
  80.8 2.9 %shard_map.188 = (bf16[768,768]{1,0:T(8,128)(2,1)S(1)}, bf16[768,768]{1,0:T(8,128)(2,1)S(1)}) custom-call(bf16[192,768]{1,0:T(8,128)(2,1)S(1)} %copy-done.2, bf16[192,768]{1,0:T(8,128)(2,1)S(1)} %collective-permute-done.14.z1, bf16[192,768]{1,0:T(8,128)(2,1)S(1)} %collective-permute-done.23.z2, bf16[96,768]{1,0:T(8,128)(2,1)S(1)} %collective-permute-done.15.z3u, ...), custom_call_target="tpu_custom_call" | custom-call | bytes 5000000 | tf_op jit(solution)/shard_map/pallas_call | solution.py:1077
  84.4 2.3 %collective-permute-done.29.y2d = bf16[96,768]{1,0:T(8,128)(2,1)S(1)} collective-permute-done((bf16[96,768]{1,0:T(8,128)(2,1)S(1)}, bf16[96,768]{1,0:T(8,128)(2,1)S(1)}, u32[]{:S(2)}, u32[]{:S(2)}) %collective-permute-start.29) | collective-permute-done | bytes 147488 | tf_op jit(solution)/shard_map/ppermute | solution.py:962
  86.7 2.3 %shard_map.189 = (bf16[384,768]{1,0:T(8,128)(2,1)S(1)}, bf16[384,768]{1,0:T(8,128)(2,1)S(1)}, bf16[384,768]{1,0:T(8,128)(2,1)S(1)}, bf16[384,768]{1,0:T(8,128)(2...) custom-call(bf16[192,768]{1,0:T(8,128)(2,1)S(1)} %get-tuple-element., ...), custom_call_target="tpu_custom_call", output_to_operand_aliasing={{6}: (7, {}), {7}: (8, {})} | custom-call | flops 3000000000 | bytes 6000000 | tf_op jit(solution)/shard_map/pallas_call | solution.py:1092
  94.6 7.0 %shard_map.192 = (bf16[2,4,96,768]{3,2,1,0:T(8,128)(2,1)S(1)}, bf16[2,4,96,768]{3,2,1,0:T(8,128)(2,1)S(1)}, f32[1,768]{1,0:T(1,128)S(1)}, f32[2,192,768]{2,1,0:T(8,128)S(1)}, bf16[2,192,768]{2,1,0:T(8,128)(2,1)S(1)}) custom-call(bf16[768,768]{1,0:T(8,128)(2,1)S(1)} %get-tuple-element.287.hs, bf16[768,768]{1,0:T(8,128)(2,1)S(1)} %get-tuple-element.288.dys, ...), custom_call_target="tpu_custom_call" | custom-call | flops 3000000000 | bytes 6000000 | tf_op jit(solution)/shard_map/pallas_call | solution.py:1130
  105.1 10.3 %shard_map.194 = (bf16[2,2,4,120,384]{4,3,2,1,0:T(8,128)(2,1)S(1)}, bf16[2,2,4,120,384]{4,3,2,1,0:T(8,128)(2,1)S(1)}, bf16[192,384]{1,0:T(8,128)(2,1)S(1)}, bf16[960,768]{1,0:T(8,128)(2,1)S(1)}) custom-call(s32[1,384]{1,0:T(1,128)S(1)} %get-tuple-element.292.start_in, bf16[192,768]{1,0:T(8,128)(2,1)S(1)} %get-tuple-element.293.q_in, ...), custom_call_target="tpu_custom_call" | custom-call | flops 5000000000 | bytes 10000000 | tf_op jit(solution)/shard_map/pallas_call | solution.py:1166
  120.4 2.0 collective-permute-start.40
  122.4 10.8 %shard_map.195 = (bf16[192,384]{1,0:T(8,128)(2,1)S(1)}, bf16[960,768]{1,0:T(8,128)(2,1)S(1)}, f32[192,768]{1,0:T(8,128)S(1)}, bf16[2,192,768]{2,1,0:T(8,128)(2,1...) custom-call(s32[1,384]{1,0:T(1,128)S(1)} %get-tuple-element.292.start_in, ...), custom_call_target="tpu_custom_call" | custom-call | flops 6000000000 | bytes 10000000 | tf_op jit(solution)/shard_map/pallas_call | solution.py:1193
  135.6 4.8 %shard_map.196 = (bf16[2,2,4,80,384]{4,3,2,1,0:T(8,128)(2,1)S(1)}, bf16[2,2,4,80,384]{4,3,2,1,0:T(8,128)(2,1)S(1)}) custom-call(bf16[960,768]{1,0:T(8,128)(2,1)S(1)} %get-tuple-element.295.h_in, bf16[192,384]{1,0:T(8,128)(2,1)S(1)} %get-tuple-element.326.dq, bf16[960,768]{1,0:T(8,128)(2,1)S(1)} %get-tuple-element.327.dkv, ...), custom_call_target="tpu_custom_call" | custom-call | flops 3000000000 | bytes 6000000 | tf_op jit(solution)/shard_map/pallas_call | solution.py:1218
  141.2 2.3 %collective-permute-start.45 = (bf16[96,768]{1,0:T(8,128)(2,1)S(1)}, bf16[96,768]{1,0:T(8,128)(2,1)S(1)}, u32[]{:S(2)}, u32[]{:S(2)}) collective-permute-start(bf16[96,768]{1,0:T(8,128)(2,1)S(1)} %fusion.25), channel_id=1, source_target_pairs={{0,2},{1,3},{2,4},{3,5},{4,6},{5,7},{6,0},{7,1},{8,10},{9,11},{10,... | collective-permute-start | bytes 442376 | tf_op jit(solution)/shard_map/ppermute | solution.py:962
  143.6 5.3 %collective-permute-done.45 = bf16[96,768]{1,0:T(8,128)(2,1)S(1)} collective-permute-done((bf16[96,768]{1,0:T(8,128)(2,1)S(1)}, bf16[96,768]{1,0:T(8,128)(2,1)S(1)}, u32[]{:S(2)}, u32[]{:S(2)}) %collective-permute-start.45) | collective-permute-done | bytes 147488 | tf_op jit(solution)/shard_map/ppermute | solution.py:962
  149.4 2.2 %collective-permute-done.43 = bf16[2,4,120,384]{3,2,1,0:T(8,128)(2,1)S(1)} collective-permute-done((bf16[2,4,120,384]{3,2,1,0:T(8,128)(2,1)S(1)}, bf16[2,4,120,384]{3,2,1,0:T(8,128)(2,1)S(1)}, u32[]{:S(2)}, u32[]{:S(2)}) %collective-permute-start.43) | collective-permute-done | bytes 737312 | tf_op jit(solution)/shard_map/ppermute | solution.py:946
  151.7 2.4 %collective-permute-start.48 = (bf16[192,768]{1,0:T(8,128)(2,1)S(1)}, bf16[192,768]{1,0:T(8,128)(2,1)S(1)}, u32[]{:S(2)}, u32[]{:S(2)}) collective-permute-start(bf16[192,768]{1,0:T(8,128)(2,1)S(1)} %fusion.17), channel_id=1, source_target_pairs={{0,6},{1,7},{2,0},{3,1},{4,2},{5,3},{6,4},{7,5},{8,14},{9,15},{10,... | collective-permute-start | bytes 884744 | tf_op jit(solution)/shard_map/ppermute | solution.py:962
  156.8 3.8 %collective-permute-start.50 = (bf16[96,768]{1,0:T(8,128)(2,1)S(1)}, bf16[96,768]{1,0:T(8,128)(2,1)S(1)}, u32[]{:S(2)}, u32[]{:S(2)}) collective-permute-start(bf16[96,768]{1,0:T(8,128)(2,1)S(1)} %get-tuple-element.378), channel_id=1, source_target_pairs={{0,6},{1,7},{2,0},{3,1},{4,2},{5,3},{6,4},{7,5},{8,14},{9,15},{10,... | collective-permute-start | bytes 442376 | tf_op jit(solution)/shard_map/ppermute | solution.py:962
  160.7 4.4 %collective-permute-done.49 = bf16[96,768]{1,0:T(8,128)(2,1)S(1)} collective-permute-done((bf16[96,768]{1,0:T(8,128)(2,1)S(1)}, bf16[96,768]{1,0:T(8,128)(2,1)S(1)}, u32[]{:S(2)}, u32[]{:S(2)}) %collective-permute-start.49) | collective-permute-done | bytes 147488 | tf_op jit(solution)/shard_map/ppermute | solution.py:962
  166.1 4.1 %collective-permute-start.52 = (bf16[192,768]{1,0:T(8,128)(2,1)S(1)}, bf16[192,768]{1,0:T(8,128)(2,1)S(1)}, u32[]{:S(2)}, u32[]{:S(2)}) collective-permute-start(bf16[192,768]{1,0:T(8,128)(2,1)S(1)} %get-tuple-element.388), channel_id=1, source_target_pairs={{0,6},{1,7},{2,0},{3,1},{4,2},{5,3},{6,4},{7,5},{8,14},{9,15},{10,... | collective-permute-start | bytes 884744 | tf_op jit(solution)/shard_map/ppermute | solution.py:962
  171.4 5.2 %collective-permute-done.51 = bf16[4,80,384]{2,1,0:T(8,128)(2,1)S(1)} collective-permute-done((bf16[4,80,384]{2,1,0:T(8,128)(2,1)S(1)}, bf16[4,80,384]{2,1,0:T(8,128)(2,1)S(1)}, u32[]{:S(2)}, u32[]{:S(2)}) %collective-permute-start.51) | collective-permute-done | bytes 245792 | tf_op jit(solution)/shard_map/ppermute | solution.py:958
  177.1 2.7 %collective-permute-start.55 = (bf16[200,384]{1,0:T(8,128)(2,1)S(1)}, bf16[200,384]{1,0:T(8,128)(2,1)S(1)}, u32[]{:S(2)}, u32[]{:S(2)}) collective-permute-start(bf16[200,384]{1,0:T(8,128)(2,1)S(1)} %pad_maximum_fusion.7), channel_id=1, source_target_pairs={{0,6},{1,7},{2,0},{3,1},{4,2},{5,3},{6,4},{7,5},{8,14},{9,15},{10,... | collective-permute-start | bytes 460808 | tf_op jit(solution)/shard_map/ppermute | solution.py:962
  180.6 4.3 %collective-permute-done.55 = bf16[200,384]{1,0:T(8,128)(2,1)S(1)} collective-permute-done((bf16[200,384]{1,0:T(8,128)(2,1)S(1)}, bf16[200,384]{1,0:T(8,128)(2,1)S(1)}, u32[]{:S(2)}, u32[]{:S(2)}) %collective-permute-start.55) | collective-permute-done | bytes 153632 | tf_op jit(solution)/shard_map/ppermute | solution.py:962
  184.9 5.9 %collective-permute-done.54 = bf16[200,384]{1,0:T(8,128)(2,1)S(1)} collective-permute-done((bf16[200,384]{1,0:T(8,128)(2,1)S(1)}, bf16[200,384]{1,0:T(8,128)(2,1)S(1)}, u32[]{:S(2)}, u32[]{:S(2)}) %collective-permute-start.54) | collective-permute-done | bytes 153632 | tf_op jit(solution)/shard_map/ppermute | solution.py:962
  193.8 2.0 shard_map.198
  (157 shorter events, 53.6 us)
Async XLA Ops:
  0.6 16.3 %collective-permute-start.3 = (bf16[192,768]{1,0:T(8,128)(2,1)}, bf16[192,768]{1,0:T(8,128)(2,1)S(1)}, u32[]{:S(2)}, u32[]{:S(2)}) collective-permute-start(bf16[192,768]{1,0:T(8,128)(2,1)} %bitcast.218), channel_id=1, source_target_pairs={{0,16},{8,24},{16,0},{24,8},{1,17},{9,25},{17,1},{25,9},{2,18},{10... | collective-permute-start | bytes 884744 | tf_op jit(solution)/shard_map/ppermute | solution.py:946
  16.9 14.0 %collective-permute-start.5 = (bf16[200,768]{1,0:T(8,128)(2,1)}, bf16[200,768]{1,0:T(8,128)(2,1)S(1)}, u32[]{:S(2)}, u32[]{:S(2)}) collective-permute-start(bf16[200,768]{1,0:T(8,128)(2,1)} %get-tuple-element.197.xo), channel_id=1, source_target_pairs={{0,2},{1,3},{2,4},{3,5},{4,6},{5,7},{6,0},{7,1},{8,10},{9,11},{10,... | collective-permute-start | bytes 921608 | tf_op jit(solution)/shard_map/ppermute | solution.py:962
  18.1 12.9 %collective-permute-start.7 = (bf16[192,768]{1,0:T(8,128)(2,1)}, bf16[192,768]{1,0:T(8,128)(2,1)S(1)}, u32[]{:S(2)}, u32[]{:S(2)}) collective-permute-start(bf16[192,768]{1,0:T(8,128)(2,1)} %get-tuple-element.216.own), channel_id=1, source_target_pairs={{0,1},{1,0},{2,3},{3,2},{4,5},{5,4},{6,7},{7,6},{8,9},{9,8},{10,11... | collective-permute-start | bytes 884744 | tf_op jit(solution)/shard_map/ppermute | solution.py:958
  19.6 11.3 %collective-permute-start.4 = (bf16[48,1664]{1,0:T(8,128)(2,1)S(1)}, bf16[48,1664]{1,0:T(8,128)(2,1)S(1)}, u32[]{:S(2)}, u32[]{:S(2)}) collective-permute-start(bf16[48,1664]{1,0:T(8,128)(2,1)S(1)} %collective-permute-done), channel_id=1, source_target_pairs={{0,2},{1,3},{2,4},{3,5},{4,6},{5,7},{6,0},{7,1},{8,10},{9,11},{10,... | collective-permute-start | bytes 479240 | tf_op jit(solution)/shard_map/ppermute | solution.py:962
  20.4 10.6 %collective-permute-start.6 = (bf16[48,1664]{1,0:T(8,128)(2,1)S(1)}, bf16[48,1664]{1,0:T(8,128)(2,1)S(1)}, u32[]{:S(2)}, u32[]{:S(2)}) collective-permute-start(bf16[48,1664]{1,0:T(8,128)(2,1)S(1)} %collective-permute-done.2), channel_id=1, source_target_pairs={{0,16},{8,24},{16,0},{24,8},{1,17},{9,25},{17,1},{25,9},{2,18},{10... | collective-permute-start | bytes 479240 | tf_op jit(solution)/shard_map/ppermute | solution.py:946
  31.0 13.0 %collective-permute-start.8 = (bf16[144,1664]{1,0:T(8,128)(2,1)S(1)}, bf16[144,1664]{1,0:T(8,128)(2,1)S(1)}, u32[]{:S(2)}, u32[]{:S(2)}) collective-permute-start(bf16[144,1664]{1,0:T(8,128)(2,1)S(1)} %pad_maximum_fusion.3), channel_id=1, source_target_pairs={{0,1},{1,0},{2,3},{3,2},{4,5},{5,4},{6,7},{7,6},{8,9},{9,8},{10,11... | collective-permute-start | bytes 1437704 | tf_op jit(solution)/shard_map/ppermute | solution.py:958
  32.6 11.4 %collective-permute-start.9 = (bf16[144,1664]{1,0:T(8,128)(2,1)S(1)}, bf16[144,1664]{1,0:T(8,128)(2,1)S(1)}, u32[]{:S(2)}, u32[]{:S(2)}) collective-permute-start(bf16[144,1664]{1,0:T(8,128)(2,1)S(1)} %pad_maximum_fusion.3), channel_id=1, source_target_pairs={{0,16},{8,24},{16,0},{24,8},{1,17},{9,25},{17,1},{25,9},{2,18},{10... | collective-permute-start | bytes 1437704 | tf_op jit(solution)/shard_map/ppermute | solution.py:946
  33.1 10.9 %collective-permute-start.10 = (bf16[200,768]{1,0:T(8,128)(2,1)S(1)}, bf16[200,768]{1,0:T(8,128)(2,1)S(1)}, u32[]{:S(2)}, u32[]{:S(2)}) collective-permute-start(bf16[200,768]{1,0:T(8,128)(2,1)S(1)} %collective-permute-done.5.x2), channel_id=1, source_target_pairs={{0,2},{1,3},{2,4},{3,5},{4,6},{5,7},{6,0},{7,1},{8,10},{9,11},{10,... | collective-permute-start | bytes 921608 | tf_op jit(solution)/shard_map/ppermute | solution.py:962
  33.1 10.8 %collective-permute-start.11 = (bf16[96,768]{1,0:T(8,128)(2,1)}, bf16[96,768]{1,0:T(8,128)(2,1)S(1)}, u32[]{:S(2)}, u32[]{:S(2)}) collective-permute-start(bf16[96,768]{1,0:T(8,128)(2,1)} %get-tuple-element.208), channel_id=1, source_target_pairs={{0,6},{1,7},{2,0},{3,1},{4,2},{5,3},{6,4},{7,5},{8,14},{9,15},{10,... | collective-permute-start | bytes 442376 | tf_op jit(solution)/shard_map/ppermute | solution.py:962
  44.1 12.7 %collective-permute-start.12 = (bf16[2,200,768]{2,1,0:T(8,128)(2,1)S(1)}, bf16[2,200,768]{2,1,0:T(8,128)(2,1)S(1)}, u32[]{:S(2)}, u32[]{:S(2)}) collective-permute-start(bf16[2,200,768]{2,1,0:T(8,128)(2,1)S(1)} %pad_maximum_fusion), channel_id=1, source_target_pairs={{0,1},{1,0},{2,3},{3,2},{4,5},{5,4},{6,7},{7,6},{8,9},{9,8},{10,11... | collective-permute-start | bytes 1843208 | tf_op jit(solution)/shard_map/ppermute | solution.py:958
  44.7 10.2 %collective-permute-start.13 = (bf16[144,1664]{1,0:T(8,128)(2,1)S(1)}, bf16[144,1664]{1,0:T(8,128)(2,1)S(1)}, u32[]{:S(2)}, u32[]{:S(2)}) collective-permute-start(bf16[144,1664]{1,0:T(8,128)(2,1)S(1)} %collective-permute-done.8), channel_id=1, source_target_pairs={{0,16},{8,24},{16,0},{24,8},{1,17},{9,25},{17,1},{25,9},{2,18},{10... | collective-permute-start | bytes 1437704 | tf_op jit(solution)/shard_map/ppermute | solution.py:946
  61.2 15.3 %collective-permute-start.24 = (bf16[192,768]{1,0:T(8,128)(2,1)S(1)}, bf16[192,768]{1,0:T(8,128)(2,1)S(1)}, u32[]{:S(2)}, u32[]{:S(2)}) collective-permute-start(bf16[192,768]{1,0:T(8,128)(2,1)S(1)} %bitcast.219), channel_id=1, source_target_pairs={{0,8},{8,0},{16,24},{24,16},{1,9},{9,1},{17,25},{25,17},{2,10},{10... | collective-permute-start | bytes 884744 | tf_op jit(solution)/shard_map/ppermute | solution.py:946
  61.5 15.0 %collective-permute-start.25 = (bf16[192,768]{1,0:T(8,128)(2,1)S(1)}, bf16[192,768]{1,0:T(8,128)(2,1)S(1)}, u32[]{:S(2)}, u32[]{:S(2)}) collective-permute-start(bf16[192,768]{1,0:T(8,128)(2,1)S(1)} %collective-permute-done.3.dy_x), channel_id=1, source_target_pairs={{0,8},{8,0},{16,24},{24,16},{1,9},{9,1},{17,25},{25,17},{2,10},{10... | collective-permute-start | bytes 884744 | tf_op jit(solution)/shard_map/ppermute | solution.py:946
  61.7 15.6 %collective-permute-start.22 = (bf16[384,768]{1,0:T(8,128)(2,1)S(1)}, bf16[384,768]{1,0:T(8,128)(2,1)S(1)}, u32[]{:S(2)}, u32[]{:S(2)}) collective-permute-start(bf16[384,768]{1,0:T(8,128)(2,1)S(1)} %pad_maximum_fusion.1), channel_id=1, source_target_pairs={{0,1},{1,0},{2,3},{3,2},{4,5},{5,4},{6,7},{7,6},{8,9},{9,8},{10,11... | collective-permute-start | bytes 1769480 | tf_op jit(solution)/shard_map/ppermute | solution.py:958
  62.3 14.2 %collective-permute-start.23 = (bf16[192,768]{1,0:T(8,128)(2,1)S(1)}, bf16[192,768]{1,0:T(8,128)(2,1)S(1)}, u32[]{:S(2)}, u32[]{:S(2)}) collective-permute-start(bf16[192,768]{1,0:T(8,128)(2,1)S(1)} %collective-permute-done.14.z1), channel_id=1, source_target_pairs={{0,2},{1,3},{2,4},{3,5},{4,6},{5,7},{6,0},{7,1},{8,10},{9,11},{10,... | collective-permute-start | bytes 884744 | tf_op jit(solution)/shard_map/ppermute | solution.py:962
  77.3 9.4 %collective-permute-start.26 = (bf16[192,768]{1,0:T(8,128)(2,1)S(1)}, bf16[192,768]{1,0:T(8,128)(2,1)S(1)}, u32[]{:S(2)}, u32[]{:S(2)}) collective-permute-start(bf16[192,768]{1,0:T(8,128)(2,1)S(1)} %get-tuple-element.250.h_own), channel_id=1, source_target_pairs={{0,16},{8,24},{16,0},{24,8},{1,17},{9,25},{17,1},{25,9},{2,18},{10... | collective-permute-start | bytes 884744 | tf_op jit(solution)/shard_map/ppermute | solution.py:946
  102.2 14.6 %collective-permute-start.34 = (bf16[4,96,768]{2,1,0:T(8,128)(2,1)S(1)}, bf16[4,96,768]{2,1,0:T(8,128)(2,1)S(1)}, u32[]{:S(2)}, u32[]{:S(2)}) collective-permute-start(bf16[4,96,768]{2,1,0:T(8,128)(2,1)S(1)} %slice_bitcast_fusion.1), channel_id=1, source_target_pairs={{0,1},{1,0},{2,3},{3,2},{4,5},{5,4},{6,7},{7,6},{8,9},{9,8},{10,11... | collective-permute-start | bytes 1769480 | tf_op jit(solution)/shard_map/ppermute | solution.py:958
  103.8 13.1 %collective-permute-start.35 = (bf16[2,192,768]{2,1,0:T(8,128)(2,1)S(1)}, bf16[2,192,768]{2,1,0:T(8,128)(2,1)S(1)}, u32[]{:S(2)}, u32[]{:S(2)}) collective-permute-start(bf16[2,192,768]{2,1,0:T(8,128)(2,1)S(1)} %get-tuple-element.312), channel_id=1, source_target_pairs={{0,8},{8,0},{16,24},{24,16},{1,9},{9,1},{17,25},{25,17},{2,10},{10... | collective-permute-start | bytes 1769480 | tf_op jit(solution)/shard_map/ppermute | solution.py:946
  116.9 16.4 %collective-permute-start.36 = (bf16[2,2,4,120,384]{4,3,2,1,0:T(8,128)(2,1)S(1)}, bf16[2,2,4,120,384]{4,3,2,1,0:T(8,128)(2,1)S(1)}, u32[]{:S(2)}, u32[]{:S(2)}) collective-permute-start(bf16[2,2,4,120,384]{4,3,2,1,0:T(8,128)(2,1)S(1)} %get-tuple-element.321), channel_id=1, source_target_pairs={{0,8},{8,0},{16,24},{24,16},{1,9},{9,1},{17,25},{25,17},{2,10},{10... | collective-permute-start | bytes 4423688 | tf_op jit(solution)/shard_map/ppermute | solution.py:946
  116.9 16.4 %collective-permute-start.37 = (bf16[4,96,768]{2,1,0:T(8,128)(2,1)S(1)}, bf16[4,96,768]{2,1,0:T(8,128)(2,1)S(1)}, u32[]{:S(2)}, u32[]{:S(2)}) collective-permute-start(bf16[4,96,768]{2,1,0:T(8,128)(2,1)S(1)} %slice_bitcast_fusion), channel_id=1, source_target_pairs={{0,1},{1,0},{2,3},{3,2},{4,5},{5,4},{6,7},{7,6},{8,9},{9,8},{10,11... | collective-permute-start | bytes 1769480 | tf_op jit(solution)/shard_map/ppermute | solution.py:958
  118.5 14.7 %collective-permute-start.38 = (bf16[96,768]{1,0:T(8,128)(2,1)S(1)}, bf16[96,768]{1,0:T(8,128)(2,1)S(1)}, u32[]{:S(2)}, u32[]{:S(2)}) collective-permute-start(bf16[96,768]{1,0:T(8,128)(2,1)S(1)} %get-tuple-element.382), channel_id=1, source_target_pairs={{0,2},{1,3},{2,4},{3,5},{4,6},{5,7},{6,0},{7,1},{8,10},{9,11},{10,... | collective-permute-start | bytes 442376 | tf_op jit(solution)/shard_map/ppermute | solution.py:962
  118.6 14.7 %collective-permute-start.39 = (bf16[96,768]{1,0:T(8,128)(2,1)S(1)}, bf16[96,768]{1,0:T(8,128)(2,1)S(1)}, u32[]{:S(2)}, u32[]{:S(2)}) collective-permute-start(bf16[96,768]{1,0:T(8,128)(2,1)S(1)} %get-tuple-element.381), channel_id=1, source_target_pairs={{0,4},{1,5},{2,6},{3,7},{4,0},{5,1},{6,2},{7,3},{8,12},{9,13},{10,... | collective-permute-start | bytes 442376 | tf_op jit(solution)/shard_map/ppermute | solution.py:962
  120.4 12.9 %collective-permute-start.40 = (bf16[96,768]{1,0:T(8,128)(2,1)S(1)}, bf16[96,768]{1,0:T(8,128)(2,1)S(1)}, u32[]{:S(2)}, u32[]{:S(2)}) collective-permute-start(bf16[96,768]{1,0:T(8,128)(2,1)S(1)} %get-tuple-element.380), channel_id=1, source_target_pairs={{0,6},{1,7},{2,0},{3,1},{4,2},{5,3},{6,4},{7,5},{8,14},{9,15},{10,... | collective-permute-start | bytes 442376 | tf_op jit(solution)/shard_map/ppermute | solution.py:962
  133.5 18.1 %collective-permute-start.43 = (bf16[2,4,120,384]{3,2,1,0:T(8,128)(2,1)S(1)}, bf16[2,4,120,384]{3,2,1,0:T(8,128)(2,1)S(1)}, u32[]{:S(2)}, u32[]{:S(2)}) collective-permute-start(bf16[2,4,120,384]{3,2,1,0:T(8,128)(2,1)S(1)} %fusion.1), channel_id=1, source_target_pairs={{0,16},{8,24},{16,0},{24,8},{1,17},{9,25},{17,1},{25,9},{2,18},{10... | collective-permute-start | bytes 2211848 | tf_op jit(solution)/shard_map/ppermute | solution.py:946
  134.8 14.6 %collective-permute-start.44 = (bf16[2,192,768]{2,1,0:T(8,128)(2,1)S(1)}, bf16[2,192,768]{2,1,0:T(8,128)(2,1)S(1)}, u32[]{:S(2)}, u32[]{:S(2)}) collective-permute-start(bf16[2,192,768]{2,1,0:T(8,128)(2,1)S(1)} %get-tuple-element.330), channel_id=1, source_target_pairs={{0,1},{1,0},{2,3},{3,2},{4,5},{5,4},{6,7},{7,6},{8,9},{9,8},{10,11... | collective-permute-start | bytes 1769480 | tf_op jit(solution)/shard_map/ppermute | solution.py:958
  151.7 14.1 %collective-permute-start.48 = (bf16[192,768]{1,0:T(8,128)(2,1)S(1)}, bf16[192,768]{1,0:T(8,128)(2,1)S(1)}, u32[]{:S(2)}, u32[]{:S(2)}) collective-permute-start(bf16[192,768]{1,0:T(8,128)(2,1)S(1)} %fusion.17), channel_id=1, source_target_pairs={{0,6},{1,7},{2,0},{3,1},{4,2},{5,3},{6,4},{7,5},{8,14},{9,15},{10,... | collective-permute-start | bytes 884744 | tf_op jit(solution)/shard_map/ppermute | solution.py:962
  154.2 11.7 %collective-permute-start.46 = (bf16[2,4,80,384]{3,2,1,0:T(8,128)(2,1)S(1)}, bf16[2,4,80,384]{3,2,1,0:T(8,128)(2,1)S(1)}, u32[]{:S(2)}, u32[]{:S(2)}) collective-permute-start(bf16[2,4,80,384]{3,2,1,0:T(8,128)(2,1)S(1)} %fusion), channel_id=1, source_target_pairs={{0,16},{8,24},{16,0},{24,8},{1,17},{9,25},{17,1},{25,9},{2,18},{10... | collective-permute-start | bytes 1474568 | tf_op jit(solution)/shard_map/ppermute | solution.py:946
  155.1 10.7 %collective-permute-start.47 = (bf16[4,120,384]{2,1,0:T(8,128)(2,1)S(1)}, bf16[4,120,384]{2,1,0:T(8,128)(2,1)S(1)}, u32[]{:S(2)}, u32[]{:S(2)}) collective-permute-start(bf16[4,120,384]{2,1,0:T(8,128)(2,1)S(1)} %fusion.2), channel_id=1, source_target_pairs={{0,1},{1,0},{2,3},{3,2},{4,5},{5,4},{6,7},{7,6},{8,9},{9,8},{10,11... | collective-permute-start | bytes 1105928 | tf_op jit(solution)/shard_map/ppermute | solution.py:958
  166.1 10.5 %collective-permute-start.52 = (bf16[192,768]{1,0:T(8,128)(2,1)S(1)}, bf16[192,768]{1,0:T(8,128)(2,1)S(1)}, u32[]{:S(2)}, u32[]{:S(2)}) collective-permute-start(bf16[192,768]{1,0:T(8,128)(2,1)S(1)} %get-tuple-element.388), channel_id=1, source_target_pairs={{0,6},{1,7},{2,0},{3,1},{4,2},{5,3},{6,4},{7,5},{8,14},{9,15},{10,... | collective-permute-start | bytes 884744 | tf_op jit(solution)/shard_map/ppermute | solution.py:962
  176.6 14.2 %collective-permute-start.56 = (bf16[384,768]{1,0:T(8,128)(2,1)S(1)}, bf16[384,768]{1,0:T(8,128)(2,1)S(1)}, u32[]{:S(2)}, u32[]{:S(2)}) collective-permute-start(bf16[384,768]{1,0:T(8,128)(2,1)S(1)} %pad_maximum_fusion.2), channel_id=1, source_target_pairs={{0,16},{8,24},{16,0},{24,8},{1,17},{9,25},{17,1},{25,9},{2,18},{10... | collective-permute-start | bytes 1769480 | tf_op jit(solution)/shard_map/ppermute | solution.py:946
  179.9 10.9 %collective-permute-start.54 = (bf16[200,384]{1,0:T(8,128)(2,1)S(1)}, bf16[200,384]{1,0:T(8,128)(2,1)S(1)}, u32[]{:S(2)}, u32[]{:S(2)}) collective-permute-start(bf16[200,384]{1,0:T(8,128)(2,1)S(1)} %pad_maximum_fusion.6), channel_id=1, source_target_pairs={{0,4},{1,5},{2,6},{3,7},{4,0},{5,1},{6,2},{7,3},{8,12},{9,13},{10,... | collective-permute-start | bytes 460808 | tf_op jit(solution)/shard_map/ppermute | solution.py:962
  180.0 10.8 %collective-permute-start.53 = (bf16[200,384]{1,0:T(8,128)(2,1)S(1)}, bf16[200,384]{1,0:T(8,128)(2,1)S(1)}, u32[]{:S(2)}, u32[]{:S(2)}) collective-permute-start(bf16[200,384]{1,0:T(8,128)(2,1)S(1)} %pad_maximum_fusion.5), channel_id=1, source_target_pairs={{0,2},{1,3},{2,4},{3,5},{4,6},{5,7},{6,0},{7,1},{8,10},{9,11},{10,... | collective-permute-start | bytes 460808 | tf_op jit(solution)/shard_map/ppermute | solution.py:962
  (38 other events, 273.8 us)

commit v13 on v12

--- a/solution.py
+++ b/solution.py
@@ -574,7 +574,7 @@
         lse_out[number] = top + jnp.log(total)
         return carry
 
-    lax.fori_loop(0, width // 128, pair, 0, unroll=2)
+    lax.fori_loop(0, width // 128, pair, 0, unroll=3)
     residual = f32(xo[pl.ds(0, tok), :]) + dot_nn(a_out[...], wo_out[...]) + vec[6:7]
     r_out[...] = residual
     hat, _rate = norm_parts(residual)

time: 200 us -> 200 us (level)
  transfers between devices with their start and end apart: 62 -> 62, of which waited for: 25 -> 25; matrix products, arithmetic and copies ran while one was open for 1% -> 1% of each run, Pallas kernels for 31% -> 30%
where the time goes in v13:
time: 200 us
  waiting for transfers between devices  69.4 us (35%)
  starting transfers between devices  64.1 us (32%)
  Pallas kernels  62 us (31%)
  other arithmetic  3.03 us (2%)
    ppermute x21, waiting for transfers between devices, to_z(): lax.ppermute(value, 'seq', [(k, (k + 2 * steps) % 8) for k in range(8)])  50.1 us
    ppermute x21, starting transfers between devices, to_z(): lax.ppermute(value, 'seq', [(k, (k + 2 * steps) % 8) for k in range(8)])  36.7 us
    ppermute x30, starting transfers between devices, swap_rep(): return lax.ppermute(value, 'rep', [(k, k ^ bit) for k in range(4)])  14.9 us
    pallas_call x1, Pallas kernels, on_device_fast(): call(front_kernel, [VM] * 6 + [AN] * 15, [VM] * 11, [shape_of((tok, width...  12.6 us
    ppermute x11, starting transfers between devices, to_y(): return lax.ppermute(value, 'seq', [(k, k ^ 1) for k in range(8)])  12.5 us
    ppermute x11, waiting for transfers between devices, to_y(): return lax.ppermute(value, 'seq', [(k, k ^ 1) for k in range(8)])  10.9 us
    pallas_call x1, Pallas kernels, on_device_fast(): call(back_b_kernel, [VM] * 14 + [AN] * 13, [VM] * 6, [shape_of((tok, widt...  10.8 us
    pallas_call x1, Pallas kernels, on_device_fast(): call(back_a_kernel, [VM] * 7, [AN] * 2 + [VM] * 2, [shape_of((2, 2, 4, 12...  10.3 us
  transfers between devices with their start and end apart: 62, of which 25 were waited for; matrix products, arithmetic and copies ran while one was open for 1% of the time, Pallas kernels for 30%

profile of v13, /device:TPU:0, one launch (start us, length us, event | category | flops | bytes accessed | tf_op | source)
XLA Modules:
  0.0 200.0 jit_solution(9676674538961642620)
XLA Ops:
  0.6 3.0 %collective-permute-start.3 = (bf16[192,768]{1,0:T(8,128)(2,1)}, bf16[192,768]{1,0:T(8,128)(2,1)S(1)}, u32[]{:S(2)}, u32[]{:S(2)}) collective-permute-start(bf16[192,768]{1,0:T(8,128)(2,1)} %bitcast.218), channel_id=1, source_target_pairs={{0,16},{8,24},{16,0},{24,8},{1,17},{9,25},{17,1},{25,9},{2,18},{10... | collective-permute-start | bytes 884744 | tf_op jit(solution)/shard_map/ppermute | solution.py:946
  3.6 2.7 %shard_map.186 = (bf16[200,768]{1,0:T(8,128)(2,1)}, bf16[48,1664]{1,0:T(8,128)(2,1)}, bf16[192,768]{1,0:T(8,128)(2,1)}, bf16[96,768]{1,0:T(8,128)(2,1)}, bf16[96,768]{1,0:T(8,128)(2,1)}) custom-call(bf16[1,192,768]{2,1,0:T(8,128)(2,1)} %tokens.1, s32[1,192]{1,0:T(1,128)} %segs.1, bf16[96,2304]{1,0:T(8,128)(2,1)} %own.3, bf16[96,768]{1,0:T(8,128)(2,1)} %own_o.1, ...), custom_call_target="tpu_custom_call" | custom-call | bytes 4000000 | tf_op jit(solution)/shard_map/pallas_call | solution.py:990
  8.0 2.2 %collective-permute-start.1 = (bf16[48,1664]{1,0:T(8,128)(2,1)}, bf16[48,1664]{1,0:T(8,128)(2,1)S(1)}, u32[]{:S(2)}, u32[]{:S(2)}) collective-permute-start(bf16[48,1664]{1,0:T(8,128)(2,1)} %get-tuple-element.192.first), channel_id=1, source_target_pairs={{0,6},{1,7},{2,0},{3,1},{4,2},{5,3},{6,4},{7,5},{8,14},{9,15},{10,... | collective-permute-start | bytes 479240 | tf_op jit(solution)/shard_map/ppermute | solution.py:962
  11.8 3.7 %collective-permute-done = bf16[48,1664]{1,0:T(8,128)(2,1)S(1)} collective-permute-done((bf16[48,1664]{1,0:T(8,128)(2,1)}, bf16[48,1664]{1,0:T(8,128)(2,1)S(1)}, u32[]{:S(2)}, u32[]{:S(2)}) %collective-permute-start) | collective-permute-done | bytes 159776 | tf_op jit(solution)/shard_map/ppermute | solution.py:962
  20.9 10.0 %collective-permute-done.4 = bf16[48,1664]{1,0:T(8,128)(2,1)S(1)} collective-permute-done((bf16[48,1664]{1,0:T(8,128)(2,1)S(1)}, bf16[48,1664]{1,0:T(8,128)(2,1)S(1)}, u32[]{:S(2)}, u32[]{:S(2)}) %collective-permute-start.4) | collective-permute-done | bytes 159776 | tf_op jit(solution)/shard_map/ppermute | solution.py:962
  33.1 3.8 %collective-permute-start.11 = (bf16[96,768]{1,0:T(8,128)(2,1)}, bf16[96,768]{1,0:T(8,128)(2,1)S(1)}, u32[]{:S(2)}, u32[]{:S(2)}) collective-permute-start(bf16[96,768]{1,0:T(8,128)(2,1)} %get-tuple-element.208), channel_id=1, source_target_pairs={{0,6},{1,7},{2,0},{3,1},{4,2},{5,3},{6,4},{7,5},{8,14},{9,15},{10,... | collective-permute-start | bytes 442376 | tf_op jit(solution)/shard_map/ppermute | solution.py:962
  36.9 7.0 %collective-permute-done.11.z3d = bf16[96,768]{1,0:T(8,128)(2,1)S(1)} collective-permute-done((bf16[96,768]{1,0:T(8,128)(2,1)}, bf16[96,768]{1,0:T(8,128)(2,1)S(1)}, u32[]{:S(2)}, u32[]{:S(2)}) %collective-permute-start.11) | collective-permute-done | bytes 147488 | tf_op jit(solution)/shard_map/ppermute | solution.py:962
  46.5 3.5 %collective-permute-start.15 = (bf16[96,768]{1,0:T(8,128)(2,1)S(1)}, bf16[96,768]{1,0:T(8,128)(2,1)S(1)}, u32[]{:S(2)}, u32[]{:S(2)}) collective-permute-start(bf16[96,768]{1,0:T(8,128)(2,1)S(1)} %copy-done.7), channel_id=1, source_target_pairs={{0,6},{1,7},{2,0},{3,1},{4,2},{5,3},{6,4},{7,5},{8,14},{9,15},{10,... | collective-permute-start | bytes 442376 | tf_op jit(solution)/shard_map/ppermute | solution.py:962
  50.0 4.9 %collective-permute-done.15.z3u = bf16[96,768]{1,0:T(8,128)(2,1)S(1)} collective-permute-done((bf16[96,768]{1,0:T(8,128)(2,1)S(1)}, bf16[96,768]{1,0:T(8,128)(2,1)S(1)}, u32[]{:S(2)}, u32[]{:S(2)}) %collective-permute-start.15) | collective-permute-done | bytes 147488 | tf_op jit(solution)/shard_map/ppermute | solution.py:962
  58.6 2.6 %collective-permute-done.20 = bf16[48,1664]{1,0:T(8,128)(2,1)S(1)} collective-permute-done((bf16[48,1664]{1,0:T(8,128)(2,1)S(1)}, bf16[48,1664]{1,0:T(8,128)(2,1)S(1)}, u32[]{:S(2)}, u32[]{:S(2)}) %collective-permute-start.20) | collective-permute-done | bytes 159776 | tf_op jit(solution)/shard_map/ppermute | solution.py:946
  63.8 12.6 %shard_map.187 = (bf16[192,768]{1,0:T(8,128)(2,1)S(1)}, bf16[960,1536]{1,0:T(8,128)(2,1)S(1)}, bf16[960,768]{1,0:T(8,128)(2,1)S(1)}, bf16[192,768]{1,0:T(8,128)(...) custom-call(s32[1,384]{1,0:T(1,128)S(1)} %pad_add_fusion.seg, ...), custom_call_target="tpu_custom_call" | custom-call | flops 7000000000 | bytes 12000000 | tf_op jit(solution)/shard_map/pallas_call | solution.py:1046
  78.7 2.0 %collective-permute-start.29 = (bf16[96,768]{1,0:T(8,128)(2,1)S(1)}, bf16[96,768]{1,0:T(8,128)(2,1)S(1)}, u32[]{:S(2)}, u32[]{:S(2)}) collective-permute-start(bf16[96,768]{1,0:T(8,128)(2,1)S(1)} %slice.252), channel_id=1, source_target_pairs={{0,2},{1,3},{2,4},{3,5},{4,6},{5,7},{6,0},{7,1},{8,10},{9,11},{10,... | collective-permute-start | bytes 442376 | tf_op jit(solution)/shard_map/ppermute | solution.py:962
  80.7 2.9 %shard_map.188 = (bf16[768,768]{1,0:T(8,128)(2,1)S(1)}, bf16[768,768]{1,0:T(8,128)(2,1)S(1)}) custom-call(bf16[192,768]{1,0:T(8,128)(2,1)S(1)} %copy-done.2, bf16[192,768]{1,0:T(8,128)(2,1)S(1)} %collective-permute-done.14.z1, bf16[192,768]{1,0:T(8,128)(2,1)S(1)} %collective-permute-done.23.z2, bf16[96,768]{1,0:T(8,128)(2,1)S(1)} %collective-permute-done.15.z3u, ...), custom_call_target="tpu_custom_call" | custom-call | bytes 5000000 | tf_op jit(solution)/shard_map/pallas_call | solution.py:1077
  84.4 2.3 %collective-permute-done.29.y2d = bf16[96,768]{1,0:T(8,128)(2,1)S(1)} collective-permute-done((bf16[96,768]{1,0:T(8,128)(2,1)S(1)}, bf16[96,768]{1,0:T(8,128)(2,1)S(1)}, u32[]{:S(2)}, u32[]{:S(2)}) %collective-permute-start.29) | collective-permute-done | bytes 147488 | tf_op jit(solution)/shard_map/ppermute | solution.py:962
  86.7 2.3 %shard_map.189 = (bf16[384,768]{1,0:T(8,128)(2,1)S(1)}, bf16[384,768]{1,0:T(8,128)(2,1)S(1)}, bf16[384,768]{1,0:T(8,128)(2,1)S(1)}, bf16[384,768]{1,0:T(8,128)(2...) custom-call(bf16[192,768]{1,0:T(8,128)(2,1)S(1)} %get-tuple-element., ...), custom_call_target="tpu_custom_call", output_to_operand_aliasing={{6}: (7, {}), {7}: (8, {})} | custom-call | flops 3000000000 | bytes 6000000 | tf_op jit(solution)/shard_map/pallas_call | solution.py:1092
  94.5 7.0 %shard_map.192 = (bf16[2,4,96,768]{3,2,1,0:T(8,128)(2,1)S(1)}, bf16[2,4,96,768]{3,2,1,0:T(8,128)(2,1)S(1)}, f32[1,768]{1,0:T(1,128)S(1)}, f32[2,192,768]{2,1,0:T(8,128)S(1)}, bf16[2,192,768]{2,1,0:T(8,128)(2,1)S(1)}) custom-call(bf16[768,768]{1,0:T(8,128)(2,1)S(1)} %get-tuple-element.287.hs, bf16[768,768]{1,0:T(8,128)(2,1)S(1)} %get-tuple-element.288.dys, ...), custom_call_target="tpu_custom_call" | custom-call | flops 3000000000 | bytes 6000000 | tf_op jit(solution)/shard_map/pallas_call | solution.py:1130
  105.1 10.3 %shard_map.194 = (bf16[2,2,4,120,384]{4,3,2,1,0:T(8,128)(2,1)S(1)}, bf16[2,2,4,120,384]{4,3,2,1,0:T(8,128)(2,1)S(1)}, bf16[192,384]{1,0:T(8,128)(2,1)S(1)}, bf16[960,768]{1,0:T(8,128)(2,1)S(1)}) custom-call(s32[1,384]{1,0:T(1,128)S(1)} %get-tuple-element.292.start_in, bf16[192,768]{1,0:T(8,128)(2,1)S(1)} %get-tuple-element.293.q_in, ...), custom_call_target="tpu_custom_call" | custom-call | flops 5000000000 | bytes 10000000 | tf_op jit(solution)/shard_map/pallas_call | solution.py:1166
  120.4 2.0 collective-permute-start.40
  122.4 10.8 %shard_map.195 = (bf16[192,384]{1,0:T(8,128)(2,1)S(1)}, bf16[960,768]{1,0:T(8,128)(2,1)S(1)}, f32[192,768]{1,0:T(8,128)S(1)}, bf16[2,192,768]{2,1,0:T(8,128)(2,1...) custom-call(s32[1,384]{1,0:T(1,128)S(1)} %get-tuple-element.292.start_in, ...), custom_call_target="tpu_custom_call" | custom-call | flops 6000000000 | bytes 10000000 | tf_op jit(solution)/shard_map/pallas_call | solution.py:1193
  135.6 4.8 %shard_map.196 = (bf16[2,2,4,80,384]{4,3,2,1,0:T(8,128)(2,1)S(1)}, bf16[2,2,4,80,384]{4,3,2,1,0:T(8,128)(2,1)S(1)}) custom-call(bf16[960,768]{1,0:T(8,128)(2,1)S(1)} %get-tuple-element.295.h_in, bf16[192,384]{1,0:T(8,128)(2,1)S(1)} %get-tuple-element.326.dq, bf16[960,768]{1,0:T(8,128)(2,1)S(1)} %get-tuple-element.327.dkv, ...), custom_call_target="tpu_custom_call" | custom-call | flops 3000000000 | bytes 6000000 | tf_op jit(solution)/shard_map/pallas_call | solution.py:1218
  141.2 2.2 %collective-permute-start.45 = (bf16[96,768]{1,0:T(8,128)(2,1)S(1)}, bf16[96,768]{1,0:T(8,128)(2,1)S(1)}, u32[]{:S(2)}, u32[]{:S(2)}) collective-permute-start(bf16[96,768]{1,0:T(8,128)(2,1)S(1)} %fusion.25), channel_id=1, source_target_pairs={{0,2},{1,3},{2,4},{3,5},{4,6},{5,7},{6,0},{7,1},{8,10},{9,11},{10,... | collective-permute-start | bytes 442376 | tf_op jit(solution)/shard_map/ppermute | solution.py:962
  143.4 5.4 %collective-permute-done.45 = bf16[96,768]{1,0:T(8,128)(2,1)S(1)} collective-permute-done((bf16[96,768]{1,0:T(8,128)(2,1)S(1)}, bf16[96,768]{1,0:T(8,128)(2,1)S(1)}, u32[]{:S(2)}, u32[]{:S(2)}) %collective-permute-start.45) | collective-permute-done | bytes 147488 | tf_op jit(solution)/shard_map/ppermute | solution.py:962
  149.4 2.2 %collective-permute-done.43 = bf16[2,4,120,384]{3,2,1,0:T(8,128)(2,1)S(1)} collective-permute-done((bf16[2,4,120,384]{3,2,1,0:T(8,128)(2,1)S(1)}, bf16[2,4,120,384]{3,2,1,0:T(8,128)(2,1)S(1)}, u32[]{:S(2)}, u32[]{:S(2)}) %collective-permute-start.43) | collective-permute-done | bytes 737312 | tf_op jit(solution)/shard_map/ppermute | solution.py:946
  151.7 2.4 %collective-permute-start.48 = (bf16[192,768]{1,0:T(8,128)(2,1)S(1)}, bf16[192,768]{1,0:T(8,128)(2,1)S(1)}, u32[]{:S(2)}, u32[]{:S(2)}) collective-permute-start(bf16[192,768]{1,0:T(8,128)(2,1)S(1)} %fusion.17), channel_id=1, source_target_pairs={{0,6},{1,7},{2,0},{3,1},{4,2},{5,3},{6,4},{7,5},{8,14},{9,15},{10,... | collective-permute-start | bytes 884744 | tf_op jit(solution)/shard_map/ppermute | solution.py:962
  156.8 3.8 %collective-permute-start.50 = (bf16[96,768]{1,0:T(8,128)(2,1)S(1)}, bf16[96,768]{1,0:T(8,128)(2,1)S(1)}, u32[]{:S(2)}, u32[]{:S(2)}) collective-permute-start(bf16[96,768]{1,0:T(8,128)(2,1)S(1)} %get-tuple-element.378), channel_id=1, source_target_pairs={{0,6},{1,7},{2,0},{3,1},{4,2},{5,3},{6,4},{7,5},{8,14},{9,15},{10,... | collective-permute-start | bytes 442376 | tf_op jit(solution)/shard_map/ppermute | solution.py:962
  160.7 4.4 %collective-permute-done.49 = bf16[96,768]{1,0:T(8,128)(2,1)S(1)} collective-permute-done((bf16[96,768]{1,0:T(8,128)(2,1)S(1)}, bf16[96,768]{1,0:T(8,128)(2,1)S(1)}, u32[]{:S(2)}, u32[]{:S(2)}) %collective-permute-start.49) | collective-permute-done | bytes 147488 | tf_op jit(solution)/shard_map/ppermute | solution.py:962
  166.1 4.1 %collective-permute-start.52 = (bf16[192,768]{1,0:T(8,128)(2,1)S(1)}, bf16[192,768]{1,0:T(8,128)(2,1)S(1)}, u32[]{:S(2)}, u32[]{:S(2)}) collective-permute-start(bf16[192,768]{1,0:T(8,128)(2,1)S(1)} %get-tuple-element.388), channel_id=1, source_target_pairs={{0,6},{1,7},{2,0},{3,1},{4,2},{5,3},{6,4},{7,5},{8,14},{9,15},{10,... | collective-permute-start | bytes 884744 | tf_op jit(solution)/shard_map/ppermute | solution.py:962
  171.4 5.2 %collective-permute-done.51 = bf16[4,80,384]{2,1,0:T(8,128)(2,1)S(1)} collective-permute-done((bf16[4,80,384]{2,1,0:T(8,128)(2,1)S(1)}, bf16[4,80,384]{2,1,0:T(8,128)(2,1)S(1)}, u32[]{:S(2)}, u32[]{:S(2)}) %collective-permute-start.51) | collective-permute-done | bytes 245792 | tf_op jit(solution)/shard_map/ppermute | solution.py:958
  177.1 2.7 %collective-permute-start.55 = (bf16[200,384]{1,0:T(8,128)(2,1)S(1)}, bf16[200,384]{1,0:T(8,128)(2,1)S(1)}, u32[]{:S(2)}, u32[]{:S(2)}) collective-permute-start(bf16[200,384]{1,0:T(8,128)(2,1)S(1)} %pad_maximum_fusion.7), channel_id=1, source_target_pairs={{0,6},{1,7},{2,0},{3,1},{4,2},{5,3},{6,4},{7,5},{8,14},{9,15},{10,... | collective-permute-start | bytes 460808 | tf_op jit(solution)/shard_map/ppermute | solution.py:962
  180.6 4.3 %collective-permute-done.55 = bf16[200,384]{1,0:T(8,128)(2,1)S(1)} collective-permute-done((bf16[200,384]{1,0:T(8,128)(2,1)S(1)}, bf16[200,384]{1,0:T(8,128)(2,1)S(1)}, u32[]{:S(2)}, u32[]{:S(2)}) %collective-permute-start.55) | collective-permute-done | bytes 153632 | tf_op jit(solution)/shard_map/ppermute | solution.py:962
  184.9 5.9 %collective-permute-done.54 = bf16[200,384]{1,0:T(8,128)(2,1)S(1)} collective-permute-done((bf16[200,384]{1,0:T(8,128)(2,1)S(1)}, bf16[200,384]{1,0:T(8,128)(2,1)S(1)}, u32[]{:S(2)}, u32[]{:S(2)}) %collective-permute-start.54) | collective-permute-done | bytes 153632 | tf_op jit(solution)/shard_map/ppermute | solution.py:962
  193.9 2.0 shard_map.198
  (157 shorter events, 53.7 us)
Async XLA Ops:
  0.6 16.3 %collective-permute-start.3 = (bf16[192,768]{1,0:T(8,128)(2,1)}, bf16[192,768]{1,0:T(8,128)(2,1)S(1)}, u32[]{:S(2)}, u32[]{:S(2)}) collective-permute-start(bf16[192,768]{1,0:T(8,128)(2,1)} %bitcast.218), channel_id=1, source_target_pairs={{0,16},{8,24},{16,0},{24,8},{1,17},{9,25},{17,1},{25,9},{2,18},{10... | collective-permute-start | bytes 884744 | tf_op jit(solution)/shard_map/ppermute | solution.py:946
  16.9 14.0 %collective-permute-start.5 = (bf16[200,768]{1,0:T(8,128)(2,1)}, bf16[200,768]{1,0:T(8,128)(2,1)S(1)}, u32[]{:S(2)}, u32[]{:S(2)}) collective-permute-start(bf16[200,768]{1,0:T(8,128)(2,1)} %get-tuple-element.197.xo), channel_id=1, source_target_pairs={{0,2},{1,3},{2,4},{3,5},{4,6},{5,7},{6,0},{7,1},{8,10},{9,11},{10,... | collective-permute-start | bytes 921608 | tf_op jit(solution)/shard_map/ppermute | solution.py:962
  18.1 12.9 %collective-permute-start.7 = (bf16[192,768]{1,0:T(8,128)(2,1)}, bf16[192,768]{1,0:T(8,128)(2,1)S(1)}, u32[]{:S(2)}, u32[]{:S(2)}) collective-permute-start(bf16[192,768]{1,0:T(8,128)(2,1)} %get-tuple-element.216.own), channel_id=1, source_target_pairs={{0,1},{1,0},{2,3},{3,2},{4,5},{5,4},{6,7},{7,6},{8,9},{9,8},{10,11... | collective-permute-start | bytes 884744 | tf_op jit(solution)/shard_map/ppermute | solution.py:958
  19.6 11.3 %collective-permute-start.4 = (bf16[48,1664]{1,0:T(8,128)(2,1)S(1)}, bf16[48,1664]{1,0:T(8,128)(2,1)S(1)}, u32[]{:S(2)}, u32[]{:S(2)}) collective-permute-start(bf16[48,1664]{1,0:T(8,128)(2,1)S(1)} %collective-permute-done), channel_id=1, source_target_pairs={{0,2},{1,3},{2,4},{3,5},{4,6},{5,7},{6,0},{7,1},{8,10},{9,11},{10,... | collective-permute-start | bytes 479240 | tf_op jit(solution)/shard_map/ppermute | solution.py:962
  20.4 10.6 %collective-permute-start.6 = (bf16[48,1664]{1,0:T(8,128)(2,1)S(1)}, bf16[48,1664]{1,0:T(8,128)(2,1)S(1)}, u32[]{:S(2)}, u32[]{:S(2)}) collective-permute-start(bf16[48,1664]{1,0:T(8,128)(2,1)S(1)} %collective-permute-done.2), channel_id=1, source_target_pairs={{0,16},{8,24},{16,0},{24,8},{1,17},{9,25},{17,1},{25,9},{2,18},{10... | collective-permute-start | bytes 479240 | tf_op jit(solution)/shard_map/ppermute | solution.py:946
  31.0 13.0 %collective-permute-start.8 = (bf16[144,1664]{1,0:T(8,128)(2,1)S(1)}, bf16[144,1664]{1,0:T(8,128)(2,1)S(1)}, u32[]{:S(2)}, u32[]{:S(2)}) collective-permute-start(bf16[144,1664]{1,0:T(8,128)(2,1)S(1)} %pad_maximum_fusion.3), channel_id=1, source_target_pairs={{0,1},{1,0},{2,3},{3,2},{4,5},{5,4},{6,7},{7,6},{8,9},{9,8},{10,11... | collective-permute-start | bytes 1437704 | tf_op jit(solution)/shard_map/ppermute | solution.py:958
  32.6 11.4 %collective-permute-start.9 = (bf16[144,1664]{1,0:T(8,128)(2,1)S(1)}, bf16[144,1664]{1,0:T(8,128)(2,1)S(1)}, u32[]{:S(2)}, u32[]{:S(2)}) collective-permute-start(bf16[144,1664]{1,0:T(8,128)(2,1)S(1)} %pad_maximum_fusion.3), channel_id=1, source_target_pairs={{0,16},{8,24},{16,0},{24,8},{1,17},{9,25},{17,1},{25,9},{2,18},{10... | collective-permute-start | bytes 1437704 | tf_op jit(solution)/shard_map/ppermute | solution.py:946
  33.1 10.9 %collective-permute-start.10 = (bf16[200,768]{1,0:T(8,128)(2,1)S(1)}, bf16[200,768]{1,0:T(8,128)(2,1)S(1)}, u32[]{:S(2)}, u32[]{:S(2)}) collective-permute-start(bf16[200,768]{1,0:T(8,128)(2,1)S(1)} %collective-permute-done.5.x2), channel_id=1, source_target_pairs={{0,2},{1,3},{2,4},{3,5},{4,6},{5,7},{6,0},{7,1},{8,10},{9,11},{10,... | collective-permute-start | bytes 921608 | tf_op jit(solution)/shard_map/ppermute | solution.py:962
  33.1 10.8 %collective-permute-start.11 = (bf16[96,768]{1,0:T(8,128)(2,1)}, bf16[96,768]{1,0:T(8,128)(2,1)S(1)}, u32[]{:S(2)}, u32[]{:S(2)}) collective-permute-start(bf16[96,768]{1,0:T(8,128)(2,1)} %get-tuple-element.208), channel_id=1, source_target_pairs={{0,6},{1,7},{2,0},{3,1},{4,2},{5,3},{6,4},{7,5},{8,14},{9,15},{10,... | collective-permute-start | bytes 442376 | tf_op jit(solution)/shard_map/ppermute | solution.py:962
  44.1 12.7 %collective-permute-start.12 = (bf16[2,200,768]{2,1,0:T(8,128)(2,1)S(1)}, bf16[2,200,768]{2,1,0:T(8,128)(2,1)S(1)}, u32[]{:S(2)}, u32[]{:S(2)}) collective-permute-start(bf16[2,200,768]{2,1,0:T(8,128)(2,1)S(1)} %pad_maximum_fusion), channel_id=1, source_target_pairs={{0,1},{1,0},{2,3},{3,2},{4,5},{5,4},{6,7},{7,6},{8,9},{9,8},{10,11... | collective-permute-start | bytes 1843208 | tf_op jit(solution)/shard_map/ppermute | solution.py:958
  44.7 10.2 %collective-permute-start.13 = (bf16[144,1664]{1,0:T(8,128)(2,1)S(1)}, bf16[144,1664]{1,0:T(8,128)(2,1)S(1)}, u32[]{:S(2)}, u32[]{:S(2)}) collective-permute-start(bf16[144,1664]{1,0:T(8,128)(2,1)S(1)} %collective-permute-done.8), channel_id=1, source_target_pairs={{0,16},{8,24},{16,0},{24,8},{1,17},{9,25},{17,1},{25,9},{2,18},{10... | collective-permute-start | bytes 1437704 | tf_op jit(solution)/shard_map/ppermute | solution.py:946
  61.2 15.2 %collective-permute-start.24 = (bf16[192,768]{1,0:T(8,128)(2,1)S(1)}, bf16[192,768]{1,0:T(8,128)(2,1)S(1)}, u32[]{:S(2)}, u32[]{:S(2)}) collective-permute-start(bf16[192,768]{1,0:T(8,128)(2,1)S(1)} %bitcast.219), channel_id=1, source_target_pairs={{0,8},{8,0},{16,24},{24,16},{1,9},{9,1},{17,25},{25,17},{2,10},{10... | collective-permute-start | bytes 884744 | tf_op jit(solution)/shard_map/ppermute | solution.py:946
  61.5 14.9 %collective-permute-start.25 = (bf16[192,768]{1,0:T(8,128)(2,1)S(1)}, bf16[192,768]{1,0:T(8,128)(2,1)S(1)}, u32[]{:S(2)}, u32[]{:S(2)}) collective-permute-start(bf16[192,768]{1,0:T(8,128)(2,1)S(1)} %collective-permute-done.3.dy_x), channel_id=1, source_target_pairs={{0,8},{8,0},{16,24},{24,16},{1,9},{9,1},{17,25},{25,17},{2,10},{10... | collective-permute-start | bytes 884744 | tf_op jit(solution)/shard_map/ppermute | solution.py:946
  61.7 15.6 %collective-permute-start.22 = (bf16[384,768]{1,0:T(8,128)(2,1)S(1)}, bf16[384,768]{1,0:T(8,128)(2,1)S(1)}, u32[]{:S(2)}, u32[]{:S(2)}) collective-permute-start(bf16[384,768]{1,0:T(8,128)(2,1)S(1)} %pad_maximum_fusion.1), channel_id=1, source_target_pairs={{0,1},{1,0},{2,3},{3,2},{4,5},{5,4},{6,7},{7,6},{8,9},{9,8},{10,11... | collective-permute-start | bytes 1769480 | tf_op jit(solution)/shard_map/ppermute | solution.py:958
  62.3 14.0 %collective-permute-start.23 = (bf16[192,768]{1,0:T(8,128)(2,1)S(1)}, bf16[192,768]{1,0:T(8,128)(2,1)S(1)}, u32[]{:S(2)}, u32[]{:S(2)}) collective-permute-start(bf16[192,768]{1,0:T(8,128)(2,1)S(1)} %collective-permute-done.14.z1), channel_id=1, source_target_pairs={{0,2},{1,3},{2,4},{3,5},{4,6},{5,7},{6,0},{7,1},{8,10},{9,11},{10,... | collective-permute-start | bytes 884744 | tf_op jit(solution)/shard_map/ppermute | solution.py:962
  77.3 9.4 %collective-permute-start.26 = (bf16[192,768]{1,0:T(8,128)(2,1)S(1)}, bf16[192,768]{1,0:T(8,128)(2,1)S(1)}, u32[]{:S(2)}, u32[]{:S(2)}) collective-permute-start(bf16[192,768]{1,0:T(8,128)(2,1)S(1)} %get-tuple-element.250.h_own), channel_id=1, source_target_pairs={{0,16},{8,24},{16,0},{24,8},{1,17},{9,25},{17,1},{25,9},{2,18},{10... | collective-permute-start | bytes 884744 | tf_op jit(solution)/shard_map/ppermute | solution.py:946
  102.2 14.6 %collective-permute-start.34 = (bf16[4,96,768]{2,1,0:T(8,128)(2,1)S(1)}, bf16[4,96,768]{2,1,0:T(8,128)(2,1)S(1)}, u32[]{:S(2)}, u32[]{:S(2)}) collective-permute-start(bf16[4,96,768]{2,1,0:T(8,128)(2,1)S(1)} %slice_bitcast_fusion.1), channel_id=1, source_target_pairs={{0,1},{1,0},{2,3},{3,2},{4,5},{5,4},{6,7},{7,6},{8,9},{9,8},{10,11... | collective-permute-start | bytes 1769480 | tf_op jit(solution)/shard_map/ppermute | solution.py:958
  103.8 13.1 %collective-permute-start.35 = (bf16[2,192,768]{2,1,0:T(8,128)(2,1)S(1)}, bf16[2,192,768]{2,1,0:T(8,128)(2,1)S(1)}, u32[]{:S(2)}, u32[]{:S(2)}) collective-permute-start(bf16[2,192,768]{2,1,0:T(8,128)(2,1)S(1)} %get-tuple-element.312), channel_id=1, source_target_pairs={{0,8},{8,0},{16,24},{24,16},{1,9},{9,1},{17,25},{25,17},{2,10},{10... | collective-permute-start | bytes 1769480 | tf_op jit(solution)/shard_map/ppermute | solution.py:946
  116.9 16.4 %collective-permute-start.36 = (bf16[2,2,4,120,384]{4,3,2,1,0:T(8,128)(2,1)S(1)}, bf16[2,2,4,120,384]{4,3,2,1,0:T(8,128)(2,1)S(1)}, u32[]{:S(2)}, u32[]{:S(2)}) collective-permute-start(bf16[2,2,4,120,384]{4,3,2,1,0:T(8,128)(2,1)S(1)} %get-tuple-element.321), channel_id=1, source_target_pairs={{0,8},{8,0},{16,24},{24,16},{1,9},{9,1},{17,25},{25,17},{2,10},{10... | collective-permute-start | bytes 4423688 | tf_op jit(solution)/shard_map/ppermute | solution.py:946
  116.9 16.4 %collective-permute-start.37 = (bf16[4,96,768]{2,1,0:T(8,128)(2,1)S(1)}, bf16[4,96,768]{2,1,0:T(8,128)(2,1)S(1)}, u32[]{:S(2)}, u32[]{:S(2)}) collective-permute-start(bf16[4,96,768]{2,1,0:T(8,128)(2,1)S(1)} %slice_bitcast_fusion), channel_id=1, source_target_pairs={{0,1},{1,0},{2,3},{3,2},{4,5},{5,4},{6,7},{7,6},{8,9},{9,8},{10,11... | collective-permute-start | bytes 1769480 | tf_op jit(solution)/shard_map/ppermute | solution.py:958
  118.5 14.7 %collective-permute-start.38 = (bf16[96,768]{1,0:T(8,128)(2,1)S(1)}, bf16[96,768]{1,0:T(8,128)(2,1)S(1)}, u32[]{:S(2)}, u32[]{:S(2)}) collective-permute-start(bf16[96,768]{1,0:T(8,128)(2,1)S(1)} %get-tuple-element.382), channel_id=1, source_target_pairs={{0,2},{1,3},{2,4},{3,5},{4,6},{5,7},{6,0},{7,1},{8,10},{9,11},{10,... | collective-permute-start | bytes 442376 | tf_op jit(solution)/shard_map/ppermute | solution.py:962
  118.6 14.7 %collective-permute-start.39 = (bf16[96,768]{1,0:T(8,128)(2,1)S(1)}, bf16[96,768]{1,0:T(8,128)(2,1)S(1)}, u32[]{:S(2)}, u32[]{:S(2)}) collective-permute-start(bf16[96,768]{1,0:T(8,128)(2,1)S(1)} %get-tuple-element.381), channel_id=1, source_target_pairs={{0,4},{1,5},{2,6},{3,7},{4,0},{5,1},{6,2},{7,3},{8,12},{9,13},{10,... | collective-permute-start | bytes 442376 | tf_op jit(solution)/shard_map/ppermute | solution.py:962
  120.4 12.9 %collective-permute-start.40 = (bf16[96,768]{1,0:T(8,128)(2,1)S(1)}, bf16[96,768]{1,0:T(8,128)(2,1)S(1)}, u32[]{:S(2)}, u32[]{:S(2)}) collective-permute-start(bf16[96,768]{1,0:T(8,128)(2,1)S(1)} %get-tuple-element.380), channel_id=1, source_target_pairs={{0,6},{1,7},{2,0},{3,1},{4,2},{5,3},{6,4},{7,5},{8,14},{9,15},{10,... | collective-permute-start | bytes 442376 | tf_op jit(solution)/shard_map/ppermute | solution.py:962
  133.5 18.1 %collective-permute-start.43 = (bf16[2,4,120,384]{3,2,1,0:T(8,128)(2,1)S(1)}, bf16[2,4,120,384]{3,2,1,0:T(8,128)(2,1)S(1)}, u32[]{:S(2)}, u32[]{:S(2)}) collective-permute-start(bf16[2,4,120,384]{3,2,1,0:T(8,128)(2,1)S(1)} %fusion.1), channel_id=1, source_target_pairs={{0,16},{8,24},{16,0},{24,8},{1,17},{9,25},{17,1},{25,9},{2,18},{10... | collective-permute-start | bytes 2211848 | tf_op jit(solution)/shard_map/ppermute | solution.py:946
  134.8 14.6 %collective-permute-start.44 = (bf16[2,192,768]{2,1,0:T(8,128)(2,1)S(1)}, bf16[2,192,768]{2,1,0:T(8,128)(2,1)S(1)}, u32[]{:S(2)}, u32[]{:S(2)}) collective-permute-start(bf16[2,192,768]{2,1,0:T(8,128)(2,1)S(1)} %get-tuple-element.330), channel_id=1, source_target_pairs={{0,1},{1,0},{2,3},{3,2},{4,5},{5,4},{6,7},{7,6},{8,9},{9,8},{10,11... | collective-permute-start | bytes 1769480 | tf_op jit(solution)/shard_map/ppermute | solution.py:958
  151.7 14.1 %collective-permute-start.48 = (bf16[192,768]{1,0:T(8,128)(2,1)S(1)}, bf16[192,768]{1,0:T(8,128)(2,1)S(1)}, u32[]{:S(2)}, u32[]{:S(2)}) collective-permute-start(bf16[192,768]{1,0:T(8,128)(2,1)S(1)} %fusion.17), channel_id=1, source_target_pairs={{0,6},{1,7},{2,0},{3,1},{4,2},{5,3},{6,4},{7,5},{8,14},{9,15},{10,... | collective-permute-start | bytes 884744 | tf_op jit(solution)/shard_map/ppermute | solution.py:962
  154.2 11.7 %collective-permute-start.46 = (bf16[2,4,80,384]{3,2,1,0:T(8,128)(2,1)S(1)}, bf16[2,4,80,384]{3,2,1,0:T(8,128)(2,1)S(1)}, u32[]{:S(2)}, u32[]{:S(2)}) collective-permute-start(bf16[2,4,80,384]{3,2,1,0:T(8,128)(2,1)S(1)} %fusion), channel_id=1, source_target_pairs={{0,16},{8,24},{16,0},{24,8},{1,17},{9,25},{17,1},{25,9},{2,18},{10... | collective-permute-start | bytes 1474568 | tf_op jit(solution)/shard_map/ppermute | solution.py:946
  155.1 10.7 %collective-permute-start.47 = (bf16[4,120,384]{2,1,0:T(8,128)(2,1)S(1)}, bf16[4,120,384]{2,1,0:T(8,128)(2,1)S(1)}, u32[]{:S(2)}, u32[]{:S(2)}) collective-permute-start(bf16[4,120,384]{2,1,0:T(8,128)(2,1)S(1)} %fusion.2), channel_id=1, source_target_pairs={{0,1},{1,0},{2,3},{3,2},{4,5},{5,4},{6,7},{7,6},{8,9},{9,8},{10,11... | collective-permute-start | bytes 1105928 | tf_op jit(solution)/shard_map/ppermute | solution.py:958
  166.1 10.5 %collective-permute-start.52 = (bf16[192,768]{1,0:T(8,128)(2,1)S(1)}, bf16[192,768]{1,0:T(8,128)(2,1)S(1)}, u32[]{:S(2)}, u32[]{:S(2)}) collective-permute-start(bf16[192,768]{1,0:T(8,128)(2,1)S(1)} %get-tuple-element.388), channel_id=1, source_target_pairs={{0,6},{1,7},{2,0},{3,1},{4,2},{5,3},{6,4},{7,5},{8,14},{9,15},{10,... | collective-permute-start | bytes 884744 | tf_op jit(solution)/shard_map/ppermute | solution.py:962
  176.6 14.2 %collective-permute-start.56 = (bf16[384,768]{1,0:T(8,128)(2,1)S(1)}, bf16[384,768]{1,0:T(8,128)(2,1)S(1)}, u32[]{:S(2)}, u32[]{:S(2)}) collective-permute-start(bf16[384,768]{1,0:T(8,128)(2,1)S(1)} %pad_maximum_fusion.2), channel_id=1, source_target_pairs={{0,16},{8,24},{16,0},{24,8},{1,17},{9,25},{17,1},{25,9},{2,18},{10... | collective-permute-start | bytes 1769480 | tf_op jit(solution)/shard_map/ppermute | solution.py:946
  179.9 10.9 %collective-permute-start.54 = (bf16[200,384]{1,0:T(8,128)(2,1)S(1)}, bf16[200,384]{1,0:T(8,128)(2,1)S(1)}, u32[]{:S(2)}, u32[]{:S(2)}) collective-permute-start(bf16[200,384]{1,0:T(8,128)(2,1)S(1)} %pad_maximum_fusion.6), channel_id=1, source_target_pairs={{0,4},{1,5},{2,6},{3,7},{4,0},{5,1},{6,2},{7,3},{8,12},{9,13},{10,... | collective-permute-start | bytes 460808 | tf_op jit(solution)/shard_map/ppermute | solution.py:962
  180.0 10.8 %collective-permute-start.53 = (bf16[200,384]{1,0:T(8,128)(2,1)S(1)}, bf16[200,384]{1,0:T(8,128)(2,1)S(1)}, u32[]{:S(2)}, u32[]{:S(2)}) collective-permute-start(bf16[200,384]{1,0:T(8,128)(2,1)S(1)} %pad_maximum_fusion.5), channel_id=1, source_target_pairs={{0,2},{1,3},{2,4},{3,5},{4,6},{5,7},{6,0},{7,1},{8,10},{9,11},{10,... | collective-permute-start | bytes 460808 | tf_op jit(solution)/shard_map/ppermute | solution.py:962
  (38 other events, 273.9 us)
